TPU v7x, 128 devices: a whole 4x4x4 slice. The times are simulated.
128 devices in a mesh: seq: 32 (over x, z, core), head: 4 (over y).
Axes of the slice: x: 4, y: 4, z: 4, core: 2. Of those that a mesh axis runs over, the one named last changes fastest.
Arguments:
- tokens: bfloat16 [32768, 2048], P('seq', 'head'), may hold values from -64 to 64
- project_weights: bfloat16 [2048, 3, 2048], P(None, None, 'head'), may hold values from -0.125 to 0.125
- output_weights: bfloat16 [2048, 2048], P('head'), may hold values from -0.125 to 0.125
- cluster_ids: int32 [16, 32768, 1], P('head', 'seq'), may hold values from 0 to 255; in each aligned block of 1024 rows (0 to 1023, 1024 to 2047, ..., all dimensions but the last counted through in order) at most 8 rows name the same one
Outputs:
- mixed: bfloat16 [32768, 2048], P('seq', 'head')
- key_sums: float32 [16, 256, 128], P('head', 'seq')
Inputs may be any that keep to these rules, and one draw needn't show every extreme that they name: `cluster_ids`: in each head, the 1024 rows of one index of seq name no cluster more than 8 times.
All inputs are finite; a program needn't handle non-finite values.
Results may differ from a plain program's by a relative error of at most 0.012.
The roundings to bfloat16 on the way count: a program that leaves them out, or rounds other values in their place, can miss the bound.
Values may be sent and summed in bfloat16 or wider, within the bound.
No kernel may reach another device: no remote copies, remote signals or barrier semaphores. Data moves between devices by JAX's collectives and lax.ppermute only.
A program may use at most 128 MiB of HBM per device.

v0:
```python
import functools
import math

import jax
import jax.numpy as jnp
from jax import lax
from jax.experimental import pallas as pl
from jax.experimental.pallas import tpu as pltpu
from jax.sharding import Mesh
from jax.sharding import PartitionSpec as P

HEAD_DIM = 128
CLUST_DEV = 8
SLOT = 8
SEQ = ("seq_0", "seq_1", "seq_2")
F32 = jnp.float32
BF16 = jnp.bfloat16


def shifted(array, by):
    count = lax.axis_size("head")
    return lax.ppermute(array, "head", [(i, (i + by) % count) for i in range(count)])


def params(**more):
    return pltpu.CompilerParams(vmem_limit_bytes=56 * 1024 * 1024, **more)


def first_blocks_kernel(where, own, left, right, w_own, w_left, w_right, out):
    total = jnp.dot(own[...], w_own[0], preferred_element_type=F32)
    total += jnp.dot(left[...], w_left[0], preferred_element_type=F32)
    total += jnp.dot(right[...], w_right[0], preferred_element_type=F32)
    out[0] = total


def first_blocks(where, own, left, right, weights):
    kinds, _, width = weights.shape
    rows, depth = own.shape
    whole = pl.BlockSpec((rows, depth), lambda j, w: (0, 0))
    return pl.pallas_call(
        first_blocks_kernel,
        out_shape=jax.ShapeDtypeStruct((kinds, rows, width), F32),
        grid_spec=pltpu.PrefetchScalarGridSpec(
            num_scalar_prefetch=1,
            grid=(kinds,),
            in_specs=[whole, whole, whole]
            + [pl.BlockSpec((1, depth, width), functools.partial(lambda b, j, w: (j, w[b], 0), b)) for b in range(3)],
            out_specs=pl.BlockSpec((1, rows, width), lambda j, w: (j, 0, 0)),
        ),
        compiler_params=params(),
        name="first_blocks",
    )(where, own, left, right, weights, weights, weights)


def pack_kernel(where, part, far_top, far_bottom, w_far, slot_of, out, projected):
    head = pl.program_id(0)
    kinds, rows, width = part.shape
    half = rows // 2
    heads = width // HEAD_DIM

    @pl.when(head == 0)
    def _():
        for kind in range(kinds):
            top = part[kind, :half] + jnp.dot(far_top[...], w_far[kind], preferred_element_type=F32)
            bottom = part[kind, half:] + jnp.dot(far_bottom[...], w_far[kind], preferred_element_type=F32)
            for h in range(heads):
                cols = slice(h * HEAD_DIM, (h + 1) * HEAD_DIM)
                to = slice(kind * HEAD_DIM, (kind + 1) * HEAD_DIM)
                projected[h, :half, to] = top[:, cols].astype(BF16)
                projected[h, half:, to] = bottom[:, cols].astype(BF16)

    rows_in = projected[head]
    slot_row = slot_of[0]
    devices, _, per_device, _ = out.shape
    step = 4
    chunk = step * per_device

    def body(i, carry):
        iota = lax.broadcasted_iota(jnp.int32, (chunk, rows), 0) + i * chunk
        onehot = jnp.where(iota == slot_row, 1.0, 0.0).astype(BF16)
        packed = jnp.dot(onehot, rows_in, preferred_element_type=F32).astype(BF16)
        out[pl.ds(i * step, step), 0] = packed.reshape(step, per_device, packed.shape[-1])
        return carry

    lax.fori_loop(0, devices // step, body, 0, unroll=2)


def pack(where, part, far_top, far_bottom, weights, slot_index, devices):
    kinds, rows, width = part.shape
    heads = width // HEAD_DIM
    depth = far_top.shape[1]
    lanes = kinds * HEAD_DIM
    per_device = CLUST_DEV * SLOT
    return pl.pallas_call(
        pack_kernel,
        out_shape=jax.ShapeDtypeStruct((devices, heads, per_device, lanes), BF16),
        grid_spec=pltpu.PrefetchScalarGridSpec(
            num_scalar_prefetch=1,
            grid=(heads,),
            in_specs=[
                pl.BlockSpec((kinds, rows, width), lambda h, w: (0, 0, 0)),
                pl.BlockSpec((rows // 2, depth), lambda h, w: (0, 0)),
                pl.BlockSpec((rows // 2, depth), lambda h, w: (0, 0)),
                pl.BlockSpec((kinds, depth, width), lambda h, w: (0, w[3], 0)),
                pl.BlockSpec((1, 1, rows), lambda h, w: (h, 0, 0)),
            ],
            out_specs=pl.BlockSpec((devices, 1, per_device, lanes), lambda h, w: (0, h, 0, 0)),
            scratch_shapes=[pltpu.VMEM((heads, rows, lanes), BF16)],
        ),
        compiler_params=params(),
        name="pack",
    )(where, part, far_top, far_bottom, weights, slot_index[:, None, :])


def attend_kernel(received, bias, out):
    devices, heads, _, slot, _ = received.shape
    bucket = devices * slot
    scale = 1.0 / math.sqrt(HEAD_DIM)
    rows = lax.broadcasted_iota(jnp.int32, (bucket, bucket), 0)
    cols = lax.broadcasted_iota(jnp.int32, (bucket, bucket), 1)
    causal = cols <= rows
    for h in range(heads):
        both = received[:, h, 0].reshape(bucket, 3 * HEAD_DIM)
        query, key, value = (both[:, i * HEAD_DIM : (i + 1) * HEAD_DIM] for i in range(3))
        scores = lax.dot_general(query, key, (((1,), (1,)), ((), ())), preferred_element_type=F32) * scale
        scores = jnp.where(causal & (bias[0, h : h + 1] > 0), scores, -1e30)
        row_max = jnp.max(scores, axis=-1, keepdims=True)
        exponentials = jnp.exp(scores - row_max)
        weights = (exponentials / jnp.sum(exponentials, axis=-1, keepdims=True)).astype(BF16)
        result = jnp.dot(weights, value, preferred_element_type=F32).astype(BF16)
        out[:, h, 0] = result.reshape(devices, slot, HEAD_DIM)


def attend(received, live):
    devices, heads, clusters, slot, lanes = received.shape
    bucket = devices * slot
    return pl.pallas_call(
        attend_kernel,
        out_shape=jax.ShapeDtypeStruct((devices, heads, clusters, slot, HEAD_DIM), BF16),
        grid=(clusters,),
        in_specs=[
            pl.BlockSpec((devices, heads, 1, slot, lanes), lambda c: (0, 0, c, 0, 0)),
            pl.BlockSpec((1, heads, bucket), lambda c: (c, 0, 0)),
        ],
        out_specs=pl.BlockSpec((devices, heads, 1, slot, HEAD_DIM), lambda c: (0, 0, c, 0, 0)),
        compiler_params=params(),
        name="attend",
    )(received, live)


def key_sums_kernel(keys, out):
    devices, heads, _, slot, width = keys.shape
    for h in range(heads):
        key = keys[:, h, 0].astype(F32)
        scaled = key * lax.rsqrt(jnp.mean(key * key, axis=-1, keepdims=True) + 1e-06)
        unit = (scaled / math.sqrt(width)).astype(BF16).astype(F32)
        out[0, h : h + 1] = jnp.sum(jnp.sum(unit, axis=0), axis=0, keepdims=True)


def key_sums(received):
    devices, heads, clusters, slot, _ = received.shape
    return pl.pallas_call(
        key_sums_kernel,
        out_shape=jax.ShapeDtypeStruct((clusters, heads, HEAD_DIM), F32),
        grid=(clusters,),
        in_specs=[pl.BlockSpec((devices, heads, 1, slot, HEAD_DIM), lambda c: (0, 0, c, 0, 1))],
        out_specs=pl.BlockSpec((1, heads, HEAD_DIM), lambda c: (c, 0, 0)),
        compiler_params=params(),
        name="key_sums",
    )(received)


def unpack_kernel(returned, slot_of, out):
    devices, _, per_device, width = returned.shape
    slots = devices * per_device
    rows = out.shape[0]
    source = returned[:, 0].reshape(slots, width)
    chunk = 256

    def body(i, carry):
        at = pl.ds(pl.multiple_of(i * chunk, chunk), chunk)
        iota = lax.broadcasted_iota(jnp.int32, (chunk, slots), 1)
        onehot = jnp.where(iota == slot_of[0, at], 1.0, 0.0).astype(BF16)
        out[at] = jnp.dot(onehot, source, preferred_element_type=F32).astype(BF16)
        return carry

    lax.fori_loop(0, rows // chunk, body, 0, unroll=2)


def unpack(returned, slot_index):
    devices, heads, per_device, width = returned.shape
    rows = slot_index.shape[1]
    return pl.pallas_call(
        unpack_kernel,
        out_shape=jax.ShapeDtypeStruct((rows, heads * width), BF16),
        grid=(heads,),
        in_specs=[
            pl.BlockSpec((devices, 1, per_device, width), lambda h: (0, h, 0, 0)),
            pl.BlockSpec((1, rows, 1), lambda h: (h, 0, 0)),
        ],
        out_specs=pl.BlockSpec((rows, width), lambda h: (0, h)),
        compiler_params=params(),
        name="unpack",
    )(returned, slot_index[:, :, None])


def ring(block):
    half = block.shape[0] // 2
    left = shifted(block, 1)
    right = shifted(block, -1)
    return left, right, shifted(left[:half], 1), shifted(right[half:], -1)


def local(tokens, project_weights, output_weights, cluster_ids):
    seq_count = lax.axis_size(SEQ)
    groups = lax.axis_size("head")
    here = lax.axis_index("head")
    width = output_weights.shape[0]
    heads = width // HEAD_DIM
    rows = tokens.shape[0]
    clusters = CLUST_DEV * seq_count

    assigned = cluster_ids[:, :, 0]
    matches = assigned[:, :, None] == jnp.arange(clusters, dtype=jnp.int32)
    counts = jnp.sum(matches.astype(jnp.int32), axis=1)
    row_iota = jnp.arange(rows, dtype=jnp.int32)
    earlier = (row_iota[None, :] < row_iota[:, None]).astype(BF16)
    before = jnp.einsum("ts,hsc->htc", earlier, matches.astype(BF16), preferred_element_type=F32)
    slot_rank = jnp.sum(jnp.where(matches, before, 0.0), axis=2).astype(jnp.int32)
    slot_index = assigned * SLOT + slot_rank

    by_owner = counts.T.reshape(seq_count, CLUST_DEV, heads)
    filled = lax.all_to_all(by_owner, SEQ, 0, 0, tiled=True)
    live = (filled.transpose(1, 2, 0)[..., None] > jnp.arange(SLOT, dtype=jnp.int32)).astype(F32)
    live = live.reshape(CLUST_DEV, heads, seq_count * SLOT)

    weights = project_weights.transpose(1, 0, 2)
    where = jnp.stack([here, (here - 1) % groups, (here + 1) % groups, (here + 2) % groups]).astype(jnp.int32)
    left, right, far_top, far_bottom = ring(tokens)
    part = first_blocks(where, tokens, left, right, weights)
    packed = pack(where, part, far_top, far_bottom, weights, slot_index, seq_count)

    received = lax.all_to_all(packed, SEQ, 0, 0, tiled=True)

    out_weights, _ = lax.optimization_barrier((output_weights, far_top))
    out_blocks = []
    for by in range(groups):
        block = lax.dynamic_slice(out_weights, (0, (here + by) % groups * width), (width, width))
        out_blocks.append(shifted(block, by) if by else block)

    received = received.reshape(seq_count, heads, CLUST_DEV, SLOT, 3 * HEAD_DIM)
    bucket_out = attend(received, live)
    owned = key_sums(received)
    returned = lax.all_to_all(bucket_out.reshape(seq_count, heads, CLUST_DEV * SLOT, HEAD_DIM), SEQ, 0, 0, tiled=True)
    attended = unpack(returned, slot_index)
    left, right, far_top, far_bottom = ring(attended)

    def times(block, by):
        return jnp.dot(block, out_blocks[by], preferred_element_type=F32)

    near = times(attended, 0) + times(left, 1) + times(right, 3)
    mixed = (near + times(jnp.concatenate([far_top, far_bottom]), 2)).astype(BF16)
    return (mixed, owned.transpose(1, 0, 2))


def solution(mesh):
    split = Mesh(
        mesh.devices.reshape(4, 4, 2, mesh.shape["head"]), ("seq_0", "seq_1", "seq_2", "head")
    )
    in_specs = (P(SEQ, "head"), P(None, None, "head"), P("head", None), P("head", SEQ, None))
    out_specs = (P(SEQ, "head"), P("head", SEQ, None))
    return jax.shard_map(local, mesh=split, in_specs=in_specs, out_specs=out_specs, check_vma=False)
```

profile of v0, /device:TPU:1, one launch (start us, length us, event | category | flops | bytes accessed | tf_op | source)
XLA Modules:
  0.0 277.4 jit_solution(10301807551105727126)
XLA Ops:
  0.6 2.2 collective-permute-start
  2.8 1.5 collective-permute-start.1
  4.3 0.7 copy.43
  5.1 0.5 convert_reduce_fusion
  5.6 0.1 reshape.49
  5.7 0.7 copy.32
  6.3 9.0 %all-to-all-start.1 = ((s32[32,8,4]{1,2,0:T(4,128)}), s32[32,8,4]{1,2,0:T(4,128)S(1)}, u32[]{:S(2)}, u32[]{:S(2)}) async-start(s32[32,8,4]{1,2,0:T(4,128)} %copy.32), calls=%async_computation.1 | async-start | bytes 131072 | tf_op jit(solution)/shard_map/all_to_all | solution.py:233
  15.4 1.4 copy.29
  16.7 2.5 fusion
  19.3 2.0 copy.36
  21.2 6.0 %collective-permute-done.left = bf16[1024,512]{1,0:T(8,128)(2,1)S(1)} collective-permute-done((bf16[1024,512]{1,0:T(8,128)(2,1)}, bf16[1024,512]{1,0:T(8,128)(2,1)S(1)}, u32[]{:S(2)}, u32[]{:S(2)}) %collective-permute-start) | collective-permute-done | bytes 1048608 | tf_op jit(solution)/shard_map/ppermute | solution.py:22
  27.4 1.3 slice.17
  28.7 2.5 collective-permute-start.3
  31.2 3.4 %multiply_add_fusion = (s32[4,1024,1]{2,1,0:T(8,128)}, s32[4,1024]{1,0:T(4,128)S(1)}) fusion(s32[4,1024,1]{2,1,0:T(8,128)} %copy.36, s32[4,1024,1]{2,1,0:T(8,128)S(1)} %copy.29), kind=kLoop, calls=%fused_computation.9 | loop fusion | flops 8192 | bytes 65536 | tf_op jit(solution)/shard_map/add | solution.py:230
  34.6 0.6 reshape_add_fusion.slot_of
  35.2 0.6 pad_add_fusion.where
  35.8 10.2 %first_blocks.1.part = f32[3,1024,512]{2,1,0:T(8,128)} custom-call(s32[4]{0:T(128)} %pad_add_fusion.where, bf16[1024,512]{1,0:T(8,128)(2,1)} %own.1, bf16[1024,512]{1,0:T(8,128)(2,1)} %copy-done.1, bf16[1024,512]{1,0:T(8,128)(2,1)} %collective-permute-done.1.right, bf16[3,2048,512]{2,1,0:T(8,128)(2,1)} %bitcast.36, bf16[3,2048,512]{2,1,0:T(8,128)(2,1)} %bitcast.37, ...), custom_call_target="tpu_custom_call" | custom-call | tf_op jit(solution)/shard_map/first_blocks/pallas_call | solution.py:40
  46.1 0.8 copy-done.2
  46.9 0.8 copy-done.3
  47.6 18.7 %pack.1 = bf16[32,4,64,384]{3,2,1,0:T(8,128)(2,1)} custom-call(s32[4]{0:T(128)} %pad_add_fusion.where, f32[3,1024,512]{2,1,0:T(8,128)} %first_blocks.1.part, bf16[512,512]{1,0:T(8,128)(2,1)} %copy-done.2, bf16[512,512]{1,0:T(8,128)(2,1)} %copy-done.3, bf16[3,2048,512]{2,1,0:T(8,128)(2,1)} %bitcast.39, s32[4,1,1024]{2,1,0:T(1,128)} %reshape_add_fusion.slot_of), custom_call_target="tpu_custom_call" | custom-call | tf_op jit(solution)/shard_map/pack/pallas_call | solution.py:94
  66.3 9.9 %all-to-all-start = ((bf16[32,4,64,384]{3,2,1,0:T(8,128)(2,1)}), bf16[32,4,64,384]{3,2,1,0:T(8,128)(2,1)}, u32[]{:S(2)}, u32[]{:S(2)}) async-start(bf16[32,4,64,384]{3,2,1,0:T(8,128)(2,1)} %pack.1), calls=%async_computation | async-start | bytes 12582912 | tf_op jit(solution)/shard_map/all_to_all | solution.py:243
  76.2 0.1 gt.23
  76.3 0.1 copy.33
  76.4 0.2 gt.20
  76.6 0.3 gt.21
  76.9 0.6 fusion.15.bias
  77.5 76.0 %all-to-all-done = bf16[32,4,64,384]{3,2,1,0:T(8,128)(2,1)} async-done(((bf16[32,4,64,384]{3,2,1,0:T(8,128)(2,1)}), bf16[32,4,64,384]{3,2,1,0:T(8,128)(2,1)}, u32[]{:S(2)}, u32[]{:S(2)}) %all-to-all-start) | async-done | bytes 6291488 | tf_op jit(solution)/shard_map/all_to_all | solution.py:243
  153.5 11.2 %attend.1 = bf16[32,4,8,8,128]{4,3,2,1,0:T(8,128)(2,1)} custom-call(bf16[32,4,8,8,384]{4,3,2,1,0:T(8,128)(2,1)} %bitcast.7.received.keys, f32[8,4,256]{2,1,0:T(4,128)} %fusion.15.bias), custom_call_target="tpu_custom_call" | custom-call | tf_op jit(solution)/shard_map/attend/pallas_call | solution.py:137
  164.7 42.9 %all_to_all.15.returned = bf16[32,4,64,128]{3,2,1,0:T(8,128)(2,1)} all-to-all(bf16[32,4,64,128]{3,2,1,0:T(8,128)(2,1)} %bitcast.40), channel_id=1, replica_groups=mesh['seq_0'=4,'seq_1'=4,'seq_2'=2,'head'=4] {'seq_0','seq_1','seq_2'}, dimensions={0} | all-to-all | bytes 4194304 | tf_op jit(solution)/shard_map/all_to_all | solution.py:254
  207.7 8.3 %unpack.1 = bf16[1024,512]{1,0:T(8,128)(2,1)} custom-call(bf16[32,4,64,128]{3,2,1,0:T(8,128)(2,1)} %all_to_all.15.returned, s32[4,1024,1]{2,1,0:T(8,128)} %get-tuple-element.17.slot_of), custom_call_target="tpu_custom_call" | custom-call | tf_op jit(solution)/shard_map/unpack/pallas_call | solution.py:193
  216.0 0.3 collective-permute-start.6
  216.2 1.2 collective-permute-start.4
  217.4 2.3 constant_dynamic-slice_fusion
  219.7 1.5 collective-permute-start.7
  221.2 1.2 collective-permute-start.10
  222.4 6.0 %key_sums.1 = f32[8,4,128]{2,1,0:T(4,128)} custom-call(bf16[32,4,8,8,384]{4,3,2,1,0:T(8,128)(2,1)} %bitcast.7.received.keys), custom_call_target="tpu_custom_call" | custom-call | tf_op jit(solution)/shard_map/key_sums/pallas_call | solution.py:162
  228.4 1.3 copy.37
  229.7 1.7 fusion.13
  231.4 9.4 %collective-permute-done.6 = bf16[1024,512]{1,0:T(8,128)(2,1)S(1)} collective-permute-done((bf16[1024,512]{1,0:T(8,128)(2,1)}, bf16[1024,512]{1,0:T(8,128)(2,1)S(1)}, u32[]{:S(2)}, u32[]{:S(2)}) %collective-permute-start.6) | collective-permute-done | bytes 1048608 | tf_op jit(solution)/shard_map/ppermute | solution.py:22
  240.8 1.5 collective-permute-start.9
  242.4 0.1 collective-permute-start.8
  242.5 9.6 %collective-permute-done.7 = bf16[512,512]{1,0:T(8,128)(2,1)} collective-permute-done((bf16[512,512]{1,0:T(8,128)(2,1)}, bf16[512,512]{1,0:T(8,128)(2,1)}, u32[]{:S(2)}, u32[]{:S(2)}) %collective-permute-start.7) | collective-permute-done | bytes 524320 | tf_op jit(solution)/shard_map/ppermute | solution.py:22
  252.1 1.7 fusion.19
  253.9 9.8 %collective-permute-done.5 = bf16[512,512]{1,0:T(8,128)(2,1)S(1)} collective-permute-done((bf16[512,512]{1,0:T(8,128)(2,1)S(1)}, bf16[512,512]{1,0:T(8,128)(2,1)S(1)}, u32[]{:S(2)}, u32[]{:S(2)}) %collective-permute-start.5) | collective-permute-done | bytes 524320 | tf_op jit(solution)/shard_map/ppermute | solution.py:22
  263.7 0.7 fusion.18
  264.4 10.1 %collective-permute-done.9 = bf16[512,512]{1,0:T(8,128)(2,1)S(1)} collective-permute-done((bf16[512,512]{1,0:T(8,128)(2,1)S(1)}, bf16[512,512]{1,0:T(8,128)(2,1)S(1)}, u32[]{:S(2)}, u32[]{:S(2)}) %collective-permute-start.9) | collective-permute-done | bytes 524320 | tf_op jit(solution)/shard_map/ppermute | solution.py:22
  274.5 1.1 collective-permute-done.8
  275.7 1.7 add_convert_fusion
  (19 shorter events, 0.2 us)
Async XLA Ops:
  0.6 26.6 %collective-permute-start = (bf16[1024,512]{1,0:T(8,128)(2,1)}, bf16[1024,512]{1,0:T(8,128)(2,1)S(1)}, u32[]{:S(2)}, u32[]{:S(2)}) collective-permute-start(bf16[1024,512]{1,0:T(8,128)(2,1)} %own.1), channel_id=1, source_target_pairs={{0,1},{1,2},{2,3},{3,0},{4,5},{5,6},{6,7},{7,4},{8,9},{9,10},{10,1... | collective-permute-start | bytes 3145736 | tf_op jit(solution)/shard_map/ppermute | solution.py:22
  2.8 24.5 %collective-permute-start.1 = (bf16[1024,512]{1,0:T(8,128)(2,1)}, bf16[1024,512]{1,0:T(8,128)(2,1)}, u32[]{:S(2)}, u32[]{:S(2)}) collective-permute-start(bf16[1024,512]{1,0:T(8,128)(2,1)} %own.1), channel_id=1, source_target_pairs={{0,3},{1,0},{2,1},{3,2},{4,7},{5,4},{6,5},{7,6},{8,11},{9,8},{10,9... | collective-permute-start | bytes 3145736 | tf_op jit(solution)/shard_map/ppermute | solution.py:22
  6.3 60.0 %all-to-all-start.1 = ((s32[32,8,4]{1,2,0:T(4,128)}), s32[32,8,4]{1,2,0:T(4,128)S(1)}, u32[]{:S(2)}, u32[]{:S(2)}) async-start(s32[32,8,4]{1,2,0:T(4,128)} %copy.32), calls=%async_computation.1 | async-start | bytes 131072 | tf_op jit(solution)/shard_map/all_to_all | solution.py:233
  27.2 7.4 %copy-start.1 = (bf16[1024,512]{1,0:T(8,128)(2,1)}, bf16[1024,512]{1,0:T(8,128)(2,1)S(1)}, u32[]{:S(2)}) copy-start(bf16[1024,512]{1,0:T(8,128)(2,1)S(1)} %collective-permute-done.left) | copy-start | bytes 3145732
  27.3 18.8 %collective-permute-start.2 = (bf16[512,512]{1,0:T(8,128)(2,1)S(1)}, bf16[512,512]{1,0:T(8,128)(2,1)S(1)}, u32[]{:S(2)}, u32[]{:S(2)}) collective-permute-start(bf16[512,512]{1,0:T(8,128)(2,1)S(1)} %slice.16), channel_id=1, source_target_pairs={{0,1},{1,2},{2,3},{3,0},{4,5},{5,6},{6,7},{7,4},{8,9},{9,10},{10,1... | collective-permute-start | bytes 1572872 | tf_op jit(solution)/shard_map/ppermute | solution.py:22
  28.7 17.4 %collective-permute-start.3 = (bf16[512,512]{1,0:T(8,128)(2,1)S(1)}, bf16[512,512]{1,0:T(8,128)(2,1)S(1)}, u32[]{:S(2)}, u32[]{:S(2)}) collective-permute-start(bf16[512,512]{1,0:T(8,128)(2,1)S(1)} %slice.17), channel_id=1, source_target_pairs={{0,3},{1,0},{2,1},{3,2},{4,7},{5,4},{6,5},{7,6},{8,11},{9,8},{10,9... | collective-permute-start | bytes 1572872 | tf_op jit(solution)/shard_map/ppermute | solution.py:22
  46.1 0.8 copy-start.2
  46.9 0.8 copy-start.3
  66.3 87.2 %all-to-all-start = ((bf16[32,4,64,384]{3,2,1,0:T(8,128)(2,1)}), bf16[32,4,64,384]{3,2,1,0:T(8,128)(2,1)}, u32[]{:S(2)}, u32[]{:S(2)}) async-start(bf16[32,4,64,384]{3,2,1,0:T(8,128)(2,1)} %pack.1), calls=%async_computation | async-start | bytes 12582912 | tf_op jit(solution)/shard_map/all_to_all | solution.py:243
  216.0 24.8 %collective-permute-start.6 = (bf16[1024,512]{1,0:T(8,128)(2,1)}, bf16[1024,512]{1,0:T(8,128)(2,1)S(1)}, u32[]{:S(2)}, u32[]{:S(2)}) collective-permute-start(bf16[1024,512]{1,0:T(8,128)(2,1)} %unpack.1), channel_id=1, source_target_pairs={{0,3},{1,0},{2,1},{3,2},{4,7},{5,4},{6,5},{7,6},{8,11},{9,8},{10,9... | collective-permute-start | bytes 3145736 | tf_op jit(solution)/shard_map/ppermute | solution.py:22
  216.2 26.1 %collective-permute-start.4 = (bf16[1024,512]{1,0:T(8,128)(2,1)}, bf16[1024,512]{1,0:T(8,128)(2,1)S(1)}, u32[]{:S(2)}, u32[]{:S(2)}) collective-permute-start(bf16[1024,512]{1,0:T(8,128)(2,1)} %unpack.1), channel_id=1, source_target_pairs={{0,1},{1,2},{2,3},{3,0},{4,5},{5,6},{6,7},{7,4},{8,9},{9,10},{10,1... | collective-permute-start | bytes 3145736 | tf_op jit(solution)/shard_map/ppermute | solution.py:22
  219.7 32.4 %collective-permute-start.7 = (bf16[512,512]{1,0:T(8,128)(2,1)}, bf16[512,512]{1,0:T(8,128)(2,1)}, u32[]{:S(2)}, u32[]{:S(2)}) collective-permute-start(bf16[512,512]{1,0:T(8,128)(2,1)} %get-tuple-element.15), channel_id=1, source_target_pairs={{0,3},{1,0},{2,1},{3,2},{4,7},{5,4},{6,5},{7,6},{8,11},{9,8},{10,9... | collective-permute-start | bytes 1572872 | tf_op jit(solution)/shard_map/ppermute | solution.py:22
  221.2 42.5 %collective-permute-start.5 = (bf16[512,512]{1,0:T(8,128)(2,1)S(1)}, bf16[512,512]{1,0:T(8,128)(2,1)S(1)}, u32[]{:S(2)}, u32[]{:S(2)}) collective-permute-start(bf16[512,512]{1,0:T(8,128)(2,1)S(1)} %get-tuple-element.16), channel_id=1, source_target_pairs={{0,1},{1,2},{2,3},{3,0},{4,5},{5,6},{6,7},{7,4},{8,9},{9,10},{10,1... | collective-permute-start | bytes 1572872 | tf_op jit(solution)/shard_map/ppermute | solution.py:22
  221.2 8.5 %copy-start = (bf16[1024,512]{1,0:T(8,128)(2,1)S(1)}, bf16[1024,512]{1,0:T(8,128)(2,1)}, u32[]{:S(2)}) copy-start(bf16[1024,512]{1,0:T(8,128)(2,1)} %unpack.1) | copy-start | bytes 3145732
  221.2 43.2 %collective-permute-start.10 = (bf16[512,512]{1,0:T(8,128)(2,1)S(1)}, bf16[512,512]{1,0:T(8,128)(2,1)S(1)}, u32[]{:S(2)}, u32[]{:S(2)}) collective-permute-start(bf16[512,512]{1,0:T(8,128)(2,1)S(1)} %get-tuple-element.14), channel_id=1, source_target_pairs={{0,2},{1,3},{2,0},{3,1},{4,6},{5,7},{6,4},{7,5},{8,10},{9,11},{10,... | collective-permute-start | bytes 1572872 | tf_op jit(solution)/shard_map/ppermute | solution.py:22
  240.8 33.7 %collective-permute-start.9 = (bf16[512,512]{1,0:T(8,128)(2,1)S(1)}, bf16[512,512]{1,0:T(8,128)(2,1)S(1)}, u32[]{:S(2)}, u32[]{:S(2)}) collective-permute-start(bf16[512,512]{1,0:T(8,128)(2,1)S(1)} %slice.19), channel_id=1, source_target_pairs={{0,3},{1,0},{2,1},{3,2},{4,7},{5,4},{6,5},{7,6},{8,11},{9,8},{10,9... | collective-permute-start | bytes 1572872 | tf_op jit(solution)/shard_map/ppermute | solution.py:22
  242.4 33.3 %collective-permute-start.8 = (bf16[512,512]{1,0:T(8,128)(2,1)S(1)}, bf16[512,512]{1,0:T(8,128)(2,1)S(1)}, u32[]{:S(2)}, u32[]{:S(2)}) collective-permute-start(bf16[512,512]{1,0:T(8,128)(2,1)S(1)} %slice.18), channel_id=1, source_target_pairs={{0,1},{1,2},{2,3},{3,0},{4,5},{5,6},{6,7},{7,4},{8,9},{9,10},{10,1... | collective-permute-start | bytes 1572872 | tf_op jit(solution)/shard_map/ppermute | solution.py:22
where the time goes:
time: 278 us; the launch traced here: 277 us
  waiting for transfers between devices  122 us (44%)
  Pallas kernels  54.4 us (20%)
  blocking collectives  42.9 us (15%)
  starting transfers between devices  30.9 us (11%)
  local copies, waits for them, and re-layouts  12.1 us (4%)
  matrix products  8.39 us (3%)
  other arithmetic  5.82 us (2%)
    all_to_all x1, waiting for transfers between devices, local(): received = lax.all_to_all(packed, SEQ, 0, 0, tiled=True)  76 us
    ppermute x11, waiting for transfers between devices, shifted(): lax.ppermute(array, 'head', [(i, (i + by) % count) for i in range(count)])  46.1 us
    all_to_all x1, blocking collectives, local(): lax.all_to_all(bucket_out.reshape(seq_count, heads, CLUST_DEV * SLOT, HEA...  42.9 us
    pallas_call x1, Pallas kernels, pack(): pl.pallas_call(pack_kernel, out_shape=jax.ShapeDtypeStruct((devices, head...  18.7 us
    ppermute x11, starting transfers between devices, shifted(): lax.ppermute(array, 'head', [(i, (i + by) % count) for i in range(count)])  12 us
    pallas_call x1, Pallas kernels, attend(): pl.pallas_call(attend_kernel, out_shape=jax.ShapeDtypeStruct((devices, he...  11.2 us
    pallas_call x1, Pallas kernels, first_blocks(): pl.pallas_call(first_blocks_kernel, out_shape=jax.ShapeDtypeStruct((kinds...  10.2 us
    all_to_all x1, starting transfers between devices, local(): received = lax.all_to_all(packed, SEQ, 0, 0, tiled=True)  9.89 us
  transfers between devices with their start and end apart: 13, of which 7 were waited for; matrix products, arithmetic and copies ran while one was open for 8% of the time, Pallas kernels for 13%

commit v1 on v0

--- a/solution.py
+++ b/solution.py
@@ -9,6 +9,7 @@
 from jax.sharding import Mesh
 from jax.sharding import PartitionSpec as P
 
+
 HEAD_DIM = 128
 CLUST_DEV = 8
 SLOT = 8
@@ -20,6 +21,10 @@
 def shifted(array, by):
     count = lax.axis_size("head")
     return lax.ppermute(array, "head", [(i, (i + by) % count) for i in range(count)])
+
+
+def in_hbm(array):
+    return pltpu.with_memory_space_constraint(array, pltpu.HBM)
 
 
 def params(**more):
@@ -71,45 +76,44 @@
 
     rows_in = projected[head]
     slot_row = slot_of[0]
-    devices, _, per_device, _ = out.shape
+    devices, _, clusters, slot, lanes = out.shape
     step = 4
-    chunk = step * per_device
+    chunk = step * clusters * slot
 
     def body(i, carry):
         iota = lax.broadcasted_iota(jnp.int32, (chunk, rows), 0) + i * chunk
         onehot = jnp.where(iota == slot_row, 1.0, 0.0).astype(BF16)
         packed = jnp.dot(onehot, rows_in, preferred_element_type=F32).astype(BF16)
-        out[pl.ds(i * step, step), 0] = packed.reshape(step, per_device, packed.shape[-1])
+        out[pl.ds(i * step, step), 0] = packed.reshape(step, clusters, slot, lanes)
         return carry
 
     lax.fori_loop(0, devices // step, body, 0, unroll=2)
 
 
-def pack(where, part, far_top, far_bottom, weights, slot_index, devices):
-    kinds, rows, width = part.shape
-    heads = width // HEAD_DIM
+def pack(where, part, far_top, far_bottom, weights, slot_index, devices, group, heads):
+    kinds, rows, _ = part.shape
+    width = heads * HEAD_DIM
     depth = far_top.shape[1]
     lanes = kinds * HEAD_DIM
-    per_device = CLUST_DEV * SLOT
     return pl.pallas_call(
         pack_kernel,
-        out_shape=jax.ShapeDtypeStruct((devices, heads, per_device, lanes), BF16),
+        out_shape=jax.ShapeDtypeStruct((devices, heads, CLUST_DEV, SLOT, lanes), BF16),
         grid_spec=pltpu.PrefetchScalarGridSpec(
             num_scalar_prefetch=1,
             grid=(heads,),
             in_specs=[
-                pl.BlockSpec((kinds, rows, width), lambda h, w: (0, 0, 0)),
+                pl.BlockSpec((kinds, rows, width), lambda h, w: (0, 0, group)),
                 pl.BlockSpec((rows // 2, depth), lambda h, w: (0, 0)),
                 pl.BlockSpec((rows // 2, depth), lambda h, w: (0, 0)),
-                pl.BlockSpec((kinds, depth, width), lambda h, w: (0, w[3], 0)),
-                pl.BlockSpec((1, 1, rows), lambda h, w: (h, 0, 0)),
+                pl.BlockSpec((kinds, depth, width), lambda h, w: (0, w[3], group)),
+                pl.BlockSpec((1, 1, rows), lambda h, w: (group * heads + h, 0, 0)),
             ],
-            out_specs=pl.BlockSpec((devices, 1, per_device, lanes), lambda h, w: (0, h, 0, 0)),
+            out_specs=pl.BlockSpec((devices, 1, CLUST_DEV, SLOT, lanes), lambda h, w: (0, h, 0, 0, 0)),
             scratch_shapes=[pltpu.VMEM((heads, rows, lanes), BF16)],
         ),
         compiler_params=params(),
         name="pack",
-    )(where, part, far_top, far_bottom, weights, slot_index[:, None, :])
+    )(where, part, far_top, far_bottom, weights, slot_index)
 
 
 def attend_kernel(received, bias, out):
@@ -149,7 +153,7 @@
 
 
 def key_sums_kernel(keys, out):
-    devices, heads, _, slot, width = keys.shape
+    _, heads, _, _, width = keys.shape
     for h in range(heads):
         key = keys[:, h, 0].astype(F32)
         scaled = key * lax.rsqrt(jnp.mean(key * key, axis=-1, keepdims=True) + 1e-06)
@@ -171,8 +175,8 @@
 
 
 def unpack_kernel(returned, slot_of, out):
-    devices, _, per_device, width = returned.shape
-    slots = devices * per_device
+    devices, _, clusters, slot, width = returned.shape
+    slots = devices * clusters * slot
     rows = out.shape[0]
     source = returned[:, 0].reshape(slots, width)
     chunk = 256
@@ -187,28 +191,21 @@
     lax.fori_loop(0, rows // chunk, body, 0, unroll=2)
 
 
-def unpack(returned, slot_index):
-    devices, heads, per_device, width = returned.shape
+def unpack(returned, slot_index, group):
+    devices, heads, clusters, slot, width = returned.shape
     rows = slot_index.shape[1]
     return pl.pallas_call(
         unpack_kernel,
         out_shape=jax.ShapeDtypeStruct((rows, heads * width), BF16),
         grid=(heads,),
         in_specs=[
-            pl.BlockSpec((devices, 1, per_device, width), lambda h: (0, h, 0, 0)),
-            pl.BlockSpec((1, rows, 1), lambda h: (h, 0, 0)),
+            pl.BlockSpec((devices, 1, clusters, slot, width), lambda h: (0, h, 0, 0, 0)),
+            pl.BlockSpec((1, rows, 1), lambda h: (group * heads + h, 0, 0)),
         ],
         out_specs=pl.BlockSpec((rows, width), lambda h: (0, h)),
         compiler_params=params(),
         name="unpack",
-    )(returned, slot_index[:, :, None])
-
-
-def ring(block):
-    half = block.shape[0] // 2
-    left = shifted(block, 1)
-    right = shifted(block, -1)
-    return left, right, shifted(left[:half], 1), shifted(right[half:], -1)
+    )(returned, slot_index)
 
 
 def local(tokens, project_weights, output_weights, cluster_ids):
@@ -236,31 +233,45 @@
 
     weights = project_weights.transpose(1, 0, 2)
     where = jnp.stack([here, (here - 1) % groups, (here + 1) % groups, (here + 2) % groups]).astype(jnp.int32)
-    left, right, far_top, far_bottom = ring(tokens)
+    slot_rows, slot_cols = slot_index[:, None, :], slot_index[:, :, None]
+    left, right = shifted(tokens, 1), shifted(tokens, -1)
+    left, right, slot_rows, slot_cols, where = lax.optimization_barrier((left, right, slot_rows, slot_cols, where))
+    half = rows // 2
+    far_top, far_bottom = shifted(left[:half], 1), shifted(right[half:], -1)
+    left, right = in_hbm(left), in_hbm(right)
     part = first_blocks(where, tokens, left, right, weights)
-    packed = pack(where, part, far_top, far_bottom, weights, slot_index, seq_count)
-
-    received = lax.all_to_all(packed, SEQ, 0, 0, tiled=True)
-
-    out_weights, _ = lax.optimization_barrier((output_weights, far_top))
+
+    out_weights, far_top, far_bottom = lax.optimization_barrier((output_weights, far_top, far_bottom))
     out_blocks = []
     for by in range(groups):
         block = lax.dynamic_slice(out_weights, (0, (here + by) % groups * width), (width, width))
         out_blocks.append(shifted(block, by) if by else block)
 
-    received = received.reshape(seq_count, heads, CLUST_DEV, SLOT, 3 * HEAD_DIM)
-    bucket_out = attend(received, live)
-    owned = key_sums(received)
-    returned = lax.all_to_all(bucket_out.reshape(seq_count, heads, CLUST_DEV * SLOT, HEAD_DIM), SEQ, 0, 0, tiled=True)
-    attended = unpack(returned, slot_index)
-    left, right, far_top, far_bottom = ring(attended)
-
-    def times(block, by):
-        return jnp.dot(block, out_blocks[by], preferred_element_type=F32)
-
-    near = times(attended, 0) + times(left, 1) + times(right, 3)
-    mixed = (near + times(jnp.concatenate([far_top, far_bottom]), 2)).astype(BF16)
-    return (mixed, owned.transpose(1, 0, 2))
+    chunks = 2
+    some = heads // chunks
+    received = []
+    for chunk in range(chunks):
+        packed = pack(where, part, in_hbm(far_top), in_hbm(far_bottom), weights, slot_rows, seq_count, chunk, some)
+        arrived = lax.all_to_all(packed, SEQ, 0, 0, tiled=True)
+        received.append(in_hbm(arrived))
+
+    owned, gathered = [], []
+    for chunk in range(chunks):
+        buckets = attend(received[chunk], live[:, chunk * some : (chunk + 1) * some])
+        owned.append(key_sums(received[chunk]))
+        returned = lax.all_to_all(buckets, SEQ, 0, 0, tiled=True)
+        attended = unpack(in_hbm(returned), slot_cols, chunk)
+        gathered.append([attended] + [shifted(attended, by) for by in range(1, groups)])
+
+    mixed = None
+    for chunk in range(chunks):
+        for by in (0, 1, 3, 2):
+            depth = gathered[chunk][by].shape[1]
+            share = out_blocks[by][chunk * depth : (chunk + 1) * depth]
+            term = jnp.dot(gathered[chunk][by], share, preferred_element_type=F32)
+            mixed = term if mixed is None else mixed + term
+    owned = jnp.concatenate(owned, axis=1).transpose(1, 0, 2)
+    return (mixed.astype(BF16), owned)
 
 
 def solution(mesh):

time: 278 us -> 268 us (0.964)
  the two profiles are of different devices: /device:TPU:1 before, /device:TPU:26 now
where the time goes in v1:
time: 268 us; the launch traced here: 267 us
  waiting for transfers between devices  107 us (40%)
  Pallas kernels  72.4 us (27%)
  starting transfers between devices  53.7 us (20%)
  local copies, waits for them, and re-layouts  13.7 us (5%)
  matrix products  13.1 us (5%)
  other arithmetic  5.89 us (2%)
    all_to_all x2, waiting for transfers between devices, local(): arrived = lax.all_to_all(packed, SEQ, 0, 0, tiled=True)  52.7 us
    ppermute x13, waiting for transfers between devices, shifted(): lax.ppermute(array, 'head', [(i, (i + by) % count) for i in range(count)])  49.1 us
    pallas_call x2, Pallas kernels, pack(): pl.pallas_call(pack_kernel, out_shape=jax.ShapeDtypeStruct((devices, head...  22.1 us
    pallas_call x2, Pallas kernels, attend(): pl.pallas_call(attend_kernel, out_shape=jax.ShapeDtypeStruct((devices, he...  19 us
    ppermute x13, starting transfers between devices, shifted(): lax.ppermute(array, 'head', [(i, (i + by) % count) for i in range(count)])  17 us
    all_to_all x2, starting transfers between devices, local(): arrived = lax.all_to_all(packed, SEQ, 0, 0, tiled=True)  15.2 us
    all_to_all x2, starting transfers between devices, local(): returned = lax.all_to_all(buckets, SEQ, 0, 0, tiled=True)  13.1 us
    pallas_call x2, Pallas kernels, key_sums(): pl.pallas_call(key_sums_kernel, out_shape=jax.ShapeDtypeStruct((clusters,...  11 us
  transfers between devices with their start and end apart: 18, of which 9 were waited for; matrix products, arithmetic and copies ran while one was open for 10% of the time, Pallas kernels for 27%

profile of v1, /device:TPU:26, one launch (start us, length us, event | category | flops | bytes accessed | tf_op | source)
XLA Modules:
  0.0 266.6 jit_solution(830526779190927883)
XLA Ops:
  0.9 1.8 collective-permute-start.1
  3.4 2.5 fusion
  6.6 1.9 copy.26
  9.2 3.4 %multiply_add_fusion = (s32[4,1024,1]{2,1,0:T(8,128)}, s32[4,1024]{1,0:T(4,128)S(1)}) fusion(s32[4,1024,1]{2,1,0:T(8,128)} %copy.26, s32[4,1024,1]{2,1,0:T(8,128)S(1)} %copy.24), kind=kLoop, calls=%fused_computation.9 | loop fusion | flops 8192 | bytes 65536 | tf_op jit(solution)/shard_map/add | solution.py:227
  13.2 12.6 %collective-permute-done.left = bf16[1024,512]{1,0:T(8,128)(2,1)S(1)} collective-permute-done((bf16[1024,512]{1,0:T(8,128)(2,1)}, bf16[1024,512]{1,0:T(8,128)(2,1)S(1)}, u32[]{:S(2)}, u32[]{:S(2)}) %collective-permute-start) | collective-permute-done | bytes 1048608 | tf_op jit(solution)/shard_map/ppermute | solution.py:23
  25.8 1.4 collective-permute-done.1.right
  27.5 1.1 slice.37
  28.6 1.9 collective-permute-start.3
  31.8 8.5 %all-to-all-start.1 = ((s32[32,8,4]{1,2,0:T(4,128)}), s32[32,8,4]{1,2,0:T(4,128)S(1)}, u32[]{:S(2)}, u32[]{:S(2)}) async-start(s32[32,8,4]{1,2,0:T(4,128)} %copy.27), calls=%async_computation.1 | async-start | bytes 131072 | tf_op jit(solution)/shard_map/all_to_all | solution.py:230
  40.2 10.3 %first_blocks.1.part = f32[3,1024,512]{2,1,0:T(8,128)} custom-call(s32[4]{0:T(128)} %pad_add_fusion.where, bf16[1024,512]{1,0:T(8,128)(2,1)} %own.1, bf16[1024,512]{1,0:T(8,128)(2,1)} %copy-done.3, bf16[1024,512]{1,0:T(8,128)(2,1)} %collective-permute-done.1.right, bf16[3,2048,512]{2,1,0:T(8,128)(2,1)} %bitcast.37, bf16[3,2048,512]{2,1,0:T(8,128)(2,1)} %bitcast.38, ...), custom_call_target="tpu_custom_call" | custom-call | tf_op jit(solution)/shard_map/first_blocks/pallas_call | solution.py:45
  50.5 0.8 copy-done.4
  51.3 0.8 copy-done.5
  52.1 11.0 %pack.2 = bf16[32,2,8,8,384]{4,3,2,1,0:T(8,128)(2,1)} custom-call(s32[4]{0:T(128)} %pad_add_fusion.where, f32[3,1024,512]{2,1,0:T(8,128)} %first_blocks.1.part, bf16[512,512]{1,0:T(8,128)(2,1)} %copy-done.4, bf16[512,512]{1,0:T(8,128)(2,1)} %copy-done.5, bf16[3,2048,512]{2,1,0:T(8,128)(2,1)} %bitcast.40, s32[4,1,1024]{2,1,0:T(1,128)} %reshape_add_fusion.slot_of), custom_call_target="tpu_custom_call" | custom-call | tf_op jit(solution)/shard_map/pack/pallas_call | solution.py:98
  63.1 7.4 %all-to-all-start = ((bf16[32,2,8,8,384]{4,3,2,1,0:T(8,128)(2,1)}), bf16[32,2,8,8,384]{4,3,2,1,0:T(8,128)(2,1)S(1)}, u32[]{:S(2)}, u32[]{:S(2)}) async-start(bf16[32,2,8,8,384]{4,3,2,1,0:T(8,128)(2,1)} %pack.2), calls=%async_computation | async-start | bytes 6291456 | tf_op jit(solution)/shard_map/all_to_all | solution.py:255
  70.5 11.0 %pack.3 = bf16[32,2,8,8,384]{4,3,2,1,0:T(8,128)(2,1)} custom-call(s32[4]{0:T(128)} %pad_add_fusion.where, f32[3,1024,512]{2,1,0:T(8,128)} %first_blocks.1.part, bf16[512,512]{1,0:T(8,128)(2,1)} %copy-done.4, bf16[512,512]{1,0:T(8,128)(2,1)} %copy-done.5, bf16[3,2048,512]{2,1,0:T(8,128)(2,1)} %bitcast.41, s32[4,1,1024]{2,1,0:T(1,128)} %reshape_add_fusion.slot_of), custom_call_target="tpu_custom_call" | custom-call | tf_op jit(solution)/shard_map/pack/pallas_call | solution.py:98
  81.6 26.0 %all-to-all-done.received.keys = bf16[32,2,8,8,384]{4,3,2,1,0:T(8,128)(2,1)S(1)} async-done(((bf16[32,2,8,8,384]{4,3,2,1,0:T(8,128)(2,1)}), bf16[32,2,8,8,384]{4,3,2,1,0:T(8,128)(2,1)S(1)}, u32[]{:S(2)}, u32[]{:S(2)}) %all-to-all-start) | async-done | bytes 3145760 | tf_op jit(solution)/shard_map/all_to_all | solution.py:255
  107.6 1.7 copy-done
  109.3 7.8 %all-to-all-start.3 = ((bf16[32,2,8,8,384]{4,3,2,1,0:T(8,128)(2,1)}), bf16[32,2,8,8,384]{4,3,2,1,0:T(8,128)(2,1)}, u32[]{:S(2)}, u32[]{:S(2)}) async-start(bf16[32,2,8,8,384]{4,3,2,1,0:T(8,128)(2,1)} %pack.3), calls=%async_computation.3 | async-start | bytes 6291456 | tf_op jit(solution)/shard_map/all_to_all | solution.py:255
  118.4 9.5 %attend.2 = bf16[32,2,8,8,128]{4,3,2,1,0:T(8,128)(2,1)} custom-call(bf16[32,2,8,8,384]{4,3,2,1,0:T(8,128)(2,1)} %copy-done, f32[8,2,256]{2,1,0:T(2,128)} %get-tuple-element.31.bias), custom_call_target="tpu_custom_call" | custom-call | tf_op jit(solution)/shard_map/attend/pallas_call | solution.py:141
  127.9 26.7 %all-to-all-done.3.received.keys = bf16[32,2,8,8,384]{4,3,2,1,0:T(8,128)(2,1)} async-done(((bf16[32,2,8,8,384]{4,3,2,1,0:T(8,128)(2,1)}), bf16[32,2,8,8,384]{4,3,2,1,0:T(8,128)(2,1)}, u32[]{:S(2)}, u32[]{:S(2)}) %all-to-all-start.3) | async-done | bytes 3145760 | tf_op jit(solution)/shard_map/all_to_all | solution.py:255
  154.6 6.7 %all-to-all-start.2 = ((bf16[32,2,8,8,128]{4,3,2,1,0:T(8,128)(2,1)}), bf16[32,2,8,8,128]{4,3,2,1,0:T(8,128)(2,1)S(1)}, u32[]{:S(2)}, u32[]{:S(2)}) async-start(bf16[32,2,8,8,128]{4,3,2,1,0:T(8,128)(2,1)} %attend.2), calls=%async_computation.2 | async-start | bytes 2097152 | tf_op jit(solution)/shard_map/all_to_all | solution.py:262
  161.3 9.5 %attend.3 = bf16[32,2,8,8,128]{4,3,2,1,0:T(8,128)(2,1)} custom-call(bf16[32,2,8,8,384]{4,3,2,1,0:T(8,128)(2,1)} %all-to-all-done.3.received.keys, f32[8,2,256]{2,1,0:T(2,128)} %get-tuple-element.32.bias), custom_call_target="tpu_custom_call" | custom-call | tf_op jit(solution)/shard_map/attend/pallas_call | solution.py:141
  170.8 5.0 %all-to-all-done.2.returned = bf16[32,2,8,8,128]{4,3,2,1,0:T(8,128)(2,1)S(1)} async-done(((bf16[32,2,8,8,128]{4,3,2,1,0:T(8,128)(2,1)}), bf16[32,2,8,8,128]{4,3,2,1,0:T(8,128)(2,1)S(1)}, u32[]{:S(2)}, u32[]{:S(2)}) %all-to-all-start.2) | async-done | bytes 1048608 | tf_op jit(solution)/shard_map/all_to_all | solution.py:262
  175.8 6.4 %all-to-all-start.4 = ((bf16[32,2,8,8,128]{4,3,2,1,0:T(8,128)(2,1)}), bf16[32,2,8,8,128]{4,3,2,1,0:T(8,128)(2,1)S(1)}, u32[]{:S(2)}, u32[]{:S(2)}) async-start(bf16[32,2,8,8,128]{4,3,2,1,0:T(8,128)(2,1)} %attend.3), calls=%async_computation.4 | async-start | bytes 2097152 | tf_op jit(solution)/shard_map/all_to_all | solution.py:262
  182.2 2.4 constant_dynamic-slice_fusion
  184.6 1.4 collective-permute-start.5
  186.6 1.2 collective-permute-start.9
  187.8 5.5 %key_sums.2 = f32[8,2,128]{2,1,0:T(2,128)} custom-call(bf16[32,2,8,8,384]{4,3,2,1,0:T(8,128)(2,1)} %copy-done), custom_call_target="tpu_custom_call" | custom-call | tf_op jit(solution)/shard_map/key_sums/pallas_call | solution.py:166
  193.3 5.5 %key_sums.3 = f32[8,2,128]{2,1,0:T(2,128)} custom-call(bf16[32,2,8,8,384]{4,3,2,1,0:T(8,128)(2,1)} %all-to-all-done.3.received.keys), custom_call_target="tpu_custom_call" | custom-call | tf_op jit(solution)/shard_map/key_sums/pallas_call | solution.py:166
  200.1 5.1 %unpack.2 = bf16[1024,256]{1,0:T(8,128)(2,1)} custom-call(bf16[32,2,8,8,128]{4,3,2,1,0:T(8,128)(2,1)} %copy-done.1, s32[4,1024,1]{2,1,0:T(8,128)} %get-tuple-element.16.slot_of), custom_call_target="tpu_custom_call" | custom-call | tf_op jit(solution)/shard_map/unpack/pallas_call | solution.py:197
  205.2 1.9 collective-permute-start.4
  207.1 1.0 copy-done.2
  208.1 5.1 %unpack.3 = bf16[1024,256]{1,0:T(8,128)(2,1)} custom-call(bf16[32,2,8,8,128]{4,3,2,1,0:T(8,128)(2,1)} %copy-done.2, s32[4,1024,1]{2,1,0:T(8,128)} %get-tuple-element.16.slot_of), custom_call_target="tpu_custom_call" | custom-call | tf_op jit(solution)/shard_map/unpack/pallas_call | solution.py:197
  213.2 1.0 collective-permute-start.10
  214.2 1.4 fusion.23
  215.5 1.4 fusion.15
  216.9 1.1 collective-permute-start.6
  218.1 4.1 %collective-permute-done.4 = bf16[1024,256]{1,0:T(8,128)(2,1)} collective-permute-done((bf16[1024,256]{1,0:T(8,128)(2,1)}, bf16[1024,256]{1,0:T(8,128)(2,1)}, u32[]{:S(2)}, u32[]{:S(2)}) %collective-permute-start.4) | collective-permute-done | bytes 524320 | tf_op jit(solution)/shard_map/ppermute | solution.py:23
  222.1 1.2 collective-permute-start.8
  223.4 1.5 fusion.21
  224.9 8.4 %collective-permute-done.10 = bf16[1024,256]{1,0:T(8,128)(2,1)S(1)} collective-permute-done((bf16[1024,256]{1,0:T(8,128)(2,1)}, bf16[1024,256]{1,0:T(8,128)(2,1)S(1)}, u32[]{:S(2)}, u32[]{:S(2)}) %collective-permute-start.10) | collective-permute-done | bytes 524320 | tf_op jit(solution)/shard_map/ppermute | solution.py:23
  233.9 1.4 fusion.13
  235.3 3.6 %collective-permute-start.12 = (bf16[1024,256]{1,0:T(8,128)(2,1)S(1)}, bf16[1024,256]{1,0:T(8,128)(2,1)S(1)}, u32[]{:S(2)}, u32[]{:S(2)}) collective-permute-start(bf16[1024,256]{1,0:T(8,128)(2,1)S(1)} %copy-done.7), channel_id=1, source_target_pairs={{0,2},{1,3},{2,0},{3,1},{4,6},{5,7},{6,4},{7,5},{8,10},{9,11},{10,... | collective-permute-start | bytes 1572872 | tf_op jit(solution)/shard_map/ppermute | solution.py:23
  238.9 1.4 fusion.19
  240.3 15.4 %collective-permute-done.11 = bf16[1024,256]{1,0:T(8,128)(2,1)S(1)} collective-permute-done((bf16[1024,256]{1,0:T(8,128)(2,1)S(1)}, bf16[1024,256]{1,0:T(8,128)(2,1)S(1)}, u32[]{:S(2)}, u32[]{:S(2)}) %collective-permute-start.11) | collective-permute-done | bytes 524320 | tf_op jit(solution)/shard_map/ppermute | solution.py:23
  255.7 1.4 fusion.11
  257.5 7.3 %collective-permute-done.12 = bf16[1024,256]{1,0:T(8,128)(2,1)S(1)} collective-permute-done((bf16[1024,256]{1,0:T(8,128)(2,1)S(1)}, bf16[1024,256]{1,0:T(8,128)(2,1)S(1)}, u32[]{:S(2)}, u32[]{:S(2)}) %collective-permute-start.12) | collective-permute-done | bytes 524320 | tf_op jit(solution)/shard_map/ppermute | solution.py:23
  264.8 1.8 add_convert_fusion
  (48 shorter events, 8.8 us)
Async XLA Ops:
  0.6 25.2 %collective-permute-start = (bf16[1024,512]{1,0:T(8,128)(2,1)}, bf16[1024,512]{1,0:T(8,128)(2,1)S(1)}, u32[]{:S(2)}, u32[]{:S(2)}) collective-permute-start(bf16[1024,512]{1,0:T(8,128)(2,1)} %own.1), channel_id=1, source_target_pairs={{0,1},{1,2},{2,3},{3,0},{4,5},{5,6},{6,7},{7,4},{8,9},{9,10},{10,1... | collective-permute-start | bytes 3145736 | tf_op jit(solution)/shard_map/ppermute | solution.py:23
  0.9 26.3 %collective-permute-start.1 = (bf16[1024,512]{1,0:T(8,128)(2,1)}, bf16[1024,512]{1,0:T(8,128)(2,1)}, u32[]{:S(2)}, u32[]{:S(2)}) collective-permute-start(bf16[1024,512]{1,0:T(8,128)(2,1)} %own.1), channel_id=1, source_target_pairs={{0,3},{1,0},{2,1},{3,2},{4,7},{5,4},{6,5},{7,6},{8,11},{9,8},{10,9... | collective-permute-start | bytes 3145736 | tf_op jit(solution)/shard_map/ppermute | solution.py:23
  3.4 2.5 copy-start.8
  25.8 14.4 %copy-start.3 = (bf16[1024,512]{1,0:T(8,128)(2,1)}, bf16[1024,512]{1,0:T(8,128)(2,1)S(1)}, u32[]{:S(2)}) copy-start(bf16[1024,512]{1,0:T(8,128)(2,1)S(1)} %collective-permute-done.left) | copy-start | bytes 3145732
  27.2 23.2 %collective-permute-start.2 = (bf16[512,512]{1,0:T(8,128)(2,1)S(1)}, bf16[512,512]{1,0:T(8,128)(2,1)S(1)}, u32[]{:S(2)}, u32[]{:S(2)}) collective-permute-start(bf16[512,512]{1,0:T(8,128)(2,1)S(1)} %slice.36), channel_id=1, source_target_pairs={{0,1},{1,2},{2,3},{3,0},{4,5},{5,6},{6,7},{7,4},{8,9},{9,10},{10,1... | collective-permute-start | bytes 1572872 | tf_op jit(solution)/shard_map/ppermute | solution.py:23
  28.6 21.9 %collective-permute-start.3 = (bf16[512,512]{1,0:T(8,128)(2,1)S(1)}, bf16[512,512]{1,0:T(8,128)(2,1)S(1)}, u32[]{:S(2)}, u32[]{:S(2)}) collective-permute-start(bf16[512,512]{1,0:T(8,128)(2,1)S(1)} %slice.37), channel_id=1, source_target_pairs={{0,3},{1,0},{2,1},{3,2},{4,7},{5,4},{6,5},{7,6},{8,11},{9,8},{10,9... | collective-permute-start | bytes 1572872 | tf_op jit(solution)/shard_map/ppermute | solution.py:23
  31.8 31.4 %all-to-all-start.1 = ((s32[32,8,4]{1,2,0:T(4,128)}), s32[32,8,4]{1,2,0:T(4,128)S(1)}, u32[]{:S(2)}, u32[]{:S(2)}) async-start(s32[32,8,4]{1,2,0:T(4,128)} %copy.27), calls=%async_computation.1 | async-start | bytes 131072 | tf_op jit(solution)/shard_map/all_to_all | solution.py:230
  50.5 0.8 copy-start.4
  51.3 0.8 copy-start.5
  63.1 44.4 %all-to-all-start = ((bf16[32,2,8,8,384]{4,3,2,1,0:T(8,128)(2,1)}), bf16[32,2,8,8,384]{4,3,2,1,0:T(8,128)(2,1)S(1)}, u32[]{:S(2)}, u32[]{:S(2)}) async-start(bf16[32,2,8,8,384]{4,3,2,1,0:T(8,128)(2,1)} %pack.2), calls=%async_computation | async-start | bytes 6291456 | tf_op jit(solution)/shard_map/all_to_all | solution.py:255
  107.6 1.7 copy-start
  109.3 45.3 %all-to-all-start.3 = ((bf16[32,2,8,8,384]{4,3,2,1,0:T(8,128)(2,1)}), bf16[32,2,8,8,384]{4,3,2,1,0:T(8,128)(2,1)}, u32[]{:S(2)}, u32[]{:S(2)}) async-start(bf16[32,2,8,8,384]{4,3,2,1,0:T(8,128)(2,1)} %pack.3), calls=%async_computation.3 | async-start | bytes 6291456 | tf_op jit(solution)/shard_map/all_to_all | solution.py:255
  154.6 21.2 %all-to-all-start.2 = ((bf16[32,2,8,8,128]{4,3,2,1,0:T(8,128)(2,1)}), bf16[32,2,8,8,128]{4,3,2,1,0:T(8,128)(2,1)S(1)}, u32[]{:S(2)}, u32[]{:S(2)}) async-start(bf16[32,2,8,8,128]{4,3,2,1,0:T(8,128)(2,1)} %attend.2), calls=%async_computation.2 | async-start | bytes 2097152 | tf_op jit(solution)/shard_map/all_to_all | solution.py:262
  175.8 8.8 %copy-start.1 = (bf16[32,2,8,8,128]{4,3,2,1,0:T(8,128)(2,1)}, bf16[32,2,8,8,128]{4,3,2,1,0:T(8,128)(2,1)S(1)}, u32[]{:S(2)}) copy-start(bf16[32,2,8,8,128]{4,3,2,1,0:T(8,128)(2,1)S(1)} %all-to-all-done.2.returned) | copy-start | bytes 3145732
  175.8 31.4 %all-to-all-start.4 = ((bf16[32,2,8,8,128]{4,3,2,1,0:T(8,128)(2,1)}), bf16[32,2,8,8,128]{4,3,2,1,0:T(8,128)(2,1)S(1)}, u32[]{:S(2)}, u32[]{:S(2)}) async-start(bf16[32,2,8,8,128]{4,3,2,1,0:T(8,128)(2,1)} %attend.3), calls=%async_computation.4 | async-start | bytes 2097152 | tf_op jit(solution)/shard_map/all_to_all | solution.py:262
  184.6 32.4 %collective-permute-start.5 = (bf16[512,512]{1,0:T(8,128)(2,1)}, bf16[512,512]{1,0:T(8,128)(2,1)}, u32[]{:S(2)}, u32[]{:S(2)}) collective-permute-start(bf16[512,512]{1,0:T(8,128)(2,1)} %get-tuple-element.28), channel_id=1, source_target_pairs={{0,1},{1,2},{2,3},{3,0},{4,5},{5,6},{6,7},{7,4},{8,9},{9,10},{10,1... | collective-permute-start | bytes 1572872 | tf_op jit(solution)/shard_map/ppermute | solution.py:23
  186.0 49.3 %collective-permute-start.7 = (bf16[512,512]{1,0:T(8,128)(2,1)S(1)}, bf16[512,512]{1,0:T(8,128)(2,1)}, u32[]{:S(2)}, u32[]{:S(2)}) collective-permute-start(bf16[512,512]{1,0:T(8,128)(2,1)S(1)} %get-tuple-element.27), channel_id=1, source_target_pairs={{0,3},{1,0},{2,1},{3,2},{4,7},{5,4},{6,5},{7,6},{8,11},{9,8},{10,9... | collective-permute-start | bytes 1572872 | tf_op jit(solution)/shard_map/ppermute | solution.py:23
  186.6 70.5 %collective-permute-start.9 = (bf16[512,512]{1,0:T(8,128)(2,1)S(1)}, bf16[512,512]{1,0:T(8,128)(2,1)S(1)}, u32[]{:S(2)}, u32[]{:S(2)}) collective-permute-start(bf16[512,512]{1,0:T(8,128)(2,1)S(1)} %get-tuple-element.26), channel_id=1, source_target_pairs={{0,2},{1,3},{2,0},{3,1},{4,6},{5,7},{6,4},{7,5},{8,10},{9,11},{10,... | collective-permute-start | bytes 1572872 | tf_op jit(solution)/shard_map/ppermute | solution.py:23
  193.3 5.5 %copy-start.9 = (f32[8,2,128]{2,1,0:T(2,128)S(1)}, f32[8,2,128]{2,1,0:T(2,128)}, u32[]{:S(2)}) copy-start(f32[8,2,128]{2,1,0:T(2,128)} %key_sums.2) | copy-start | bytes 24580
  205.2 8.9 %copy-start.6 = (bf16[1024,256]{1,0:T(8,128)(2,1)S(1)}, bf16[1024,256]{1,0:T(8,128)(2,1)}, u32[]{:S(2)}) copy-start(bf16[1024,256]{1,0:T(8,128)(2,1)} %unpack.2) | copy-start | bytes 1572868
  205.2 16.9 %collective-permute-start.4 = (bf16[1024,256]{1,0:T(8,128)(2,1)}, bf16[1024,256]{1,0:T(8,128)(2,1)}, u32[]{:S(2)}, u32[]{:S(2)}) collective-permute-start(bf16[1024,256]{1,0:T(8,128)(2,1)} %unpack.2), channel_id=1, source_target_pairs={{0,1},{1,2},{2,3},{3,0},{4,5},{5,6},{6,7},{7,4},{8,9},{9,10},{10,1... | collective-permute-start | bytes 1572872 | tf_op jit(solution)/shard_map/ppermute | solution.py:23
  207.1 1.0 copy-start.2
  213.2 2.4 copy-start.7
  213.2 20.1 %collective-permute-start.10 = (bf16[1024,256]{1,0:T(8,128)(2,1)}, bf16[1024,256]{1,0:T(8,128)(2,1)S(1)}, u32[]{:S(2)}, u32[]{:S(2)}) collective-permute-start(bf16[1024,256]{1,0:T(8,128)(2,1)} %unpack.3), channel_id=1, source_target_pairs={{0,1},{1,2},{2,3},{3,0},{4,5},{5,6},{6,7},{7,4},{8,9},{9,10},{10,1... | collective-permute-start | bytes 1572872 | tf_op jit(solution)/shard_map/ppermute | solution.py:23
  216.9 21.9 %collective-permute-start.6 = (bf16[1024,256]{1,0:T(8,128)(2,1)S(1)}, bf16[1024,256]{1,0:T(8,128)(2,1)S(1)}, u32[]{:S(2)}, u32[]{:S(2)}) collective-permute-start(bf16[1024,256]{1,0:T(8,128)(2,1)S(1)} %copy-done.6), channel_id=1, source_target_pairs={{0,3},{1,0},{2,1},{3,2},{4,7},{5,4},{6,5},{7,6},{8,11},{9,8},{10,9... | collective-permute-start | bytes 1572872 | tf_op jit(solution)/shard_map/ppermute | solution.py:23
  222.1 35.0 %collective-permute-start.8 = (bf16[1024,256]{1,0:T(8,128)(2,1)S(1)}, bf16[1024,256]{1,0:T(8,128)(2,1)S(1)}, u32[]{:S(2)}, u32[]{:S(2)}) collective-permute-start(bf16[1024,256]{1,0:T(8,128)(2,1)S(1)} %copy-done.6), channel_id=1, source_target_pairs={{0,2},{1,3},{2,0},{3,1},{4,6},{5,7},{6,4},{7,5},{8,10},{9,11},{10,... | collective-permute-start | bytes 1572872 | tf_op jit(solution)/shard_map/ppermute | solution.py:23
  233.3 22.4 %collective-permute-start.11 = (bf16[1024,256]{1,0:T(8,128)(2,1)S(1)}, bf16[1024,256]{1,0:T(8,128)(2,1)S(1)}, u32[]{:S(2)}, u32[]{:S(2)}) collective-permute-start(bf16[1024,256]{1,0:T(8,128)(2,1)S(1)} %copy-done.7), channel_id=1, source_target_pairs={{0,3},{1,0},{2,1},{3,2},{4,7},{5,4},{6,5},{7,6},{8,11},{9,8},{10,9... | collective-permute-start | bytes 1572872 | tf_op jit(solution)/shard_map/ppermute | solution.py:23
  235.3 29.5 %collective-permute-start.12 = (bf16[1024,256]{1,0:T(8,128)(2,1)S(1)}, bf16[1024,256]{1,0:T(8,128)(2,1)S(1)}, u32[]{:S(2)}, u32[]{:S(2)}) collective-permute-start(bf16[1024,256]{1,0:T(8,128)(2,1)S(1)} %copy-done.7), channel_id=1, source_target_pairs={{0,2},{1,3},{2,0},{3,1},{4,6},{5,7},{6,4},{7,5},{8,10},{9,11},{10,... | collective-permute-start | bytes 1572872 | tf_op jit(solution)/shard_map/ppermute | solution.py:23

commit v2 on v1

v2 whole, which is shorter than its diff:
```python
import functools
import math

import jax
import jax.numpy as jnp
from jax import lax
from jax.experimental import pallas as pl
from jax.experimental.pallas import tpu as pltpu
from jax.sharding import Mesh
from jax.sharding import PartitionSpec as P


HEAD_DIM = 128
CLUST_DEV = 8
SLOT = 8
SEQ = ("seq_0", "seq_1", "seq_2")
F32 = jnp.float32
BF16 = jnp.bfloat16
EMPTY = float(1 << 20)
FULL_BELOW = float(1 << 19)


def shifted(array, by):
    count = lax.axis_size("head")
    return lax.ppermute(array, "head", [(i, (i + by) % count) for i in range(count)])


def in_vmem(array):
    return pltpu.with_memory_space_constraint(array, pltpu.VMEM)


VMEM_WHOLE = pl.BlockSpec(memory_space=pltpu.VMEM)


def params():
    return pltpu.CompilerParams(vmem_limit_bytes=56 * 1024 * 1024)


def dot(a, b):
    return jnp.dot(a, b, preferred_element_type=F32)


def first_blocks_kernel(where, own, left_top, left_bottom, right_top, right_bottom, w_own, w_left, w_right, out):
    half = left_top.shape[0]
    for part, left, right in ((slice(0, half), left_top, right_top), (slice(half, None), left_bottom, right_bottom)):
        total = dot(own[part], w_own[0])
        total += dot(left[...], w_left[0])
        total += dot(right[...], w_right[0])
        out[0, part] = total


def first_blocks(where, own, halves, weights):
    kinds, _, width = weights.shape
    rows, depth = own.shape
    return pl.pallas_call(
        first_blocks_kernel,
        out_shape=jax.ShapeDtypeStruct((kinds, rows, width), F32),
        grid_spec=pltpu.PrefetchScalarGridSpec(
            num_scalar_prefetch=1,
            grid=(kinds,),
            in_specs=[pl.BlockSpec((rows, depth), lambda j, w: (0, 0))]
            + [VMEM_WHOLE] * 4
            + [pl.BlockSpec((1, depth, width), functools.partial(lambda b, j, w: (j, w[b], 0), b)) for b in range(3)],
            out_specs=pl.BlockSpec((1, rows, width), lambda j, w: (j, 0, 0)),
        ),
        compiler_params=params(),
        name="first_blocks",
    )(where, own, *[in_vmem(half) for half in halves], weights, weights, weights)


def pack_kernel(where, part, far_top, far_bottom, w_far, slot_of, out, projected):
    head = pl.program_id(0)
    kinds, rows, _ = part.shape
    half = rows // 2
    heads = projected.shape[0]

    @pl.when(head == 0)
    def _():
        for kind in range(kinds):
            to = slice(kind * HEAD_DIM, (kind + 1) * HEAD_DIM)
            for at, far in ((slice(0, half), far_top), (slice(half, rows), far_bottom)):
                done = (part[kind, at] + dot(far[...], w_far[kind])).astype(BF16)
                for h in range(heads):
                    projected[h, at, to] = done[:, h * HEAD_DIM : (h + 1) * HEAD_DIM]
        for h in range(heads):
            projected[h, :, kinds * HEAD_DIM :] = jnp.ones((rows, HEAD_DIM), BF16)

    rows_in = projected[head]
    slot_row = slot_of[0]
    devices, _, clusters, slot, _ = out.shape
    step = 4
    chunk = step * clusters * slot

    def body(i, carry):
        iota = lax.broadcasted_iota(jnp.int32, (chunk, rows), 0) + i * chunk
        onehot = jnp.where(iota == slot_row, 1.0, 0.0).astype(BF16)
        packed = dot(onehot, rows_in)
        at = pl.ds(i * step, step)
        for kind in range(kinds):
            block = packed[:, kind * HEAD_DIM : (kind + 1) * HEAD_DIM]
            if kind == 1:
                block = block + (EMPTY - EMPTY * packed[:, kinds * HEAD_DIM :])
            block = block.astype(BF16).reshape(step, clusters, slot, HEAD_DIM)
            out[at, 0, :, :, kind * HEAD_DIM : (kind + 1) * HEAD_DIM] = block
        return carry

    lax.fori_loop(0, devices // step, body, 0, unroll=2)


def pack(where, part, far_top, far_bottom, weights, slot_rows, devices, group, heads):
    kinds = weights.shape[0]
    rows = slot_rows.shape[2]
    width = heads * HEAD_DIM
    depth = far_top.shape[1]
    lanes = kinds * HEAD_DIM
    return pl.pallas_call(
        pack_kernel,
        out_shape=jax.ShapeDtypeStruct((devices, heads, CLUST_DEV, SLOT, lanes), BF16),
        grid_spec=pltpu.PrefetchScalarGridSpec(
            num_scalar_prefetch=1,
            grid=(heads,),
            in_specs=[
                pl.BlockSpec((kinds, rows, width), lambda h, w: (0, 0, group)),
                VMEM_WHOLE,
                VMEM_WHOLE,
                pl.BlockSpec((kinds, depth, width), lambda h, w: (0, w[3], group)),
                pl.BlockSpec((1, 1, rows), lambda h, w: (group * heads + h, 0, 0)),
            ],
            out_specs=pl.BlockSpec((devices, 1, CLUST_DEV, SLOT, lanes), lambda h, w: (0, h, 0, 0, 0)),
            scratch_shapes=[pltpu.VMEM((heads, rows, lanes + HEAD_DIM), BF16)],
        ),
        compiler_params=params(),
        name="pack",
    )(where, part, in_vmem(far_top), in_vmem(far_bottom), weights, slot_rows)


def attend_kernel(streamed, received, out, sums):
    devices, heads, _, slot, _ = received.shape
    bucket = devices * slot
    together = out.shape[2]
    scale = 1.0 / math.sqrt(HEAD_DIM)
    rows = lax.broadcasted_iota(jnp.int32, (bucket, bucket), 0)
    cols = lax.broadcasted_iota(jnp.int32, (bucket, bucket), 1)
    causal = cols <= rows
    first_lane = jnp.where(lax.broadcasted_iota(jnp.int32, (16, HEAD_DIM), 1) == 0, 1.0, 0.0).astype(BF16)
    for c in range(together):
        for h in range(heads):
            both = received[:, h, c if streamed else pl.program_id(0) * together + c].reshape(bucket, 3 * HEAD_DIM)
            query, key, value = (both[:, i * HEAD_DIM : (i + 1) * HEAD_DIM] for i in range(3))
            query = jnp.concatenate([query, first_lane], axis=0)
            product = lax.dot_general(query, key, (((1,), (1,)), ((), ())), preferred_element_type=F32)
            filled = product[bucket : bucket + 1] < FULL_BELOW
            scores = jnp.where(causal & filled, product[:bucket] * scale, -1e30)
            row_max = jnp.max(scores, axis=-1, keepdims=True)
            exponentials = jnp.exp(scores - row_max)
            weights = (exponentials / jnp.sum(exponentials, axis=-1, keepdims=True)).astype(BF16)
            out[:, h, c] = dot(weights, value).astype(BF16).reshape(devices, slot, HEAD_DIM)

            key = key.astype(F32)
            scaled = key * lax.rsqrt(jnp.mean(key * key, axis=-1, keepdims=True) + 1e-06)
            unit = (scaled / math.sqrt(HEAD_DIM)).astype(BF16).astype(F32)
            unit = jnp.where(key < FULL_BELOW, unit, 0.0)
            sums[c, h : h + 1] = jnp.sum(unit, axis=0, keepdims=True)


def attend(received, streamed):
    devices, heads, clusters, slot, _ = received.shape
    together = 2
    block = pl.BlockSpec((devices, heads, together, slot, 3 * HEAD_DIM), lambda c: (0, 0, c, 0, 0))
    return pl.pallas_call(
        functools.partial(attend_kernel, streamed),
        out_shape=(
            jax.ShapeDtypeStruct((devices, heads, clusters, slot, HEAD_DIM), BF16),
            jax.ShapeDtypeStruct((clusters, heads, HEAD_DIM), F32),
        ),
        grid=(clusters // together,),
        in_specs=[block if streamed else VMEM_WHOLE],
        out_specs=(
            pl.BlockSpec((devices, heads, together, slot, HEAD_DIM), lambda c: (0, 0, c, 0, 0)),
            pl.BlockSpec((together, heads, HEAD_DIM), lambda c: (c, 0, 0)),
        ),
        compiler_params=params(),
        name="attend",
    )(received if streamed else in_vmem(received))


def unpack_kernel(returned, slot_of, out):
    devices, _, clusters, slot, width = returned.shape
    slots = devices * clusters * slot
    rows = out.shape[0]
    source = returned[:, pl.program_id(0)].reshape(slots, width)
    chunk = 256

    def body(i, carry):
        at = pl.ds(pl.multiple_of(i * chunk, chunk), chunk)
        iota = lax.broadcasted_iota(jnp.int32, (chunk, slots), 1)
        onehot = jnp.where(iota == slot_of[0, at], 1.0, 0.0).astype(BF16)
        out[at] = dot(onehot, source).astype(BF16)
        return carry

    lax.fori_loop(0, rows // chunk, body, 0, unroll=2)


def unpack(returned, slot_cols, group):
    _, heads, _, _, width = returned.shape
    rows = slot_cols.shape[1]
    return pl.pallas_call(
        unpack_kernel,
        out_shape=jax.ShapeDtypeStruct((rows, heads * width), BF16),
        grid=(heads,),
        in_specs=[VMEM_WHOLE, pl.BlockSpec((1, rows, 1), lambda h: (group * heads + h, 0, 0))],
        out_specs=pl.BlockSpec((rows, width), lambda h: (0, h)),
        compiler_params=params(),
        name="unpack",
    )(in_vmem(returned), slot_cols)


def near_kernel(count, *refs):
    blocks, weights, out = refs[:count], refs[count : 2 * count], refs[-1]
    total = dot(blocks[0][...], weights[0][...])
    for block, weight in zip(blocks[1:], weights[1:]):
        total += dot(block[...], weight[...])
    out[...] = total


def finish_kernel(count, *refs):
    near, blocks, weights, out = refs[0], refs[1 : count + 1], refs[count + 1 : 2 * count + 1], refs[-1]
    rows = out.shape[0]
    at = pl.ds(pl.multiple_of(pl.program_id(0) * rows, rows), rows)
    total = near[at]
    for block, weight in zip(blocks, weights):
        total += dot(block[at], weight[...])
    out[...] = total.astype(BF16)


def weight_spec(chunk, depth, width):
    return pl.BlockSpec((depth, width), lambda *_: (chunk, 0))


def near_products(parts, rows, width):
    blocks = [in_vmem(block) for block, _, _ in parts]
    return pl.pallas_call(
        functools.partial(near_kernel, len(parts)),
        out_shape=jax.ShapeDtypeStruct((rows, width), F32),
        grid=(1,),
        in_specs=[VMEM_WHOLE] * len(parts) + [weight_spec(c, b.shape[1], width) for b, _, c in parts],
        out_specs=pl.BlockSpec((rows, width), lambda i: (0, 0)),
        compiler_params=params(),
        name="near_products",
    )(*blocks, *[w for _, w, _ in parts])


def finish(near, parts, rows, width):
    blocks = [in_vmem(block) for block, _, _ in parts]
    steps = 4
    return pl.pallas_call(
        functools.partial(finish_kernel, len(parts)),
        out_shape=jax.ShapeDtypeStruct((rows, width), BF16),
        grid=(steps,),
        in_specs=[VMEM_WHOLE] * (1 + len(parts)) + [weight_spec(c, b.shape[1], width) for b, _, c in parts],
        out_specs=pl.BlockSpec((rows // steps, width), lambda i: (i, 0)),
        compiler_params=params(),
        name="finish",
    )(in_vmem(near), *blocks, *[w for _, w, _ in parts])


def local(tokens, project_weights, output_weights, cluster_ids):
    seq_count = lax.axis_size(SEQ)
    groups = lax.axis_size("head")
    here = lax.axis_index("head")
    width = output_weights.shape[0]
    heads = width // HEAD_DIM
    rows = tokens.shape[0]
    half = rows // 2
    clusters = CLUST_DEV * seq_count

    assigned = cluster_ids[:, :, 0]
    matches = assigned[:, :, None] == jnp.arange(clusters, dtype=jnp.int32)
    row_iota = jnp.arange(rows, dtype=jnp.int32)
    earlier = (row_iota[None, :] < row_iota[:, None]).astype(BF16)
    before = jnp.einsum("ts,hsc->htc", earlier, matches.astype(BF16), preferred_element_type=F32)
    slot_rank = jnp.sum(jnp.where(matches, before, 0.0), axis=2).astype(jnp.int32)
    slot_index = assigned * SLOT + slot_rank
    slot_rows, slot_cols = slot_index[:, None, :], slot_index[:, :, None]

    weights = project_weights.transpose(1, 0, 2)
    where = jnp.stack([here, (here - 1) % groups, (here + 1) % groups, (here + 2) % groups]).astype(jnp.int32)

    top, bottom = tokens[:half], tokens[half:]
    left_top, right_bottom = shifted(top, 1), shifted(bottom, -1)
    left_bottom, right_top = shifted(bottom, 1), shifted(top, -1)
    left_top, right_bottom, slot_rows, slot_cols, where = lax.optimization_barrier(
        (left_top, right_bottom, slot_rows, slot_cols, where)
    )
    far_top, far_bottom = shifted(left_top, 1), shifted(right_bottom, -1)
    part = first_blocks(where, tokens, (left_top, left_bottom, right_top, right_bottom), weights)

    out_weights, far_top, far_bottom = lax.optimization_barrier((output_weights, far_top, far_bottom))
    out_blocks = []
    for by in range(groups):
        block = lax.dynamic_slice(out_weights, (0, (here + by) % groups * width), (width, width))
        out_blocks.append(shifted(block, by) if by else block)

    chunks = 2
    some = heads // chunks
    received = []
    for chunk in range(chunks):
        packed = pack(where, part, far_top, far_bottom, weights, slot_rows, seq_count, chunk, some)
        received.append(lax.all_to_all(packed, SEQ, 0, 0, tiled=True))

    owned, gathered = [], []
    for chunk in range(chunks):
        buckets, sums = attend(received[chunk], streamed=chunk == 0)
        owned.append(sums)
        returned = lax.all_to_all(buckets, SEQ, 0, 0, tiled=True)
        attended = unpack(returned, slot_cols, chunk)
        gathered.append([attended] + [shifted(attended, by) for by in range(1, groups)])

    parts = [(gathered[chunk][by], out_blocks[by], chunk) for chunk in range(chunks) for by in range(groups)]
    near = near_products(parts[: groups + 1], rows, width)
    mixed = finish(near, parts[groups + 1 :], rows, width)
    owned = jnp.concatenate(owned, axis=1).transpose(1, 0, 2)
    return (mixed, owned)


def solution(mesh):
    split = Mesh(
        mesh.devices.reshape(4, 4, 2, mesh.shape["head"]), ("seq_0", "seq_1", "seq_2", "head")
    )
    in_specs = (P(SEQ, "head"), P(None, None, "head"), P("head", None), P("head", SEQ, None))
    out_specs = (P(SEQ, "head"), P("head", SEQ, None))
    return jax.shard_map(local, mesh=split, in_specs=in_specs, out_specs=out_specs, check_vma=False)
```

time: 268 us -> 255 us (0.951)
  the two profiles are of different devices: /device:TPU:26 before, /device:TPU:1 now
where the time goes in v2:
time: 255 us; the launch traced here: 254 us
  waiting for transfers between devices  126 us (49%)
  Pallas kernels  62 us (24%)
  starting transfers between devices  45.8 us (18%)
  local copies, waits for them, and re-layouts  11.6 us (5%)
  other arithmetic  5.32 us (2%)
    all_to_all x2, waiting for transfers between devices, local(): received.append(lax.all_to_all(packed, SEQ, 0, 0, tiled=True))  61.9 us
    ppermute x15, waiting for transfers between devices, shifted(): lax.ppermute(array, 'head', [(i, (i + by) % count) for i in range(count)])  49.6 us
    ppermute x15, starting transfers between devices, shifted(): lax.ppermute(array, 'head', [(i, (i + by) % count) for i in range(count)])  21.7 us
    pallas_call x2, Pallas kernels, pack(): pl.pallas_call(pack_kernel, out_shape=jax.ShapeDtypeStruct((devices, head...  21.7 us
    all_to_all x2, starting transfers between devices, local(): received.append(lax.all_to_all(packed, SEQ, 0, 0, tiled=True))  15.1 us
    all_to_all x2, waiting for transfers between devices, local(): returned = lax.all_to_all(buckets, SEQ, 0, 0, tiled=True)  14.8 us
    pallas_call x2, Pallas kernels, attend(): pl.pallas_call(functools.partial(attend_kernel, streamed), out_shape=(jax...  12.7 us
    pallas_call x2, Pallas kernels, unpack(): pl.pallas_call(unpack_kernel, out_shape=jax.ShapeDtypeStruct((rows, heads...  10.2 us
  transfers between devices with their start and end apart: 19, of which 13 were waited for; matrix products, arithmetic and copies ran while one was open for 6% of the time, Pallas kernels for 19%

profile of v2, /device:TPU:1, one launch (start us, length us, event | category | flops | bytes accessed | tf_op | source)
XLA Modules:
  0.0 254.3 jit_solution(10436831497329683582)
XLA Ops:
  0.6 2.3 fusion.7
  2.9 3.6 %collective-permute-start.1 = (bf16[512,512]{1,0:T(8,128)(2,1)}, bf16[512,512]{1,0:T(8,128)(2,1)S(1)}, u32[]{:S(2)}, u32[]{:S(2)}) collective-permute-start(bf16[512,512]{1,0:T(8,128)(2,1)} %get-tuple-element.38), channel_id=1, source_target_pairs={{0,3},{1,0},{2,1},{3,2},{4,7},{5,4},{6,5},{7,6},{8,11},{9,8},{10,9... | collective-permute-start | bytes 1572872 | tf_op jit(solution)/shard_map/ppermute | solution.py:25
  6.5 2.7 %collective-permute-start.3 = (bf16[512,512]{1,0:T(8,128)(2,1)}, bf16[512,512]{1,0:T(8,128)(2,1)S(1)}, u32[]{:S(2)}, u32[]{:S(2)}) collective-permute-start(bf16[512,512]{1,0:T(8,128)(2,1)} %get-tuple-element.39), channel_id=1, source_target_pairs={{0,3},{1,0},{2,1},{3,2},{4,7},{5,4},{6,5},{7,6},{8,11},{9,8},{10,9... | collective-permute-start | bytes 1572872 | tf_op jit(solution)/shard_map/ppermute | solution.py:25
  9.1 0.7 copy.22
  9.9 2.5 fusion
  12.4 0.6 pad_add_fusion.where
  13.0 2.0 copy.16
  15.0 2.0 copy.18
  17.0 4.1 %multiply_add_fusion = (s32[4,1024,1]{2,1,0:T(8,128)}, s32[4,1024]{1,0:T(4,128)S(1)}) fusion(s32[4,1024,1]{2,1,0:T(8,128)} %copy.18, s32[4,1024,1]{2,1,0:T(8,128)} %copy.16), kind=kLoop, calls=%fused_computation.7 | loop fusion | flops 8192 | bytes 65536 | tf_op jit(solution)/shard_map/add | solution.py:283
  21.0 0.6 reshape_add_fusion.slot_of
  21.7 10.0 %collective-permute-done.left_top = bf16[512,512]{1,0:T(8,128)(2,1)S(1)} collective-permute-done((bf16[512,512]{1,0:T(8,128)(2,1)}, bf16[512,512]{1,0:T(8,128)(2,1)S(1)}, u32[]{:S(2)}, u32[]{:S(2)}) %collective-permute-start) | collective-permute-done | bytes 524320 | tf_op jit(solution)/shard_map/ppermute | solution.py:25
  31.6 2.7 %collective-permute-start.5 = (bf16[512,512]{1,0:T(8,128)(2,1)S(1)}, bf16[512,512]{1,0:T(8,128)(2,1)S(1)}, u32[]{:S(2)}, u32[]{:S(2)}) collective-permute-start(bf16[512,512]{1,0:T(8,128)(2,1)S(1)} %collective-permute-done.1.right_bottom), channel_id=1, source_target_pairs={{0,3},{1,0},{2,1},{3,2},{4,7},{5,4},{6,5},{7,6},{8,11},{9,8},{10,9... | collective-permute-start | bytes 1572872 | tf_op jit(solution)/shard_map/ppermute | solution.py:25
  34.3 9.6 %first_blocks.1.part = f32[3,1024,512]{2,1,0:T(8,128)} custom-call(s32[4]{0:T(128)} %pad_add_fusion.where, bf16[1024,512]{1,0:T(8,128)(2,1)} %own.1, bf16[512,512]{1,0:T(8,128)(2,1)S(1)} %collective-permute-done.left_top, bf16[512,512]{1,0:T(8,128)(2,1)S(1)} %collective-permute-done.2.left_bottom, bf16[512,512]{1,0:T(8,128)(2,1)S(1)} %collective-permute-done.3.right_top, ...), custom_call_target="tpu_custom_call" | custom-call | tf_op jit(solution)/shard_map/first_blocks/pallas_call | solution.py:55
  43.9 0.6 collective-permute-done.4.far_top
  44.5 10.8 %pack.2 = bf16[32,2,8,8,384]{4,3,2,1,0:T(8,128)(2,1)} custom-call(s32[4]{0:T(128)} %pad_add_fusion.where, f32[3,1024,512]{2,1,0:T(8,128)} %first_blocks.1.part, bf16[512,512]{1,0:T(8,128)(2,1)S(1)} %collective-permute-done.4.far_top, bf16[512,512]{1,0:T(8,128)(2,1)S(1)} %collective-permute-done.5.far_bottom, bf16[3,2048,512]{2,1,0:T(8,128)(2,1)} %bitcast.24, ...), custom_call_target="tpu_custom_call" | custom-call | tf_op jit(solution)/shard_map/pack/pallas_call | solution.py:116
  55.3 10.6 %all-to-all-start = ((bf16[32,2,8,8,384]{4,3,2,1,0:T(8,128)(2,1)}), bf16[32,2,8,8,384]{4,3,2,1,0:T(8,128)(2,1)}, u32[]{:S(2)}, u32[]{:S(2)}) async-start(bf16[32,2,8,8,384]{4,3,2,1,0:T(8,128)(2,1)} %pack.2), calls=%async_computation | async-start | bytes 6291456 | tf_op jit(solution)/shard_map/all_to_all | solution.py:309
  66.0 10.8 %pack.3 = bf16[32,2,8,8,384]{4,3,2,1,0:T(8,128)(2,1)} custom-call(s32[4]{0:T(128)} %pad_add_fusion.where, f32[3,1024,512]{2,1,0:T(8,128)} %first_blocks.1.part, bf16[512,512]{1,0:T(8,128)(2,1)S(1)} %collective-permute-done.4.far_top, bf16[512,512]{1,0:T(8,128)(2,1)S(1)} %collective-permute-done.5.far_bottom, bf16[3,2048,512]{2,1,0:T(8,128)(2,1)} %bitcast.25, ...), custom_call_target="tpu_custom_call" | custom-call | tf_op jit(solution)/shard_map/pack/pallas_call | solution.py:116
  76.8 29.0 %all-to-all-done.received = bf16[32,2,8,8,384]{4,3,2,1,0:T(8,128)(2,1)} async-done(((bf16[32,2,8,8,384]{4,3,2,1,0:T(8,128)(2,1)}), bf16[32,2,8,8,384]{4,3,2,1,0:T(8,128)(2,1)}, u32[]{:S(2)}, u32[]{:S(2)}) %all-to-all-start) | async-done | bytes 3145760 | tf_op jit(solution)/shard_map/all_to_all | solution.py:309
  105.8 4.4 %all-to-all-start.2 = ((bf16[32,2,8,8,384]{4,3,2,1,0:T(8,128)(2,1)}), bf16[32,2,8,8,384]{4,3,2,1,0:T(8,128)(2,1)S(1)}, u32[]{:S(2)}, u32[]{:S(2)}) async-start(bf16[32,2,8,8,384]{4,3,2,1,0:T(8,128)(2,1)} %pack.3), calls=%async_computation.2 | async-start | bytes 6291456 | tf_op jit(solution)/shard_map/all_to_all | solution.py:309
  110.2 6.9 %attend.2 = (bf16[32,2,8,8,128]{4,3,2,1,0:T(8,128)(2,1)}, f32[8,2,128]{2,1,0:T(2,128)}) custom-call(bf16[32,2,8,8,384]{4,3,2,1,0:T(8,128)(2,1)} %all-to-all-done.received), custom_call_target="tpu_custom_call" | custom-call | tf_op jit(solution)/shard_map/attend/pallas_call | solution.py:170
  117.1 32.9 %all-to-all-done.2.received = bf16[32,2,8,8,384]{4,3,2,1,0:T(8,128)(2,1)S(1)} async-done(((bf16[32,2,8,8,384]{4,3,2,1,0:T(8,128)(2,1)}), bf16[32,2,8,8,384]{4,3,2,1,0:T(8,128)(2,1)S(1)}, u32[]{:S(2)}, u32[]{:S(2)}) %all-to-all-start.2) | async-done | bytes 3145760 | tf_op jit(solution)/shard_map/all_to_all | solution.py:309
  150.0 5.1 %all-to-all-start.1 = ((bf16[32,2,8,8,128]{4,3,2,1,0:T(8,128)(2,1)}), bf16[32,2,8,8,128]{4,3,2,1,0:T(8,128)(2,1)}, u32[]{:S(2)}, u32[]{:S(2)}) async-start(bf16[32,2,8,8,128]{4,3,2,1,0:T(8,128)(2,1)} %get-tuple-element.20), calls=%async_computation.1 | async-start | bytes 2097152 | tf_op jit(solution)/shard_map/all_to_all | solution.py:315
  155.1 5.8 %attend.3 = (bf16[32,2,8,8,128]{4,3,2,1,0:T(8,128)(2,1)}, f32[8,2,128]{2,1,0:T(2,128)}) custom-call(bf16[32,2,8,8,384]{4,3,2,1,0:T(8,128)(2,1)S(1)} %all-to-all-done.2.received), custom_call_target="tpu_custom_call" | custom-call | tf_op jit(solution)/shard_map/attend/pallas_call | solution.py:170
  161.0 11.2 %all-to-all-done.1.returned = bf16[32,2,8,8,128]{4,3,2,1,0:T(8,128)(2,1)} async-done(((bf16[32,2,8,8,128]{4,3,2,1,0:T(8,128)(2,1)}), bf16[32,2,8,8,128]{4,3,2,1,0:T(8,128)(2,1)}, u32[]{:S(2)}, u32[]{:S(2)}) %all-to-all-start.1) | async-done | bytes 1048608 | tf_op jit(solution)/shard_map/all_to_all | solution.py:315
  172.2 3.9 %all-to-all-start.3 = ((bf16[32,2,8,8,128]{4,3,2,1,0:T(8,128)(2,1)}), bf16[32,2,8,8,128]{4,3,2,1,0:T(8,128)(2,1)S(1)}, u32[]{:S(2)}, u32[]{:S(2)}) async-start(bf16[32,2,8,8,128]{4,3,2,1,0:T(8,128)(2,1)} %get-tuple-element.22), calls=%async_computation.3 | async-start | bytes 2097152 | tf_op jit(solution)/shard_map/all_to_all | solution.py:315
  176.2 1.4 constant_dynamic-slice_fusion
  177.6 1.2 collective-permute-start.10
  178.8 1.5 collective-permute-start.11
  180.2 0.6 collective-permute-start.9
  180.8 5.3 %unpack.2.refs_0_ = bf16[1024,256]{1,0:T(8,128)(2,1)} custom-call(bf16[32,2,8,8,128]{4,3,2,1,0:T(8,128)(2,1)} %all-to-all-done.1.returned, s32[4,1024,1]{2,1,0:T(8,128)} %get-tuple-element.21.slot_of), custom_call_target="tpu_custom_call" | custom-call | tf_op jit(solution)/shard_map/unpack/pallas_call | solution.py:207
  186.1 1.5 collective-permute-start.6
  187.6 1.8 collective-permute-start.7
  189.4 3.6 %all-to-all-done.3.returned = bf16[32,2,8,8,128]{4,3,2,1,0:T(8,128)(2,1)S(1)} async-done(((bf16[32,2,8,8,128]{4,3,2,1,0:T(8,128)(2,1)}), bf16[32,2,8,8,128]{4,3,2,1,0:T(8,128)(2,1)S(1)}, u32[]{:S(2)}, u32[]{:S(2)}) %all-to-all-start.3) | async-done | bytes 1048608 | tf_op jit(solution)/shard_map/all_to_all | solution.py:315
  193.0 5.0 %unpack.3.refs_4_ = bf16[1024,256]{1,0:T(8,128)(2,1)} custom-call(bf16[32,2,8,8,128]{4,3,2,1,0:T(8,128)(2,1)S(1)} %all-to-all-done.3.returned, s32[4,1024,1]{2,1,0:T(8,128)} %get-tuple-element.21.slot_of), custom_call_target="tpu_custom_call" | custom-call | tf_op jit(solution)/shard_map/unpack/pallas_call | solution.py:207
  198.0 2.7 %collective-permute-start.8 = (bf16[1024,256]{1,0:T(8,128)(2,1)S(1)}, bf16[1024,256]{1,0:T(8,128)(2,1)S(1)}, u32[]{:S(2)}, u32[]{:S(2)}) collective-permute-start(bf16[1024,256]{1,0:T(8,128)(2,1)S(1)} %copy-done.1), channel_id=1, source_target_pairs={{0,3},{1,0},{2,1},{3,2},{4,7},{5,4},{6,5},{7,6},{8,11},{9,8},{10,9... | collective-permute-start | bytes 1572872 | tf_op jit(solution)/shard_map/ppermute | solution.py:25
  200.7 3.5 %collective-permute-done.11.refs_8_.refs_6_ = bf16[512,512]{1,0:T(8,128)(2,1)} collective-permute-done((bf16[512,512]{1,0:T(8,128)(2,1)}, bf16[512,512]{1,0:T(8,128)(2,1)}, u32[]{:S(2)}, u32[]{:S(2)}) %collective-permute-start.11) | collective-permute-done | bytes 524320 | tf_op jit(solution)/shard_map/ppermute | solution.py:25
  204.2 0.8 collective-permute-start.12
  205.0 2.7 %collective-permute-start.13 = (bf16[1024,256]{1,0:T(8,128)(2,1)}, bf16[1024,256]{1,0:T(8,128)(2,1)S(1)}, u32[]{:S(2)}, u32[]{:S(2)}) collective-permute-start(bf16[1024,256]{1,0:T(8,128)(2,1)} %unpack.3.refs_4_), channel_id=1, source_target_pairs={{0,2},{1,3},{2,0},{3,1},{4,6},{5,7},{6,4},{7,5},{8,10},{9,11},{10,... | collective-permute-start | bytes 1572872 | tf_op jit(solution)/shard_map/ppermute | solution.py:25
  207.7 8.4 %collective-permute-done.6.refs_1_ = bf16[1024,256]{1,0:T(8,128)(2,1)S(1)} collective-permute-done((bf16[1024,256]{1,0:T(8,128)(2,1)}, bf16[1024,256]{1,0:T(8,128)(2,1)S(1)}, u32[]{:S(2)}, u32[]{:S(2)}) %collective-permute-start.6) | collective-permute-done | bytes 524320 | tf_op jit(solution)/shard_map/ppermute | solution.py:25
  216.2 0.6 copy.19
  216.8 9.5 %collective-permute-done.7.refs_2_ = bf16[1024,256]{1,0:T(8,128)(2,1)S(1)} collective-permute-done((bf16[1024,256]{1,0:T(8,128)(2,1)}, bf16[1024,256]{1,0:T(8,128)(2,1)S(1)}, u32[]{:S(2)}, u32[]{:S(2)}) %collective-permute-start.7) | collective-permute-done | bytes 524320 | tf_op jit(solution)/shard_map/ppermute | solution.py:25
  226.6 1.0 copy-done.2
  227.7 4.1 %near_products.1.refs_0_ = f32[1024,512]{1,0:T(8,128)} custom-call(bf16[1024,256]{1,0:T(8,128)(2,1)S(1)} %copy-done.1, bf16[1024,256]{1,0:T(8,128)(2,1)S(1)} %collective-permute-done.6.refs_1_, bf16[1024,256]{1,0:T(8,128)(2,1)S(1)} %collective-permute-done.7.refs_2_, bf16[1024,256]{1,0:T(8,128)(2,1)S(1)} %collective-permute-done.8.refs_3_, ...), custom_call_target="tpu_custom_call" | custom-call | tf_op jit(solution)/shard_map/near_products/pallas_call | solution.py:242
  231.8 6.8 %collective-permute-done.12.refs_1_ = bf16[1024,256]{1,0:T(8,128)(2,1)S(1)} collective-permute-done((bf16[1024,256]{1,0:T(8,128)(2,1)}, bf16[1024,256]{1,0:T(8,128)(2,1)S(1)}, u32[]{:S(2)}, u32[]{:S(2)}) %collective-permute-start.12) | collective-permute-done | bytes 524320 | tf_op jit(solution)/shard_map/ppermute | solution.py:25
  238.6 10.2 %collective-permute-done.13.refs_2_ = bf16[1024,256]{1,0:T(8,128)(2,1)S(1)} collective-permute-done((bf16[1024,256]{1,0:T(8,128)(2,1)}, bf16[1024,256]{1,0:T(8,128)(2,1)S(1)}, u32[]{:S(2)}, u32[]{:S(2)}) %collective-permute-start.13) | collective-permute-done | bytes 524320 | tf_op jit(solution)/shard_map/ppermute | solution.py:25
  248.8 0.3 collective-permute-done.14.refs_3_
  249.1 1.6 copy-done
  250.7 3.6 %finish.1 = bf16[1024,512]{1,0:T(8,128)(2,1)} custom-call(f32[1024,512]{1,0:T(8,128)S(1)} %copy-done, bf16[1024,256]{1,0:T(8,128)(2,1)S(1)} %collective-permute-done.12.refs_1_, bf16[1024,256]{1,0:T(8,128)(2,1)S(1)} %collective-permute-done.13.refs_2_, bf16[1024,256]{1,0:T(8,128)(2,1)S(1)} %collective-permute-done.14.refs_3_, ...), custom_call_target="tpu_custom_call" | custom-call | tf_op jit(solution)/shard_map/finish/pallas_call | solution.py:256
  (27 shorter events, 0.4 us)
Async XLA Ops:
  2.9 28.7 %collective-permute-start.1 = (bf16[512,512]{1,0:T(8,128)(2,1)}, bf16[512,512]{1,0:T(8,128)(2,1)S(1)}, u32[]{:S(2)}, u32[]{:S(2)}) collective-permute-start(bf16[512,512]{1,0:T(8,128)(2,1)} %get-tuple-element.38), channel_id=1, source_target_pairs={{0,3},{1,0},{2,1},{3,2},{4,7},{5,4},{6,5},{7,6},{8,11},{9,8},{10,9... | collective-permute-start | bytes 1572872 | tf_op jit(solution)/shard_map/ppermute | solution.py:25
  6.4 27.9 %collective-permute-start.2 = (bf16[512,512]{1,0:T(8,128)(2,1)}, bf16[512,512]{1,0:T(8,128)(2,1)S(1)}, u32[]{:S(2)}, u32[]{:S(2)}) collective-permute-start(bf16[512,512]{1,0:T(8,128)(2,1)} %get-tuple-element.38), channel_id=1, source_target_pairs={{0,1},{1,2},{2,3},{3,0},{4,5},{5,6},{6,7},{7,4},{8,9},{9,10},{10,1... | collective-permute-start | bytes 1572872 | tf_op jit(solution)/shard_map/ppermute | solution.py:25
  6.4 25.2 %collective-permute-start = (bf16[512,512]{1,0:T(8,128)(2,1)}, bf16[512,512]{1,0:T(8,128)(2,1)S(1)}, u32[]{:S(2)}, u32[]{:S(2)}) collective-permute-start(bf16[512,512]{1,0:T(8,128)(2,1)} %get-tuple-element.39), channel_id=1, source_target_pairs={{0,1},{1,2},{2,3},{3,0},{4,5},{5,6},{6,7},{7,4},{8,9},{9,10},{10,1... | collective-permute-start | bytes 1572872 | tf_op jit(solution)/shard_map/ppermute | solution.py:25
  6.5 27.8 %collective-permute-start.3 = (bf16[512,512]{1,0:T(8,128)(2,1)}, bf16[512,512]{1,0:T(8,128)(2,1)S(1)}, u32[]{:S(2)}, u32[]{:S(2)}) collective-permute-start(bf16[512,512]{1,0:T(8,128)(2,1)} %get-tuple-element.39), channel_id=1, source_target_pairs={{0,3},{1,0},{2,1},{3,2},{4,7},{5,4},{6,5},{7,6},{8,11},{9,8},{10,9... | collective-permute-start | bytes 1572872 | tf_op jit(solution)/shard_map/ppermute | solution.py:25
  9.9 3.1 %copy-start.5 = (s32[4,1024,1]{1,2,0:T(1,128)S(1)}, s32[4,1024,1]{1,2,0:T(1,128)}, u32[]{:S(2)}) copy-start(s32[4,1024,1]{1,2,0:T(1,128)} %param.7) | copy-start | bytes 49156
  31.6 12.9 %collective-permute-start.4 = (bf16[512,512]{1,0:T(8,128)(2,1)S(1)}, bf16[512,512]{1,0:T(8,128)(2,1)S(1)}, u32[]{:S(2)}, u32[]{:S(2)}) collective-permute-start(bf16[512,512]{1,0:T(8,128)(2,1)S(1)} %collective-permute-done.left_top), channel_id=1, source_target_pairs={{0,1},{1,2},{2,3},{3,0},{4,5},{5,6},{6,7},{7,4},{8,9},{9,10},{10,1... | collective-permute-start | bytes 1572872 | tf_op jit(solution)/shard_map/ppermute | solution.py:25
  31.6 12.9 %collective-permute-start.5 = (bf16[512,512]{1,0:T(8,128)(2,1)S(1)}, bf16[512,512]{1,0:T(8,128)(2,1)S(1)}, u32[]{:S(2)}, u32[]{:S(2)}) collective-permute-start(bf16[512,512]{1,0:T(8,128)(2,1)S(1)} %collective-permute-done.1.right_bottom), channel_id=1, source_target_pairs={{0,3},{1,0},{2,1},{3,2},{4,7},{5,4},{6,5},{7,6},{8,11},{9,8},{10,9... | collective-permute-start | bytes 1572872 | tf_op jit(solution)/shard_map/ppermute | solution.py:25
  55.3 50.4 %all-to-all-start = ((bf16[32,2,8,8,384]{4,3,2,1,0:T(8,128)(2,1)}), bf16[32,2,8,8,384]{4,3,2,1,0:T(8,128)(2,1)}, u32[]{:S(2)}, u32[]{:S(2)}) async-start(bf16[32,2,8,8,384]{4,3,2,1,0:T(8,128)(2,1)} %pack.2), calls=%async_computation | async-start | bytes 6291456 | tf_op jit(solution)/shard_map/all_to_all | solution.py:309
  105.8 44.2 %all-to-all-start.2 = ((bf16[32,2,8,8,384]{4,3,2,1,0:T(8,128)(2,1)}), bf16[32,2,8,8,384]{4,3,2,1,0:T(8,128)(2,1)S(1)}, u32[]{:S(2)}, u32[]{:S(2)}) async-start(bf16[32,2,8,8,384]{4,3,2,1,0:T(8,128)(2,1)} %pack.3), calls=%async_computation.2 | async-start | bytes 6291456 | tf_op jit(solution)/shard_map/all_to_all | solution.py:309
  150.0 22.2 %all-to-all-start.1 = ((bf16[32,2,8,8,128]{4,3,2,1,0:T(8,128)(2,1)}), bf16[32,2,8,8,128]{4,3,2,1,0:T(8,128)(2,1)}, u32[]{:S(2)}, u32[]{:S(2)}) async-start(bf16[32,2,8,8,128]{4,3,2,1,0:T(8,128)(2,1)} %get-tuple-element.20), calls=%async_computation.1 | async-start | bytes 2097152 | tf_op jit(solution)/shard_map/all_to_all | solution.py:315
  161.0 15.2 %copy-start.4 = (bf16[512,2048]{1,0:T(8,128)(2,1)S(1)}, bf16[512,2048]{1,0:T(8,128)(2,1)}, u32[]{:S(2)}) copy-start(bf16[512,2048]{1,0:T(8,128)(2,1)} %param.6) | copy-start | bytes 6291460
  172.2 20.8 %all-to-all-start.3 = ((bf16[32,2,8,8,128]{4,3,2,1,0:T(8,128)(2,1)}), bf16[32,2,8,8,128]{4,3,2,1,0:T(8,128)(2,1)S(1)}, u32[]{:S(2)}, u32[]{:S(2)}) async-start(bf16[32,2,8,8,128]{4,3,2,1,0:T(8,128)(2,1)} %get-tuple-element.22), calls=%async_computation.3 | async-start | bytes 2097152 | tf_op jit(solution)/shard_map/all_to_all | solution.py:315
  177.6 20.4 %collective-permute-start.10 = (bf16[512,512]{1,0:T(8,128)(2,1)}, bf16[512,512]{1,0:T(8,128)(2,1)S(1)}, u32[]{:S(2)}, u32[]{:S(2)}) collective-permute-start(bf16[512,512]{1,0:T(8,128)(2,1)} %get-tuple-element.33), channel_id=1, source_target_pairs={{0,2},{1,3},{2,0},{3,1},{4,6},{5,7},{6,4},{7,5},{8,10},{9,11},{10,... | collective-permute-start | bytes 1572872 | tf_op jit(solution)/shard_map/ppermute | solution.py:25
  178.8 25.4 %collective-permute-start.11 = (bf16[512,512]{1,0:T(8,128)(2,1)}, bf16[512,512]{1,0:T(8,128)(2,1)}, u32[]{:S(2)}, u32[]{:S(2)}) collective-permute-start(bf16[512,512]{1,0:T(8,128)(2,1)} %get-tuple-element.32), channel_id=1, source_target_pairs={{0,3},{1,0},{2,1},{3,2},{4,7},{5,4},{6,5},{7,6},{8,11},{9,8},{10,9... | collective-permute-start | bytes 1572872 | tf_op jit(solution)/shard_map/ppermute | solution.py:25
  180.2 35.9 %copy-start.6 = (f32[8,2,128]{2,1,0:T(2,128)S(1)}, f32[8,2,128]{2,1,0:T(2,128)}, u32[]{:S(2)}) copy-start(f32[8,2,128]{2,1,0:T(2,128)} %get-tuple-element.24) | copy-start | bytes 24580
  180.2 35.9 %copy-start.7 = (f32[8,2,128]{2,1,0:T(2,128)S(1)}, f32[8,2,128]{2,1,0:T(2,128)}, u32[]{:S(2)}) copy-start(f32[8,2,128]{2,1,0:T(2,128)} %get-tuple-element.25) | copy-start | bytes 24580
  180.2 24.8 %collective-permute-start.9 = (bf16[512,512]{1,0:T(8,128)(2,1)}, bf16[512,512]{1,0:T(8,128)(2,1)}, u32[]{:S(2)}, u32[]{:S(2)}) collective-permute-start(bf16[512,512]{1,0:T(8,128)(2,1)} %get-tuple-element.34), channel_id=1, source_target_pairs={{0,1},{1,2},{2,3},{3,0},{4,5},{5,6},{6,7},{7,4},{8,9},{9,10},{10,1... | collective-permute-start | bytes 1572872 | tf_op jit(solution)/shard_map/ppermute | solution.py:25
  186.1 11.9 %copy-start.1 = (bf16[1024,256]{1,0:T(8,128)(2,1)S(1)}, bf16[1024,256]{1,0:T(8,128)(2,1)}, u32[]{:S(2)}) copy-start(bf16[1024,256]{1,0:T(8,128)(2,1)} %unpack.2.refs_0_) | copy-start | bytes 1572868
  186.1 30.1 %collective-permute-start.6 = (bf16[1024,256]{1,0:T(8,128)(2,1)}, bf16[1024,256]{1,0:T(8,128)(2,1)S(1)}, u32[]{:S(2)}, u32[]{:S(2)}) collective-permute-start(bf16[1024,256]{1,0:T(8,128)(2,1)} %unpack.2.refs_0_), channel_id=1, source_target_pairs={{0,1},{1,2},{2,3},{3,0},{4,5},{5,6},{6,7},{7,4},{8,9},{9,10},{10,1... | collective-permute-start | bytes 1572872 | tf_op jit(solution)/shard_map/ppermute | solution.py:25
  187.6 38.8 %collective-permute-start.7 = (bf16[1024,256]{1,0:T(8,128)(2,1)}, bf16[1024,256]{1,0:T(8,128)(2,1)S(1)}, u32[]{:S(2)}, u32[]{:S(2)}) collective-permute-start(bf16[1024,256]{1,0:T(8,128)(2,1)} %unpack.2.refs_0_), channel_id=1, source_target_pairs={{0,2},{1,3},{2,0},{3,1},{4,6},{5,7},{6,4},{7,5},{8,10},{9,11},{10,... | collective-permute-start | bytes 1572872 | tf_op jit(solution)/shard_map/ppermute | solution.py:25
  198.0 28.6 %copy-start.3 = (bf16[512,512]{1,0:T(8,128)(2,1)}, bf16[512,512]{1,0:T(8,128)(2,1)S(1)}, u32[]{:S(2)}) copy-start(bf16[512,512]{1,0:T(8,128)(2,1)S(1)} %collective-permute-done.10.refs_7_.refs_5_) | copy-start | bytes 1572868
  198.0 28.6 %collective-permute-start.8 = (bf16[1024,256]{1,0:T(8,128)(2,1)S(1)}, bf16[1024,256]{1,0:T(8,128)(2,1)S(1)}, u32[]{:S(2)}, u32[]{:S(2)}) collective-permute-start(bf16[1024,256]{1,0:T(8,128)(2,1)S(1)} %copy-done.1), channel_id=1, source_target_pairs={{0,3},{1,0},{2,1},{3,2},{4,7},{5,4},{6,5},{7,6},{8,11},{9,8},{10,9... | collective-permute-start | bytes 1572872 | tf_op jit(solution)/shard_map/ppermute | solution.py:25
  204.2 34.4 %collective-permute-start.12 = (bf16[1024,256]{1,0:T(8,128)(2,1)}, bf16[1024,256]{1,0:T(8,128)(2,1)S(1)}, u32[]{:S(2)}, u32[]{:S(2)}) collective-permute-start(bf16[1024,256]{1,0:T(8,128)(2,1)} %unpack.3.refs_4_), channel_id=1, source_target_pairs={{0,1},{1,2},{2,3},{3,0},{4,5},{5,6},{6,7},{7,4},{8,9},{9,10},{10,1... | collective-permute-start | bytes 1572872 | tf_op jit(solution)/shard_map/ppermute | solution.py:25
  205.0 43.8 %collective-permute-start.13 = (bf16[1024,256]{1,0:T(8,128)(2,1)}, bf16[1024,256]{1,0:T(8,128)(2,1)S(1)}, u32[]{:S(2)}, u32[]{:S(2)}) collective-permute-start(bf16[1024,256]{1,0:T(8,128)(2,1)} %unpack.3.refs_4_), channel_id=1, source_target_pairs={{0,2},{1,3},{2,0},{3,1},{4,6},{5,7},{6,4},{7,5},{8,10},{9,11},{10,... | collective-permute-start | bytes 1572872 | tf_op jit(solution)/shard_map/ppermute | solution.py:25
  216.2 32.9 %collective-permute-start.14 = (bf16[1024,256]{1,0:T(8,128)(2,1)}, bf16[1024,256]{1,0:T(8,128)(2,1)S(1)}, u32[]{:S(2)}, u32[]{:S(2)}) collective-permute-start(bf16[1024,256]{1,0:T(8,128)(2,1)} %unpack.3.refs_4_), channel_id=1, source_target_pairs={{0,3},{1,0},{2,1},{3,2},{4,7},{5,4},{6,5},{7,6},{8,11},{9,8},{10,9... | collective-permute-start | bytes 1572872 | tf_op jit(solution)/shard_map/ppermute | solution.py:25
  226.6 1.0 copy-start.2
  249.1 1.6 copy-start

commit v3 on v2

--- a/solution.py
+++ b/solution.py
@@ -184,21 +184,18 @@
     )(received if streamed else in_vmem(received))
 
 
-def unpack_kernel(returned, slot_of, out):
+def unpack_kernel(returned, slot_of, top, bottom):
     devices, _, clusters, slot, width = returned.shape
     slots = devices * clusters * slot
-    rows = out.shape[0]
+    half = top.shape[0]
     source = returned[:, pl.program_id(0)].reshape(slots, width)
     chunk = 256
 
-    def body(i, carry):
-        at = pl.ds(pl.multiple_of(i * chunk, chunk), chunk)
-        iota = lax.broadcasted_iota(jnp.int32, (chunk, slots), 1)
-        onehot = jnp.where(iota == slot_of[0, at], 1.0, 0.0).astype(BF16)
-        out[at] = dot(onehot, source).astype(BF16)
-        return carry
-
-    lax.fori_loop(0, rows // chunk, body, 0, unroll=2)
+    iota = lax.broadcasted_iota(jnp.int32, (chunk, slots), 1)
+    for start in range(0, 2 * half, chunk):
+        onehot = jnp.where(iota == slot_of[0, start : start + chunk], 1.0, 0.0).astype(BF16)
+        out, to = (top, start) if start < half else (bottom, start - half)
+        out[to : to + chunk] = dot(onehot, source).astype(BF16)
 
 
 def unpack(returned, slot_cols, group):
@@ -206,62 +203,45 @@
     rows = slot_cols.shape[1]
     return pl.pallas_call(
         unpack_kernel,
-        out_shape=jax.ShapeDtypeStruct((rows, heads * width), BF16),
+        out_shape=(jax.ShapeDtypeStruct((rows // 2, heads * width), BF16),) * 2,
         grid=(heads,),
         in_specs=[VMEM_WHOLE, pl.BlockSpec((1, rows, 1), lambda h: (group * heads + h, 0, 0))],
-        out_specs=pl.BlockSpec((rows, width), lambda h: (0, h)),
+        out_specs=(pl.BlockSpec((rows // 2, width), lambda h: (0, h)),) * 2,
         compiler_params=params(),
         name="unpack",
     )(in_vmem(returned), slot_cols)
 
 
-def near_kernel(count, *refs):
-    blocks, weights, out = refs[:count], refs[count : 2 * count], refs[-1]
-    total = dot(blocks[0][...], weights[0][...])
-    for block, weight in zip(blocks[1:], weights[1:]):
-        total += dot(block[...], weight[...])
-    out[...] = total
-
-
-def finish_kernel(count, *refs):
-    near, blocks, weights, out = refs[0], refs[1 : count + 1], refs[count + 1 : 2 * count + 1], refs[-1]
-    rows = out.shape[0]
-    at = pl.ds(pl.multiple_of(pl.program_id(0) * rows, rows), rows)
-    total = near[at]
-    for block, weight in zip(blocks, weights):
-        total += dot(block[at], weight[...])
-    out[...] = total.astype(BF16)
-
-
-def weight_spec(chunk, depth, width):
-    return pl.BlockSpec((depth, width), lambda *_: (chunk, 0))
-
-
-def near_products(parts, rows, width):
-    blocks = [in_vmem(block) for block, _, _ in parts]
-    return pl.pallas_call(
-        functools.partial(near_kernel, len(parts)),
-        out_shape=jax.ShapeDtypeStruct((rows, width), F32),
-        grid=(1,),
-        in_specs=[VMEM_WHOLE] * len(parts) + [weight_spec(c, b.shape[1], width) for b, _, c in parts],
-        out_specs=pl.BlockSpec((rows, width), lambda i: (0, 0)),
-        compiler_params=params(),
-        name="near_products",
-    )(*blocks, *[w for _, w, _ in parts])
-
-
-def finish(near, parts, rows, width):
-    blocks = [in_vmem(block) for block, _, _ in parts]
-    steps = 4
-    return pl.pallas_call(
-        functools.partial(finish_kernel, len(parts)),
-        out_shape=jax.ShapeDtypeStruct((rows, width), BF16),
-        grid=(steps,),
-        in_specs=[VMEM_WHOLE] * (1 + len(parts)) + [weight_spec(c, b.shape[1], width) for b, _, c in parts],
-        out_specs=pl.BlockSpec((rows // steps, width), lambda i: (i, 0)),
-        compiler_params=params(),
-        name="finish",
-    )(in_vmem(near), *blocks, *[w for _, w, _ in parts])
+def products_kernel(count, carried, *refs):
+    pairs, weights = refs[carried : carried + 2 * count], refs[carried + 2 * count : carried + 3 * count]
+    out = refs[-1]
+
+    def add(side):
+        total = refs[0][...] if carried else 0.0
+        for k in range(count):
+            total += dot(pairs[2 * k + side][...], weights[k][...])
+        out[...] = total.astype(out.dtype)
+
+    pl.when(pl.program_id(0) == 0)(lambda: add(0))
+    pl.when(pl.program_id(0) == 1)(lambda: add(1))
+
+
+def products(total, parts, chunk, kind):
+    half, depth = parts[0][0].shape
+    width = parts[0][2].shape[1]
+    block = pl.BlockSpec((half, width), lambda i: (i, 0))
+    carried = [] if total is None else [total]
+    return pl.pallas_call(
+        functools.partial(products_kernel, len(parts), len(carried)),
+        out_shape=jax.ShapeDtypeStruct((2 * half, width), kind),
+        grid=(2,),
+        in_specs=[block] * len(carried)
+        + [VMEM_WHOLE] * (2 * len(parts))
+        + [pl.BlockSpec((depth, width), lambda i: (chunk, 0))] * len(parts),
+        out_specs=block,
+        compiler_params=params(),
+        name="products",
+    )(*carried, *[in_vmem(side) for part in parts for side in part[:2]], *[part[2] for part in parts])
 
 
 def local(tokens, project_weights, output_weights, cluster_ids):
@@ -313,14 +293,20 @@
         buckets, sums = attend(received[chunk], streamed=chunk == 0)
         owned.append(sums)
         returned = lax.all_to_all(buckets, SEQ, 0, 0, tiled=True)
-        attended = unpack(returned, slot_cols, chunk)
-        gathered.append([attended] + [shifted(attended, by) for by in range(1, groups)])
-
-    parts = [(gathered[chunk][by], out_blocks[by], chunk) for chunk in range(chunks) for by in range(groups)]
-    near = near_products(parts[: groups + 1], rows, width)
-    mixed = finish(near, parts[groups + 1 :], rows, width)
+        top, bottom = unpack(returned, slot_cols, chunk)
+        left_top, right_bottom = shifted(top, 1), shifted(bottom, -1)
+        left_bottom, right_top = shifted(bottom, 1), shifted(top, -1)
+        far_top, far_bottom = shifted(left_top, 1), shifted(right_bottom, -1)
+        gathered.append(((top, bottom), (left_top, left_bottom), (far_top, far_bottom), (right_top, right_bottom)))
+
+    total = None
+    for chunk in range(chunks):
+        parts = [(*gathered[chunk][by], out_blocks[by]) for by in range(groups)]
+        last = chunk == chunks - 1
+        total = products(total, parts[:2] + parts[3:], chunk, F32)
+        total = products(total, parts[2:3], chunk, BF16 if last else F32)
     owned = jnp.concatenate(owned, axis=1).transpose(1, 0, 2)
-    return (mixed, owned)
+    return (total, owned)
 
 
 def solution(mesh):

time: 255 us -> 246 us (0.965)
  waiting for transfers between devices: 126 us -> 103 us
  starting transfers between devices: 45.8 us -> 52.4 us
  local copies, waits for them, and re-layouts: 11.6 us -> 15.1 us
  Pallas kernels: 62 us -> 65.2 us
    ppermute x15 -> x21, waiting for transfers between devices: 49.6 us -> 27.3 us  [shifted(): lax.ppermute(array, 'head', [(i, (i + by) % count) for i in range(count)])]
    ppermute x15 -> x21, starting transfers between devices: 21.7 us -> 28.3 us  [shifted(): lax.ppermute(array, 'head', [(i, (i + by) % count) for i in range(count)])]
    pallas_call x4 -> x6, Pallas kernels: 18 us -> 21.2 us  [the longest x4 12.5 us: products(): pl.pallas_call(functools.partial(products_kernel, len(parts), len(carried...]
    unnamed x19 -> x29, local copies, waits for them, and re-layouts: 5.98 us -> 8.92 us
  transfers between devices with their start and end apart: 19 -> 25, of which waited for: 13 -> 11; matrix products, arithmetic and copies ran while one was open for 6% -> 7% of each run, Pallas kernels for 19% -> 21%
where the time goes in v3:
time: 246 us; the launch traced here: 244 us
  waiting for transfers between devices  103 us (42%)
  Pallas kernels  65.2 us (27%)
  starting transfers between devices  52.4 us (21%)
  local copies, waits for them, and re-layouts  15.1 us (6%)
  other arithmetic  5.28 us (2%)
  matrix products  2.48 us (1%)
    all_to_all x2, waiting for transfers between devices, local(): received.append(lax.all_to_all(packed, SEQ, 0, 0, tiled=True))  60.9 us
    ppermute x21, starting transfers between devices, shifted(): lax.ppermute(array, 'head', [(i, (i + by) % count) for i in range(count)])  28.3 us
    ppermute x21, waiting for transfers between devices, shifted(): lax.ppermute(array, 'head', [(i, (i + by) % count) for i in range(count)])  27.3 us
    pallas_call x2, Pallas kernels, pack(): pl.pallas_call(pack_kernel, out_shape=jax.ShapeDtypeStruct((devices, head...  21.6 us
    all_to_all x2, starting transfers between devices, local(): received.append(lax.all_to_all(packed, SEQ, 0, 0, tiled=True))  15.7 us
    all_to_all x2, waiting for transfers between devices, local(): returned = lax.all_to_all(buckets, SEQ, 0, 0, tiled=True)  14.9 us
    pallas_call x2, Pallas kernels, attend(): pl.pallas_call(functools.partial(attend_kernel, streamed), out_shape=(jax...  12.7 us
    pallas_call x4, Pallas kernels, products(): pl.pallas_call(functools.partial(products_kernel, len(parts), len(carried...  12.5 us
  transfers between devices with their start and end apart: 25, of which 11 were waited for; matrix products, arithmetic and copies ran while one was open for 7% of the time, Pallas kernels for 21%

profile of v3, /device:TPU:1, one launch (start us, length us, event | category | flops | bytes accessed | tf_op | source)
XLA Modules:
  0.0 244.3 jit_solution(14326839264887516950)
XLA Ops:
  0.6 1.3 fusion.7
  1.9 3.6 %collective-permute-start.1 = (bf16[512,512]{1,0:T(8,128)(2,1)S(1)}, bf16[512,512]{1,0:T(8,128)(2,1)S(1)}, u32[]{:S(2)}, u32[]{:S(2)}) collective-permute-start(bf16[512,512]{1,0:T(8,128)(2,1)S(1)} %get-tuple-element.46), channel_id=1, source_target_pairs={{0,3},{1,0},{2,1},{3,2},{4,7},{5,4},{6,5},{7,6},{8,11},{9,8},{10,9... | collective-permute-start | bytes 1572872 | tf_op jit(solution)/shard_map/ppermute | solution.py:25
  5.6 2.7 %collective-permute-start.3 = (bf16[512,512]{1,0:T(8,128)(2,1)S(1)}, bf16[512,512]{1,0:T(8,128)(2,1)S(1)}, u32[]{:S(2)}, u32[]{:S(2)}) collective-permute-start(bf16[512,512]{1,0:T(8,128)(2,1)S(1)} %get-tuple-element.47), channel_id=1, source_target_pairs={{0,3},{1,0},{2,1},{3,2},{4,7},{5,4},{6,5},{7,6},{8,11},{9,8},{10,9... | collective-permute-start | bytes 1572872 | tf_op jit(solution)/shard_map/ppermute | solution.py:25
  8.9 2.5 %fusion = f32[4,1024]{1,0:T(4,128)S(1)} fusion(s32[4,1024]{1,0:T(4,128)S(1)} %bitcast.26), kind=kOutput, calls=%fused_computation.1 | convolution fusion | flops 2152722432 | bytes 32768 | tf_op jit(solution)/shard_map/ts,hsc->htc/dot_general | solution.py:261
  12.1 2.0 copy.16
  14.1 1.9 copy.18
  16.0 4.0 %multiply_add_fusion = (s32[4,1024,1]{2,1,0:T(8,128)}, s32[4,1024]{1,0:T(4,128)S(1)}) fusion(s32[4,1024,1]{2,1,0:T(8,128)} %copy.18, s32[4,1024,1]{2,1,0:T(8,128)} %copy.16), kind=kLoop, calls=%fused_computation.7 | loop fusion | flops 8192 | bytes 65536 | tf_op jit(solution)/shard_map/add | solution.py:263
  20.7 9.8 %collective-permute-done.left_top = bf16[512,512]{1,0:T(8,128)(2,1)S(1)} collective-permute-done((bf16[512,512]{1,0:T(8,128)(2,1)S(1)}, bf16[512,512]{1,0:T(8,128)(2,1)S(1)}, u32[]{:S(2)}, u32[]{:S(2)}) %collective-permute-start) | collective-permute-done | bytes 524320 | tf_op jit(solution)/shard_map/ppermute | solution.py:25
  30.5 2.7 %collective-permute-start.5 = (bf16[512,512]{1,0:T(8,128)(2,1)S(1)}, bf16[512,512]{1,0:T(8,128)(2,1)S(1)}, u32[]{:S(2)}, u32[]{:S(2)}) collective-permute-start(bf16[512,512]{1,0:T(8,128)(2,1)S(1)} %collective-permute-done.1.right_bottom), channel_id=1, source_target_pairs={{0,3},{1,0},{2,1},{3,2},{4,7},{5,4},{6,5},{7,6},{8,11},{9,8},{10,9... | collective-permute-start | bytes 1572872 | tf_op jit(solution)/shard_map/ppermute | solution.py:25
  33.2 9.6 %first_blocks.1.part = f32[3,1024,512]{2,1,0:T(8,128)} custom-call(s32[4]{0:T(128)} %pad_add_fusion.where, bf16[1024,512]{1,0:T(8,128)(2,1)} %own.1, bf16[512,512]{1,0:T(8,128)(2,1)S(1)} %collective-permute-done.left_top, bf16[512,512]{1,0:T(8,128)(2,1)S(1)} %collective-permute-done.2.left_bottom, bf16[512,512]{1,0:T(8,128)(2,1)S(1)} %collective-permute-done.3.right_top, ...), custom_call_target="tpu_custom_call" | custom-call | tf_op jit(solution)/shard_map/first_blocks/pallas_call | solution.py:55
  43.4 10.8 %pack.3 = bf16[32,2,8,8,384]{4,3,2,1,0:T(8,128)(2,1)} custom-call(s32[4]{0:T(128)} %pad_add_fusion.where, f32[3,1024,512]{2,1,0:T(8,128)} %first_blocks.1.part, bf16[512,512]{1,0:T(8,128)(2,1)S(1)} %collective-permute-done.4.far_top, bf16[512,512]{1,0:T(8,128)(2,1)S(1)} %collective-permute-done.5.far_bottom, bf16[3,2048,512]{2,1,0:T(8,128)(2,1)} %bitcast.24, ...), custom_call_target="tpu_custom_call" | custom-call | tf_op jit(solution)/shard_map/pack/pallas_call | solution.py:116
  54.2 0.8 copy-done
  55.7 10.6 %all-to-all-start.2 = ((bf16[32,2,8,8,384]{4,3,2,1,0:T(8,128)(2,1)}), bf16[32,2,8,8,384]{4,3,2,1,0:T(8,128)(2,1)S(1)}, u32[]{:S(2)}, u32[]{:S(2)}) async-start(bf16[32,2,8,8,384]{4,3,2,1,0:T(8,128)(2,1)} %pack.3), calls=%async_computation.2 | async-start | bytes 6291456 | tf_op jit(solution)/shard_map/all_to_all | solution.py:289
  66.4 1.0 copy-done.1
  67.4 1.0 copy-done.3
  68.4 10.8 %pack.2 = bf16[32,2,8,8,384]{4,3,2,1,0:T(8,128)(2,1)} custom-call(s32[4]{0:T(128)} %pad_add_fusion.where, f32[3,1024,512]{2,1,0:T(8,128)} %first_blocks.1.part, bf16[512,512]{1,0:T(8,128)(2,1)S(1)} %copy-done.1, bf16[512,512]{1,0:T(8,128)(2,1)S(1)} %copy-done.3, bf16[3,2048,512]{2,1,0:T(8,128)(2,1)} %bitcast.25, s32[4,1,1024]{2,1,0:T(1,128)} %reshape_add_fusion.slot_of), custom_call_target="tpu_custom_call" | custom-call | tf_op jit(solution)/shard_map/pack/pallas_call | solution.py:116
  79.3 26.8 %all-to-all-done.2.received = bf16[32,2,8,8,384]{4,3,2,1,0:T(8,128)(2,1)S(1)} async-done(((bf16[32,2,8,8,384]{4,3,2,1,0:T(8,128)(2,1)}), bf16[32,2,8,8,384]{4,3,2,1,0:T(8,128)(2,1)S(1)}, u32[]{:S(2)}, u32[]{:S(2)}) %all-to-all-start.2) | async-done | bytes 3145760 | tf_op jit(solution)/shard_map/all_to_all | solution.py:289
  106.1 5.1 %all-to-all-start = ((bf16[32,2,8,8,384]{4,3,2,1,0:T(8,128)(2,1)}), bf16[32,2,8,8,384]{4,3,2,1,0:T(8,128)(2,1)}, u32[]{:S(2)}, u32[]{:S(2)}) async-start(bf16[32,2,8,8,384]{4,3,2,1,0:T(8,128)(2,1)} %pack.2), calls=%async_computation | async-start | bytes 6291456 | tf_op jit(solution)/shard_map/all_to_all | solution.py:289
  111.1 5.8 %attend.3 = (bf16[32,2,8,8,128]{4,3,2,1,0:T(8,128)(2,1)}, f32[8,2,128]{2,1,0:T(2,128)}) custom-call(bf16[32,2,8,8,384]{4,3,2,1,0:T(8,128)(2,1)S(1)} %all-to-all-done.2.received), custom_call_target="tpu_custom_call" | custom-call | tf_op jit(solution)/shard_map/attend/pallas_call | solution.py:170
  117.0 34.1 %all-to-all-done.received = bf16[32,2,8,8,384]{4,3,2,1,0:T(8,128)(2,1)} async-done(((bf16[32,2,8,8,384]{4,3,2,1,0:T(8,128)(2,1)}), bf16[32,2,8,8,384]{4,3,2,1,0:T(8,128)(2,1)}, u32[]{:S(2)}, u32[]{:S(2)}) %all-to-all-start) | async-done | bytes 3145760 | tf_op jit(solution)/shard_map/all_to_all | solution.py:289
  151.0 4.5 %all-to-all-start.3 = ((bf16[32,2,8,8,128]{4,3,2,1,0:T(8,128)(2,1)}), bf16[32,2,8,8,128]{4,3,2,1,0:T(8,128)(2,1)S(1)}, u32[]{:S(2)}, u32[]{:S(2)}) async-start(bf16[32,2,8,8,128]{4,3,2,1,0:T(8,128)(2,1)} %get-tuple-element.29), calls=%async_computation.3 | async-start | bytes 2097152 | tf_op jit(solution)/shard_map/all_to_all | solution.py:295
  155.6 6.9 %attend.2 = (bf16[32,2,8,8,128]{4,3,2,1,0:T(8,128)(2,1)}, f32[8,2,128]{2,1,0:T(2,128)}) custom-call(bf16[32,2,8,8,384]{4,3,2,1,0:T(8,128)(2,1)} %all-to-all-done.received), custom_call_target="tpu_custom_call" | custom-call | tf_op jit(solution)/shard_map/attend/pallas_call | solution.py:170
  162.5 10.0 %all-to-all-done.3.returned = bf16[32,2,8,8,128]{4,3,2,1,0:T(8,128)(2,1)S(1)} async-done(((bf16[32,2,8,8,128]{4,3,2,1,0:T(8,128)(2,1)}), bf16[32,2,8,8,128]{4,3,2,1,0:T(8,128)(2,1)S(1)}, u32[]{:S(2)}, u32[]{:S(2)}) %all-to-all-start.3) | async-done | bytes 1048608 | tf_op jit(solution)/shard_map/all_to_all | solution.py:295
  172.5 3.9 %all-to-all-start.1 = ((bf16[32,2,8,8,128]{4,3,2,1,0:T(8,128)(2,1)}), bf16[32,2,8,8,128]{4,3,2,1,0:T(8,128)(2,1)S(1)}, u32[]{:S(2)}, u32[]{:S(2)}) async-start(bf16[32,2,8,8,128]{4,3,2,1,0:T(8,128)(2,1)} %get-tuple-element.24), calls=%async_computation.1 | async-start | bytes 2097152 | tf_op jit(solution)/shard_map/all_to_all | solution.py:295
  176.5 2.9 %constant_dynamic-slice_fusion = (bf16[512,512]{1,0:T(8,128)(2,1)}, bf16[512,512]{1,0:T(8,128)(2,1)}, bf16[512,512]{1,0:T(8,128)(2,1)}, bf16[512,512]{1,0:T(8,128)(2,1)}) fusion(bf16[512,2048]{1,0:T(8,128)(2,1)} %param.6, s32[]{:T(128)S(6)} %select_n.52, s32[]{:T(128)S(6)} %select_n.51, s32[]{:T(128)S(6)} %select_n.49, s32[]{:T(128)S(6)} %select_n.48), kind=kLoop, calls=%fused_computation.12 | loop fusion | bytes 4194320 | tf_op jit(solution)/shard_map/dynamic_slice | solution.py:281
  179.4 2.7 %collective-permute-start.11 = (bf16[512,512]{1,0:T(8,128)(2,1)}, bf16[512,512]{1,0:T(8,128)(2,1)S(1)}, u32[]{:S(2)}, u32[]{:S(2)}) collective-permute-start(bf16[512,512]{1,0:T(8,128)(2,1)} %get-tuple-element.41), channel_id=1, source_target_pairs={{0,3},{1,0},{2,1},{3,2},{4,7},{5,4},{6,5},{7,6},{8,11},{9,8},{10,9... | collective-permute-start | bytes 1572872 | tf_op jit(solution)/shard_map/ppermute | solution.py:25
  182.1 1.2 collective-permute-start.14
  183.3 4.3 %unpack.3 = (bf16[512,256]{1,0:T(8,128)(2,1)}, bf16[512,256]{1,0:T(8,128)(2,1)}) custom-call(bf16[32,2,8,8,128]{4,3,2,1,0:T(8,128)(2,1)S(1)} %all-to-all-done.3.returned, s32[4,1024,1]{2,1,0:T(8,128)} %get-tuple-element.25.slot_of), custom_call_target="tpu_custom_call" | custom-call | tf_op jit(solution)/shard_map/unpack/pallas_call | solution.py:204
  187.6 0.9 collective-permute-start.15
  188.4 4.9 %all-to-all-done.1.returned = bf16[32,2,8,8,128]{4,3,2,1,0:T(8,128)(2,1)S(1)} async-done(((bf16[32,2,8,8,128]{4,3,2,1,0:T(8,128)(2,1)}), bf16[32,2,8,8,128]{4,3,2,1,0:T(8,128)(2,1)S(1)}, u32[]{:S(2)}, u32[]{:S(2)}) %all-to-all-start.1) | async-done | bytes 1048608 | tf_op jit(solution)/shard_map/all_to_all | solution.py:295
  193.3 4.4 %unpack.2 = (bf16[512,256]{1,0:T(8,128)(2,1)}, bf16[512,256]{1,0:T(8,128)(2,1)}) custom-call(bf16[32,2,8,8,128]{4,3,2,1,0:T(8,128)(2,1)S(1)} %all-to-all-done.1.returned, s32[4,1024,1]{2,1,0:T(8,128)} %get-tuple-element.25.slot_of), custom_call_target="tpu_custom_call" | custom-call | tf_op jit(solution)/shard_map/unpack/pallas_call | solution.py:204
  197.7 2.7 %collective-permute-start.18 = (bf16[512,256]{1,0:T(8,128)(2,1)S(1)}, bf16[512,256]{1,0:T(8,128)(2,1)S(1)}, u32[]{:S(2)}, u32[]{:S(2)}) collective-permute-start(bf16[512,256]{1,0:T(8,128)(2,1)S(1)} %copy-done.5), channel_id=1, source_target_pairs={{0,3},{1,0},{2,1},{3,2},{4,7},{5,4},{6,5},{7,6},{8,11},{9,8},{10,9... | collective-permute-start | bytes 786440 | tf_op jit(solution)/shard_map/ppermute | solution.py:25
  200.5 3.2 %collective-permute-done.11.refs_8_.refs_9_ = bf16[512,512]{1,0:T(8,128)(2,1)S(1)} collective-permute-done((bf16[512,512]{1,0:T(8,128)(2,1)}, bf16[512,512]{1,0:T(8,128)(2,1)S(1)}, u32[]{:S(2)}, u32[]{:S(2)}) %collective-permute-start.11) | collective-permute-done | bytes 524320 | tf_op jit(solution)/shard_map/ppermute | solution.py:25
  203.7 3.9 %collective-permute-start.9 = (bf16[512,256]{1,0:T(8,128)(2,1)}, bf16[512,256]{1,0:T(8,128)(2,1)S(1)}, u32[]{:S(2)}, u32[]{:S(2)}) collective-permute-start(bf16[512,256]{1,0:T(8,128)(2,1)} %get-tuple-element.27.refs_1_), channel_id=1, source_target_pairs={{0,3},{1,0},{2,1},{3,2},{4,7},{5,4},{6,5},{7,6},{8,11},{9,8},{10,9... | collective-permute-start | bytes 786440 | tf_op jit(solution)/shard_map/ppermute | solution.py:25
  207.6 3.3 %collective-permute-done.15.refs_3_ = bf16[512,256]{1,0:T(8,128)(2,1)S(1)} collective-permute-done((bf16[512,256]{1,0:T(8,128)(2,1)}, bf16[512,256]{1,0:T(8,128)(2,1)S(1)}, u32[]{:S(2)}, u32[]{:S(2)}) %collective-permute-start.15) | collective-permute-done | bytes 262176 | tf_op jit(solution)/shard_map/ppermute | solution.py:25
  210.9 1.5 collective-permute-start.8
  212.4 4.1 %collective-permute-done.6.refs_2_ = bf16[512,256]{1,0:T(8,128)(2,1)S(1)} collective-permute-done((bf16[512,256]{1,0:T(8,128)(2,1)}, bf16[512,256]{1,0:T(8,128)(2,1)S(1)}, u32[]{:S(2)}, u32[]{:S(2)}) %collective-permute-start.6) | collective-permute-done | bytes 262176 | tf_op jit(solution)/shard_map/ppermute | solution.py:25
  216.8 2.5 %collective-permute-start.13 = (bf16[512,256]{1,0:T(8,128)(2,1)S(1)}, bf16[512,256]{1,0:T(8,128)(2,1)S(1)}, u32[]{:S(2)}, u32[]{:S(2)}) collective-permute-start(bf16[512,256]{1,0:T(8,128)(2,1)S(1)} %collective-permute-done.9.refs_5_), channel_id=1, source_target_pairs={{0,3},{1,0},{2,1},{3,2},{4,7},{5,4},{6,5},{7,6},{8,11},{9,8},{10,9... | collective-permute-start | bytes 786440 | tf_op jit(solution)/shard_map/ppermute | solution.py:25
  219.3 2.9 %collective-permute-done.7.refs_3_ = bf16[512,256]{1,0:T(8,128)(2,1)S(1)} collective-permute-done((bf16[512,256]{1,0:T(8,128)(2,1)}, bf16[512,256]{1,0:T(8,128)(2,1)S(1)}, u32[]{:S(2)}, u32[]{:S(2)}) %collective-permute-start.7) | collective-permute-done | bytes 262176 | tf_op jit(solution)/shard_map/ppermute | solution.py:25
  222.2 1.5 collective-permute-start.17
  224.4 3.4 %collective-permute-done.12.refs_1_ = bf16[512,256]{1,0:T(8,128)(2,1)S(1)} collective-permute-done((bf16[512,256]{1,0:T(8,128)(2,1)S(1)}, bf16[512,256]{1,0:T(8,128)(2,1)S(1)}, u32[]{:S(2)}, u32[]{:S(2)}) %collective-permute-start.12) | collective-permute-done | bytes 262176 | tf_op jit(solution)/shard_map/ppermute | solution.py:25
  227.8 1.5 collective-permute-start.20
  229.9 0.9 copy-done.6
  230.9 0.9 copy-done.7
  231.8 3.3 %products.4.refs_0_ = f32[1024,512]{1,0:T(8,128)} custom-call(bf16[512,256]{1,0:T(8,128)(2,1)S(1)} %copy-done.6, bf16[512,256]{1,0:T(8,128)(2,1)S(1)} %copy-done.7, bf16[512,256]{1,0:T(8,128)(2,1)S(1)} %collective-permute-done.6.refs_2_, bf16[512,256]{1,0:T(8,128)(2,1)S(1)} %collective-permute-done.7.refs_3_, ...), custom_call_target="tpu_custom_call" | custom-call | tf_op jit(solution)/shard_map/products/pallas_call | solution.py:234
  235.1 2.9 %products.5.refs_0_ = f32[1024,512]{1,0:T(8,128)} custom-call(f32[1024,512]{1,0:T(8,128)} %products.4.refs_0_, bf16[512,256]{1,0:T(8,128)(2,1)S(1)} %collective-permute-done.12.refs_1_, bf16[512,256]{1,0:T(8,128)(2,1)S(1)} %collective-permute-done.13.refs_2_, bf16[512,512]{1,0:T(8,128)(2,1)} %collective-permute-done.14.refs_3_), custom_call_target="tpu_custom_call" | custom-call | tf_op jit(solution)/shard_map/products/pallas_call | solution.py:234
  238.0 3.6 %products.6.refs_0_ = f32[1024,512]{1,0:T(8,128)} custom-call(f32[1024,512]{1,0:T(8,128)} %products.5.refs_0_, bf16[512,256]{1,0:T(8,128)(2,1)S(1)} %copy-done.4, bf16[512,256]{1,0:T(8,128)(2,1)S(1)} %copy-done.5, bf16[512,256]{1,0:T(8,128)(2,1)S(1)} %collective-permute-done.15.refs_3_, bf16[512,256]{1,0:T(8,128)(2,1)S(1)} %collective-permute-done.16.refs_4_, ...), custom_call_target="tpu_custom_call" | custom-call | tf_op jit(solution)/shard_map/products/pallas_call | solution.py:234
  241.6 2.7 %products.7 = bf16[1024,512]{1,0:T(8,128)(2,1)} custom-call(f32[1024,512]{1,0:T(8,128)} %products.6.refs_0_, bf16[512,256]{1,0:T(8,128)(2,1)S(1)} %collective-permute-done.19.refs_1_, bf16[512,256]{1,0:T(8,128)(2,1)S(1)} %collective-permute-done.20.refs_2_, bf16[512,512]{1,0:T(8,128)(2,1)} %collective-permute-done.14.refs_3_), custom_call_target="tpu_custom_call" | custom-call | tf_op jit(solution)/shard_map/products/pallas_call | solution.py:234
  (51 shorter events, 5.0 us)
Async XLA Ops:
  1.9 28.6 %collective-permute-start.1 = (bf16[512,512]{1,0:T(8,128)(2,1)S(1)}, bf16[512,512]{1,0:T(8,128)(2,1)S(1)}, u32[]{:S(2)}, u32[]{:S(2)}) collective-permute-start(bf16[512,512]{1,0:T(8,128)(2,1)S(1)} %get-tuple-element.46), channel_id=1, source_target_pairs={{0,3},{1,0},{2,1},{3,2},{4,7},{5,4},{6,5},{7,6},{8,11},{9,8},{10,9... | collective-permute-start | bytes 1572872 | tf_op jit(solution)/shard_map/ppermute | solution.py:25
  5.5 27.7 %collective-permute-start.2 = (bf16[512,512]{1,0:T(8,128)(2,1)S(1)}, bf16[512,512]{1,0:T(8,128)(2,1)S(1)}, u32[]{:S(2)}, u32[]{:S(2)}) collective-permute-start(bf16[512,512]{1,0:T(8,128)(2,1)S(1)} %get-tuple-element.46), channel_id=1, source_target_pairs={{0,1},{1,2},{2,3},{3,0},{4,5},{5,6},{6,7},{7,4},{8,9},{9,10},{10,1... | collective-permute-start | bytes 1572872 | tf_op jit(solution)/shard_map/ppermute | solution.py:25
  5.5 25.0 %collective-permute-start = (bf16[512,512]{1,0:T(8,128)(2,1)S(1)}, bf16[512,512]{1,0:T(8,128)(2,1)S(1)}, u32[]{:S(2)}, u32[]{:S(2)}) collective-permute-start(bf16[512,512]{1,0:T(8,128)(2,1)S(1)} %get-tuple-element.47), channel_id=1, source_target_pairs={{0,1},{1,2},{2,3},{3,0},{4,5},{5,6},{6,7},{7,4},{8,9},{9,10},{10,1... | collective-permute-start | bytes 1572872 | tf_op jit(solution)/shard_map/ppermute | solution.py:25
  5.6 27.6 %collective-permute-start.3 = (bf16[512,512]{1,0:T(8,128)(2,1)S(1)}, bf16[512,512]{1,0:T(8,128)(2,1)S(1)}, u32[]{:S(2)}, u32[]{:S(2)}) collective-permute-start(bf16[512,512]{1,0:T(8,128)(2,1)S(1)} %get-tuple-element.47), channel_id=1, source_target_pairs={{0,3},{1,0},{2,1},{3,2},{4,7},{5,4},{6,5},{7,6},{8,11},{9,8},{10,9... | collective-permute-start | bytes 1572872 | tf_op jit(solution)/shard_map/ppermute | solution.py:25
  8.9 3.1 %copy-start.10 = (s32[4,1024,1]{1,2,0:T(1,128)S(1)}, s32[4,1024,1]{1,2,0:T(1,128)}, u32[]{:S(2)}) copy-start(s32[4,1024,1]{1,2,0:T(1,128)} %param.7) | copy-start | bytes 49156
  30.5 12.9 %collective-permute-start.4 = (bf16[512,512]{1,0:T(8,128)(2,1)S(1)}, bf16[512,512]{1,0:T(8,128)(2,1)S(1)}, u32[]{:S(2)}, u32[]{:S(2)}) collective-permute-start(bf16[512,512]{1,0:T(8,128)(2,1)S(1)} %collective-permute-done.left_top), channel_id=1, source_target_pairs={{0,1},{1,2},{2,3},{3,0},{4,5},{5,6},{6,7},{7,4},{8,9},{9,10},{10,1... | collective-permute-start | bytes 1572872 | tf_op jit(solution)/shard_map/ppermute | solution.py:25
  30.5 12.9 %collective-permute-start.5 = (bf16[512,512]{1,0:T(8,128)(2,1)S(1)}, bf16[512,512]{1,0:T(8,128)(2,1)S(1)}, u32[]{:S(2)}, u32[]{:S(2)}) collective-permute-start(bf16[512,512]{1,0:T(8,128)(2,1)S(1)} %collective-permute-done.1.right_bottom), channel_id=1, source_target_pairs={{0,3},{1,0},{2,1},{3,2},{4,7},{5,4},{6,5},{7,6},{8,11},{9,8},{10,9... | collective-permute-start | bytes 1572872 | tf_op jit(solution)/shard_map/ppermute | solution.py:25
  54.2 0.8 copy-start
  54.9 0.8 copy-start.2
  55.7 50.3 %all-to-all-start.2 = ((bf16[32,2,8,8,384]{4,3,2,1,0:T(8,128)(2,1)}), bf16[32,2,8,8,384]{4,3,2,1,0:T(8,128)(2,1)S(1)}, u32[]{:S(2)}, u32[]{:S(2)}) async-start(bf16[32,2,8,8,384]{4,3,2,1,0:T(8,128)(2,1)} %pack.3), calls=%async_computation.2 | async-start | bytes 6291456 | tf_op jit(solution)/shard_map/all_to_all | solution.py:289
  66.3 1.0 copy-start.1
  67.4 1.0 copy-start.3
  106.1 45.0 %all-to-all-start = ((bf16[32,2,8,8,384]{4,3,2,1,0:T(8,128)(2,1)}), bf16[32,2,8,8,384]{4,3,2,1,0:T(8,128)(2,1)}, u32[]{:S(2)}, u32[]{:S(2)}) async-start(bf16[32,2,8,8,384]{4,3,2,1,0:T(8,128)(2,1)} %pack.2), calls=%async_computation | async-start | bytes 6291456 | tf_op jit(solution)/shard_map/all_to_all | solution.py:289
  151.0 21.5 %all-to-all-start.3 = ((bf16[32,2,8,8,128]{4,3,2,1,0:T(8,128)(2,1)}), bf16[32,2,8,8,128]{4,3,2,1,0:T(8,128)(2,1)S(1)}, u32[]{:S(2)}, u32[]{:S(2)}) async-start(bf16[32,2,8,8,128]{4,3,2,1,0:T(8,128)(2,1)} %get-tuple-element.29), calls=%async_computation.3 | async-start | bytes 2097152 | tf_op jit(solution)/shard_map/all_to_all | solution.py:295
  172.5 20.8 %all-to-all-start.1 = ((bf16[32,2,8,8,128]{4,3,2,1,0:T(8,128)(2,1)}), bf16[32,2,8,8,128]{4,3,2,1,0:T(8,128)(2,1)S(1)}, u32[]{:S(2)}, u32[]{:S(2)}) async-start(bf16[32,2,8,8,128]{4,3,2,1,0:T(8,128)(2,1)} %get-tuple-element.24), calls=%async_computation.1 | async-start | bytes 2097152 | tf_op jit(solution)/shard_map/all_to_all | solution.py:295
  179.4 18.3 %collective-permute-start.10 = (bf16[512,512]{1,0:T(8,128)(2,1)}, bf16[512,512]{1,0:T(8,128)(2,1)S(1)}, u32[]{:S(2)}, u32[]{:S(2)}) collective-permute-start(bf16[512,512]{1,0:T(8,128)(2,1)} %get-tuple-element.42), channel_id=1, source_target_pairs={{0,1},{1,2},{2,3},{3,0},{4,5},{5,6},{6,7},{7,4},{8,9},{9,10},{10,1... | collective-permute-start | bytes 1572872 | tf_op jit(solution)/shard_map/ppermute | solution.py:25
  179.4 24.3 %collective-permute-start.11 = (bf16[512,512]{1,0:T(8,128)(2,1)}, bf16[512,512]{1,0:T(8,128)(2,1)S(1)}, u32[]{:S(2)}, u32[]{:S(2)}) collective-permute-start(bf16[512,512]{1,0:T(8,128)(2,1)} %get-tuple-element.41), channel_id=1, source_target_pairs={{0,3},{1,0},{2,1},{3,2},{4,7},{5,4},{6,5},{7,6},{8,11},{9,8},{10,9... | collective-permute-start | bytes 1572872 | tf_op jit(solution)/shard_map/ppermute | solution.py:25
  182.1 47.2 %copy-start.11 = (f32[8,2,128]{2,1,0:T(2,128)S(1)}, f32[8,2,128]{2,1,0:T(2,128)}, u32[]{:S(2)}) copy-start(f32[8,2,128]{2,1,0:T(2,128)} %get-tuple-element.33) | copy-start | bytes 24580
  182.1 47.2 %copy-start.12 = (f32[8,2,128]{2,1,0:T(2,128)S(1)}, f32[8,2,128]{2,1,0:T(2,128)}, u32[]{:S(2)}) copy-start(f32[8,2,128]{2,1,0:T(2,128)} %get-tuple-element.32) | copy-start | bytes 24580
  182.1 25.5 %collective-permute-start.14 = (bf16[512,512]{1,0:T(8,128)(2,1)}, bf16[512,512]{1,0:T(8,128)(2,1)}, u32[]{:S(2)}, u32[]{:S(2)}) collective-permute-start(bf16[512,512]{1,0:T(8,128)(2,1)} %get-tuple-element.40), channel_id=1, source_target_pairs={{0,2},{1,3},{2,0},{3,1},{4,6},{5,7},{6,4},{7,5},{8,10},{9,11},{10,... | collective-permute-start | bytes 1572872 | tf_op jit(solution)/shard_map/ppermute | solution.py:25
  187.6 10.1 %copy-start.5 = (bf16[512,256]{1,0:T(8,128)(2,1)S(1)}, bf16[512,256]{1,0:T(8,128)(2,1)}, u32[]{:S(2)}) copy-start(bf16[512,256]{1,0:T(8,128)(2,1)} %get-tuple-element.31.refs_2_) | copy-start | bytes 786436
  187.6 34.6 %copy-start.4 = (bf16[512,256]{1,0:T(8,128)(2,1)S(1)}, bf16[512,256]{1,0:T(8,128)(2,1)}, u32[]{:S(2)}) copy-start(bf16[512,256]{1,0:T(8,128)(2,1)} %get-tuple-element.30.refs_1_) | copy-start | bytes 786436
  187.6 23.3 %collective-permute-start.15 = (bf16[512,256]{1,0:T(8,128)(2,1)}, bf16[512,256]{1,0:T(8,128)(2,1)S(1)}, u32[]{:S(2)}, u32[]{:S(2)}) collective-permute-start(bf16[512,256]{1,0:T(8,128)(2,1)} %get-tuple-element.30.refs_1_), channel_id=1, source_target_pairs={{0,1},{1,2},{2,3},{3,0},{4,5},{5,6},{6,7},{7,4},{8,9},{9,10},{10,1... | collective-permute-start | bytes 786440 | tf_op jit(solution)/shard_map/ppermute | solution.py:25
  197.7 18.8 %collective-permute-start.6 = (bf16[512,256]{1,0:T(8,128)(2,1)}, bf16[512,256]{1,0:T(8,128)(2,1)S(1)}, u32[]{:S(2)}, u32[]{:S(2)}) collective-permute-start(bf16[512,256]{1,0:T(8,128)(2,1)} %get-tuple-element.26.refs_0_), channel_id=1, source_target_pairs={{0,1},{1,2},{2,3},{3,0},{4,5},{5,6},{6,7},{7,4},{8,9},{9,10},{10,1... | collective-permute-start | bytes 786440 | tf_op jit(solution)/shard_map/ppermute | solution.py:25
  197.7 32.2 %copy-start.8 = (bf16[512,512]{1,0:T(8,128)(2,1)}, bf16[512,512]{1,0:T(8,128)(2,1)S(1)}, u32[]{:S(2)}) copy-start(bf16[512,512]{1,0:T(8,128)(2,1)S(1)} %collective-permute-done.10.refs_7_.refs_8_) | copy-start | bytes 1572868
  197.7 18.8 %collective-permute-start.18 = (bf16[512,256]{1,0:T(8,128)(2,1)S(1)}, bf16[512,256]{1,0:T(8,128)(2,1)S(1)}, u32[]{:S(2)}, u32[]{:S(2)}) collective-permute-start(bf16[512,256]{1,0:T(8,128)(2,1)S(1)} %copy-done.5), channel_id=1, source_target_pairs={{0,3},{1,0},{2,1},{3,2},{4,7},{5,4},{6,5},{7,6},{8,11},{9,8},{10,9... | collective-permute-start | bytes 786440 | tf_op jit(solution)/shard_map/ppermute | solution.py:25
  203.7 26.2 %copy-start.9 = (bf16[512,512]{1,0:T(8,128)(2,1)}, bf16[512,512]{1,0:T(8,128)(2,1)S(1)}, u32[]{:S(2)}) copy-start(bf16[512,512]{1,0:T(8,128)(2,1)S(1)} %collective-permute-done.11.refs_8_.refs_9_) | copy-start | bytes 1572868
  203.7 13.1 %collective-permute-start.9 = (bf16[512,256]{1,0:T(8,128)(2,1)}, bf16[512,256]{1,0:T(8,128)(2,1)S(1)}, u32[]{:S(2)}, u32[]{:S(2)}) collective-permute-start(bf16[512,256]{1,0:T(8,128)(2,1)} %get-tuple-element.27.refs_1_), channel_id=1, source_target_pairs={{0,3},{1,0},{2,1},{3,2},{4,7},{5,4},{6,5},{7,6},{8,11},{9,8},{10,9... | collective-permute-start | bytes 786440 | tf_op jit(solution)/shard_map/ppermute | solution.py:25
  207.6 14.6 %collective-permute-start.7 = (bf16[512,256]{1,0:T(8,128)(2,1)}, bf16[512,256]{1,0:T(8,128)(2,1)S(1)}, u32[]{:S(2)}, u32[]{:S(2)}) collective-permute-start(bf16[512,256]{1,0:T(8,128)(2,1)} %get-tuple-element.27.refs_1_), channel_id=1, source_target_pairs={{0,1},{1,2},{2,3},{3,0},{4,5},{5,6},{6,7},{7,4},{8,9},{9,10},{10,1... | collective-permute-start | bytes 786440 | tf_op jit(solution)/shard_map/ppermute | solution.py:25
  210.9 12.7 %collective-permute-start.8 = (bf16[512,256]{1,0:T(8,128)(2,1)}, bf16[512,256]{1,0:T(8,128)(2,1)S(1)}, u32[]{:S(2)}, u32[]{:S(2)}) collective-permute-start(bf16[512,256]{1,0:T(8,128)(2,1)} %get-tuple-element.26.refs_0_), channel_id=1, source_target_pairs={{0,3},{1,0},{2,1},{3,2},{4,7},{5,4},{6,5},{7,6},{8,11},{9,8},{10,9... | collective-permute-start | bytes 786440 | tf_op jit(solution)/shard_map/ppermute | solution.py:25
  216.5 11.2 %collective-permute-start.12 = (bf16[512,256]{1,0:T(8,128)(2,1)S(1)}, bf16[512,256]{1,0:T(8,128)(2,1)S(1)}, u32[]{:S(2)}, u32[]{:S(2)}) collective-permute-start(bf16[512,256]{1,0:T(8,128)(2,1)S(1)} %collective-permute-done.6.refs_2_), channel_id=1, source_target_pairs={{0,1},{1,2},{2,3},{3,0},{4,5},{5,6},{6,7},{7,4},{8,9},{9,10},{10,1... | collective-permute-start | bytes 786440 | tf_op jit(solution)/shard_map/ppermute | solution.py:25
  216.5 21.5 %collective-permute-start.16 = (bf16[512,256]{1,0:T(8,128)(2,1)S(1)}, bf16[512,256]{1,0:T(8,128)(2,1)S(1)}, u32[]{:S(2)}, u32[]{:S(2)}) collective-permute-start(bf16[512,256]{1,0:T(8,128)(2,1)S(1)} %copy-done.5), channel_id=1, source_target_pairs={{0,1},{1,2},{2,3},{3,0},{4,5},{5,6},{6,7},{7,4},{8,9},{9,10},{10,1... | collective-permute-start | bytes 786440 | tf_op jit(solution)/shard_map/ppermute | solution.py:25
  216.8 18.3 %collective-permute-start.13 = (bf16[512,256]{1,0:T(8,128)(2,1)S(1)}, bf16[512,256]{1,0:T(8,128)(2,1)S(1)}, u32[]{:S(2)}, u32[]{:S(2)}) collective-permute-start(bf16[512,256]{1,0:T(8,128)(2,1)S(1)} %collective-permute-done.9.refs_5_), channel_id=1, source_target_pairs={{0,3},{1,0},{2,1},{3,2},{4,7},{5,4},{6,5},{7,6},{8,11},{9,8},{10,9... | collective-permute-start | bytes 786440 | tf_op jit(solution)/shard_map/ppermute | solution.py:25
  222.2 15.8 %collective-permute-start.17 = (bf16[512,256]{1,0:T(8,128)(2,1)S(1)}, bf16[512,256]{1,0:T(8,128)(2,1)S(1)}, u32[]{:S(2)}, u32[]{:S(2)}) collective-permute-start(bf16[512,256]{1,0:T(8,128)(2,1)S(1)} %copy-done.4), channel_id=1, source_target_pairs={{0,3},{1,0},{2,1},{3,2},{4,7},{5,4},{6,5},{7,6},{8,11},{9,8},{10,9... | collective-permute-start | bytes 786440 | tf_op jit(solution)/shard_map/ppermute | solution.py:25
  223.7 17.9 %collective-permute-start.19 = (bf16[512,256]{1,0:T(8,128)(2,1)S(1)}, bf16[512,256]{1,0:T(8,128)(2,1)S(1)}, u32[]{:S(2)}, u32[]{:S(2)}) collective-permute-start(bf16[512,256]{1,0:T(8,128)(2,1)S(1)} %collective-permute-done.15.refs_3_), channel_id=1, source_target_pairs={{0,1},{1,2},{2,3},{3,0},{4,5},{5,6},{6,7},{7,4},{8,9},{9,10},{10,1... | collective-permute-start | bytes 786440 | tf_op jit(solution)/shard_map/ppermute | solution.py:25
  227.8 13.8 %collective-permute-start.20 = (bf16[512,256]{1,0:T(8,128)(2,1)S(1)}, bf16[512,256]{1,0:T(8,128)(2,1)S(1)}, u32[]{:S(2)}, u32[]{:S(2)}) collective-permute-start(bf16[512,256]{1,0:T(8,128)(2,1)S(1)} %collective-permute-done.18.refs_6_), channel_id=1, source_target_pairs={{0,3},{1,0},{2,1},{3,2},{4,7},{5,4},{6,5},{7,6},{8,11},{9,8},{10,9... | collective-permute-start | bytes 786440 | tf_op jit(solution)/shard_map/ppermute | solution.py:25
  229.9 1.0 copy-start.6
  230.9 0.9 copy-start.7

commit v4 on v3

--- a/solution.py
+++ b/solution.py
@@ -18,6 +18,8 @@
 BF16 = jnp.bfloat16
 EMPTY = float(1 << 20)
 FULL_BELOW = float(1 << 19)
+
+TURNS = tuple((dz, dc) for dz in range(4) for dc in range(2))
 
 
 def shifted(array, by):
@@ -134,27 +136,42 @@
     )(where, part, in_vmem(far_top), in_vmem(far_bottom), weights, slot_rows)
 
 
-def attend_kernel(streamed, received, out, sums):
-    devices, heads, _, slot, _ = received.shape
-    bucket = devices * slot
-    together = out.shape[2]
+def attend_kernel(outputs, streamed, turn, received, *outs):
+    outs, sums = outs[:outputs], outs[outputs]
+    spans, within, heads, _, slot, _ = received.shape
+    span = within * slot
+    bucket = spans * span
+    together = outs[0].shape[2]
+    first = turn[0] if outputs > 1 else 0
     scale = 1.0 / math.sqrt(HEAD_DIM)
-    rows = lax.broadcasted_iota(jnp.int32, (bucket, bucket), 0)
+    rows = (lax.broadcasted_iota(jnp.int32, (bucket, bucket), 0) + first * span) & (bucket - 1)
     cols = lax.broadcasted_iota(jnp.int32, (bucket, bucket), 1)
     causal = cols <= rows
     first_lane = jnp.where(lax.broadcasted_iota(jnp.int32, (16, HEAD_DIM), 1) == 0, 1.0, 0.0).astype(BF16)
     for c in range(together):
+        at = c if streamed else pl.program_id(0) * together + c
         for h in range(heads):
-            both = received[:, h, c if streamed else pl.program_id(0) * together + c].reshape(bucket, 3 * HEAD_DIM)
-            query, key, value = (both[:, i * HEAD_DIM : (i + 1) * HEAD_DIM] for i in range(3))
-            query = jnp.concatenate([query, first_lane], axis=0)
+            key, value = (
+                received[:, :, h, at, :, i * HEAD_DIM : (i + 1) * HEAD_DIM].reshape(bucket, HEAD_DIM) for i in (1, 2)
+            )
+            if outputs > 1:
+                query = [
+                    received[(first + k) & (spans - 1), :, h, at, :, :HEAD_DIM].reshape(span, HEAD_DIM)
+                    for k in range(spans)
+                ]
+            else:
+                query = [received[:, :, h, at, :, :HEAD_DIM].reshape(bucket, HEAD_DIM)]
+            query = jnp.concatenate([*query, first_lane], axis=0)
             product = lax.dot_general(query, key, (((1,), (1,)), ((), ())), preferred_element_type=F32)
             filled = product[bucket : bucket + 1] < FULL_BELOW
             scores = jnp.where(causal & filled, product[:bucket] * scale, -1e30)
             row_max = jnp.max(scores, axis=-1, keepdims=True)
             exponentials = jnp.exp(scores - row_max)
             weights = (exponentials / jnp.sum(exponentials, axis=-1, keepdims=True)).astype(BF16)
-            out[:, h, c] = dot(weights, value).astype(BF16).reshape(devices, slot, HEAD_DIM)
+            result = dot(weights, value).astype(BF16)
+            rows_out = bucket // outputs
+            for k, out in enumerate(outs):
+                out[:, h, c] = result[k * rows_out : (k + 1) * rows_out].reshape(rows_out // slot, slot, HEAD_DIM)
 
             key = key.astype(F32)
             scaled = key * lax.rsqrt(jnp.mean(key * key, axis=-1, keepdims=True) + 1e-06)
@@ -163,34 +180,65 @@
             sums[c, h : h + 1] = jnp.sum(unit, axis=0, keepdims=True)
 
 
-def attend(received, streamed):
-    devices, heads, clusters, slot, _ = received.shape
+def attend(turn, received, streamed, outputs):
+    spans, within, heads, clusters, slot, _ = received.shape
     together = 2
-    block = pl.BlockSpec((devices, heads, together, slot, 3 * HEAD_DIM), lambda c: (0, 0, c, 0, 0))
-    return pl.pallas_call(
-        functools.partial(attend_kernel, streamed),
-        out_shape=(
-            jax.ShapeDtypeStruct((devices, heads, clusters, slot, HEAD_DIM), BF16),
-            jax.ShapeDtypeStruct((clusters, heads, HEAD_DIM), F32),
+    per_output = spans * within // outputs
+    block = pl.BlockSpec((spans, within, heads, together, slot, 3 * HEAD_DIM), lambda c, t: (0, 0, 0, c, 0, 0))
+    return pl.pallas_call(
+        functools.partial(attend_kernel, outputs, streamed),
+        out_shape=[jax.ShapeDtypeStruct((per_output, heads, clusters, slot, HEAD_DIM), BF16)] * outputs
+        + [jax.ShapeDtypeStruct((clusters, heads, HEAD_DIM), F32)],
+        grid_spec=pltpu.PrefetchScalarGridSpec(
+            num_scalar_prefetch=1,
+            grid=(clusters // together,),
+            in_specs=[block if streamed else VMEM_WHOLE],
+            out_specs=[pl.BlockSpec((per_output, heads, together, slot, HEAD_DIM), lambda c, t: (0, 0, c, 0, 0))] * outputs
+            + [pl.BlockSpec((together, heads, HEAD_DIM), lambda c, t: (c, 0, 0))],
         ),
-        grid=(clusters // together,),
-        in_specs=[block if streamed else VMEM_WHOLE],
-        out_specs=(
-            pl.BlockSpec((devices, heads, together, slot, HEAD_DIM), lambda c: (0, 0, c, 0, 0)),
-            pl.BlockSpec((together, heads, HEAD_DIM), lambda c: (c, 0, 0)),
+        compiler_params=params(),
+        name="attend",
+    )(turn, received if streamed else in_vmem(received))
+
+
+def regroup_kernel(turn, *refs):
+    count = len(TURNS)
+    pieces, outs, sems = refs[:-count - 1], refs[-count - 1 : -1], refs[-1]
+    copies = []
+    for k, (dz, dc) in enumerate(TURNS):
+        at = ((turn[1] + dz) & 3) * 2 + (turn[2] ^ dc)
+        for d, piece in enumerate(pieces):
+            copies.append(pltpu.make_async_copy(piece.at[at], outs[k].at[d], sems.at[k, d]))
+    for copy in copies:
+        copy.start()
+    for copy in copies:
+        copy.wait()
+
+
+def regroup(turn, pieces):
+    shape = (len(pieces), *pieces[0].shape[1:])
+    return pl.pallas_call(
+        regroup_kernel,
+        out_shape=[jax.ShapeDtypeStruct(shape, BF16)] * len(TURNS),
+        grid_spec=pltpu.PrefetchScalarGridSpec(
+            num_scalar_prefetch=1,
+            grid=(1,),
+            in_specs=[pl.BlockSpec(memory_space=pl.ANY)] * len(pieces),
+            out_specs=[pl.BlockSpec(memory_space=pl.ANY)] * len(TURNS),
+            scratch_shapes=[pltpu.SemaphoreType.DMA((len(TURNS), len(pieces)))],
         ),
         compiler_params=params(),
-        name="attend",
-    )(received if streamed else in_vmem(received))
-
-
-def unpack_kernel(returned, slot_of, top, bottom):
-    devices, _, clusters, slot, width = returned.shape
-    slots = devices * clusters * slot
-    half = top.shape[0]
-    source = returned[:, pl.program_id(0)].reshape(slots, width)
+        name="regroup",
+    )(turn, *pieces)
+
+
+def unpack_kernel(count, *refs):
+    pieces, slot_of, top, bottom = refs[:count], refs[count], refs[count + 1], refs[count + 2]
+    half, width = top.shape
+    source = [piece[:, pl.program_id(0)].reshape(-1, width) for piece in pieces]
+    source = jnp.concatenate(source, axis=0) if count > 1 else source[0]
+    slots = source.shape[0]
     chunk = 256
-
     iota = lax.broadcasted_iota(jnp.int32, (chunk, slots), 1)
     for start in range(0, 2 * half, chunk):
         onehot = jnp.where(iota == slot_of[0, start : start + chunk], 1.0, 0.0).astype(BF16)
@@ -198,18 +246,18 @@
         out[to : to + chunk] = dot(onehot, source).astype(BF16)
 
 
-def unpack(returned, slot_cols, group):
-    _, heads, _, _, width = returned.shape
+def unpack(pieces, slot_cols):
+    _, heads, _, _, width = pieces[0].shape
     rows = slot_cols.shape[1]
     return pl.pallas_call(
-        unpack_kernel,
+        functools.partial(unpack_kernel, len(pieces)),
         out_shape=(jax.ShapeDtypeStruct((rows // 2, heads * width), BF16),) * 2,
         grid=(heads,),
-        in_specs=[VMEM_WHOLE, pl.BlockSpec((1, rows, 1), lambda h: (group * heads + h, 0, 0))],
+        in_specs=[VMEM_WHOLE] * len(pieces) + [pl.BlockSpec((1, rows, 1), lambda h: (h, 0, 0))],
         out_specs=(pl.BlockSpec((rows // 2, width), lambda h: (0, h)),) * 2,
         compiler_params=params(),
         name="unpack",
-    )(in_vmem(returned), slot_cols)
+    )(*[in_vmem(piece) for piece in pieces], slot_cols)
 
 
 def products_kernel(count, carried, *refs):
@@ -261,7 +309,8 @@
     before = jnp.einsum("ts,hsc->htc", earlier, matches.astype(BF16), preferred_element_type=F32)
     slot_rank = jnp.sum(jnp.where(matches, before, 0.0), axis=2).astype(jnp.int32)
     slot_index = assigned * SLOT + slot_rank
-    slot_rows, slot_cols = slot_index[:, None, :], slot_index[:, :, None]
+    slot_rows = slot_index[:, None, :]
+    turn = jnp.stack([lax.axis_index(axis) for axis in SEQ]).astype(jnp.int32)
 
     weights = project_weights.transpose(1, 0, 2)
     where = jnp.stack([here, (here - 1) % groups, (here + 1) % groups, (here + 2) % groups]).astype(jnp.int32)
@@ -269,9 +318,7 @@
     top, bottom = tokens[:half], tokens[half:]
     left_top, right_bottom = shifted(top, 1), shifted(bottom, -1)
     left_bottom, right_top = shifted(bottom, 1), shifted(top, -1)
-    left_top, right_bottom, slot_rows, slot_cols, where = lax.optimization_barrier(
-        (left_top, right_bottom, slot_rows, slot_cols, where)
-    )
+    left_top, right_bottom, slot_rows, where = lax.optimization_barrier((left_top, right_bottom, slot_rows, where))
     far_top, far_bottom = shifted(left_top, 1), shifted(right_bottom, -1)
     part = first_blocks(where, tokens, (left_top, left_bottom, right_top, right_bottom), weights)
 
@@ -288,23 +335,39 @@
         packed = pack(where, part, far_top, far_bottom, weights, slot_rows, seq_count, chunk, some)
         received.append(lax.all_to_all(packed, SEQ, 0, 0, tiled=True))
 
+    def offset(by, count):
+        return [(i, (i + by) % count) for i in range(count)]
+
     owned, gathered = [], []
     for chunk in range(chunks):
-        buckets, sums = attend(received[chunk], streamed=chunk == 0)
+        early = chunk == 0
+        slot_of = slot_index[chunk * some : (chunk + 1) * some]
+        arrived = received[chunk].reshape(4, seq_count // 4, some, CLUST_DEV, SLOT, 3 * HEAD_DIM)
+        *buckets, sums = attend(turn, arrived, early, 4 if early else 1)
         owned.append(sums)
-        returned = lax.all_to_all(buckets, SEQ, 0, 0, tiled=True)
-        top, bottom = unpack(returned, slot_cols, chunk)
+        if early:
+            pieces = list(buckets[:1]) + [lax.ppermute(buckets[d], SEQ[0], offset(d, 4)) for d in range(1, 4)]
+            pieces = list(regroup(turn, pieces))
+            for k, (dz, dc) in enumerate(TURNS):
+                if k:
+                    to = [(z * 2 + c, (z + dz) % 4 * 2 + (c ^ dc)) for z in range(4) for c in range(2)]
+                    pieces[k] = lax.ppermute(pieces[k], SEQ[1:], to)
+            owner = slot_of // (CLUST_DEV * SLOT)
+            x, z, core = owner // 8, owner // 2 % 4, owner % 2
+            piece = (((turn[1] - z) & 3) * 2 + (turn[2] ^ core)) * 4 + ((turn[0] - x) & 3)
+            slot_of = piece * (CLUST_DEV * SLOT) + slot_of % (CLUST_DEV * SLOT)
+        else:
+            pieces = [lax.all_to_all(buckets[0], SEQ, 0, 0, tiled=True)]
+        top, bottom = unpack(pieces, slot_of[:, :, None])
         left_top, right_bottom = shifted(top, 1), shifted(bottom, -1)
         left_bottom, right_top = shifted(bottom, 1), shifted(top, -1)
         far_top, far_bottom = shifted(left_top, 1), shifted(right_bottom, -1)
         gathered.append(((top, bottom), (left_top, left_bottom), (far_top, far_bottom), (right_top, right_bottom)))
 
-    total = None
-    for chunk in range(chunks):
-        parts = [(*gathered[chunk][by], out_blocks[by]) for by in range(groups)]
-        last = chunk == chunks - 1
-        total = products(total, parts[:2] + parts[3:], chunk, F32)
-        total = products(total, parts[2:3], chunk, BF16 if last else F32)
+    first, second = ([(*blocks[by], out_blocks[by]) for by in range(groups)] for blocks in gathered)
+    total = products(None, first, 0, F32)
+    total = products(total, second[:2] + second[3:], 1, F32)
+    total = products(total, second[2:3], 1, BF16)
     owned = jnp.concatenate(owned, axis=1).transpose(1, 0, 2)
     return (total, owned)
 

time: 246 us -> 275 us (1.12)
  Pallas kernels: 65.2 us -> 98.2 us
  starting transfers between devices: 52.4 us -> 65 us
  waiting for transfers between devices: 103 us -> 91.5 us
  local copies, waits for them, and re-layouts: 15.1 us -> 11.8 us
  other arithmetic: 5.28 us -> 2.03 us
    pallas_call x4 -> x5, Pallas kernels: 21.4 us -> 56.8 us  [the longest x1 33.8 us: regroup(): pl.pallas_call(regroup_kernel, out_shape=[jax.ShapeDtypeStruct(shape, BF1...]
    ppermute x0 -> x10, starting transfers between devices: none -> 16.5 us  [the longest x7 11.5 us: local(): pieces[k] = lax.ppermute(pieces[k], SEQ[1:], to)]
    all_to_all x2 -> x1, waiting for transfers between devices: 14.9 us -> 0.01 us  [local(): pieces = [lax.all_to_all(buckets[0], SEQ, 0, 0, tiled=True)]]
    all_to_all x2, waiting for transfers between devices: 60.9 us -> 55.2 us  [local(): received.append(lax.all_to_all(packed, SEQ, 0, 0, tiled=True))]
    ppermute x0 -> x10, waiting for transfers between devices: none -> 5.15 us  [the longest x7 5.14 us: local(): pieces[k] = lax.ppermute(pieces[k], SEQ[1:], to)]
    unnamed x29 -> x30, local copies, waits for them, and re-layouts: 8.92 us -> 3.94 us
    add x2, other arithmetic: 4.66 us -> 0.64 us  [local(): slot_index = assigned * SLOT + slot_rank]
    ppermute x21, waiting for transfers between devices: 27.3 us -> 31.1 us  [shifted(): lax.ppermute(array, 'head', [(i, (i + by) % count) for i in range(count)])]
  transfers between devices with their start and end apart: 25 -> 34, of which waited for: 11 -> 11; matrix products, arithmetic and copies ran while one was open for 7% -> 4% of each run, Pallas kernels for 21% -> 31%
where the time goes in v4:
time: 275 us; the launch traced here: 272 us
  Pallas kernels  98.2 us (36%)
  waiting for transfers between devices  91.5 us (33%)
  starting transfers between devices  65 us (24%)
  local copies, waits for them, and re-layouts  11.8 us (4%)
    all_to_all x2, waiting for transfers between devices, local(): received.append(lax.all_to_all(packed, SEQ, 0, 0, tiled=True))  55.2 us
    pallas_call x1, Pallas kernels, regroup(): pl.pallas_call(regroup_kernel, out_shape=[jax.ShapeDtypeStruct(shape, BF1...  33.8 us
    ppermute x21, waiting for transfers between devices, shifted(): lax.ppermute(array, 'head', [(i, (i + by) % count) for i in range(count)])  31.1 us
    ppermute x21, starting transfers between devices, shifted(): lax.ppermute(array, 'head', [(i, (i + by) % count) for i in range(count)])  25.1 us
    pallas_call x2, Pallas kernels, pack(): pl.pallas_call(pack_kernel, out_shape=jax.ShapeDtypeStruct((devices, head...  21.7 us
    all_to_all x2, starting transfers between devices, local(): received.append(lax.all_to_all(packed, SEQ, 0, 0, tiled=True))  15.1 us
    pallas_call x2, Pallas kernels, attend(): pl.pallas_call(functools.partial(attend_kernel, outputs, streamed), out_s...  14.3 us
    ppermute x7, starting transfers between devices, local(): pieces[k] = lax.ppermute(pieces[k], SEQ[1:], to)  11.5 us
  transfers between devices with their start and end apart: 34, of which 11 were waited for; matrix products, arithmetic and copies ran while one was open for 4% of the time, Pallas kernels for 31%

profile of v4, /device:TPU:1, one launch (start us, length us, event | category | flops | bytes accessed | tf_op | source)
XLA Modules:
  0.0 271.9 jit_solution(13398339713058921206)
XLA Ops:
  0.6 2.3 fusion.15
  2.9 3.6 %collective-permute-start.1 = (bf16[512,512]{1,0:T(8,128)(2,1)}, bf16[512,512]{1,0:T(8,128)(2,1)S(1)}, u32[]{:S(2)}, u32[]{:S(2)}) collective-permute-start(bf16[512,512]{1,0:T(8,128)(2,1)} %get-tuple-element.62), channel_id=1, source_target_pairs={{0,3},{1,0},{2,1},{3,2},{4,7},{5,4},{6,5},{7,6},{8,11},{9,8},{10,9... | collective-permute-start | bytes 1572872 | tf_op jit(solution)/shard_map/ppermute | solution.py:27
  6.5 2.7 collective-permute-start.3
  9.9 2.5 fusion
  13.7 17.9 %collective-permute-done.left_top = bf16[512,512]{1,0:T(8,128)(2,1)S(1)} collective-permute-done((bf16[512,512]{1,0:T(8,128)(2,1)}, bf16[512,512]{1,0:T(8,128)(2,1)S(1)}, u32[]{:S(2)}, u32[]{:S(2)}) %collective-permute-start) | collective-permute-done | bytes 524320 | tf_op jit(solution)/shard_map/ppermute | solution.py:27
  31.6 2.7 collective-permute-start.5
  34.3 9.6 %first_blocks.1.part = f32[3,1024,512]{2,1,0:T(8,128)} custom-call(s32[4]{0:T(128)} %pad_add_fusion.1.where, bf16[1024,512]{1,0:T(8,128)(2,1)} %own.1, bf16[512,512]{1,0:T(8,128)(2,1)S(1)} %collective-permute-done.left_top, bf16[512,512]{1,0:T(8,128)(2,1)S(1)} %collective-permute-done.2.left_bottom, bf16[512,512]{1,0:T(8,128)(2,1)S(1)} %collective-permute-done.3.right_top, ...), custom_call_target="tpu_custom_call" | custom-call | tf_op jit(solution)/shard_map/first_blocks/pallas_call | solution.py:57
  44.5 10.8 %pack.2 = bf16[32,2,8,8,384]{4,3,2,1,0:T(8,128)(2,1)} custom-call(s32[4]{0:T(128)} %pad_add_fusion.1.where, f32[3,1024,512]{2,1,0:T(8,128)} %first_blocks.1.part, bf16[512,512]{1,0:T(8,128)(2,1)S(1)} %collective-permute-done.4.far_top, bf16[512,512]{1,0:T(8,128)(2,1)S(1)} %collective-permute-done.5.far_bottom, bf16[3,2048,512]{2,1,0:T(8,128)(2,1)} %bitcast.36, ...), custom_call_target="tpu_custom_call" | custom-call | tf_op jit(solution)/shard_map/pack/pallas_call | solution.py:118
  55.3 10.6 %all-to-all-start = ((bf16[32,2,8,8,384]{4,3,2,1,0:T(8,128)(2,1)}), bf16[32,2,8,8,384]{4,3,2,1,0:T(8,128)(2,1)}, u32[]{:S(2)}, u32[]{:S(2)}) async-start(bf16[32,2,8,8,384]{4,3,2,1,0:T(8,128)(2,1)} %pack.2), calls=%async_computation | async-start | bytes 6291456 | tf_op jit(solution)/shard_map/all_to_all | solution.py:336
  66.0 10.9 %pack.3 = bf16[32,2,8,8,384]{4,3,2,1,0:T(8,128)(2,1)} custom-call(s32[4]{0:T(128)} %pad_add_fusion.1.where, f32[3,1024,512]{2,1,0:T(8,128)} %first_blocks.1.part, bf16[512,512]{1,0:T(8,128)(2,1)S(1)} %collective-permute-done.4.far_top, bf16[512,512]{1,0:T(8,128)(2,1)S(1)} %collective-permute-done.5.far_bottom, bf16[3,2048,512]{2,1,0:T(8,128)(2,1)} %bitcast.37, ...), custom_call_target="tpu_custom_call" | custom-call | tf_op jit(solution)/shard_map/pack/pallas_call | solution.py:118
  76.9 28.9 %all-to-all-done = bf16[32,2,8,8,384]{4,3,2,1,0:T(8,128)(2,1)} async-done(((bf16[32,2,8,8,384]{4,3,2,1,0:T(8,128)(2,1)}), bf16[32,2,8,8,384]{4,3,2,1,0:T(8,128)(2,1)}, u32[]{:S(2)}, u32[]{:S(2)}) %all-to-all-start) | async-done | bytes 3145760 | tf_op jit(solution)/shard_map/all_to_all | solution.py:336
  105.8 4.4 %all-to-all-start.1 = ((bf16[32,2,8,8,384]{4,3,2,1,0:T(8,128)(2,1)}), bf16[32,2,8,8,384]{4,3,2,1,0:T(8,128)(2,1)S(1)}, u32[]{:S(2)}, u32[]{:S(2)}) async-start(bf16[32,2,8,8,384]{4,3,2,1,0:T(8,128)(2,1)} %pack.3), calls=%async_computation.1 | async-start | bytes 6291456 | tf_op jit(solution)/shard_map/all_to_all | solution.py:336
  110.8 7.9 %attend.2 = (bf16[8,2,8,8,128]{4,3,2,1,0:T(8,128)(2,1)}, bf16[8,2,8,8,128]{4,3,2,1,0:T(8,128)(2,1)}, bf16[8,2,8,8,128]{4,3,2,1,0:T(8,128)(2,1)}, bf16[8,2,8,8,128]{4,3,2,1,0:T(8,128)(2,1)}, f32[8,2,128]{2,1,0:T(2,128)}) custom-call(s32[3]{0:T(128)} %pad_add_fusion.turn, bf16[4,8,2,8,8,384]{5,4,3,2,1,0:T(8,128)(2,1)} %bitcast.11.received), custom_call_target="tpu_custom_call" | custom-call | tf_op jit(solution)/shard_map/attend/pallas_call | solution.py:188
  118.7 1.4 collective-permute-start.6
  120.0 2.5 collective-permute-start.7
  122.5 1.1 collective-permute-start.8
  123.7 26.3 %all-to-all-done.1 = bf16[32,2,8,8,384]{4,3,2,1,0:T(8,128)(2,1)S(1)} async-done(((bf16[32,2,8,8,384]{4,3,2,1,0:T(8,128)(2,1)}), bf16[32,2,8,8,384]{4,3,2,1,0:T(8,128)(2,1)S(1)}, u32[]{:S(2)}, u32[]{:S(2)}) %all-to-all-start.1) | async-done | bytes 3145760 | tf_op jit(solution)/shard_map/all_to_all | solution.py:336
  150.0 6.5 %attend.3 = (bf16[32,2,8,8,128]{4,3,2,1,0:T(8,128)(2,1)}, f32[8,2,128]{2,1,0:T(2,128)}) custom-call(s32[3]{0:T(128)} %pad_add_fusion.turn, bf16[4,8,2,8,8,384]{5,4,3,2,1,0:T(8,128)(2,1)S(1)} %bitcast.32), custom_call_target="tpu_custom_call" | custom-call | tf_op jit(solution)/shard_map/attend/pallas_call | solution.py:188
  156.5 8.4 %all-to-all-start.2 = ((bf16[32,2,8,8,128]{4,3,2,1,0:T(8,128)(2,1)}), bf16[32,2,8,8,128]{4,3,2,1,0:T(8,128)(2,1)S(1)}, u32[]{:S(2)}, u32[]{:S(2)}) async-start(bf16[32,2,8,8,128]{4,3,2,1,0:T(8,128)(2,1)} %get-tuple-element.49), calls=%async_computation.2 | async-start | bytes 2097152 | tf_op jit(solution)/shard_map/all_to_all | solution.py:360
  165.6 33.8 %regroup.1 = (bf16[4,2,8,8,128]{4,3,2,1,0:T(8,128)(2,1)}, bf16[4,2,8,8,128]{4,3,2,1,0:T(8,128)(2,1)}, bf16[4,2,8,8,128]{4,3,2,1,0:T(8,128)(2,1)}, bf16[4,2,8,8,1...) custom-call(s32[3]{0:T(128)} %pad_add_fusion.turn, ...), custom_call_target="tpu_custom_call" | custom-call | tf_op jit(solution)/shard_map/regroup/pallas_call | solution.py:220
  199.5 1.4 collective-permute-start.10
  200.9 1.7 collective-permute-start.11
  202.6 1.2 collective-permute-start.12
  203.8 2.9 %constant_dynamic-slice_fusion = (bf16[512,512]{1,0:T(8,128)(2,1)}, bf16[512,512]{1,0:T(8,128)(2,1)}, bf16[512,512]{1,0:T(8,128)(2,1)}, bf16[512,512]{1,0:T(8,128)(2,1)}) fusion(bf16[512,2048]{1,0:T(8,128)(2,1)} %param.6, s32[]{:T(128)S(6)} %select_n.83, s32[]{:T(128)S(6)} %select_n.81, s32[]{:T(128)S(6)} %select_n.80, s32[]{:T(128)S(6)} %select_n.79), kind=kLoop, calls=%fused_computation.36 | loop fusion | bytes 4194320 | tf_op jit(solution)/shard_map/dynamic_slice | solution.py:328
  206.7 3.8 %collective-permute-start.23 = (bf16[512,512]{1,0:T(8,128)(2,1)}, bf16[512,512]{1,0:T(8,128)(2,1)}, u32[]{:S(2)}, u32[]{:S(2)}) collective-permute-start(bf16[512,512]{1,0:T(8,128)(2,1)} %get-tuple-element.59), channel_id=1, source_target_pairs={{0,2},{1,3},{2,0},{3,1},{4,6},{5,7},{6,4},{7,5},{8,10},{9,11},{10,... | collective-permute-start | bytes 1572872 | tf_op jit(solution)/shard_map/ppermute | solution.py:27
  210.6 2.4 collective-permute-start.13
  213.0 1.5 collective-permute-start.14
  214.5 3.4 %collective-permute-done.13.refs_5_ = bf16[4,2,8,8,128]{4,3,2,1,0:T(8,128)(2,1)S(1)} collective-permute-done((bf16[4,2,8,8,128]{4,3,2,1,0:T(8,128)(2,1)S(1)}, bf16[4,2,8,8,128]{4,3,2,1,0:T(8,128)(2,1)S(1)}, u32[]{:S(2)}, u32[]{:S(2)}) %collective-permute-start.13) | collective-permute-done | bytes 131104 | tf_op jit(solution)/shard_map/ppermute | solution.py:354
  217.9 2.8 %collective-permute-start.15 = (bf16[4,2,8,8,128]{4,3,2,1,0:T(8,128)(2,1)}, bf16[4,2,8,8,128]{4,3,2,1,0:T(8,128)(2,1)S(1)}, u32[]{:S(2)}, u32[]{:S(2)}) collective-permute-start(bf16[4,2,8,8,128]{4,3,2,1,0:T(8,128)(2,1)} %get-tuple-element.45), channel_id=1, source_target_pairs={{0,28},{4,24},{8,4},{12,0},{16,12},{20,8},{24,20},{28,16},{1,29},{... | collective-permute-start | bytes 393224 | tf_op jit(solution)/shard_map/ppermute | solution.py:354
  221.3 1.3 copy.11.refs_8_
  222.7 1.6 collective-permute-done.15.refs_7_
  224.3 4.3 %unpack.2 = (bf16[512,256]{1,0:T(8,128)(2,1)}, bf16[512,256]{1,0:T(8,128)(2,1)}) custom-call(bf16[4,2,8,8,128]{4,3,2,1,0:T(8,128)(2,1)S(1)} %copy-done.4, bf16[4,2,8,8,128]{4,3,2,1,0:T(8,128)(2,1)S(1)} %collective-permute-done.9.refs_1_, bf16[4,2,8,8,128]{4,3,2,1,0:T(8,128)(2,1)S(1)} %collective-permute-done.10.refs_2_, ...), custom_call_target="tpu_custom_call" | custom-call | tf_op jit(solution)/shard_map/unpack/pallas_call | solution.py:252
  228.7 1.4 collective-permute-start.16
  230.0 1.3 collective-permute-start.19
  231.4 1.3 copy.12.refs_1_
  232.7 4.3 %unpack.3 = (bf16[512,256]{1,0:T(8,128)(2,1)}, bf16[512,256]{1,0:T(8,128)(2,1)}) custom-call(bf16[32,2,8,8,128]{4,3,2,1,0:T(8,128)(2,1)S(1)} %all-to-all-done.2.refs_0_, s32[2,1024,1]{2,1,0:T(8,128)} %copy.12.refs_1_), custom_call_target="tpu_custom_call" | custom-call | tf_op jit(solution)/shard_map/unpack/pallas_call | solution.py:252
  237.3 2.5 collective-permute-start.21
  240.1 2.7 collective-permute-start.28
  242.8 2.6 collective-permute-done.17.refs_3_
  245.4 1.5 collective-permute-start.26
  246.9 4.1 %collective-permute-done.18.refs_4_ = bf16[512,256]{1,0:T(8,128)(2,1)S(1)} collective-permute-done((bf16[512,256]{1,0:T(8,128)(2,1)S(1)}, bf16[512,256]{1,0:T(8,128)(2,1)S(1)}, u32[]{:S(2)}, u32[]{:S(2)}) %collective-permute-start.18) | collective-permute-done | bytes 262176 | tf_op jit(solution)/shard_map/ppermute | solution.py:27
  251.0 5.6 %collective-permute-done.25.refs_3_ = bf16[512,256]{1,0:T(8,128)(2,1)S(1)} collective-permute-done((bf16[512,256]{1,0:T(8,128)(2,1)}, bf16[512,256]{1,0:T(8,128)(2,1)S(1)}, u32[]{:S(2)}, u32[]{:S(2)}) %collective-permute-start.25) | collective-permute-done | bytes 262176 | tf_op jit(solution)/shard_map/ppermute | solution.py:27
  256.6 2.7 collective-permute-start.30
  260.0 0.9 copy-done
  260.9 0.9 copy-done.1
  261.9 3.7 %products.3.refs_0_ = f32[1024,512]{1,0:T(8,128)} custom-call(bf16[512,256]{1,0:T(8,128)(2,1)S(1)} %copy-done, bf16[512,256]{1,0:T(8,128)(2,1)S(1)} %copy-done.1, bf16[512,256]{1,0:T(8,128)(2,1)S(1)} %collective-permute-done.16.refs_2_, bf16[512,256]{1,0:T(8,128)(2,1)S(1)} %collective-permute-done.17.refs_3_, ...), custom_call_target="tpu_custom_call" | custom-call | tf_op jit(solution)/shard_map/products/pallas_call | solution.py:282
  265.6 3.6 %products.4.refs_0_ = f32[1024,512]{1,0:T(8,128)} custom-call(f32[1024,512]{1,0:T(8,128)} %products.3.refs_0_, bf16[512,256]{1,0:T(8,128)(2,1)S(1)} %copy-done.2, bf16[512,256]{1,0:T(8,128)(2,1)S(1)} %copy-done.3, bf16[512,256]{1,0:T(8,128)(2,1)S(1)} %collective-permute-done.25.refs_3_, bf16[512,256]{1,0:T(8,128)(2,1)S(1)} %collective-permute-done.26.refs_4_, ...), custom_call_target="tpu_custom_call" | custom-call | tf_op jit(solution)/shard_map/products/pallas_call | solution.py:282
  269.2 2.7 %products.5 = bf16[1024,512]{1,0:T(8,128)(2,1)} custom-call(f32[1024,512]{1,0:T(8,128)} %products.4.refs_0_, bf16[512,256]{1,0:T(8,128)(2,1)S(1)} %collective-permute-done.29.refs_1_, bf16[512,256]{1,0:T(8,128)(2,1)S(1)} %collective-permute-done.30.refs_2_, bf16[512,512]{1,0:T(8,128)(2,1)} %collective-permute-done.23.refs_10_.refs_3_), custom_call_target="tpu_custom_call" | custom-call | tf_op jit(solution)/shard_map/products/pallas_call | solution.py:282
  (73 shorter events, 5.8 us)
Async XLA Ops:
  2.9 28.7 %collective-permute-start.1 = (bf16[512,512]{1,0:T(8,128)(2,1)}, bf16[512,512]{1,0:T(8,128)(2,1)S(1)}, u32[]{:S(2)}, u32[]{:S(2)}) collective-permute-start(bf16[512,512]{1,0:T(8,128)(2,1)} %get-tuple-element.62), channel_id=1, source_target_pairs={{0,3},{1,0},{2,1},{3,2},{4,7},{5,4},{6,5},{7,6},{8,11},{9,8},{10,9... | collective-permute-start | bytes 1572872 | tf_op jit(solution)/shard_map/ppermute | solution.py:27
  6.4 27.9 %collective-permute-start.2 = (bf16[512,512]{1,0:T(8,128)(2,1)}, bf16[512,512]{1,0:T(8,128)(2,1)S(1)}, u32[]{:S(2)}, u32[]{:S(2)}) collective-permute-start(bf16[512,512]{1,0:T(8,128)(2,1)} %get-tuple-element.62), channel_id=1, source_target_pairs={{0,1},{1,2},{2,3},{3,0},{4,5},{5,6},{6,7},{7,4},{8,9},{9,10},{10,1... | collective-permute-start | bytes 1572872 | tf_op jit(solution)/shard_map/ppermute | solution.py:27
  6.4 25.2 %collective-permute-start = (bf16[512,512]{1,0:T(8,128)(2,1)}, bf16[512,512]{1,0:T(8,128)(2,1)S(1)}, u32[]{:S(2)}, u32[]{:S(2)}) collective-permute-start(bf16[512,512]{1,0:T(8,128)(2,1)} %get-tuple-element.63), channel_id=1, source_target_pairs={{0,1},{1,2},{2,3},{3,0},{4,5},{5,6},{6,7},{7,4},{8,9},{9,10},{10,1... | collective-permute-start | bytes 1572872 | tf_op jit(solution)/shard_map/ppermute | solution.py:27
  6.5 27.8 %collective-permute-start.3 = (bf16[512,512]{1,0:T(8,128)(2,1)}, bf16[512,512]{1,0:T(8,128)(2,1)S(1)}, u32[]{:S(2)}, u32[]{:S(2)}) collective-permute-start(bf16[512,512]{1,0:T(8,128)(2,1)} %get-tuple-element.63), channel_id=1, source_target_pairs={{0,3},{1,0},{2,1},{3,2},{4,7},{5,4},{6,5},{7,6},{8,11},{9,8},{10,9... | collective-permute-start | bytes 1572872 | tf_op jit(solution)/shard_map/ppermute | solution.py:27
  9.9 3.2 %copy-start.8 = (s32[4,1024,1]{1,2,0:T(1,128)S(1)}, s32[4,1024,1]{1,2,0:T(1,128)}, u32[]{:S(2)}) copy-start(s32[4,1024,1]{1,2,0:T(1,128)} %param.7) | copy-start | bytes 49156
  31.6 12.9 %collective-permute-start.4 = (bf16[512,512]{1,0:T(8,128)(2,1)S(1)}, bf16[512,512]{1,0:T(8,128)(2,1)S(1)}, u32[]{:S(2)}, u32[]{:S(2)}) collective-permute-start(bf16[512,512]{1,0:T(8,128)(2,1)S(1)} %collective-permute-done.left_top), channel_id=1, source_target_pairs={{0,1},{1,2},{2,3},{3,0},{4,5},{5,6},{6,7},{7,4},{8,9},{9,10},{10,1... | collective-permute-start | bytes 1572872 | tf_op jit(solution)/shard_map/ppermute | solution.py:27
  31.6 12.9 %collective-permute-start.5 = (bf16[512,512]{1,0:T(8,128)(2,1)S(1)}, bf16[512,512]{1,0:T(8,128)(2,1)S(1)}, u32[]{:S(2)}, u32[]{:S(2)}) collective-permute-start(bf16[512,512]{1,0:T(8,128)(2,1)S(1)} %collective-permute-done.1.right_bottom), channel_id=1, source_target_pairs={{0,3},{1,0},{2,1},{3,2},{4,7},{5,4},{6,5},{7,6},{8,11},{9,8},{10,9... | collective-permute-start | bytes 1572872 | tf_op jit(solution)/shard_map/ppermute | solution.py:27
  55.3 50.4 %all-to-all-start = ((bf16[32,2,8,8,384]{4,3,2,1,0:T(8,128)(2,1)}), bf16[32,2,8,8,384]{4,3,2,1,0:T(8,128)(2,1)}, u32[]{:S(2)}, u32[]{:S(2)}) async-start(bf16[32,2,8,8,384]{4,3,2,1,0:T(8,128)(2,1)} %pack.2), calls=%async_computation | async-start | bytes 6291456 | tf_op jit(solution)/shard_map/all_to_all | solution.py:336
  105.8 44.2 %all-to-all-start.1 = ((bf16[32,2,8,8,384]{4,3,2,1,0:T(8,128)(2,1)}), bf16[32,2,8,8,384]{4,3,2,1,0:T(8,128)(2,1)S(1)}, u32[]{:S(2)}, u32[]{:S(2)}) async-start(bf16[32,2,8,8,384]{4,3,2,1,0:T(8,128)(2,1)} %pack.3), calls=%async_computation.1 | async-start | bytes 6291456 | tf_op jit(solution)/shard_map/all_to_all | solution.py:336
  118.7 46.2 %collective-permute-start.6 = (bf16[8,2,8,8,128]{4,3,2,1,0:T(8,128)(2,1)}, bf16[8,2,8,8,128]{4,3,2,1,0:T(8,128)(2,1)S(1)}, u32[]{:S(2)}, u32[]{:S(2)}) collective-permute-start(bf16[8,2,8,8,128]{4,3,2,1,0:T(8,128)(2,1)} %get-tuple-element.35), channel_id=1, source_target_pairs={{0,32},{32,64},{64,96},{96,0},{1,33},{33,65},{65,97},{97,1},{2,34}... | collective-permute-start | bytes 786440 | tf_op jit(solution)/shard_map/ppermute | solution.py:349
  120.0 44.9 %collective-permute-start.7 = (bf16[8,2,8,8,128]{4,3,2,1,0:T(8,128)(2,1)}, bf16[8,2,8,8,128]{4,3,2,1,0:T(8,128)(2,1)}, u32[]{:S(2)}, u32[]{:S(2)}) collective-permute-start(bf16[8,2,8,8,128]{4,3,2,1,0:T(8,128)(2,1)} %get-tuple-element.36), channel_id=1, source_target_pairs={{0,64},{32,96},{64,0},{96,32},{1,65},{33,97},{65,1},{97,33},{2,66}... | collective-permute-start | bytes 786440 | tf_op jit(solution)/shard_map/ppermute | solution.py:349
  122.5 42.4 %collective-permute-start.8 = (bf16[8,2,8,8,128]{4,3,2,1,0:T(8,128)(2,1)}, bf16[8,2,8,8,128]{4,3,2,1,0:T(8,128)(2,1)}, u32[]{:S(2)}, u32[]{:S(2)}) collective-permute-start(bf16[8,2,8,8,128]{4,3,2,1,0:T(8,128)(2,1)} %get-tuple-element.37), channel_id=1, source_target_pairs={{0,96},{32,0},{64,32},{96,64},{1,97},{33,1},{65,33},{97,65},{2,98}... | collective-permute-start | bytes 786440 | tf_op jit(solution)/shard_map/ppermute | solution.py:349
  156.5 76.2 %all-to-all-start.2 = ((bf16[32,2,8,8,128]{4,3,2,1,0:T(8,128)(2,1)}), bf16[32,2,8,8,128]{4,3,2,1,0:T(8,128)(2,1)S(1)}, u32[]{:S(2)}, u32[]{:S(2)}) async-start(bf16[32,2,8,8,128]{4,3,2,1,0:T(8,128)(2,1)} %get-tuple-element.49), calls=%async_computation.2 | async-start | bytes 2097152 | tf_op jit(solution)/shard_map/all_to_all | solution.py:360
  164.9 0.7 copy-start.7
  199.4 11.1 %copy-start.13 = (bf16[4,2,8,8,128]{4,3,2,1,0:T(8,128)(2,1)S(1)}, bf16[4,2,8,8,128]{4,3,2,1,0:T(8,128)(2,1)}, u32[]{:S(2)}) copy-start(bf16[4,2,8,8,128]{4,3,2,1,0:T(8,128)(2,1)} %get-tuple-element.43) | copy-start | bytes 393220
  199.4 13.6 %copy-start.12 = (bf16[4,2,8,8,128]{4,3,2,1,0:T(8,128)(2,1)S(1)}, bf16[4,2,8,8,128]{4,3,2,1,0:T(8,128)(2,1)}, u32[]{:S(2)}) copy-start(bf16[4,2,8,8,128]{4,3,2,1,0:T(8,128)(2,1)} %get-tuple-element.44) | copy-start | bytes 393220
  199.5 21.4 %copy-start.11 = (bf16[4,2,8,8,128]{4,3,2,1,0:T(8,128)(2,1)S(1)}, bf16[4,2,8,8,128]{4,3,2,1,0:T(8,128)(2,1)}, u32[]{:S(2)}) copy-start(bf16[4,2,8,8,128]{4,3,2,1,0:T(8,128)(2,1)} %get-tuple-element.39) | copy-start | bytes 393220
  199.5 24.9 %copy-start.4 = (bf16[4,2,8,8,128]{4,3,2,1,0:T(8,128)(2,1)S(1)}, bf16[4,2,8,8,128]{4,3,2,1,0:T(8,128)(2,1)}, u32[]{:S(2)}) copy-start(bf16[4,2,8,8,128]{4,3,2,1,0:T(8,128)(2,1)} %get-tuple-element.38.refs_0_) | copy-start | bytes 393220
  199.5 11.1 %collective-permute-start.10 = (bf16[4,2,8,8,128]{4,3,2,1,0:T(8,128)(2,1)}, bf16[4,2,8,8,128]{4,3,2,1,0:T(8,128)(2,1)S(1)}, u32[]{:S(2)}, u32[]{:S(2)}) collective-permute-start(bf16[4,2,8,8,128]{4,3,2,1,0:T(8,128)(2,1)} %get-tuple-element.40), channel_id=1, source_target_pairs={{0,8},{4,12},{8,16},{12,20},{16,24},{20,28},{24,0},{28,4},{1,9},{5... | collective-permute-start | bytes 393224 | tf_op jit(solution)/shard_map/ppermute | solution.py:354
  200.9 9.7 %collective-permute-start.11 = (bf16[4,2,8,8,128]{4,3,2,1,0:T(8,128)(2,1)}, bf16[4,2,8,8,128]{4,3,2,1,0:T(8,128)(2,1)S(1)}, u32[]{:S(2)}, u32[]{:S(2)}) collective-permute-start(bf16[4,2,8,8,128]{4,3,2,1,0:T(8,128)(2,1)} %get-tuple-element.41), channel_id=1, source_target_pairs={{0,12},{4,8},{8,20},{12,16},{16,28},{20,24},{24,4},{28,0},{1,13},{... | collective-permute-start | bytes 393224 | tf_op jit(solution)/shard_map/ppermute | solution.py:354
  202.6 10.4 %collective-permute-start.12 = (bf16[4,2,8,8,128]{4,3,2,1,0:T(8,128)(2,1)}, bf16[4,2,8,8,128]{4,3,2,1,0:T(8,128)(2,1)S(1)}, u32[]{:S(2)}, u32[]{:S(2)}) collective-permute-start(bf16[4,2,8,8,128]{4,3,2,1,0:T(8,128)(2,1)} %get-tuple-element.42), channel_id=1, source_target_pairs={{0,16},{4,20},{8,24},{12,28},{16,0},{20,4},{24,8},{28,12},{1,17},{... | collective-permute-start | bytes 393224 | tf_op jit(solution)/shard_map/ppermute | solution.py:354
  206.7 52.6 %copy-start.9 = (f32[8,2,128]{2,1,0:T(2,128)S(1)}, f32[8,2,128]{2,1,0:T(2,128)}, u32[]{:S(2)}) copy-start(f32[8,2,128]{2,1,0:T(2,128)} %get-tuple-element.52) | copy-start | bytes 24580
  206.7 52.6 %copy-start.10 = (f32[8,2,128]{2,1,0:T(2,128)S(1)}, f32[8,2,128]{2,1,0:T(2,128)}, u32[]{:S(2)}) copy-start(f32[8,2,128]{2,1,0:T(2,128)} %get-tuple-element.53) | copy-start | bytes 24580
  206.7 30.3 %collective-permute-start.22 = (bf16[512,512]{1,0:T(8,128)(2,1)}, bf16[512,512]{1,0:T(8,128)(2,1)S(1)}, u32[]{:S(2)}, u32[]{:S(2)}) collective-permute-start(bf16[512,512]{1,0:T(8,128)(2,1)} %get-tuple-element.60), channel_id=1, source_target_pairs={{0,1},{1,2},{2,3},{3,0},{4,5},{5,6},{6,7},{7,4},{8,9},{9,10},{10,1... | collective-permute-start | bytes 1572872 | tf_op jit(solution)/shard_map/ppermute | solution.py:27
  206.7 30.5 %collective-permute-start.23 = (bf16[512,512]{1,0:T(8,128)(2,1)}, bf16[512,512]{1,0:T(8,128)(2,1)}, u32[]{:S(2)}, u32[]{:S(2)}) collective-permute-start(bf16[512,512]{1,0:T(8,128)(2,1)} %get-tuple-element.59), channel_id=1, source_target_pairs={{0,2},{1,3},{2,0},{3,1},{4,6},{5,7},{6,4},{7,5},{8,10},{9,11},{10,... | collective-permute-start | bytes 1572872 | tf_op jit(solution)/shard_map/ppermute | solution.py:27
  210.6 29.5 %collective-permute-start.24 = (bf16[512,512]{1,0:T(8,128)(2,1)}, bf16[512,512]{1,0:T(8,128)(2,1)S(1)}, u32[]{:S(2)}, u32[]{:S(2)}) collective-permute-start(bf16[512,512]{1,0:T(8,128)(2,1)} %get-tuple-element.58), channel_id=1, source_target_pairs={{0,3},{1,0},{2,1},{3,2},{4,7},{5,4},{6,5},{7,6},{8,11},{9,8},{10,9... | collective-permute-start | bytes 1572872 | tf_op jit(solution)/shard_map/ppermute | solution.py:27
  210.6 7.4 %collective-permute-start.13 = (bf16[4,2,8,8,128]{4,3,2,1,0:T(8,128)(2,1)S(1)}, bf16[4,2,8,8,128]{4,3,2,1,0:T(8,128)(2,1)S(1)}, u32[]{:S(2)}, u32[]{:S(2)}) collective-permute-start(bf16[4,2,8,8,128]{4,3,2,1,0:T(8,128)(2,1)S(1)} %copy-done.13), channel_id=1, source_target_pairs={{0,20},{4,16},{8,28},{12,24},{16,4},{20,0},{24,12},{28,8},{1,21},{... | collective-permute-start | bytes 393224 | tf_op jit(solution)/shard_map/ppermute | solution.py:354
  213.0 7.8 %collective-permute-start.14 = (bf16[4,2,8,8,128]{4,3,2,1,0:T(8,128)(2,1)S(1)}, bf16[4,2,8,8,128]{4,3,2,1,0:T(8,128)(2,1)S(1)}, u32[]{:S(2)}, u32[]{:S(2)}) collective-permute-start(bf16[4,2,8,8,128]{4,3,2,1,0:T(8,128)(2,1)S(1)} %copy-done.12), channel_id=1, source_target_pairs={{0,24},{4,28},{8,0},{12,4},{16,8},{20,12},{24,16},{28,20},{1,25},{... | collective-permute-start | bytes 393224 | tf_op jit(solution)/shard_map/ppermute | solution.py:354
  217.9 6.4 %collective-permute-start.15 = (bf16[4,2,8,8,128]{4,3,2,1,0:T(8,128)(2,1)}, bf16[4,2,8,8,128]{4,3,2,1,0:T(8,128)(2,1)S(1)}, u32[]{:S(2)}, u32[]{:S(2)}) collective-permute-start(bf16[4,2,8,8,128]{4,3,2,1,0:T(8,128)(2,1)} %get-tuple-element.45), channel_id=1, source_target_pairs={{0,28},{4,24},{8,4},{12,0},{16,12},{20,8},{24,20},{28,16},{1,29},{... | collective-permute-start | bytes 393224 | tf_op jit(solution)/shard_map/ppermute | solution.py:354
  220.8 3.5 %collective-permute-start.9 = (bf16[4,2,8,8,128]{4,3,2,1,0:T(8,128)(2,1)S(1)}, bf16[4,2,8,8,128]{4,3,2,1,0:T(8,128)(2,1)S(1)}, u32[]{:S(2)}, u32[]{:S(2)}) collective-permute-start(bf16[4,2,8,8,128]{4,3,2,1,0:T(8,128)(2,1)S(1)} %copy-done.11), channel_id=1, source_target_pairs={{0,4},{4,0},{8,12},{12,8},{16,20},{20,16},{24,28},{28,24},{1,5},{5... | collective-permute-start | bytes 393224 | tf_op jit(solution)/shard_map/ppermute | solution.py:354
  228.7 11.3 %collective-permute-start.16 = (bf16[512,256]{1,0:T(8,128)(2,1)}, bf16[512,256]{1,0:T(8,128)(2,1)S(1)}, u32[]{:S(2)}, u32[]{:S(2)}) collective-permute-start(bf16[512,256]{1,0:T(8,128)(2,1)} %get-tuple-element.46.refs_0_), channel_id=1, source_target_pairs={{0,1},{1,2},{2,3},{3,0},{4,5},{5,6},{6,7},{7,4},{8,9},{9,10},{10,1... | collective-permute-start | bytes 786440 | tf_op jit(solution)/shard_map/ppermute | solution.py:27
  230.0 10.1 %collective-permute-start.19 = (bf16[512,256]{1,0:T(8,128)(2,1)}, bf16[512,256]{1,0:T(8,128)(2,1)S(1)}, u32[]{:S(2)}, u32[]{:S(2)}) collective-permute-start(bf16[512,256]{1,0:T(8,128)(2,1)} %get-tuple-element.47.refs_1_), channel_id=1, source_target_pairs={{0,3},{1,0},{2,1},{3,2},{4,7},{5,4},{6,5},{7,6},{8,11},{9,8},{10,9... | collective-permute-start | bytes 786440 | tf_op jit(solution)/shard_map/ppermute | solution.py:27
  237.0 22.9 %copy-start.5 = (bf16[512,512]{1,0:T(8,128)(2,1)}, bf16[512,512]{1,0:T(8,128)(2,1)S(1)}, u32[]{:S(2)}) copy-start(bf16[512,512]{1,0:T(8,128)(2,1)S(1)} %collective-permute-done.22.refs_9_.refs_8_) | copy-start | bytes 1572868
  237.0 8.4 %collective-permute-start.17 = (bf16[512,256]{1,0:T(8,128)(2,1)}, bf16[512,256]{1,0:T(8,128)(2,1)S(1)}, u32[]{:S(2)}, u32[]{:S(2)}) collective-permute-start(bf16[512,256]{1,0:T(8,128)(2,1)} %get-tuple-element.47.refs_1_), channel_id=1, source_target_pairs={{0,1},{1,2},{2,3},{3,0},{4,5},{5,6},{6,7},{7,4},{8,9},{9,10},{10,1... | collective-permute-start | bytes 786440 | tf_op jit(solution)/shard_map/ppermute | solution.py:27
  237.3 8.1 %collective-permute-start.21 = (bf16[512,256]{1,0:T(8,128)(2,1)}, bf16[512,256]{1,0:T(8,128)(2,1)S(1)}, u32[]{:S(2)}, u32[]{:S(2)}) collective-permute-start(bf16[512,256]{1,0:T(8,128)(2,1)} %get-tuple-element.46.refs_0_), channel_id=1, source_target_pairs={{0,3},{1,0},{2,1},{3,2},{4,7},{5,4},{6,5},{7,6},{8,11},{9,8},{10,9... | collective-permute-start | bytes 786440 | tf_op jit(solution)/shard_map/ppermute | solution.py:27
  240.0 11.0 %collective-permute-start.18 = (bf16[512,256]{1,0:T(8,128)(2,1)S(1)}, bf16[512,256]{1,0:T(8,128)(2,1)S(1)}, u32[]{:S(2)}, u32[]{:S(2)}) collective-permute-start(bf16[512,256]{1,0:T(8,128)(2,1)S(1)} %collective-permute-done.16.refs_2_), channel_id=1, source_target_pairs={{0,1},{1,2},{2,3},{3,0},{4,5},{5,6},{6,7},{7,4},{8,9},{9,10},{10,1... | collective-permute-start | bytes 786440 | tf_op jit(solution)/shard_map/ppermute | solution.py:27
  240.0 19.9 %copy-start.6 = (bf16[512,512]{1,0:T(8,128)(2,1)}, bf16[512,512]{1,0:T(8,128)(2,1)S(1)}, u32[]{:S(2)}) copy-start(bf16[512,512]{1,0:T(8,128)(2,1)S(1)} %collective-permute-done.24.refs_11_.refs_9_) | copy-start | bytes 1572868
  240.0 16.6 %collective-permute-start.25 = (bf16[512,256]{1,0:T(8,128)(2,1)}, bf16[512,256]{1,0:T(8,128)(2,1)S(1)}, u32[]{:S(2)}, u32[]{:S(2)}) collective-permute-start(bf16[512,256]{1,0:T(8,128)(2,1)} %get-tuple-element.50.refs_1_), channel_id=1, source_target_pairs={{0,1},{1,2},{2,3},{3,0},{4,5},{5,6},{6,7},{7,4},{8,9},{9,10},{10,1... | collective-permute-start | bytes 786440 | tf_op jit(solution)/shard_map/ppermute | solution.py:27
  240.1 16.5 %collective-permute-start.28 = (bf16[512,256]{1,0:T(8,128)(2,1)}, bf16[512,256]{1,0:T(8,128)(2,1)S(1)}, u32[]{:S(2)}, u32[]{:S(2)}) collective-permute-start(bf16[512,256]{1,0:T(8,128)(2,1)} %get-tuple-element.51.refs_2_), channel_id=1, source_target_pairs={{0,3},{1,0},{2,1},{3,2},{4,7},{5,4},{6,5},{7,6},{8,11},{9,8},{10,9... | collective-permute-start | bytes 786440 | tf_op jit(solution)/shard_map/ppermute | solution.py:27
  245.4 14.5 %collective-permute-start.20 = (bf16[512,256]{1,0:T(8,128)(2,1)S(1)}, bf16[512,256]{1,0:T(8,128)(2,1)S(1)}, u32[]{:S(2)}, u32[]{:S(2)}) collective-permute-start(bf16[512,256]{1,0:T(8,128)(2,1)S(1)} %collective-permute-done.19.refs_7_), channel_id=1, source_target_pairs={{0,3},{1,0},{2,1},{3,2},{4,7},{5,4},{6,5},{7,6},{8,11},{9,8},{10,9... | collective-permute-start | bytes 786440 | tf_op jit(solution)/shard_map/ppermute | solution.py:27
  245.4 20.1 %collective-permute-start.26 = (bf16[512,256]{1,0:T(8,128)(2,1)}, bf16[512,256]{1,0:T(8,128)(2,1)S(1)}, u32[]{:S(2)}, u32[]{:S(2)}) collective-permute-start(bf16[512,256]{1,0:T(8,128)(2,1)} %get-tuple-element.51.refs_2_), channel_id=1, source_target_pairs={{0,1},{1,2},{2,3},{3,0},{4,5},{5,6},{6,7},{7,4},{8,9},{9,10},{10,1... | collective-permute-start | bytes 786440 | tf_op jit(solution)/shard_map/ppermute | solution.py:27
  251.0 14.5 %collective-permute-start.27 = (bf16[512,256]{1,0:T(8,128)(2,1)}, bf16[512,256]{1,0:T(8,128)(2,1)S(1)}, u32[]{:S(2)}, u32[]{:S(2)}) collective-permute-start(bf16[512,256]{1,0:T(8,128)(2,1)} %get-tuple-element.50.refs_1_), channel_id=1, source_target_pairs={{0,3},{1,0},{2,1},{3,2},{4,7},{5,4},{6,5},{7,6},{8,11},{9,8},{10,9... | collective-permute-start | bytes 786440 | tf_op jit(solution)/shard_map/ppermute | solution.py:27
  256.6 12.5 %collective-permute-start.29 = (bf16[512,256]{1,0:T(8,128)(2,1)S(1)}, bf16[512,256]{1,0:T(8,128)(2,1)S(1)}, u32[]{:S(2)}, u32[]{:S(2)}) collective-permute-start(bf16[512,256]{1,0:T(8,128)(2,1)S(1)} %collective-permute-done.25.refs_3_), channel_id=1, source_target_pairs={{0,1},{1,2},{2,3},{3,0},{4,5},{5,6},{6,7},{7,4},{8,9},{9,10},{10,1... | collective-permute-start | bytes 786440 | tf_op jit(solution)/shard_map/ppermute | solution.py:27
  256.6 12.5 %collective-permute-start.30 = (bf16[512,256]{1,0:T(8,128)(2,1)S(1)}, bf16[512,256]{1,0:T(8,128)(2,1)S(1)}, u32[]{:S(2)}, u32[]{:S(2)}) collective-permute-start(bf16[512,256]{1,0:T(8,128)(2,1)S(1)} %collective-permute-done.28.refs_6_), channel_id=1, source_target_pairs={{0,3},{1,0},{2,1},{3,2},{4,7},{5,4},{6,5},{7,6},{8,11},{9,8},{10,9... | collective-permute-start | bytes 786440 | tf_op jit(solution)/shard_map/ppermute | solution.py:27
  260.0 1.0 copy-start
  260.9 0.9 copy-start.1
  261.9 3.7 %copy-start.2 = (bf16[512,256]{1,0:T(8,128)(2,1)S(1)}, bf16[512,256]{1,0:T(8,128)(2,1)}, u32[]{:S(2)}) copy-start(bf16[512,256]{1,0:T(8,128)(2,1)} %get-tuple-element.50.refs_1_) | copy-start | bytes 786436
  261.9 3.7 %copy-start.3 = (bf16[512,256]{1,0:T(8,128)(2,1)S(1)}, bf16[512,256]{1,0:T(8,128)(2,1)}, u32[]{:S(2)}) copy-start(bf16[512,256]{1,0:T(8,128)(2,1)} %get-tuple-element.51.refs_2_) | copy-start | bytes 786436

commit v5 on v3

--- a/solution.py
+++ b/solution.py
@@ -40,32 +40,58 @@
     return jnp.dot(a, b, preferred_element_type=F32)
 
 
-def first_blocks_kernel(where, own, left_top, left_bottom, right_top, right_bottom, w_own, w_left, w_right, out):
+def early_blocks_kernel(where, own, left_top, right_bottom, w_own, w_left, w_right, out):
     half = left_top.shape[0]
-    for part, left, right in ((slice(0, half), left_top, right_top), (slice(half, None), left_bottom, right_bottom)):
-        total = dot(own[part], w_own[0])
-        total += dot(left[...], w_left[0])
-        total += dot(right[...], w_right[0])
-        out[0, part] = total
-
-
-def first_blocks(where, own, halves, weights):
+    top, bottom = slice(0, half), slice(half, None)
+    out[0, top] = dot(own[top], w_own[0]) + dot(left_top[...], w_left[0])
+    out[0, bottom] = dot(own[bottom], w_own[0]) + dot(right_bottom[...], w_right[0])
+
+
+def later_blocks_kernel(where, part, left_bottom, right_top, w_left, w_right, out):
+    half = left_bottom.shape[0]
+    top, bottom = slice(0, half), slice(half, None)
+    out[0, top] = part[0, top] + dot(right_top[...], w_right[0])
+    out[0, bottom] = part[0, bottom] + dot(left_bottom[...], w_left[0])
+
+
+def weight_block(block, depth, width):
+    return pl.BlockSpec((1, depth, width), lambda j, w: (j, w[block], 0))
+
+
+def early_blocks(where, own, left_top, right_bottom, weights):
     kinds, _, width = weights.shape
     rows, depth = own.shape
     return pl.pallas_call(
-        first_blocks_kernel,
+        early_blocks_kernel,
         out_shape=jax.ShapeDtypeStruct((kinds, rows, width), F32),
         grid_spec=pltpu.PrefetchScalarGridSpec(
             num_scalar_prefetch=1,
             grid=(kinds,),
-            in_specs=[pl.BlockSpec((rows, depth), lambda j, w: (0, 0))]
-            + [VMEM_WHOLE] * 4
-            + [pl.BlockSpec((1, depth, width), functools.partial(lambda b, j, w: (j, w[b], 0), b)) for b in range(3)],
+            in_specs=[pl.BlockSpec((rows, depth), lambda j, w: (0, 0)), VMEM_WHOLE, VMEM_WHOLE]
+            + [weight_block(b, depth, width) for b in range(3)],
             out_specs=pl.BlockSpec((1, rows, width), lambda j, w: (j, 0, 0)),
         ),
         compiler_params=params(),
-        name="first_blocks",
-    )(where, own, *[in_vmem(half) for half in halves], weights, weights, weights)
+        name="early_blocks",
+    )(where, own, in_vmem(left_top), in_vmem(right_bottom), weights, weights, weights)
+
+
+def later_blocks(where, part, left_bottom, right_top, weights):
+    kinds, rows, width = part.shape
+    depth = left_bottom.shape[1]
+    whole = pl.BlockSpec((1, rows, width), lambda j, w: (j, 0, 0))
+    return pl.pallas_call(
+        later_blocks_kernel,
+        out_shape=jax.ShapeDtypeStruct((kinds, rows, width), F32),
+        grid_spec=pltpu.PrefetchScalarGridSpec(
+            num_scalar_prefetch=1,
+            grid=(kinds,),
+            in_specs=[whole, VMEM_WHOLE, VMEM_WHOLE] + [weight_block(b, depth, width) for b in (1, 2)],
+            out_specs=whole,
+        ),
+        compiler_params=params(),
+        name="later_blocks",
+    )(where, part, in_vmem(left_bottom), in_vmem(right_top), weights, weights)
 
 
 def pack_kernel(where, part, far_top, far_bottom, w_far, slot_of, out, projected):
@@ -226,22 +252,26 @@
     pl.when(pl.program_id(0) == 1)(lambda: add(1))
 
 
-def products(total, parts, chunk, kind):
+def products(total, parts, chunk, kind, own):
     half, depth = parts[0][0].shape
     width = parts[0][2].shape[1]
     block = pl.BlockSpec((half, width), lambda i: (i, 0))
+    fetched = pl.BlockSpec((half, depth), lambda i: (0, 0))
     carried = [] if total is None else [total]
+    sides = [side for part in parts for side in part[:2]]
+    here = 2 if own else 0
     return pl.pallas_call(
         functools.partial(products_kernel, len(parts), len(carried)),
         out_shape=jax.ShapeDtypeStruct((2 * half, width), kind),
         grid=(2,),
         in_specs=[block] * len(carried)
-        + [VMEM_WHOLE] * (2 * len(parts))
+        + [fetched] * here
+        + [VMEM_WHOLE] * (len(sides) - here)
         + [pl.BlockSpec((depth, width), lambda i: (chunk, 0))] * len(parts),
         out_specs=block,
         compiler_params=params(),
         name="products",
-    )(*carried, *[in_vmem(side) for part in parts for side in part[:2]], *[part[2] for part in parts])
+    )(*carried, *sides[:here], *[in_vmem(side) for side in sides[here:]], *[part[2] for part in parts])
 
 
 def local(tokens, project_weights, output_weights, cluster_ids):
@@ -261,7 +291,7 @@
     before = jnp.einsum("ts,hsc->htc", earlier, matches.astype(BF16), preferred_element_type=F32)
     slot_rank = jnp.sum(jnp.where(matches, before, 0.0), axis=2).astype(jnp.int32)
     slot_index = assigned * SLOT + slot_rank
-    slot_rows, slot_cols = slot_index[:, None, :], slot_index[:, :, None]
+    slot_rows = slot_index[:, None, :]
 
     weights = project_weights.transpose(1, 0, 2)
     where = jnp.stack([here, (here - 1) % groups, (here + 1) % groups, (here + 2) % groups]).astype(jnp.int32)
@@ -269,13 +299,15 @@
     top, bottom = tokens[:half], tokens[half:]
     left_top, right_bottom = shifted(top, 1), shifted(bottom, -1)
     left_bottom, right_top = shifted(bottom, 1), shifted(top, -1)
-    left_top, right_bottom, slot_rows, slot_cols, where = lax.optimization_barrier(
-        (left_top, right_bottom, slot_rows, slot_cols, where)
+    left_top, right_bottom, slot_rows, where = lax.optimization_barrier((left_top, right_bottom, slot_rows, where))
+    far_top, far_bottom = shifted(left_top, 1), shifted(right_bottom, -1)
+    part = early_blocks(where, tokens, left_top, right_bottom, weights)
+    part = later_blocks(where, part, left_bottom, right_top, weights)
+
+    out_weights, late_rows, far_top, far_bottom = lax.optimization_barrier(
+        (output_weights, slot_rows, far_top, far_bottom)
     )
-    far_top, far_bottom = shifted(left_top, 1), shifted(right_bottom, -1)
-    part = first_blocks(where, tokens, (left_top, left_bottom, right_top, right_bottom), weights)
-
-    out_weights, far_top, far_bottom = lax.optimization_barrier((output_weights, far_top, far_bottom))
+    slot_cols = late_rows[:, 0, :, None]
     out_blocks = []
     for by in range(groups):
         block = lax.dynamic_slice(out_weights, (0, (here + by) % groups * width), (width, width))
@@ -299,12 +331,10 @@
         far_top, far_bottom = shifted(left_top, 1), shifted(right_bottom, -1)
         gathered.append(((top, bottom), (left_top, left_bottom), (far_top, far_bottom), (right_top, right_bottom)))
 
-    total = None
-    for chunk in range(chunks):
-        parts = [(*gathered[chunk][by], out_blocks[by]) for by in range(groups)]
-        last = chunk == chunks - 1
-        total = products(total, parts[:2] + parts[3:], chunk, F32)
-        total = products(total, parts[2:3], chunk, BF16 if last else F32)
+    first, second = ([(*blocks[by], out_blocks[by]) for by in range(groups)] for blocks in gathered)
+    total = products(None, first, 0, F32, own=True)
+    total = products(total, second[:2] + second[3:], 1, F32, own=True)
+    total = products(total, second[2:3], 1, BF16, own=False)
     owned = jnp.concatenate(owned, axis=1).transpose(1, 0, 2)
     return (total, owned)
 

time: 246 us -> 250 us (1.016)
  waiting for transfers between devices: 103 us -> 114 us
  Pallas kernels: 65.2 us -> 70.6 us
  starting transfers between devices: 52.4 us -> 47.6 us
  other arithmetic: 5.28 us -> 1.29 us
  local copies, waits for them, and re-layouts: 15.1 us -> 11.4 us
    ppermute x21, waiting for transfers between devices: 27.3 us -> 39.5 us  [shifted(): lax.ppermute(array, 'head', [(i, (i + by) % count) for i in range(count)])]
    pallas_call x1 -> x2, Pallas kernels: 9.64 us -> 17.3 us  [the longest x1 8.75 us: later_blocks(): pl.pallas_call(later_blocks_kernel, out_shape=jax.ShapeDtypeStruct((kinds...]
    ppermute x21, starting transfers between devices: 28.3 us -> 24 us  [shifted(): lax.ppermute(array, 'head', [(i, (i + by) % count) for i in range(count)])]
    add x2 -> x1, other arithmetic: 4.66 us -> 0.63 us  [local(): slot_index = assigned * SLOT + slot_rank]
    unnamed x29 -> x22, local copies, waits for them, and re-layouts: 8.92 us -> 5.02 us
    pallas_call x4 -> x3, Pallas kernels: 12.5 us -> 10.3 us  [products(): pl.pallas_call(functools.partial(products_kernel, len(parts), len(carried...]
  transfers between devices with their start and end apart: 25 -> 25, of which waited for: 11 -> 13; matrix products, arithmetic and copies ran while one was open for 7% -> 4% of each run, Pallas kernels for 21% -> 23%
where the time goes in v5:
time: 250 us; the launch traced here: 249 us
  waiting for transfers between devices  114 us (46%)
  Pallas kernels  70.6 us (28%)
  starting transfers between devices  47.6 us (19%)
  local copies, waits for them, and re-layouts  11.4 us (5%)
    all_to_all x2, waiting for transfers between devices, local(): received.append(lax.all_to_all(packed, SEQ, 0, 0, tiled=True))  60.9 us
    ppermute x21, waiting for transfers between devices, shifted(): lax.ppermute(array, 'head', [(i, (i + by) % count) for i in range(count)])  39.5 us
    ppermute x21, starting transfers between devices, shifted(): lax.ppermute(array, 'head', [(i, (i + by) % count) for i in range(count)])  24 us
    pallas_call x2, Pallas kernels, pack(): pl.pallas_call(pack_kernel, out_shape=jax.ShapeDtypeStruct((devices, head...  21.6 us
    all_to_all x2, starting transfers between devices, local(): received.append(lax.all_to_all(packed, SEQ, 0, 0, tiled=True))  15.4 us
    all_to_all x2, waiting for transfers between devices, local(): returned = lax.all_to_all(buckets, SEQ, 0, 0, tiled=True)  14.1 us
    pallas_call x2, Pallas kernels, attend(): pl.pallas_call(functools.partial(attend_kernel, streamed), out_shape=(jax...  12.7 us
    pallas_call x3, Pallas kernels, products(): pl.pallas_call(functools.partial(products_kernel, len(parts), len(carried...  10.3 us
  transfers between devices with their start and end apart: 25, of which 13 were waited for; matrix products, arithmetic and copies ran while one was open for 4% of the time, Pallas kernels for 23%

profile of v5, /device:TPU:1, one launch (start us, length us, event | category | flops | bytes accessed | tf_op | source)
XLA Modules:
  0.0 248.7 jit_solution(890051168511846336)
XLA Ops:
  0.6 1.3 fusion.7
  1.9 3.6 %collective-permute-start.1 = (bf16[512,512]{1,0:T(8,128)(2,1)S(1)}, bf16[512,512]{1,0:T(8,128)(2,1)S(1)}, u32[]{:S(2)}, u32[]{:S(2)}) collective-permute-start(bf16[512,512]{1,0:T(8,128)(2,1)S(1)} %get-tuple-element.42), channel_id=1, source_target_pairs={{0,3},{1,0},{2,1},{3,2},{4,7},{5,4},{6,5},{7,6},{8,11},{9,8},{10,9... | collective-permute-start | bytes 1572872 | tf_op jit(solution)/shard_map/ppermute | solution.py:25
  5.6 2.7 %collective-permute-start.3 = (bf16[512,512]{1,0:T(8,128)(2,1)S(1)}, bf16[512,512]{1,0:T(8,128)(2,1)S(1)}, u32[]{:S(2)}, u32[]{:S(2)}) collective-permute-start(bf16[512,512]{1,0:T(8,128)(2,1)S(1)} %get-tuple-element.43), channel_id=1, source_target_pairs={{0,3},{1,0},{2,1},{3,2},{4,7},{5,4},{6,5},{7,6},{8,11},{9,8},{10,9... | collective-permute-start | bytes 1572872 | tf_op jit(solution)/shard_map/ppermute | solution.py:25
  8.2 0.7 copy.15
  8.9 2.5 fusion
  11.5 0.6 pad_add_fusion.where
  12.1 0.6 bitcast_add_fusion.slot_of
  12.7 17.8 %collective-permute-done.left_top = bf16[512,512]{1,0:T(8,128)(2,1)S(1)} collective-permute-done((bf16[512,512]{1,0:T(8,128)(2,1)S(1)}, bf16[512,512]{1,0:T(8,128)(2,1)S(1)}, u32[]{:S(2)}, u32[]{:S(2)}) %collective-permute-start) | collective-permute-done | bytes 524320 | tf_op jit(solution)/shard_map/ppermute | solution.py:25
  30.5 2.7 %collective-permute-start.5 = (bf16[512,512]{1,0:T(8,128)(2,1)S(1)}, bf16[512,512]{1,0:T(8,128)(2,1)S(1)}, u32[]{:S(2)}, u32[]{:S(2)}) collective-permute-start(bf16[512,512]{1,0:T(8,128)(2,1)S(1)} %collective-permute-done.1.right_bottom), channel_id=1, source_target_pairs={{0,3},{1,0},{2,1},{3,2},{4,7},{5,4},{6,5},{7,6},{8,11},{9,8},{10,9... | collective-permute-start | bytes 1572872 | tf_op jit(solution)/shard_map/ppermute | solution.py:25
  33.2 8.5 %early_blocks.1.part = f32[3,1024,512]{2,1,0:T(8,128)} custom-call(s32[4]{0:T(128)} %pad_add_fusion.where, bf16[1024,512]{1,0:T(8,128)(2,1)} %own.1, bf16[512,512]{1,0:T(8,128)(2,1)S(1)} %collective-permute-done.left_top, bf16[512,512]{1,0:T(8,128)(2,1)S(1)} %collective-permute-done.1.right_bottom, bf16[3,2048,512]{2,1,0:T(8,128)(2,1)} %bitcast.21, ...), custom_call_target="tpu_custom_call" | custom-call | tf_op jit(solution)/shard_map/early_blocks/pallas_call | solution.py:64
  41.7 8.8 %later_blocks.1.part = f32[3,1024,512]{2,1,0:T(8,128)} custom-call(s32[4]{0:T(128)} %pad_add_fusion.where, f32[3,1024,512]{2,1,0:T(8,128)} %early_blocks.1.part, bf16[512,512]{1,0:T(8,128)(2,1)S(1)} %collective-permute-done.2.left_bottom, bf16[512,512]{1,0:T(8,128)(2,1)S(1)} %collective-permute-done.3.right_top, bf16[3,2048,512]{2,1,0:T(8,128)(2,1)} %bitcast.24, ...), custom_call_target="tpu_custom_call" | custom-call | tf_op jit(solution)/shard_map/later_blocks/pallas_call | solution.py:83
  50.5 10.8 %pack.3 = bf16[32,2,8,8,384]{4,3,2,1,0:T(8,128)(2,1)} custom-call(s32[4]{0:T(128)} %pad_add_fusion.where, f32[3,1024,512]{2,1,0:T(8,128)} %later_blocks.1.part, bf16[512,512]{1,0:T(8,128)(2,1)S(1)} %collective-permute-done.4.far_top, bf16[512,512]{1,0:T(8,128)(2,1)S(1)} %collective-permute-done.5.far_bottom, bf16[3,2048,512]{2,1,0:T(8,128)(2,1)} %bitcast.26, ...), custom_call_target="tpu_custom_call" | custom-call | tf_op jit(solution)/shard_map/pack/pallas_call | solution.py:142
  61.3 0.8 copy-done
  62.1 0.8 copy-done.2
  62.9 10.3 %all-to-all-start.2 = ((bf16[32,2,8,8,384]{4,3,2,1,0:T(8,128)(2,1)}), bf16[32,2,8,8,384]{4,3,2,1,0:T(8,128)(2,1)S(1)}, u32[]{:S(2)}, u32[]{:S(2)}) async-start(bf16[32,2,8,8,384]{4,3,2,1,0:T(8,128)(2,1)} %pack.3), calls=%async_computation.2 | async-start | bytes 6291456 | tf_op jit(solution)/shard_map/all_to_all | solution.py:321
  73.2 1.0 copy-done.1
  74.2 1.0 copy-done.3
  75.3 10.8 %pack.2 = bf16[32,2,8,8,384]{4,3,2,1,0:T(8,128)(2,1)} custom-call(s32[4]{0:T(128)} %pad_add_fusion.where, f32[3,1024,512]{2,1,0:T(8,128)} %later_blocks.1.part, bf16[512,512]{1,0:T(8,128)(2,1)S(1)} %copy-done.1, bf16[512,512]{1,0:T(8,128)(2,1)S(1)} %copy-done.3, bf16[3,2048,512]{2,1,0:T(8,128)(2,1)} %bitcast.27, s32[4,1,1024]{2,1,0:T(1,128)} %bitcast_add_fusion.slot_of), custom_call_target="tpu_custom_call" | custom-call | tf_op jit(solution)/shard_map/pack/pallas_call | solution.py:142
  86.1 26.8 %all-to-all-done.2.received = bf16[32,2,8,8,384]{4,3,2,1,0:T(8,128)(2,1)S(1)} async-done(((bf16[32,2,8,8,384]{4,3,2,1,0:T(8,128)(2,1)}), bf16[32,2,8,8,384]{4,3,2,1,0:T(8,128)(2,1)S(1)}, u32[]{:S(2)}, u32[]{:S(2)}) %all-to-all-start.2) | async-done | bytes 3145760 | tf_op jit(solution)/shard_map/all_to_all | solution.py:321
  112.9 5.1 %all-to-all-start = ((bf16[32,2,8,8,384]{4,3,2,1,0:T(8,128)(2,1)}), bf16[32,2,8,8,384]{4,3,2,1,0:T(8,128)(2,1)}, u32[]{:S(2)}, u32[]{:S(2)}) async-start(bf16[32,2,8,8,384]{4,3,2,1,0:T(8,128)(2,1)} %pack.2), calls=%async_computation | async-start | bytes 6291456 | tf_op jit(solution)/shard_map/all_to_all | solution.py:321
  118.0 5.8 %attend.3 = (bf16[32,2,8,8,128]{4,3,2,1,0:T(8,128)(2,1)}, f32[8,2,128]{2,1,0:T(2,128)}) custom-call(bf16[32,2,8,8,384]{4,3,2,1,0:T(8,128)(2,1)S(1)} %all-to-all-done.2.received), custom_call_target="tpu_custom_call" | custom-call | tf_op jit(solution)/shard_map/attend/pallas_call | solution.py:196
  123.8 34.1 %all-to-all-done.received = bf16[32,2,8,8,384]{4,3,2,1,0:T(8,128)(2,1)} async-done(((bf16[32,2,8,8,384]{4,3,2,1,0:T(8,128)(2,1)}), bf16[32,2,8,8,384]{4,3,2,1,0:T(8,128)(2,1)}, u32[]{:S(2)}, u32[]{:S(2)}) %all-to-all-start) | async-done | bytes 3145760 | tf_op jit(solution)/shard_map/all_to_all | solution.py:321
  157.9 4.4 %all-to-all-start.3 = ((bf16[32,2,8,8,128]{4,3,2,1,0:T(8,128)(2,1)}), bf16[32,2,8,8,128]{4,3,2,1,0:T(8,128)(2,1)S(1)}, u32[]{:S(2)}, u32[]{:S(2)}) async-start(bf16[32,2,8,8,128]{4,3,2,1,0:T(8,128)(2,1)} %get-tuple-element.29), calls=%async_computation.3 | async-start | bytes 2097152 | tf_op jit(solution)/shard_map/all_to_all | solution.py:327
  162.3 6.9 %attend.2 = (bf16[32,2,8,8,128]{4,3,2,1,0:T(8,128)(2,1)}, f32[8,2,128]{2,1,0:T(2,128)}) custom-call(bf16[32,2,8,8,384]{4,3,2,1,0:T(8,128)(2,1)} %all-to-all-done.received), custom_call_target="tpu_custom_call" | custom-call | tf_op jit(solution)/shard_map/attend/pallas_call | solution.py:196
  169.2 10.0 %all-to-all-done.3.returned = bf16[32,2,8,8,128]{4,3,2,1,0:T(8,128)(2,1)S(1)} async-done(((bf16[32,2,8,8,128]{4,3,2,1,0:T(8,128)(2,1)}), bf16[32,2,8,8,128]{4,3,2,1,0:T(8,128)(2,1)S(1)}, u32[]{:S(2)}, u32[]{:S(2)}) %all-to-all-start.3) | async-done | bytes 1048608 | tf_op jit(solution)/shard_map/all_to_all | solution.py:327
  179.2 3.9 %all-to-all-start.1 = ((bf16[32,2,8,8,128]{4,3,2,1,0:T(8,128)(2,1)}), bf16[32,2,8,8,128]{4,3,2,1,0:T(8,128)(2,1)S(1)}, u32[]{:S(2)}, u32[]{:S(2)}) async-start(bf16[32,2,8,8,128]{4,3,2,1,0:T(8,128)(2,1)} %get-tuple-element.24), calls=%async_computation.1 | async-start | bytes 2097152 | tf_op jit(solution)/shard_map/all_to_all | solution.py:327
  183.1 2.9 %constant_dynamic-slice_fusion = (bf16[512,512]{1,0:T(8,128)(2,1)}, bf16[512,512]{1,0:T(8,128)(2,1)}, bf16[512,512]{1,0:T(8,128)(2,1)}, bf16[512,512]{1,0:T(8,128)(2,1)}) fusion(bf16[512,2048]{1,0:T(8,128)(2,1)} %param.6, s32[]{:T(128)S(6)} %select_n.52, s32[]{:T(128)S(6)} %select_n.50, s32[]{:T(128)S(6)} %select_n.49, s32[]{:T(128)S(6)} %select_n.48), kind=kLoop, calls=%fused_computation.10 | loop fusion | bytes 4194320 | tf_op jit(solution)/shard_map/dynamic_slice | solution.py:313
  186.1 0.9 collective-permute-start.13
  187.0 1.8 collective-permute-start.14
  188.8 2.2 broadcast_in_dim_squeeze.4.slot_of
  191.0 4.3 %unpack.3 = (bf16[512,256]{1,0:T(8,128)(2,1)}, bf16[512,256]{1,0:T(8,128)(2,1)}) custom-call(bf16[32,2,8,8,128]{4,3,2,1,0:T(8,128)(2,1)S(1)} %all-to-all-done.3.returned, s32[4,1024,1]{2,1,0:T(8,128)} %broadcast_in_dim_squeeze.4.slot_of), custom_call_target="tpu_custom_call" | custom-call | tf_op jit(solution)/shard_map/unpack/pallas_call | solution.py:230
  195.4 0.6 collective-permute-start.15
  195.9 4.1 %all-to-all-done.1.returned = bf16[32,2,8,8,128]{4,3,2,1,0:T(8,128)(2,1)S(1)} async-done(((bf16[32,2,8,8,128]{4,3,2,1,0:T(8,128)(2,1)}), bf16[32,2,8,8,128]{4,3,2,1,0:T(8,128)(2,1)S(1)}, u32[]{:S(2)}, u32[]{:S(2)}) %all-to-all-start.1) | async-done | bytes 1048608 | tf_op jit(solution)/shard_map/all_to_all | solution.py:327
  200.0 4.3 %unpack.2 = (bf16[512,256]{1,0:T(8,128)(2,1)}, bf16[512,256]{1,0:T(8,128)(2,1)}) custom-call(bf16[32,2,8,8,128]{4,3,2,1,0:T(8,128)(2,1)S(1)} %all-to-all-done.1.returned, s32[4,1024,1]{2,1,0:T(8,128)} %broadcast_in_dim_squeeze.4.slot_of), custom_call_target="tpu_custom_call" | custom-call | tf_op jit(solution)/shard_map/unpack/pallas_call | solution.py:230
  204.3 7.6 %collective-permute-done.12.refs_9_.refs_8_ = bf16[512,512]{1,0:T(8,128)(2,1)S(1)} collective-permute-done((bf16[512,512]{1,0:T(8,128)(2,1)}, bf16[512,512]{1,0:T(8,128)(2,1)S(1)}, u32[]{:S(2)}, u32[]{:S(2)}) %collective-permute-start.12) | collective-permute-done | bytes 524320 | tf_op jit(solution)/shard_map/ppermute | solution.py:25
  212.0 2.7 %collective-permute-start.18 = (bf16[512,256]{1,0:T(8,128)(2,1)}, bf16[512,256]{1,0:T(8,128)(2,1)S(1)}, u32[]{:S(2)}, u32[]{:S(2)}) collective-permute-start(bf16[512,256]{1,0:T(8,128)(2,1)} %get-tuple-element.31.refs_2_), channel_id=1, source_target_pairs={{0,3},{1,0},{2,1},{3,2},{4,7},{5,4},{6,5},{7,6},{8,11},{9,8},{10,9... | collective-permute-start | bytes 786440 | tf_op jit(solution)/shard_map/ppermute | solution.py:25
  214.9 2.6 %collective-permute-done.15.refs_3_ = bf16[512,256]{1,0:T(8,128)(2,1)S(1)} collective-permute-done((bf16[512,256]{1,0:T(8,128)(2,1)}, bf16[512,256]{1,0:T(8,128)(2,1)S(1)}, u32[]{:S(2)}, u32[]{:S(2)}) %collective-permute-start.15) | collective-permute-done | bytes 262176 | tf_op jit(solution)/shard_map/ppermute | solution.py:25
  217.9 2.6 %collective-permute-start.10 = (bf16[512,256]{1,0:T(8,128)(2,1)S(1)}, bf16[512,256]{1,0:T(8,128)(2,1)S(1)}, u32[]{:S(2)}, u32[]{:S(2)}) collective-permute-start(bf16[512,256]{1,0:T(8,128)(2,1)S(1)} %collective-permute-done.9.refs_7_), channel_id=1, source_target_pairs={{0,3},{1,0},{2,1},{3,2},{4,7},{5,4},{6,5},{7,6},{8,11},{9,8},{10,9... | collective-permute-start | bytes 786440 | tf_op jit(solution)/shard_map/ppermute | solution.py:25
  220.6 2.6 %collective-permute-done.6.refs_2_ = bf16[512,256]{1,0:T(8,128)(2,1)S(1)} collective-permute-done((bf16[512,256]{1,0:T(8,128)(2,1)}, bf16[512,256]{1,0:T(8,128)(2,1)S(1)}, u32[]{:S(2)}, u32[]{:S(2)}) %collective-permute-start.6) | collective-permute-done | bytes 262176 | tf_op jit(solution)/shard_map/ppermute | solution.py:25
  223.5 0.8 collective-permute-start.16
  224.4 4.8 %collective-permute-done.11.refs_6_ = bf16[512,256]{1,0:T(8,128)(2,1)S(1)} collective-permute-done((bf16[512,256]{1,0:T(8,128)(2,1)}, bf16[512,256]{1,0:T(8,128)(2,1)S(1)}, u32[]{:S(2)}, u32[]{:S(2)}) %collective-permute-start.11) | collective-permute-done | bytes 262176 | tf_op jit(solution)/shard_map/ppermute | solution.py:25
  229.2 2.6 %collective-permute-start.17 = (bf16[512,256]{1,0:T(8,128)(2,1)}, bf16[512,256]{1,0:T(8,128)(2,1)S(1)}, u32[]{:S(2)}, u32[]{:S(2)}) collective-permute-start(bf16[512,256]{1,0:T(8,128)(2,1)} %get-tuple-element.30.refs_1_), channel_id=1, source_target_pairs={{0,3},{1,0},{2,1},{3,2},{4,7},{5,4},{6,5},{7,6},{8,11},{9,8},{10,9... | collective-permute-start | bytes 786440 | tf_op jit(solution)/shard_map/ppermute | solution.py:25
  231.8 3.0 %collective-permute-done.10.refs_5_ = bf16[512,256]{1,0:T(8,128)(2,1)S(1)} collective-permute-done((bf16[512,256]{1,0:T(8,128)(2,1)S(1)}, bf16[512,256]{1,0:T(8,128)(2,1)S(1)}, u32[]{:S(2)}, u32[]{:S(2)}) %collective-permute-start.10) | collective-permute-done | bytes 262176 | tf_op jit(solution)/shard_map/ppermute | solution.py:25
  234.8 2.6 %collective-permute-start.20 = (bf16[512,256]{1,0:T(8,128)(2,1)S(1)}, bf16[512,256]{1,0:T(8,128)(2,1)S(1)}, u32[]{:S(2)}, u32[]{:S(2)}) collective-permute-start(bf16[512,256]{1,0:T(8,128)(2,1)S(1)} %collective-permute-done.18.refs_6_), channel_id=1, source_target_pairs={{0,3},{1,0},{2,1},{3,2},{4,7},{5,4},{6,5},{7,6},{8,11},{9,8},{10,9... | collective-permute-start | bytes 786440 | tf_op jit(solution)/shard_map/ppermute | solution.py:25
  237.4 0.6 copy.12
  238.1 3.8 %products.3.refs_0_ = f32[1024,512]{1,0:T(8,128)} custom-call(bf16[512,256]{1,0:T(8,128)(2,1)} %get-tuple-element.26.refs_0_, bf16[512,256]{1,0:T(8,128)(2,1)} %get-tuple-element.27.refs_1_, bf16[512,256]{1,0:T(8,128)(2,1)S(1)} %collective-permute-done.6.refs_2_, bf16[512,256]{1,0:T(8,128)(2,1)S(1)} %collective-permute-done.7.refs_3_, ...), custom_call_target="tpu_custom_call" | custom-call | tf_op jit(solution)/shard_map/products/pallas_call | solution.py:263
  241.9 3.8 %products.4.refs_0_ = f32[1024,512]{1,0:T(8,128)} custom-call(f32[1024,512]{1,0:T(8,128)} %products.3.refs_0_, bf16[512,256]{1,0:T(8,128)(2,1)} %get-tuple-element.30.refs_1_, bf16[512,256]{1,0:T(8,128)(2,1)} %get-tuple-element.31.refs_2_, bf16[512,256]{1,0:T(8,128)(2,1)S(1)} %collective-permute-done.15.refs_3_, ...), custom_call_target="tpu_custom_call" | custom-call | tf_op jit(solution)/shard_map/products/pallas_call | solution.py:263
  246.0 2.7 %products.5 = bf16[1024,512]{1,0:T(8,128)(2,1)} custom-call(f32[1024,512]{1,0:T(8,128)} %products.4.refs_0_, bf16[512,256]{1,0:T(8,128)(2,1)S(1)} %collective-permute-done.19.refs_1_, bf16[512,256]{1,0:T(8,128)(2,1)S(1)} %collective-permute-done.20.refs_2_, bf16[512,512]{1,0:T(8,128)(2,1)} %collective-permute-done.13.refs_10_.refs_3_), custom_call_target="tpu_custom_call" | custom-call | tf_op jit(solution)/shard_map/products/pallas_call | solution.py:263
  (44 shorter events, 1.5 us)
Async XLA Ops:
  1.9 28.6 %collective-permute-start.1 = (bf16[512,512]{1,0:T(8,128)(2,1)S(1)}, bf16[512,512]{1,0:T(8,128)(2,1)S(1)}, u32[]{:S(2)}, u32[]{:S(2)}) collective-permute-start(bf16[512,512]{1,0:T(8,128)(2,1)S(1)} %get-tuple-element.42), channel_id=1, source_target_pairs={{0,3},{1,0},{2,1},{3,2},{4,7},{5,4},{6,5},{7,6},{8,11},{9,8},{10,9... | collective-permute-start | bytes 1572872 | tf_op jit(solution)/shard_map/ppermute | solution.py:25
  5.5 36.2 %collective-permute-start.2 = (bf16[512,512]{1,0:T(8,128)(2,1)S(1)}, bf16[512,512]{1,0:T(8,128)(2,1)S(1)}, u32[]{:S(2)}, u32[]{:S(2)}) collective-permute-start(bf16[512,512]{1,0:T(8,128)(2,1)S(1)} %get-tuple-element.42), channel_id=1, source_target_pairs={{0,1},{1,2},{2,3},{3,0},{4,5},{5,6},{6,7},{7,4},{8,9},{9,10},{10,1... | collective-permute-start | bytes 1572872 | tf_op jit(solution)/shard_map/ppermute | solution.py:25
  5.5 25.0 %collective-permute-start = (bf16[512,512]{1,0:T(8,128)(2,1)S(1)}, bf16[512,512]{1,0:T(8,128)(2,1)S(1)}, u32[]{:S(2)}, u32[]{:S(2)}) collective-permute-start(bf16[512,512]{1,0:T(8,128)(2,1)S(1)} %get-tuple-element.43), channel_id=1, source_target_pairs={{0,1},{1,2},{2,3},{3,0},{4,5},{5,6},{6,7},{7,4},{8,9},{9,10},{10,1... | collective-permute-start | bytes 1572872 | tf_op jit(solution)/shard_map/ppermute | solution.py:25
  5.6 36.2 %collective-permute-start.3 = (bf16[512,512]{1,0:T(8,128)(2,1)S(1)}, bf16[512,512]{1,0:T(8,128)(2,1)S(1)}, u32[]{:S(2)}, u32[]{:S(2)}) collective-permute-start(bf16[512,512]{1,0:T(8,128)(2,1)S(1)} %get-tuple-element.43), channel_id=1, source_target_pairs={{0,3},{1,0},{2,1},{3,2},{4,7},{5,4},{6,5},{7,6},{8,11},{9,8},{10,9... | collective-permute-start | bytes 1572872 | tf_op jit(solution)/shard_map/ppermute | solution.py:25
  8.9 3.2 %copy-start.7 = (s32[4,1024,1]{1,2,0:T(1,128)S(1)}, s32[4,1024,1]{1,2,0:T(1,128)}, u32[]{:S(2)}) copy-start(s32[4,1024,1]{1,2,0:T(1,128)} %param.7) | copy-start | bytes 49156
  30.5 20.0 %collective-permute-start.4 = (bf16[512,512]{1,0:T(8,128)(2,1)S(1)}, bf16[512,512]{1,0:T(8,128)(2,1)S(1)}, u32[]{:S(2)}, u32[]{:S(2)}) collective-permute-start(bf16[512,512]{1,0:T(8,128)(2,1)S(1)} %collective-permute-done.left_top), channel_id=1, source_target_pairs={{0,1},{1,2},{2,3},{3,0},{4,5},{5,6},{6,7},{7,4},{8,9},{9,10},{10,1... | collective-permute-start | bytes 1572872 | tf_op jit(solution)/shard_map/ppermute | solution.py:25
  30.5 20.0 %collective-permute-start.5 = (bf16[512,512]{1,0:T(8,128)(2,1)S(1)}, bf16[512,512]{1,0:T(8,128)(2,1)S(1)}, u32[]{:S(2)}, u32[]{:S(2)}) collective-permute-start(bf16[512,512]{1,0:T(8,128)(2,1)S(1)} %collective-permute-done.1.right_bottom), channel_id=1, source_target_pairs={{0,3},{1,0},{2,1},{3,2},{4,7},{5,4},{6,5},{7,6},{8,11},{9,8},{10,9... | collective-permute-start | bytes 1572872 | tf_op jit(solution)/shard_map/ppermute | solution.py:25
  61.3 0.8 copy-start
  62.1 0.8 copy-start.2
  62.9 50.0 %all-to-all-start.2 = ((bf16[32,2,8,8,384]{4,3,2,1,0:T(8,128)(2,1)}), bf16[32,2,8,8,384]{4,3,2,1,0:T(8,128)(2,1)S(1)}, u32[]{:S(2)}, u32[]{:S(2)}) async-start(bf16[32,2,8,8,384]{4,3,2,1,0:T(8,128)(2,1)} %pack.3), calls=%async_computation.2 | async-start | bytes 6291456 | tf_op jit(solution)/shard_map/all_to_all | solution.py:321
  73.2 1.0 copy-start.1
  74.2 1.0 copy-start.3
  112.9 45.0 %all-to-all-start = ((bf16[32,2,8,8,384]{4,3,2,1,0:T(8,128)(2,1)}), bf16[32,2,8,8,384]{4,3,2,1,0:T(8,128)(2,1)}, u32[]{:S(2)}, u32[]{:S(2)}) async-start(bf16[32,2,8,8,384]{4,3,2,1,0:T(8,128)(2,1)} %pack.2), calls=%async_computation | async-start | bytes 6291456 | tf_op jit(solution)/shard_map/all_to_all | solution.py:321
  157.9 21.3 %all-to-all-start.3 = ((bf16[32,2,8,8,128]{4,3,2,1,0:T(8,128)(2,1)}), bf16[32,2,8,8,128]{4,3,2,1,0:T(8,128)(2,1)S(1)}, u32[]{:S(2)}, u32[]{:S(2)}) async-start(bf16[32,2,8,8,128]{4,3,2,1,0:T(8,128)(2,1)} %get-tuple-element.29), calls=%async_computation.3 | async-start | bytes 2097152 | tf_op jit(solution)/shard_map/all_to_all | solution.py:327
  162.3 26.5 %copy-start.6 = (s32[4,1,1024]{2,1,0:T(1,128)S(1)}, s32[4,1,1024]{2,1,0:T(1,128)}, u32[]{:S(2)}) copy-start(s32[4,1,1024]{2,1,0:T(1,128)} %bitcast_add_fusion.slot_of) | copy-start | bytes 49156
  179.2 20.8 %all-to-all-start.1 = ((bf16[32,2,8,8,128]{4,3,2,1,0:T(8,128)(2,1)}), bf16[32,2,8,8,128]{4,3,2,1,0:T(8,128)(2,1)S(1)}, u32[]{:S(2)}, u32[]{:S(2)}) async-start(bf16[32,2,8,8,128]{4,3,2,1,0:T(8,128)(2,1)} %get-tuple-element.24), calls=%async_computation.1 | async-start | bytes 2097152 | tf_op jit(solution)/shard_map/all_to_all | solution.py:327
  186.1 25.9 %collective-permute-start.12 = (bf16[512,512]{1,0:T(8,128)(2,1)}, bf16[512,512]{1,0:T(8,128)(2,1)S(1)}, u32[]{:S(2)}, u32[]{:S(2)}) collective-permute-start(bf16[512,512]{1,0:T(8,128)(2,1)} %get-tuple-element.40), channel_id=1, source_target_pairs={{0,1},{1,2},{2,3},{3,0},{4,5},{5,6},{6,7},{7,4},{8,9},{9,10},{10,1... | collective-permute-start | bytes 1572872 | tf_op jit(solution)/shard_map/ppermute | solution.py:25
  186.1 25.9 %collective-permute-start.13 = (bf16[512,512]{1,0:T(8,128)(2,1)}, bf16[512,512]{1,0:T(8,128)(2,1)}, u32[]{:S(2)}, u32[]{:S(2)}) collective-permute-start(bf16[512,512]{1,0:T(8,128)(2,1)} %get-tuple-element.39), channel_id=1, source_target_pairs={{0,2},{1,3},{2,0},{3,1},{4,6},{5,7},{6,4},{7,5},{8,10},{9,11},{10,... | collective-permute-start | bytes 1572872 | tf_op jit(solution)/shard_map/ppermute | solution.py:25
  187.0 27.7 %collective-permute-start.14 = (bf16[512,512]{1,0:T(8,128)(2,1)}, bf16[512,512]{1,0:T(8,128)(2,1)S(1)}, u32[]{:S(2)}, u32[]{:S(2)}) collective-permute-start(bf16[512,512]{1,0:T(8,128)(2,1)} %get-tuple-element.38), channel_id=1, source_target_pairs={{0,3},{1,0},{2,1},{3,2},{4,7},{5,4},{6,5},{7,6},{8,11},{9,8},{10,9... | collective-permute-start | bytes 1572872 | tf_op jit(solution)/shard_map/ppermute | solution.py:25
  188.8 48.6 %copy-start.8 = (f32[8,2,128]{2,1,0:T(2,128)S(1)}, f32[8,2,128]{2,1,0:T(2,128)}, u32[]{:S(2)}) copy-start(f32[8,2,128]{2,1,0:T(2,128)} %get-tuple-element.33) | copy-start | bytes 24580
  188.8 48.6 %copy-start.9 = (f32[8,2,128]{2,1,0:T(2,128)S(1)}, f32[8,2,128]{2,1,0:T(2,128)}, u32[]{:S(2)}) copy-start(f32[8,2,128]{2,1,0:T(2,128)} %get-tuple-element.32) | copy-start | bytes 24580
  195.4 22.2 %collective-permute-start.15 = (bf16[512,256]{1,0:T(8,128)(2,1)}, bf16[512,256]{1,0:T(8,128)(2,1)S(1)}, u32[]{:S(2)}, u32[]{:S(2)}) collective-permute-start(bf16[512,256]{1,0:T(8,128)(2,1)} %get-tuple-element.30.refs_1_), channel_id=1, source_target_pairs={{0,1},{1,2},{2,3},{3,0},{4,5},{5,6},{6,7},{7,4},{8,9},{9,10},{10,1... | collective-permute-start | bytes 786440 | tf_op jit(solution)/shard_map/ppermute | solution.py:25
  204.3 13.6 %collective-permute-start.9 = (bf16[512,256]{1,0:T(8,128)(2,1)}, bf16[512,256]{1,0:T(8,128)(2,1)S(1)}, u32[]{:S(2)}, u32[]{:S(2)}) collective-permute-start(bf16[512,256]{1,0:T(8,128)(2,1)} %get-tuple-element.27.refs_1_), channel_id=1, source_target_pairs={{0,3},{1,0},{2,1},{3,2},{4,7},{5,4},{6,5},{7,6},{8,11},{9,8},{10,9... | collective-permute-start | bytes 786440 | tf_op jit(solution)/shard_map/ppermute | solution.py:25
  212.0 26.1 %copy-start.4 = (bf16[512,512]{1,0:T(8,128)(2,1)}, bf16[512,512]{1,0:T(8,128)(2,1)S(1)}, u32[]{:S(2)}) copy-start(bf16[512,512]{1,0:T(8,128)(2,1)S(1)} %collective-permute-done.12.refs_9_.refs_8_) | copy-start | bytes 1572868
  212.0 11.2 %collective-permute-start.6 = (bf16[512,256]{1,0:T(8,128)(2,1)}, bf16[512,256]{1,0:T(8,128)(2,1)S(1)}, u32[]{:S(2)}, u32[]{:S(2)}) collective-permute-start(bf16[512,256]{1,0:T(8,128)(2,1)} %get-tuple-element.26.refs_0_), channel_id=1, source_target_pairs={{0,1},{1,2},{2,3},{3,0},{4,5},{5,6},{6,7},{7,4},{8,9},{9,10},{10,1... | collective-permute-start | bytes 786440 | tf_op jit(solution)/shard_map/ppermute | solution.py:25
  212.0 11.6 %collective-permute-start.18 = (bf16[512,256]{1,0:T(8,128)(2,1)}, bf16[512,256]{1,0:T(8,128)(2,1)S(1)}, u32[]{:S(2)}, u32[]{:S(2)}) collective-permute-start(bf16[512,256]{1,0:T(8,128)(2,1)} %get-tuple-element.31.refs_2_), channel_id=1, source_target_pairs={{0,3},{1,0},{2,1},{3,2},{4,7},{5,4},{6,5},{7,6},{8,11},{9,8},{10,9... | collective-permute-start | bytes 786440 | tf_op jit(solution)/shard_map/ppermute | solution.py:25
  214.6 23.4 %copy-start.5 = (bf16[512,512]{1,0:T(8,128)(2,1)}, bf16[512,512]{1,0:T(8,128)(2,1)S(1)}, u32[]{:S(2)}) copy-start(bf16[512,512]{1,0:T(8,128)(2,1)S(1)} %collective-permute-done.14.refs_11_.refs_9_) | copy-start | bytes 1572868
  214.6 14.5 %collective-permute-start.11 = (bf16[512,256]{1,0:T(8,128)(2,1)}, bf16[512,256]{1,0:T(8,128)(2,1)S(1)}, u32[]{:S(2)}, u32[]{:S(2)}) collective-permute-start(bf16[512,256]{1,0:T(8,128)(2,1)} %get-tuple-element.26.refs_0_), channel_id=1, source_target_pairs={{0,3},{1,0},{2,1},{3,2},{4,7},{5,4},{6,5},{7,6},{8,11},{9,8},{10,9... | collective-permute-start | bytes 786440 | tf_op jit(solution)/shard_map/ppermute | solution.py:25
  217.6 14.2 %collective-permute-start.7 = (bf16[512,256]{1,0:T(8,128)(2,1)}, bf16[512,256]{1,0:T(8,128)(2,1)S(1)}, u32[]{:S(2)}, u32[]{:S(2)}) collective-permute-start(bf16[512,256]{1,0:T(8,128)(2,1)} %get-tuple-element.27.refs_1_), channel_id=1, source_target_pairs={{0,1},{1,2},{2,3},{3,0},{4,5},{5,6},{6,7},{7,4},{8,9},{9,10},{10,1... | collective-permute-start | bytes 786440 | tf_op jit(solution)/shard_map/ppermute | solution.py:25
  217.9 16.9 %collective-permute-start.10 = (bf16[512,256]{1,0:T(8,128)(2,1)S(1)}, bf16[512,256]{1,0:T(8,128)(2,1)S(1)}, u32[]{:S(2)}, u32[]{:S(2)}) collective-permute-start(bf16[512,256]{1,0:T(8,128)(2,1)S(1)} %collective-permute-done.9.refs_7_), channel_id=1, source_target_pairs={{0,3},{1,0},{2,1},{3,2},{4,7},{5,4},{6,5},{7,6},{8,11},{9,8},{10,9... | collective-permute-start | bytes 786440 | tf_op jit(solution)/shard_map/ppermute | solution.py:25
  223.2 14.9 %collective-permute-start.8 = (bf16[512,256]{1,0:T(8,128)(2,1)S(1)}, bf16[512,256]{1,0:T(8,128)(2,1)S(1)}, u32[]{:S(2)}, u32[]{:S(2)}) collective-permute-start(bf16[512,256]{1,0:T(8,128)(2,1)S(1)} %collective-permute-done.6.refs_2_), channel_id=1, source_target_pairs={{0,1},{1,2},{2,3},{3,0},{4,5},{5,6},{6,7},{7,4},{8,9},{9,10},{10,1... | collective-permute-start | bytes 786440 | tf_op jit(solution)/shard_map/ppermute | solution.py:25
  223.5 18.3 %collective-permute-start.16 = (bf16[512,256]{1,0:T(8,128)(2,1)}, bf16[512,256]{1,0:T(8,128)(2,1)S(1)}, u32[]{:S(2)}, u32[]{:S(2)}) collective-permute-start(bf16[512,256]{1,0:T(8,128)(2,1)} %get-tuple-element.31.refs_2_), channel_id=1, source_target_pairs={{0,1},{1,2},{2,3},{3,0},{4,5},{5,6},{6,7},{7,4},{8,9},{9,10},{10,1... | collective-permute-start | bytes 786440 | tf_op jit(solution)/shard_map/ppermute | solution.py:25
  229.2 12.7 %collective-permute-start.17 = (bf16[512,256]{1,0:T(8,128)(2,1)}, bf16[512,256]{1,0:T(8,128)(2,1)S(1)}, u32[]{:S(2)}, u32[]{:S(2)}) collective-permute-start(bf16[512,256]{1,0:T(8,128)(2,1)} %get-tuple-element.30.refs_1_), channel_id=1, source_target_pairs={{0,3},{1,0},{2,1},{3,2},{4,7},{5,4},{6,5},{7,6},{8,11},{9,8},{10,9... | collective-permute-start | bytes 786440 | tf_op jit(solution)/shard_map/ppermute | solution.py:25
  231.8 13.9 %collective-permute-start.19 = (bf16[512,256]{1,0:T(8,128)(2,1)S(1)}, bf16[512,256]{1,0:T(8,128)(2,1)S(1)}, u32[]{:S(2)}, u32[]{:S(2)}) collective-permute-start(bf16[512,256]{1,0:T(8,128)(2,1)S(1)} %collective-permute-done.15.refs_3_), channel_id=1, source_target_pairs={{0,1},{1,2},{2,3},{3,0},{4,5},{5,6},{6,7},{7,4},{8,9},{9,10},{10,1... | collective-permute-start | bytes 786440 | tf_op jit(solution)/shard_map/ppermute | solution.py:25
  234.8 11.2 %collective-permute-start.20 = (bf16[512,256]{1,0:T(8,128)(2,1)S(1)}, bf16[512,256]{1,0:T(8,128)(2,1)S(1)}, u32[]{:S(2)}, u32[]{:S(2)}) collective-permute-start(bf16[512,256]{1,0:T(8,128)(2,1)S(1)} %collective-permute-done.18.refs_6_), channel_id=1, source_target_pairs={{0,3},{1,0},{2,1},{3,2},{4,7},{5,4},{6,5},{7,6},{8,11},{9,8},{10,9... | collective-permute-start | bytes 786440 | tf_op jit(solution)/shard_map/ppermute | solution.py:25

commit v6 on v3

--- a/solution.py
+++ b/solution.py
@@ -38,6 +38,45 @@
 
 def dot(a, b):
     return jnp.dot(a, b, preferred_element_type=F32)
+
+
+def halves_kernel(top_in, bottom_in, top, bottom):
+    top[...] = top_in[...]
+    bottom[...] = bottom_in[...]
+
+
+def halves(array):
+    rows, width = array.shape
+    steps = 4
+    block = (rows // 2 // steps, width)
+    out = pl.BlockSpec(block, lambda i: (i, 0))
+    return pl.pallas_call(
+        halves_kernel,
+        out_shape=(jax.ShapeDtypeStruct((rows // 2, width), array.dtype),) * 2,
+        grid=(steps,),
+        in_specs=[out, pl.BlockSpec(block, lambda i: (i + steps, 0))],
+        out_specs=(out, out),
+        compiler_params=params(),
+        name="halves",
+    )(array, array)
+
+
+def columns_kernel(rows, out):
+    count = rows.shape[2]
+    out[0] = jnp.broadcast_to(rows[0], (8, count)).T[:, :1]
+
+
+def columns(rows):
+    heads, _, count = rows.shape
+    return pl.pallas_call(
+        columns_kernel,
+        out_shape=jax.ShapeDtypeStruct((heads, count, 1), rows.dtype),
+        grid=(heads,),
+        in_specs=[pl.BlockSpec((1, 1, count), lambda h: (h, 0, 0))],
+        out_specs=pl.BlockSpec((1, count, 1), lambda h: (h, 0, 0)),
+        compiler_params=params(),
+        name="columns",
+    )(rows)
 
 
 def first_blocks_kernel(where, own, left_top, left_bottom, right_top, right_bottom, w_own, w_left, w_right, out):
@@ -215,33 +254,42 @@
 def products_kernel(count, carried, *refs):
     pairs, weights = refs[carried : carried + 2 * count], refs[carried + 2 * count : carried + 3 * count]
     out = refs[-1]
+    rows = out.shape[0]
+    per_side = pairs[0].shape[0] // rows
+    step = pl.program_id(0)
+    at = pl.ds(pl.multiple_of(step % per_side * rows, rows), rows)
 
     def add(side):
         total = refs[0][...] if carried else 0.0
         for k in range(count):
-            total += dot(pairs[2 * k + side][...], weights[k][...])
+            total += dot(pairs[2 * k + side][at], weights[k][...])
         out[...] = total.astype(out.dtype)
 
-    pl.when(pl.program_id(0) == 0)(lambda: add(0))
-    pl.when(pl.program_id(0) == 1)(lambda: add(1))
-
-
-def products(total, parts, chunk, kind):
+    pl.when(step < per_side)(lambda: add(0))
+    pl.when(step >= per_side)(lambda: add(1))
+
+
+def products(total, parts, chunk, kind, own):
     half, depth = parts[0][0].shape
     width = parts[0][2].shape[1]
-    block = pl.BlockSpec((half, width), lambda i: (i, 0))
+    steps = 4
+    block = pl.BlockSpec((2 * half // steps, width), lambda i: (i, 0))
+    fetched = pl.BlockSpec((half, depth), lambda i: (0, 0))
     carried = [] if total is None else [total]
+    sides = [side for part in parts for side in part[:2]]
+    here = 2 if own else 0
     return pl.pallas_call(
         functools.partial(products_kernel, len(parts), len(carried)),
         out_shape=jax.ShapeDtypeStruct((2 * half, width), kind),
-        grid=(2,),
+        grid=(steps,),
         in_specs=[block] * len(carried)
-        + [VMEM_WHOLE] * (2 * len(parts))
+        + [fetched] * here
+        + [VMEM_WHOLE] * (len(sides) - here)
         + [pl.BlockSpec((depth, width), lambda i: (chunk, 0))] * len(parts),
         out_specs=block,
         compiler_params=params(),
         name="products",
-    )(*carried, *[in_vmem(side) for part in parts for side in part[:2]], *[part[2] for part in parts])
+    )(*carried, *sides[:here], *[in_vmem(side) for side in sides[here:]], *[part[2] for part in parts])
 
 
 def local(tokens, project_weights, output_weights, cluster_ids):
@@ -251,7 +299,6 @@
     width = output_weights.shape[0]
     heads = width // HEAD_DIM
     rows = tokens.shape[0]
-    half = rows // 2
     clusters = CLUST_DEV * seq_count
 
     assigned = cluster_ids[:, :, 0]
@@ -261,21 +308,22 @@
     before = jnp.einsum("ts,hsc->htc", earlier, matches.astype(BF16), preferred_element_type=F32)
     slot_rank = jnp.sum(jnp.where(matches, before, 0.0), axis=2).astype(jnp.int32)
     slot_index = assigned * SLOT + slot_rank
-    slot_rows, slot_cols = slot_index[:, None, :], slot_index[:, :, None]
+    slot_rows = slot_index[:, None, :]
 
     weights = project_weights.transpose(1, 0, 2)
     where = jnp.stack([here, (here - 1) % groups, (here + 1) % groups, (here + 2) % groups]).astype(jnp.int32)
 
-    top, bottom = tokens[:half], tokens[half:]
+    top, bottom = halves(tokens)
     left_top, right_bottom = shifted(top, 1), shifted(bottom, -1)
     left_bottom, right_top = shifted(bottom, 1), shifted(top, -1)
-    left_top, right_bottom, slot_rows, slot_cols, where = lax.optimization_barrier(
-        (left_top, right_bottom, slot_rows, slot_cols, where)
-    )
+    left_top, right_bottom, slot_rows, where = lax.optimization_barrier((left_top, right_bottom, slot_rows, where))
     far_top, far_bottom = shifted(left_top, 1), shifted(right_bottom, -1)
     part = first_blocks(where, tokens, (left_top, left_bottom, right_top, right_bottom), weights)
 
-    out_weights, far_top, far_bottom = lax.optimization_barrier((output_weights, far_top, far_bottom))
+    out_weights, late_rows, far_top, far_bottom = lax.optimization_barrier(
+        (output_weights, slot_rows, far_top, far_bottom)
+    )
+    slot_cols = columns(late_rows)
     out_blocks = []
     for by in range(groups):
         block = lax.dynamic_slice(out_weights, (0, (here + by) % groups * width), (width, width))
@@ -299,12 +347,10 @@
         far_top, far_bottom = shifted(left_top, 1), shifted(right_bottom, -1)
         gathered.append(((top, bottom), (left_top, left_bottom), (far_top, far_bottom), (right_top, right_bottom)))
 
-    total = None
-    for chunk in range(chunks):
-        parts = [(*gathered[chunk][by], out_blocks[by]) for by in range(groups)]
-        last = chunk == chunks - 1
-        total = products(total, parts[:2] + parts[3:], chunk, F32)
-        total = products(total, parts[2:3], chunk, BF16 if last else F32)
+    first, second = ([(*blocks[by], out_blocks[by]) for by in range(groups)] for blocks in gathered)
+    total = products(None, first, 0, F32, own=True)
+    total = products(total, second[:2] + second[3:], 1, F32, own=True)
+    total = products(total, second[2:3], 1, BF16, own=False)
     owned = jnp.concatenate(owned, axis=1).transpose(1, 0, 2)
     return (total, owned)
 

time: 246 us -> 249 us (1.012)
  Pallas kernels: 65.2 us -> 72.7 us
  local copies, waits for them, and re-layouts: 15.1 us -> 7.92 us
  waiting for transfers between devices: 103 us -> 108 us
  other arithmetic: 5.28 us -> 1.24 us
    ppermute x21, waiting for transfers between devices: 27.3 us -> 36.2 us  [shifted(): lax.ppermute(array, 'head', [(i, (i + by) % count) for i in range(count)])]
    pallas_call x0 -> x2, Pallas kernels: none -> 6.79 us  [the longest x1 3.39 us: halves(): pl.pallas_call(halves_kernel, out_shape=(jax.ShapeDtypeStruct((rows // 2,...]
    add x2 -> x1, other arithmetic: 4.66 us -> 0.63 us  [local(): slot_index = assigned * SLOT + slot_rank]
    all_to_all x2, waiting for transfers between devices: 14.9 us -> 10.9 us  [local(): returned = lax.all_to_all(buckets, SEQ, 0, 0, tiled=True)]
    unnamed x29 -> x20, local copies, waits for them, and re-layouts: 8.92 us -> 5.02 us
    pallas_call x4 -> x3, Pallas kernels: 12.5 us -> 13.3 us  [products(): pl.pallas_call(functools.partial(products_kernel, len(parts), len(carried...]
  transfers between devices with their start and end apart: 25 -> 25, of which waited for: 11 -> 11; matrix products, arithmetic and copies ran while one was open for 7% -> 3% of each run, Pallas kernels for 21% -> 22%
where the time goes in v6:
time: 249 us; the launch traced here: 247 us
  waiting for transfers between devices  108 us (43%)
  Pallas kernels  72.7 us (29%)
  starting transfers between devices  54.1 us (22%)
  local copies, waits for them, and re-layouts  7.92 us (3%)
    all_to_all x2, waiting for transfers between devices, local(): received.append(lax.all_to_all(packed, SEQ, 0, 0, tiled=True))  61 us
    ppermute x21, waiting for transfers between devices, shifted(): lax.ppermute(array, 'head', [(i, (i + by) % count) for i in range(count)])  36.2 us
    ppermute x21, starting transfers between devices, shifted(): lax.ppermute(array, 'head', [(i, (i + by) % count) for i in range(count)])  30.2 us
    pallas_call x2, Pallas kernels, pack(): pl.pallas_call(pack_kernel, out_shape=jax.ShapeDtypeStruct((devices, head...  21.6 us
    all_to_all x2, starting transfers between devices, local(): received.append(lax.all_to_all(packed, SEQ, 0, 0, tiled=True))  15.6 us
    pallas_call x3, Pallas kernels, products(): pl.pallas_call(functools.partial(products_kernel, len(parts), len(carried...  13.3 us
    pallas_call x2, Pallas kernels, attend(): pl.pallas_call(functools.partial(attend_kernel, streamed), out_shape=(jax...  12.7 us
    all_to_all x2, waiting for transfers between devices, local(): returned = lax.all_to_all(buckets, SEQ, 0, 0, tiled=True)  10.9 us
  transfers between devices with their start and end apart: 25, of which 11 were waited for; matrix products, arithmetic and copies ran while one was open for 3% of the time, Pallas kernels for 22%

profile of v6, /device:TPU:1, one launch (start us, length us, event | category | flops | bytes accessed | tf_op | source)
XLA Modules:
  0.0 247.4 jit_solution(10726636151540544223)
XLA Ops:
  0.6 3.4 %halves.1 = (bf16[512,512]{1,0:T(8,128)(2,1)}, bf16[512,512]{1,0:T(8,128)(2,1)}) custom-call(bf16[1024,512]{1,0:T(8,128)(2,1)} %own.1, bf16[1024,512]{1,0:T(8,128)(2,1)} %own.1), custom_call_target="tpu_custom_call" | custom-call | tf_op jit(solution)/shard_map/halves/pallas_call | solution.py:53
  4.0 3.6 %collective-permute-start.1 = (bf16[512,512]{1,0:T(8,128)(2,1)}, bf16[512,512]{1,0:T(8,128)(2,1)S(1)}, u32[]{:S(2)}, u32[]{:S(2)}) collective-permute-start(bf16[512,512]{1,0:T(8,128)(2,1)} %get-tuple-element.21), channel_id=1, source_target_pairs={{0,3},{1,0},{2,1},{3,2},{4,7},{5,4},{6,5},{7,6},{8,11},{9,8},{10,9... | collective-permute-start | bytes 1572872 | tf_op jit(solution)/shard_map/ppermute | solution.py:25
  7.6 2.7 %collective-permute-start.3 = (bf16[512,512]{1,0:T(8,128)(2,1)}, bf16[512,512]{1,0:T(8,128)(2,1)S(1)}, u32[]{:S(2)}, u32[]{:S(2)}) collective-permute-start(bf16[512,512]{1,0:T(8,128)(2,1)} %get-tuple-element.20), channel_id=1, source_target_pairs={{0,3},{1,0},{2,1},{3,2},{4,7},{5,4},{6,5},{7,6},{8,11},{9,8},{10,9... | collective-permute-start | bytes 1572872 | tf_op jit(solution)/shard_map/ppermute | solution.py:25
  10.3 0.7 copy.9
  11.0 2.5 %fusion = f32[4,1024]{1,0:T(4,128)S(1)} fusion(s32[4,1024]{1,0:T(4,128)S(1)} %bitcast.26), kind=kOutput, calls=%fused_computation.1 | convolution fusion | flops 2152722432 | bytes 32768 | tf_op jit(solution)/shard_map/ts,hsc->htc/dot_general | solution.py:308
  13.6 0.6 pad_add_fusion.where
  14.2 0.6 bitcast_add_fusion.slot_of.rows
  14.8 18.0 %collective-permute-done.left_top = bf16[512,512]{1,0:T(8,128)(2,1)S(1)} collective-permute-done((bf16[512,512]{1,0:T(8,128)(2,1)}, bf16[512,512]{1,0:T(8,128)(2,1)S(1)}, u32[]{:S(2)}, u32[]{:S(2)}) %collective-permute-start) | collective-permute-done | bytes 524320 | tf_op jit(solution)/shard_map/ppermute | solution.py:25
  32.8 2.7 %collective-permute-start.5 = (bf16[512,512]{1,0:T(8,128)(2,1)S(1)}, bf16[512,512]{1,0:T(8,128)(2,1)S(1)}, u32[]{:S(2)}, u32[]{:S(2)}) collective-permute-start(bf16[512,512]{1,0:T(8,128)(2,1)S(1)} %collective-permute-done.1.right_bottom), channel_id=1, source_target_pairs={{0,3},{1,0},{2,1},{3,2},{4,7},{5,4},{6,5},{7,6},{8,11},{9,8},{10,9... | collective-permute-start | bytes 1572872 | tf_op jit(solution)/shard_map/ppermute | solution.py:25
  35.4 9.6 %first_blocks.1.part = f32[3,1024,512]{2,1,0:T(8,128)} custom-call(s32[4]{0:T(128)} %pad_add_fusion.where, bf16[1024,512]{1,0:T(8,128)(2,1)} %own.1, bf16[512,512]{1,0:T(8,128)(2,1)S(1)} %collective-permute-done.left_top, bf16[512,512]{1,0:T(8,128)(2,1)S(1)} %collective-permute-done.2.left_bottom, bf16[512,512]{1,0:T(8,128)(2,1)S(1)} %collective-permute-done.3.right_top, ...), custom_call_target="tpu_custom_call" | custom-call | tf_op jit(solution)/shard_map/first_blocks/pallas_call | solution.py:94
  45.1 0.6 collective-permute-done.4.far_top
  45.7 10.8 %pack.3 = bf16[32,2,8,8,384]{4,3,2,1,0:T(8,128)(2,1)} custom-call(s32[4]{0:T(128)} %pad_add_fusion.where, f32[3,1024,512]{2,1,0:T(8,128)} %first_blocks.1.part, bf16[512,512]{1,0:T(8,128)(2,1)S(1)} %collective-permute-done.4.far_top, bf16[512,512]{1,0:T(8,128)(2,1)S(1)} %collective-permute-done.5.far_bottom, bf16[3,2048,512]{2,1,0:T(8,128)(2,1)} %bitcast.24, ...), custom_call_target="tpu_custom_call" | custom-call | tf_op jit(solution)/shard_map/pack/pallas_call | solution.py:155
  56.5 0.8 copy-done
  57.3 0.8 copy-done.2
  58.1 10.6 %all-to-all-start.2 = ((bf16[32,2,8,8,384]{4,3,2,1,0:T(8,128)(2,1)}), bf16[32,2,8,8,384]{4,3,2,1,0:T(8,128)(2,1)S(1)}, u32[]{:S(2)}, u32[]{:S(2)}) async-start(bf16[32,2,8,8,384]{4,3,2,1,0:T(8,128)(2,1)} %pack.3), calls=%async_computation.2 | async-start | bytes 6291456 | tf_op jit(solution)/shard_map/all_to_all | solution.py:337
  68.7 1.0 copy-done.1
  69.7 1.0 copy-done.3
  70.8 10.8 %pack.2 = bf16[32,2,8,8,384]{4,3,2,1,0:T(8,128)(2,1)} custom-call(s32[4]{0:T(128)} %pad_add_fusion.where, f32[3,1024,512]{2,1,0:T(8,128)} %first_blocks.1.part, bf16[512,512]{1,0:T(8,128)(2,1)S(1)} %copy-done.1, bf16[512,512]{1,0:T(8,128)(2,1)S(1)} %copy-done.3, bf16[3,2048,512]{2,1,0:T(8,128)(2,1)} %bitcast.25, s32[4,1,1024]{2,1,0:T(1,128)} %bitcast_add_fusion.slot_of.rows), custom_call_target="tpu_custom_call" | custom-call | tf_op jit(solution)/shard_map/pack/pallas_call | solution.py:155
  81.5 26.9 %all-to-all-done.2.received = bf16[32,2,8,8,384]{4,3,2,1,0:T(8,128)(2,1)S(1)} async-done(((bf16[32,2,8,8,384]{4,3,2,1,0:T(8,128)(2,1)}), bf16[32,2,8,8,384]{4,3,2,1,0:T(8,128)(2,1)S(1)}, u32[]{:S(2)}, u32[]{:S(2)}) %all-to-all-start.2) | async-done | bytes 3145760 | tf_op jit(solution)/shard_map/all_to_all | solution.py:337
  108.4 5.1 %all-to-all-start = ((bf16[32,2,8,8,384]{4,3,2,1,0:T(8,128)(2,1)}), bf16[32,2,8,8,384]{4,3,2,1,0:T(8,128)(2,1)}, u32[]{:S(2)}, u32[]{:S(2)}) async-start(bf16[32,2,8,8,384]{4,3,2,1,0:T(8,128)(2,1)} %pack.2), calls=%async_computation | async-start | bytes 6291456 | tf_op jit(solution)/shard_map/all_to_all | solution.py:337
  113.5 5.8 %attend.3 = (bf16[32,2,8,8,128]{4,3,2,1,0:T(8,128)(2,1)}, f32[8,2,128]{2,1,0:T(2,128)}) custom-call(bf16[32,2,8,8,384]{4,3,2,1,0:T(8,128)(2,1)S(1)} %all-to-all-done.2.received), custom_call_target="tpu_custom_call" | custom-call | tf_op jit(solution)/shard_map/attend/pallas_call | solution.py:209
  119.3 34.1 %all-to-all-done.received = bf16[32,2,8,8,384]{4,3,2,1,0:T(8,128)(2,1)} async-done(((bf16[32,2,8,8,384]{4,3,2,1,0:T(8,128)(2,1)}), bf16[32,2,8,8,384]{4,3,2,1,0:T(8,128)(2,1)}, u32[]{:S(2)}, u32[]{:S(2)}) %all-to-all-start) | async-done | bytes 3145760 | tf_op jit(solution)/shard_map/all_to_all | solution.py:337
  153.4 4.4 %all-to-all-start.3 = ((bf16[32,2,8,8,128]{4,3,2,1,0:T(8,128)(2,1)}), bf16[32,2,8,8,128]{4,3,2,1,0:T(8,128)(2,1)S(1)}, u32[]{:S(2)}, u32[]{:S(2)}) async-start(bf16[32,2,8,8,128]{4,3,2,1,0:T(8,128)(2,1)} %get-tuple-element.33), calls=%async_computation.3 | async-start | bytes 2097152 | tf_op jit(solution)/shard_map/all_to_all | solution.py:343
  157.7 6.9 %attend.2 = (bf16[32,2,8,8,128]{4,3,2,1,0:T(8,128)(2,1)}, f32[8,2,128]{2,1,0:T(2,128)}) custom-call(bf16[32,2,8,8,384]{4,3,2,1,0:T(8,128)(2,1)} %all-to-all-done.received), custom_call_target="tpu_custom_call" | custom-call | tf_op jit(solution)/shard_map/attend/pallas_call | solution.py:209
  164.6 10.0 %all-to-all-done.3.returned = bf16[32,2,8,8,128]{4,3,2,1,0:T(8,128)(2,1)S(1)} async-done(((bf16[32,2,8,8,128]{4,3,2,1,0:T(8,128)(2,1)}), bf16[32,2,8,8,128]{4,3,2,1,0:T(8,128)(2,1)S(1)}, u32[]{:S(2)}, u32[]{:S(2)}) %all-to-all-start.3) | async-done | bytes 1048608 | tf_op jit(solution)/shard_map/all_to_all | solution.py:343
  174.7 3.9 %all-to-all-start.1 = ((bf16[32,2,8,8,128]{4,3,2,1,0:T(8,128)(2,1)}), bf16[32,2,8,8,128]{4,3,2,1,0:T(8,128)(2,1)S(1)}, u32[]{:S(2)}, u32[]{:S(2)}) async-start(bf16[32,2,8,8,128]{4,3,2,1,0:T(8,128)(2,1)} %get-tuple-element.28), calls=%async_computation.1 | async-start | bytes 2097152 | tf_op jit(solution)/shard_map/all_to_all | solution.py:343
  178.6 2.9 %constant_dynamic-slice_fusion = (bf16[512,512]{1,0:T(8,128)(2,1)}, bf16[512,512]{1,0:T(8,128)(2,1)}, bf16[512,512]{1,0:T(8,128)(2,1)}, bf16[512,512]{1,0:T(8,128)(2,1)}) fusion(bf16[512,2048]{1,0:T(8,128)(2,1)} %param.6, s32[]{:T(128)S(6)} %select_n.52, s32[]{:T(128)S(6)} %select_n.50, s32[]{:T(128)S(6)} %select_n.49, s32[]{:T(128)S(6)} %select_n.48), kind=kLoop, calls=%fused_computation.10 | loop fusion | bytes 4194320 | tf_op jit(solution)/shard_map/dynamic_slice | solution.py:329
  181.5 3.9 %collective-permute-start.13 = (bf16[512,512]{1,0:T(8,128)(2,1)}, bf16[512,512]{1,0:T(8,128)(2,1)}, u32[]{:S(2)}, u32[]{:S(2)}) collective-permute-start(bf16[512,512]{1,0:T(8,128)(2,1)} %get-tuple-element.41), channel_id=1, source_target_pairs={{0,2},{1,3},{2,0},{3,1},{4,6},{5,7},{6,4},{7,5},{8,10},{9,11},{10,... | collective-permute-start | bytes 1572872 | tf_op jit(solution)/shard_map/ppermute | solution.py:25
  185.4 3.4 %columns.1.slot_of = s32[4,1024,1]{2,1,0:T(8,128)} custom-call(s32[4,1,1024]{2,1,0:T(1,128)} %bitcast_add_fusion.slot_of.rows), custom_call_target="tpu_custom_call" | custom-call | tf_op jit(solution)/shard_map/columns/pallas_call | solution.py:71
  188.8 4.3 %unpack.3 = (bf16[512,256]{1,0:T(8,128)(2,1)}, bf16[512,256]{1,0:T(8,128)(2,1)}) custom-call(bf16[32,2,8,8,128]{4,3,2,1,0:T(8,128)(2,1)S(1)} %all-to-all-done.3.returned, s32[4,1024,1]{2,1,0:T(8,128)} %columns.1.slot_of), custom_call_target="tpu_custom_call" | custom-call | tf_op jit(solution)/shard_map/unpack/pallas_call | solution.py:243
  193.1 1.4 collective-permute-start.15
  194.6 0.9 all-to-all-done.1.returned
  195.5 4.3 %unpack.2 = (bf16[512,256]{1,0:T(8,128)(2,1)}, bf16[512,256]{1,0:T(8,128)(2,1)}) custom-call(bf16[32,2,8,8,128]{4,3,2,1,0:T(8,128)(2,1)S(1)} %all-to-all-done.1.returned, s32[4,1024,1]{2,1,0:T(8,128)} %columns.1.slot_of), custom_call_target="tpu_custom_call" | custom-call | tf_op jit(solution)/shard_map/unpack/pallas_call | solution.py:243
  199.8 2.7 %collective-permute-start.9 = (bf16[512,256]{1,0:T(8,128)(2,1)}, bf16[512,256]{1,0:T(8,128)(2,1)S(1)}, u32[]{:S(2)}, u32[]{:S(2)}) collective-permute-start(bf16[512,256]{1,0:T(8,128)(2,1)} %get-tuple-element.31.refs_1_), channel_id=1, source_target_pairs={{0,3},{1,0},{2,1},{3,2},{4,7},{5,4},{6,5},{7,6},{8,11},{9,8},{10,9... | collective-permute-start | bytes 786440 | tf_op jit(solution)/shard_map/ppermute | solution.py:25
  202.5 6.3 %collective-permute-done.13.refs_10_.refs_3_ = bf16[512,512]{1,0:T(8,128)(2,1)} collective-permute-done((bf16[512,512]{1,0:T(8,128)(2,1)}, bf16[512,512]{1,0:T(8,128)(2,1)}, u32[]{:S(2)}, u32[]{:S(2)}) %collective-permute-start.13) | collective-permute-done | bytes 524320 | tf_op jit(solution)/shard_map/ppermute | solution.py:25
  208.8 2.2 collective-permute-start.11
  211.0 2.4 collective-permute-done.15.refs_3_
  213.4 3.2 %collective-permute-start.10 = (bf16[512,256]{1,0:T(8,128)(2,1)S(1)}, bf16[512,256]{1,0:T(8,128)(2,1)S(1)}, u32[]{:S(2)}, u32[]{:S(2)}) collective-permute-start(bf16[512,256]{1,0:T(8,128)(2,1)S(1)} %collective-permute-done.9.refs_7_), channel_id=1, source_target_pairs={{0,3},{1,0},{2,1},{3,2},{4,7},{5,4},{6,5},{7,6},{8,11},{9,8},{10,9... | collective-permute-start | bytes 786440 | tf_op jit(solution)/shard_map/ppermute | solution.py:25
  216.6 2.4 collective-permute-done.6.refs_2_
  219.0 1.4 collective-permute-start.16
  220.4 4.2 %collective-permute-done.11.refs_6_ = bf16[512,256]{1,0:T(8,128)(2,1)S(1)} collective-permute-done((bf16[512,256]{1,0:T(8,128)(2,1)}, bf16[512,256]{1,0:T(8,128)(2,1)S(1)}, u32[]{:S(2)}, u32[]{:S(2)}) %collective-permute-start.11) | collective-permute-done | bytes 262176 | tf_op jit(solution)/shard_map/ppermute | solution.py:25
  224.6 3.2 %collective-permute-start.17 = (bf16[512,256]{1,0:T(8,128)(2,1)}, bf16[512,256]{1,0:T(8,128)(2,1)S(1)}, u32[]{:S(2)}, u32[]{:S(2)}) collective-permute-start(bf16[512,256]{1,0:T(8,128)(2,1)} %get-tuple-element.34.refs_1_), channel_id=1, source_target_pairs={{0,3},{1,0},{2,1},{3,2},{4,7},{5,4},{6,5},{7,6},{8,11},{9,8},{10,9... | collective-permute-start | bytes 786440 | tf_op jit(solution)/shard_map/ppermute | solution.py:25
  227.9 2.4 collective-permute-done.10.refs_5_
  230.2 3.2 %collective-permute-start.20 = (bf16[512,256]{1,0:T(8,128)(2,1)S(1)}, bf16[512,256]{1,0:T(8,128)(2,1)S(1)}, u32[]{:S(2)}, u32[]{:S(2)}) collective-permute-start(bf16[512,256]{1,0:T(8,128)(2,1)S(1)} %collective-permute-done.18.refs_6_), channel_id=1, source_target_pairs={{0,3},{1,0},{2,1},{3,2},{4,7},{5,4},{6,5},{7,6},{8,11},{9,8},{10,9... | collective-permute-start | bytes 786440 | tf_op jit(solution)/shard_map/ppermute | solution.py:25
  233.5 0.6 copy.6
  234.1 4.4 %products.3.refs_0_ = f32[1024,512]{1,0:T(8,128)} custom-call(bf16[512,256]{1,0:T(8,128)(2,1)} %get-tuple-element.30.refs_0_, bf16[512,256]{1,0:T(8,128)(2,1)} %get-tuple-element.31.refs_1_, bf16[512,256]{1,0:T(8,128)(2,1)S(1)} %collective-permute-done.6.refs_2_, bf16[512,256]{1,0:T(8,128)(2,1)S(1)} %collective-permute-done.7.refs_3_, ...), custom_call_target="tpu_custom_call" | custom-call | tf_op jit(solution)/shard_map/products/pallas_call | solution.py:281
  238.5 4.9 %products.4.refs_0_ = f32[1024,512]{1,0:T(8,128)} custom-call(f32[1024,512]{1,0:T(8,128)} %products.3.refs_0_, bf16[512,256]{1,0:T(8,128)(2,1)} %get-tuple-element.34.refs_1_, bf16[512,256]{1,0:T(8,128)(2,1)} %get-tuple-element.35.refs_2_, bf16[512,256]{1,0:T(8,128)(2,1)S(1)} %collective-permute-done.15.refs_3_, ...), custom_call_target="tpu_custom_call" | custom-call | tf_op jit(solution)/shard_map/products/pallas_call | solution.py:281
  243.4 4.1 %products.5 = bf16[1024,512]{1,0:T(8,128)(2,1)} custom-call(f32[1024,512]{1,0:T(8,128)} %products.4.refs_0_, bf16[512,256]{1,0:T(8,128)(2,1)S(1)} %collective-permute-done.19.refs_1_, bf16[512,256]{1,0:T(8,128)(2,1)S(1)} %collective-permute-done.20.refs_2_, bf16[512,512]{1,0:T(8,128)(2,1)} %collective-permute-done.13.refs_10_.refs_3_), custom_call_target="tpu_custom_call" | custom-call | tf_op jit(solution)/shard_map/products/pallas_call | solution.py:281
  (40 shorter events, 0.1 us)
Async XLA Ops:
  4.0 28.7 %collective-permute-start.1 = (bf16[512,512]{1,0:T(8,128)(2,1)}, bf16[512,512]{1,0:T(8,128)(2,1)S(1)}, u32[]{:S(2)}, u32[]{:S(2)}) collective-permute-start(bf16[512,512]{1,0:T(8,128)(2,1)} %get-tuple-element.21), channel_id=1, source_target_pairs={{0,3},{1,0},{2,1},{3,2},{4,7},{5,4},{6,5},{7,6},{8,11},{9,8},{10,9... | collective-permute-start | bytes 1572872 | tf_op jit(solution)/shard_map/ppermute | solution.py:25
  7.6 27.9 %collective-permute-start.2 = (bf16[512,512]{1,0:T(8,128)(2,1)}, bf16[512,512]{1,0:T(8,128)(2,1)S(1)}, u32[]{:S(2)}, u32[]{:S(2)}) collective-permute-start(bf16[512,512]{1,0:T(8,128)(2,1)} %get-tuple-element.21), channel_id=1, source_target_pairs={{0,1},{1,2},{2,3},{3,0},{4,5},{5,6},{6,7},{7,4},{8,9},{9,10},{10,1... | collective-permute-start | bytes 1572872 | tf_op jit(solution)/shard_map/ppermute | solution.py:25
  7.6 25.2 %collective-permute-start = (bf16[512,512]{1,0:T(8,128)(2,1)}, bf16[512,512]{1,0:T(8,128)(2,1)S(1)}, u32[]{:S(2)}, u32[]{:S(2)}) collective-permute-start(bf16[512,512]{1,0:T(8,128)(2,1)} %get-tuple-element.20), channel_id=1, source_target_pairs={{0,1},{1,2},{2,3},{3,0},{4,5},{5,6},{6,7},{7,4},{8,9},{9,10},{10,1... | collective-permute-start | bytes 1572872 | tf_op jit(solution)/shard_map/ppermute | solution.py:25
  7.6 27.8 %collective-permute-start.3 = (bf16[512,512]{1,0:T(8,128)(2,1)}, bf16[512,512]{1,0:T(8,128)(2,1)S(1)}, u32[]{:S(2)}, u32[]{:S(2)}) collective-permute-start(bf16[512,512]{1,0:T(8,128)(2,1)} %get-tuple-element.20), channel_id=1, source_target_pairs={{0,3},{1,0},{2,1},{3,2},{4,7},{5,4},{6,5},{7,6},{8,11},{9,8},{10,9... | collective-permute-start | bytes 1572872 | tf_op jit(solution)/shard_map/ppermute | solution.py:25
  11.0 3.2 %copy-start.6 = (s32[4,1024,1]{1,2,0:T(1,128)S(1)}, s32[4,1024,1]{1,2,0:T(1,128)}, u32[]{:S(2)}) copy-start(s32[4,1024,1]{1,2,0:T(1,128)} %param.7) | copy-start | bytes 49156
  32.8 12.9 %collective-permute-start.4 = (bf16[512,512]{1,0:T(8,128)(2,1)S(1)}, bf16[512,512]{1,0:T(8,128)(2,1)S(1)}, u32[]{:S(2)}, u32[]{:S(2)}) collective-permute-start(bf16[512,512]{1,0:T(8,128)(2,1)S(1)} %collective-permute-done.left_top), channel_id=1, source_target_pairs={{0,1},{1,2},{2,3},{3,0},{4,5},{5,6},{6,7},{7,4},{8,9},{9,10},{10,1... | collective-permute-start | bytes 1572872 | tf_op jit(solution)/shard_map/ppermute | solution.py:25
  32.8 12.9 %collective-permute-start.5 = (bf16[512,512]{1,0:T(8,128)(2,1)S(1)}, bf16[512,512]{1,0:T(8,128)(2,1)S(1)}, u32[]{:S(2)}, u32[]{:S(2)}) collective-permute-start(bf16[512,512]{1,0:T(8,128)(2,1)S(1)} %collective-permute-done.1.right_bottom), channel_id=1, source_target_pairs={{0,3},{1,0},{2,1},{3,2},{4,7},{5,4},{6,5},{7,6},{8,11},{9,8},{10,9... | collective-permute-start | bytes 1572872 | tf_op jit(solution)/shard_map/ppermute | solution.py:25
  56.5 0.8 copy-start
  57.3 0.8 copy-start.2
  58.1 50.3 %all-to-all-start.2 = ((bf16[32,2,8,8,384]{4,3,2,1,0:T(8,128)(2,1)}), bf16[32,2,8,8,384]{4,3,2,1,0:T(8,128)(2,1)S(1)}, u32[]{:S(2)}, u32[]{:S(2)}) async-start(bf16[32,2,8,8,384]{4,3,2,1,0:T(8,128)(2,1)} %pack.3), calls=%async_computation.2 | async-start | bytes 6291456 | tf_op jit(solution)/shard_map/all_to_all | solution.py:337
  68.7 1.0 copy-start.1
  69.7 1.0 copy-start.3
  108.4 45.0 %all-to-all-start = ((bf16[32,2,8,8,384]{4,3,2,1,0:T(8,128)(2,1)}), bf16[32,2,8,8,384]{4,3,2,1,0:T(8,128)(2,1)}, u32[]{:S(2)}, u32[]{:S(2)}) async-start(bf16[32,2,8,8,384]{4,3,2,1,0:T(8,128)(2,1)} %pack.2), calls=%async_computation | async-start | bytes 6291456 | tf_op jit(solution)/shard_map/all_to_all | solution.py:337
  153.4 21.3 %all-to-all-start.3 = ((bf16[32,2,8,8,128]{4,3,2,1,0:T(8,128)(2,1)}), bf16[32,2,8,8,128]{4,3,2,1,0:T(8,128)(2,1)S(1)}, u32[]{:S(2)}, u32[]{:S(2)}) async-start(bf16[32,2,8,8,128]{4,3,2,1,0:T(8,128)(2,1)} %get-tuple-element.33), calls=%async_computation.3 | async-start | bytes 2097152 | tf_op jit(solution)/shard_map/all_to_all | solution.py:343
  174.7 20.8 %all-to-all-start.1 = ((bf16[32,2,8,8,128]{4,3,2,1,0:T(8,128)(2,1)}), bf16[32,2,8,8,128]{4,3,2,1,0:T(8,128)(2,1)S(1)}, u32[]{:S(2)}, u32[]{:S(2)}) async-start(bf16[32,2,8,8,128]{4,3,2,1,0:T(8,128)(2,1)} %get-tuple-element.28), calls=%async_computation.1 | async-start | bytes 2097152 | tf_op jit(solution)/shard_map/all_to_all | solution.py:343
  181.5 21.0 %collective-permute-start.12 = (bf16[512,512]{1,0:T(8,128)(2,1)}, bf16[512,512]{1,0:T(8,128)(2,1)S(1)}, u32[]{:S(2)}, u32[]{:S(2)}) collective-permute-start(bf16[512,512]{1,0:T(8,128)(2,1)} %get-tuple-element.42), channel_id=1, source_target_pairs={{0,1},{1,2},{2,3},{3,0},{4,5},{5,6},{6,7},{7,4},{8,9},{9,10},{10,1... | collective-permute-start | bytes 1572872 | tf_op jit(solution)/shard_map/ppermute | solution.py:25
  181.5 27.2 %collective-permute-start.13 = (bf16[512,512]{1,0:T(8,128)(2,1)}, bf16[512,512]{1,0:T(8,128)(2,1)}, u32[]{:S(2)}, u32[]{:S(2)}) collective-permute-start(bf16[512,512]{1,0:T(8,128)(2,1)} %get-tuple-element.41), channel_id=1, source_target_pairs={{0,2},{1,3},{2,0},{3,1},{4,6},{5,7},{6,4},{7,5},{8,10},{9,11},{10,... | collective-permute-start | bytes 1572872 | tf_op jit(solution)/shard_map/ppermute | solution.py:25
  185.4 48.1 %copy-start.7 = (f32[8,2,128]{2,1,0:T(2,128)S(1)}, f32[8,2,128]{2,1,0:T(2,128)}, u32[]{:S(2)}) copy-start(f32[8,2,128]{2,1,0:T(2,128)} %get-tuple-element.37) | copy-start | bytes 24580
  185.4 48.1 %copy-start.8 = (f32[8,2,128]{2,1,0:T(2,128)S(1)}, f32[8,2,128]{2,1,0:T(2,128)}, u32[]{:S(2)}) copy-start(f32[8,2,128]{2,1,0:T(2,128)} %get-tuple-element.36) | copy-start | bytes 24580
  185.4 23.4 %collective-permute-start.14 = (bf16[512,512]{1,0:T(8,128)(2,1)}, bf16[512,512]{1,0:T(8,128)(2,1)S(1)}, u32[]{:S(2)}, u32[]{:S(2)}) collective-permute-start(bf16[512,512]{1,0:T(8,128)(2,1)} %get-tuple-element.40), channel_id=1, source_target_pairs={{0,3},{1,0},{2,1},{3,2},{4,7},{5,4},{6,5},{7,6},{8,11},{9,8},{10,9... | collective-permute-start | bytes 1572872 | tf_op jit(solution)/shard_map/ppermute | solution.py:25
  193.1 20.3 %collective-permute-start.15 = (bf16[512,256]{1,0:T(8,128)(2,1)}, bf16[512,256]{1,0:T(8,128)(2,1)S(1)}, u32[]{:S(2)}, u32[]{:S(2)}) collective-permute-start(bf16[512,256]{1,0:T(8,128)(2,1)} %get-tuple-element.34.refs_1_), channel_id=1, source_target_pairs={{0,1},{1,2},{2,3},{3,0},{4,5},{5,6},{6,7},{7,4},{8,9},{9,10},{10,1... | collective-permute-start | bytes 786440 | tf_op jit(solution)/shard_map/ppermute | solution.py:25
  199.8 13.6 %collective-permute-start.9 = (bf16[512,256]{1,0:T(8,128)(2,1)}, bf16[512,256]{1,0:T(8,128)(2,1)S(1)}, u32[]{:S(2)}, u32[]{:S(2)}) collective-permute-start(bf16[512,256]{1,0:T(8,128)(2,1)} %get-tuple-element.31.refs_1_), channel_id=1, source_target_pairs={{0,3},{1,0},{2,1},{3,2},{4,7},{5,4},{6,5},{7,6},{8,11},{9,8},{10,9... | collective-permute-start | bytes 786440 | tf_op jit(solution)/shard_map/ppermute | solution.py:25
  202.5 31.6 %copy-start.4 = (bf16[512,512]{1,0:T(8,128)(2,1)}, bf16[512,512]{1,0:T(8,128)(2,1)S(1)}, u32[]{:S(2)}) copy-start(bf16[512,512]{1,0:T(8,128)(2,1)S(1)} %collective-permute-done.12.refs_9_.refs_8_) | copy-start | bytes 1572868
  202.5 16.5 %collective-permute-start.6 = (bf16[512,256]{1,0:T(8,128)(2,1)}, bf16[512,256]{1,0:T(8,128)(2,1)S(1)}, u32[]{:S(2)}, u32[]{:S(2)}) collective-permute-start(bf16[512,256]{1,0:T(8,128)(2,1)} %get-tuple-element.30.refs_0_), channel_id=1, source_target_pairs={{0,1},{1,2},{2,3},{3,0},{4,5},{5,6},{6,7},{7,4},{8,9},{9,10},{10,1... | collective-permute-start | bytes 786440 | tf_op jit(solution)/shard_map/ppermute | solution.py:25
  208.8 10.3 %collective-permute-start.18 = (bf16[512,256]{1,0:T(8,128)(2,1)}, bf16[512,256]{1,0:T(8,128)(2,1)S(1)}, u32[]{:S(2)}, u32[]{:S(2)}) collective-permute-start(bf16[512,256]{1,0:T(8,128)(2,1)} %get-tuple-element.35.refs_2_), channel_id=1, source_target_pairs={{0,3},{1,0},{2,1},{3,2},{4,7},{5,4},{6,5},{7,6},{8,11},{9,8},{10,9... | collective-permute-start | bytes 786440 | tf_op jit(solution)/shard_map/ppermute | solution.py:25
  208.8 25.3 %copy-start.5 = (bf16[512,512]{1,0:T(8,128)(2,1)}, bf16[512,512]{1,0:T(8,128)(2,1)S(1)}, u32[]{:S(2)}) copy-start(bf16[512,512]{1,0:T(8,128)(2,1)S(1)} %collective-permute-done.14.refs_11_.refs_9_) | copy-start | bytes 1572868
  208.8 15.8 %collective-permute-start.11 = (bf16[512,256]{1,0:T(8,128)(2,1)}, bf16[512,256]{1,0:T(8,128)(2,1)S(1)}, u32[]{:S(2)}, u32[]{:S(2)}) collective-permute-start(bf16[512,256]{1,0:T(8,128)(2,1)} %get-tuple-element.30.refs_0_), channel_id=1, source_target_pairs={{0,3},{1,0},{2,1},{3,2},{4,7},{5,4},{6,5},{7,6},{8,11},{9,8},{10,9... | collective-permute-start | bytes 786440 | tf_op jit(solution)/shard_map/ppermute | solution.py:25
  213.4 14.4 %collective-permute-start.7 = (bf16[512,256]{1,0:T(8,128)(2,1)}, bf16[512,256]{1,0:T(8,128)(2,1)S(1)}, u32[]{:S(2)}, u32[]{:S(2)}) collective-permute-start(bf16[512,256]{1,0:T(8,128)(2,1)} %get-tuple-element.31.refs_1_), channel_id=1, source_target_pairs={{0,1},{1,2},{2,3},{3,0},{4,5},{5,6},{6,7},{7,4},{8,9},{9,10},{10,1... | collective-permute-start | bytes 786440 | tf_op jit(solution)/shard_map/ppermute | solution.py:25
  213.4 16.8 %collective-permute-start.10 = (bf16[512,256]{1,0:T(8,128)(2,1)S(1)}, bf16[512,256]{1,0:T(8,128)(2,1)S(1)}, u32[]{:S(2)}, u32[]{:S(2)}) collective-permute-start(bf16[512,256]{1,0:T(8,128)(2,1)S(1)} %collective-permute-done.9.refs_7_), channel_id=1, source_target_pairs={{0,3},{1,0},{2,1},{3,2},{4,7},{5,4},{6,5},{7,6},{8,11},{9,8},{10,9... | collective-permute-start | bytes 786440 | tf_op jit(solution)/shard_map/ppermute | solution.py:25
  219.0 15.1 %collective-permute-start.8 = (bf16[512,256]{1,0:T(8,128)(2,1)S(1)}, bf16[512,256]{1,0:T(8,128)(2,1)S(1)}, u32[]{:S(2)}, u32[]{:S(2)}) collective-permute-start(bf16[512,256]{1,0:T(8,128)(2,1)S(1)} %collective-permute-done.6.refs_2_), channel_id=1, source_target_pairs={{0,1},{1,2},{2,3},{3,0},{4,5},{5,6},{6,7},{7,4},{8,9},{9,10},{10,1... | collective-permute-start | bytes 786440 | tf_op jit(solution)/shard_map/ppermute | solution.py:25
  219.0 19.4 %collective-permute-start.16 = (bf16[512,256]{1,0:T(8,128)(2,1)}, bf16[512,256]{1,0:T(8,128)(2,1)S(1)}, u32[]{:S(2)}, u32[]{:S(2)}) collective-permute-start(bf16[512,256]{1,0:T(8,128)(2,1)} %get-tuple-element.35.refs_2_), channel_id=1, source_target_pairs={{0,1},{1,2},{2,3},{3,0},{4,5},{5,6},{6,7},{7,4},{8,9},{9,10},{10,1... | collective-permute-start | bytes 786440 | tf_op jit(solution)/shard_map/ppermute | solution.py:25
  224.6 13.9 %collective-permute-start.17 = (bf16[512,256]{1,0:T(8,128)(2,1)}, bf16[512,256]{1,0:T(8,128)(2,1)S(1)}, u32[]{:S(2)}, u32[]{:S(2)}) collective-permute-start(bf16[512,256]{1,0:T(8,128)(2,1)} %get-tuple-element.34.refs_1_), channel_id=1, source_target_pairs={{0,3},{1,0},{2,1},{3,2},{4,7},{5,4},{6,5},{7,6},{8,11},{9,8},{10,9... | collective-permute-start | bytes 786440 | tf_op jit(solution)/shard_map/ppermute | solution.py:25
  227.9 15.5 %collective-permute-start.19 = (bf16[512,256]{1,0:T(8,128)(2,1)S(1)}, bf16[512,256]{1,0:T(8,128)(2,1)S(1)}, u32[]{:S(2)}, u32[]{:S(2)}) collective-permute-start(bf16[512,256]{1,0:T(8,128)(2,1)S(1)} %collective-permute-done.15.refs_3_), channel_id=1, source_target_pairs={{0,1},{1,2},{2,3},{3,0},{4,5},{5,6},{6,7},{7,4},{8,9},{9,10},{10,1... | collective-permute-start | bytes 786440 | tf_op jit(solution)/shard_map/ppermute | solution.py:25
  230.2 13.1 %collective-permute-start.20 = (bf16[512,256]{1,0:T(8,128)(2,1)S(1)}, bf16[512,256]{1,0:T(8,128)(2,1)S(1)}, u32[]{:S(2)}, u32[]{:S(2)}) collective-permute-start(bf16[512,256]{1,0:T(8,128)(2,1)S(1)} %collective-permute-done.18.refs_6_), channel_id=1, source_target_pairs={{0,3},{1,0},{2,1},{3,2},{4,7},{5,4},{6,5},{7,6},{8,11},{9,8},{10,9... | collective-permute-start | bytes 786440 | tf_op jit(solution)/shard_map/ppermute | solution.py:25

commit v7 on v6

--- a/solution.py
+++ b/solution.py
@@ -38,27 +38,6 @@
 
 def dot(a, b):
     return jnp.dot(a, b, preferred_element_type=F32)
-
-
-def halves_kernel(top_in, bottom_in, top, bottom):
-    top[...] = top_in[...]
-    bottom[...] = bottom_in[...]
-
-
-def halves(array):
-    rows, width = array.shape
-    steps = 4
-    block = (rows // 2 // steps, width)
-    out = pl.BlockSpec(block, lambda i: (i, 0))
-    return pl.pallas_call(
-        halves_kernel,
-        out_shape=(jax.ShapeDtypeStruct((rows // 2, width), array.dtype),) * 2,
-        grid=(steps,),
-        in_specs=[out, pl.BlockSpec(block, lambda i: (i + steps, 0))],
-        out_specs=(out, out),
-        compiler_params=params(),
-        name="halves",
-    )(array, array)
 
 
 def columns_kernel(rows, out):
@@ -127,7 +106,7 @@
     rows_in = projected[head]
     slot_row = slot_of[0]
     devices, _, clusters, slot, _ = out.shape
-    step = 4
+    step = 16
     chunk = step * clusters * slot
 
     def body(i, carry):
@@ -254,26 +233,21 @@
 def products_kernel(count, carried, *refs):
     pairs, weights = refs[carried : carried + 2 * count], refs[carried + 2 * count : carried + 3 * count]
     out = refs[-1]
-    rows = out.shape[0]
-    per_side = pairs[0].shape[0] // rows
-    step = pl.program_id(0)
-    at = pl.ds(pl.multiple_of(step % per_side * rows, rows), rows)
 
     def add(side):
         total = refs[0][...] if carried else 0.0
         for k in range(count):
-            total += dot(pairs[2 * k + side][at], weights[k][...])
+            total += dot(pairs[2 * k + side][...], weights[k][...])
         out[...] = total.astype(out.dtype)
 
-    pl.when(step < per_side)(lambda: add(0))
-    pl.when(step >= per_side)(lambda: add(1))
+    pl.when(pl.program_id(0) == 0)(lambda: add(0))
+    pl.when(pl.program_id(0) == 1)(lambda: add(1))
 
 
 def products(total, parts, chunk, kind, own):
     half, depth = parts[0][0].shape
     width = parts[0][2].shape[1]
-    steps = 4
-    block = pl.BlockSpec((2 * half // steps, width), lambda i: (i, 0))
+    block = pl.BlockSpec((half, width), lambda i: (i, 0))
     fetched = pl.BlockSpec((half, depth), lambda i: (0, 0))
     carried = [] if total is None else [total]
     sides = [side for part in parts for side in part[:2]]
@@ -281,7 +255,7 @@
     return pl.pallas_call(
         functools.partial(products_kernel, len(parts), len(carried)),
         out_shape=jax.ShapeDtypeStruct((2 * half, width), kind),
-        grid=(steps,),
+        grid=(2,),
         in_specs=[block] * len(carried)
         + [fetched] * here
         + [VMEM_WHOLE] * (len(sides) - here)
@@ -313,7 +287,8 @@
     weights = project_weights.transpose(1, 0, 2)
     where = jnp.stack([here, (here - 1) % groups, (here + 1) % groups, (here + 2) % groups]).astype(jnp.int32)
 
-    top, bottom = halves(tokens)
+    half = rows // 2
+    top, bottom = tokens[:half], tokens[half:]
     left_top, right_bottom = shifted(top, 1), shifted(bottom, -1)
     left_bottom, right_top = shifted(bottom, 1), shifted(top, -1)
     left_top, right_bottom, slot_rows, where = lax.optimization_barrier((left_top, right_bottom, slot_rows, where))

time: 249 us -> 242 us (0.972)
  Pallas kernels: 72.7 us -> 64.2 us
    pallas_call x1 -> x0, Pallas kernels: 3.39 us -> none  [halves(): pl.pallas_call(halves_kernel, out_shape=(jax.ShapeDtypeStruct((rows // 2,...]
    pallas_call x3, Pallas kernels: 13.3 us -> 10.3 us  [products(): pl.pallas_call(functools.partial(products_kernel, len(parts), len(carried...]
  transfers between devices with their start and end apart: 25 -> 25, of which waited for: 11 -> 11; matrix products, arithmetic and copies ran while one was open for 3% -> 3% of each run, Pallas kernels for 22% -> 21%
where the time goes in v7:
time: 242 us; the launch traced here: 241 us
  waiting for transfers between devices  109 us (45%)
  Pallas kernels  64.2 us (27%)
  starting transfers between devices  54.2 us (22%)
  local copies, waits for them, and re-layouts  9.19 us (4%)
  matrix products  2.48 us (1%)
    all_to_all x2, waiting for transfers between devices, local(): received.append(lax.all_to_all(packed, SEQ, 0, 0, tiled=True))  62 us
    ppermute x21, waiting for transfers between devices, shifted(): lax.ppermute(array, 'head', [(i, (i + by) % count) for i in range(count)])  36 us
    ppermute x21, starting transfers between devices, shifted(): lax.ppermute(array, 'head', [(i, (i + by) % count) for i in range(count)])  30.3 us
    pallas_call x2, Pallas kernels, pack(): pl.pallas_call(pack_kernel, out_shape=jax.ShapeDtypeStruct((devices, head...  19.5 us
    all_to_all x2, starting transfers between devices, local(): received.append(lax.all_to_all(packed, SEQ, 0, 0, tiled=True))  15.7 us
    pallas_call x2, Pallas kernels, attend(): pl.pallas_call(functools.partial(attend_kernel, streamed), out_shape=(jax...  12.7 us
    all_to_all x2, waiting for transfers between devices, local(): returned = lax.all_to_all(buckets, SEQ, 0, 0, tiled=True)  11 us
    pallas_call x3, Pallas kernels, products(): pl.pallas_call(functools.partial(products_kernel, len(parts), len(carried...  10.3 us
  transfers between devices with their start and end apart: 25, of which 11 were waited for; matrix products, arithmetic and copies ran while one was open for 3% of the time, Pallas kernels for 21%

profile of v7, /device:TPU:1, one launch (start us, length us, event | category | flops | bytes accessed | tf_op | source)
XLA Modules:
  0.0 241.2 jit_solution(3090542577762410815)
XLA Ops:
  0.6 1.3 fusion.7
  1.9 3.6 %collective-permute-start.1 = (bf16[512,512]{1,0:T(8,128)(2,1)S(1)}, bf16[512,512]{1,0:T(8,128)(2,1)S(1)}, u32[]{:S(2)}, u32[]{:S(2)}) collective-permute-start(bf16[512,512]{1,0:T(8,128)(2,1)S(1)} %get-tuple-element.40), channel_id=1, source_target_pairs={{0,3},{1,0},{2,1},{3,2},{4,7},{5,4},{6,5},{7,6},{8,11},{9,8},{10,9... | collective-permute-start | bytes 1572872 | tf_op jit(solution)/shard_map/ppermute | solution.py:25
  5.6 2.7 %collective-permute-start.3 = (bf16[512,512]{1,0:T(8,128)(2,1)S(1)}, bf16[512,512]{1,0:T(8,128)(2,1)S(1)}, u32[]{:S(2)}, u32[]{:S(2)}) collective-permute-start(bf16[512,512]{1,0:T(8,128)(2,1)S(1)} %get-tuple-element.41), channel_id=1, source_target_pairs={{0,3},{1,0},{2,1},{3,2},{4,7},{5,4},{6,5},{7,6},{8,11},{9,8},{10,9... | collective-permute-start | bytes 1572872 | tf_op jit(solution)/shard_map/ppermute | solution.py:25
  8.2 0.7 copy.9
  8.9 2.5 %fusion = f32[4,1024]{1,0:T(4,128)S(1)} fusion(s32[4,1024]{1,0:T(4,128)S(1)} %bitcast.26), kind=kOutput, calls=%fused_computation.1 | convolution fusion | flops 2152722432 | bytes 32768 | tf_op jit(solution)/shard_map/ts,hsc->htc/dot_general | solution.py:282
  11.5 0.6 pad_add_fusion.where
  12.1 0.6 bitcast_add_fusion.slot_of.rows
  12.7 17.8 %collective-permute-done.left_top = bf16[512,512]{1,0:T(8,128)(2,1)S(1)} collective-permute-done((bf16[512,512]{1,0:T(8,128)(2,1)S(1)}, bf16[512,512]{1,0:T(8,128)(2,1)S(1)}, u32[]{:S(2)}, u32[]{:S(2)}) %collective-permute-start) | collective-permute-done | bytes 524320 | tf_op jit(solution)/shard_map/ppermute | solution.py:25
  30.5 2.7 %collective-permute-start.5 = (bf16[512,512]{1,0:T(8,128)(2,1)S(1)}, bf16[512,512]{1,0:T(8,128)(2,1)S(1)}, u32[]{:S(2)}, u32[]{:S(2)}) collective-permute-start(bf16[512,512]{1,0:T(8,128)(2,1)S(1)} %collective-permute-done.1.right_bottom), channel_id=1, source_target_pairs={{0,3},{1,0},{2,1},{3,2},{4,7},{5,4},{6,5},{7,6},{8,11},{9,8},{10,9... | collective-permute-start | bytes 1572872 | tf_op jit(solution)/shard_map/ppermute | solution.py:25
  33.2 9.6 %first_blocks.1.part = f32[3,1024,512]{2,1,0:T(8,128)} custom-call(s32[4]{0:T(128)} %pad_add_fusion.where, bf16[1024,512]{1,0:T(8,128)(2,1)} %own.1, bf16[512,512]{1,0:T(8,128)(2,1)S(1)} %collective-permute-done.left_top, bf16[512,512]{1,0:T(8,128)(2,1)S(1)} %collective-permute-done.2.left_bottom, bf16[512,512]{1,0:T(8,128)(2,1)S(1)} %collective-permute-done.3.right_top, ...), custom_call_target="tpu_custom_call" | custom-call | tf_op jit(solution)/shard_map/first_blocks/pallas_call | solution.py:73
  42.8 0.6 collective-permute-done.4.far_top
  43.4 9.8 %pack.3 = bf16[32,2,8,8,384]{4,3,2,1,0:T(8,128)(2,1)} custom-call(s32[4]{0:T(128)} %pad_add_fusion.where, f32[3,1024,512]{2,1,0:T(8,128)} %first_blocks.1.part, bf16[512,512]{1,0:T(8,128)(2,1)S(1)} %collective-permute-done.4.far_top, bf16[512,512]{1,0:T(8,128)(2,1)S(1)} %collective-permute-done.5.far_bottom, bf16[3,2048,512]{2,1,0:T(8,128)(2,1)} %bitcast.24, ...), custom_call_target="tpu_custom_call" | custom-call | tf_op jit(solution)/shard_map/pack/pallas_call | solution.py:134
  53.2 0.8 copy-done
  54.0 0.8 copy-done.2
  54.8 10.6 %all-to-all-start.2 = ((bf16[32,2,8,8,384]{4,3,2,1,0:T(8,128)(2,1)}), bf16[32,2,8,8,384]{4,3,2,1,0:T(8,128)(2,1)S(1)}, u32[]{:S(2)}, u32[]{:S(2)}) async-start(bf16[32,2,8,8,384]{4,3,2,1,0:T(8,128)(2,1)} %pack.3), calls=%async_computation.2 | async-start | bytes 6291456 | tf_op jit(solution)/shard_map/all_to_all | solution.py:312
  65.4 1.0 copy-done.1
  66.4 1.0 copy-done.3
  67.4 9.7 %pack.2 = bf16[32,2,8,8,384]{4,3,2,1,0:T(8,128)(2,1)} custom-call(s32[4]{0:T(128)} %pad_add_fusion.where, f32[3,1024,512]{2,1,0:T(8,128)} %first_blocks.1.part, bf16[512,512]{1,0:T(8,128)(2,1)S(1)} %copy-done.1, bf16[512,512]{1,0:T(8,128)(2,1)S(1)} %copy-done.3, bf16[3,2048,512]{2,1,0:T(8,128)(2,1)} %bitcast.25, s32[4,1,1024]{2,1,0:T(1,128)} %bitcast_add_fusion.slot_of.rows), custom_call_target="tpu_custom_call" | custom-call | tf_op jit(solution)/shard_map/pack/pallas_call | solution.py:134
  77.2 27.9 %all-to-all-done.2.received = bf16[32,2,8,8,384]{4,3,2,1,0:T(8,128)(2,1)S(1)} async-done(((bf16[32,2,8,8,384]{4,3,2,1,0:T(8,128)(2,1)}), bf16[32,2,8,8,384]{4,3,2,1,0:T(8,128)(2,1)S(1)}, u32[]{:S(2)}, u32[]{:S(2)}) %all-to-all-start.2) | async-done | bytes 3145760 | tf_op jit(solution)/shard_map/all_to_all | solution.py:312
  105.1 5.1 %all-to-all-start = ((bf16[32,2,8,8,384]{4,3,2,1,0:T(8,128)(2,1)}), bf16[32,2,8,8,384]{4,3,2,1,0:T(8,128)(2,1)}, u32[]{:S(2)}, u32[]{:S(2)}) async-start(bf16[32,2,8,8,384]{4,3,2,1,0:T(8,128)(2,1)} %pack.2), calls=%async_computation | async-start | bytes 6291456 | tf_op jit(solution)/shard_map/all_to_all | solution.py:312
  110.2 5.8 %attend.3 = (bf16[32,2,8,8,128]{4,3,2,1,0:T(8,128)(2,1)}, f32[8,2,128]{2,1,0:T(2,128)}) custom-call(bf16[32,2,8,8,384]{4,3,2,1,0:T(8,128)(2,1)S(1)} %all-to-all-done.2.received), custom_call_target="tpu_custom_call" | custom-call | tf_op jit(solution)/shard_map/attend/pallas_call | solution.py:188
  116.0 34.1 %all-to-all-done.received = bf16[32,2,8,8,384]{4,3,2,1,0:T(8,128)(2,1)} async-done(((bf16[32,2,8,8,384]{4,3,2,1,0:T(8,128)(2,1)}), bf16[32,2,8,8,384]{4,3,2,1,0:T(8,128)(2,1)}, u32[]{:S(2)}, u32[]{:S(2)}) %all-to-all-start) | async-done | bytes 3145760 | tf_op jit(solution)/shard_map/all_to_all | solution.py:312
  150.1 4.3 %all-to-all-start.3 = ((bf16[32,2,8,8,128]{4,3,2,1,0:T(8,128)(2,1)}), bf16[32,2,8,8,128]{4,3,2,1,0:T(8,128)(2,1)S(1)}, u32[]{:S(2)}, u32[]{:S(2)}) async-start(bf16[32,2,8,8,128]{4,3,2,1,0:T(8,128)(2,1)} %get-tuple-element.29), calls=%async_computation.3 | async-start | bytes 2097152 | tf_op jit(solution)/shard_map/all_to_all | solution.py:318
  154.4 6.9 %attend.2 = (bf16[32,2,8,8,128]{4,3,2,1,0:T(8,128)(2,1)}, f32[8,2,128]{2,1,0:T(2,128)}) custom-call(bf16[32,2,8,8,384]{4,3,2,1,0:T(8,128)(2,1)} %all-to-all-done.received), custom_call_target="tpu_custom_call" | custom-call | tf_op jit(solution)/shard_map/attend/pallas_call | solution.py:188
  161.3 10.0 %all-to-all-done.3.returned = bf16[32,2,8,8,128]{4,3,2,1,0:T(8,128)(2,1)S(1)} async-done(((bf16[32,2,8,8,128]{4,3,2,1,0:T(8,128)(2,1)}), bf16[32,2,8,8,128]{4,3,2,1,0:T(8,128)(2,1)S(1)}, u32[]{:S(2)}, u32[]{:S(2)}) %all-to-all-start.3) | async-done | bytes 1048608 | tf_op jit(solution)/shard_map/all_to_all | solution.py:318
  171.4 3.9 %all-to-all-start.1 = ((bf16[32,2,8,8,128]{4,3,2,1,0:T(8,128)(2,1)}), bf16[32,2,8,8,128]{4,3,2,1,0:T(8,128)(2,1)S(1)}, u32[]{:S(2)}, u32[]{:S(2)}) async-start(bf16[32,2,8,8,128]{4,3,2,1,0:T(8,128)(2,1)} %get-tuple-element.24), calls=%async_computation.1 | async-start | bytes 2097152 | tf_op jit(solution)/shard_map/all_to_all | solution.py:318
  175.3 2.9 %constant_dynamic-slice_fusion = (bf16[512,512]{1,0:T(8,128)(2,1)}, bf16[512,512]{1,0:T(8,128)(2,1)}, bf16[512,512]{1,0:T(8,128)(2,1)}, bf16[512,512]{1,0:T(8,128)(2,1)}) fusion(bf16[512,2048]{1,0:T(8,128)(2,1)} %param.6, s32[]{:T(128)S(6)} %select_n.52, s32[]{:T(128)S(6)} %select_n.50, s32[]{:T(128)S(6)} %select_n.49, s32[]{:T(128)S(6)} %select_n.48), kind=kLoop, calls=%fused_computation.10 | loop fusion | bytes 4194320 | tf_op jit(solution)/shard_map/dynamic_slice | solution.py:304
  178.2 3.8 %collective-permute-start.13 = (bf16[512,512]{1,0:T(8,128)(2,1)}, bf16[512,512]{1,0:T(8,128)(2,1)}, u32[]{:S(2)}, u32[]{:S(2)}) collective-permute-start(bf16[512,512]{1,0:T(8,128)(2,1)} %get-tuple-element.37), channel_id=1, source_target_pairs={{0,2},{1,3},{2,0},{3,1},{4,6},{5,7},{6,4},{7,5},{8,10},{9,11},{10,... | collective-permute-start | bytes 1572872 | tf_op jit(solution)/shard_map/ppermute | solution.py:25
  182.1 3.4 %columns.1.slot_of = s32[4,1024,1]{2,1,0:T(8,128)} custom-call(s32[4,1,1024]{2,1,0:T(1,128)} %bitcast_add_fusion.slot_of.rows), custom_call_target="tpu_custom_call" | custom-call | tf_op jit(solution)/shard_map/columns/pallas_call | solution.py:50
  185.5 4.3 %unpack.3 = (bf16[512,256]{1,0:T(8,128)(2,1)}, bf16[512,256]{1,0:T(8,128)(2,1)}) custom-call(bf16[32,2,8,8,128]{4,3,2,1,0:T(8,128)(2,1)S(1)} %all-to-all-done.3.returned, s32[4,1024,1]{2,1,0:T(8,128)} %columns.1.slot_of), custom_call_target="tpu_custom_call" | custom-call | tf_op jit(solution)/shard_map/unpack/pallas_call | solution.py:222
  189.8 1.4 collective-permute-start.15
  191.2 0.9 all-to-all-done.1.returned
  192.2 4.3 %unpack.2 = (bf16[512,256]{1,0:T(8,128)(2,1)}, bf16[512,256]{1,0:T(8,128)(2,1)}) custom-call(bf16[32,2,8,8,128]{4,3,2,1,0:T(8,128)(2,1)S(1)} %all-to-all-done.1.returned, s32[4,1024,1]{2,1,0:T(8,128)} %columns.1.slot_of), custom_call_target="tpu_custom_call" | custom-call | tf_op jit(solution)/shard_map/unpack/pallas_call | solution.py:222
  196.5 2.7 %collective-permute-start.9 = (bf16[512,256]{1,0:T(8,128)(2,1)}, bf16[512,256]{1,0:T(8,128)(2,1)S(1)}, u32[]{:S(2)}, u32[]{:S(2)}) collective-permute-start(bf16[512,256]{1,0:T(8,128)(2,1)} %get-tuple-element.27.refs_1_), channel_id=1, source_target_pairs={{0,3},{1,0},{2,1},{3,2},{4,7},{5,4},{6,5},{7,6},{8,11},{9,8},{10,9... | collective-permute-start | bytes 786440 | tf_op jit(solution)/shard_map/ppermute | solution.py:25
  199.2 6.3 %collective-permute-done.13.refs_10_.refs_3_ = bf16[512,512]{1,0:T(8,128)(2,1)} collective-permute-done((bf16[512,512]{1,0:T(8,128)(2,1)}, bf16[512,512]{1,0:T(8,128)(2,1)}, u32[]{:S(2)}, u32[]{:S(2)}) %collective-permute-start.13) | collective-permute-done | bytes 524320 | tf_op jit(solution)/shard_map/ppermute | solution.py:25
  205.4 2.2 collective-permute-start.11
  207.7 2.4 collective-permute-done.15.refs_3_
  210.1 3.2 %collective-permute-start.10 = (bf16[512,256]{1,0:T(8,128)(2,1)S(1)}, bf16[512,256]{1,0:T(8,128)(2,1)S(1)}, u32[]{:S(2)}, u32[]{:S(2)}) collective-permute-start(bf16[512,256]{1,0:T(8,128)(2,1)S(1)} %collective-permute-done.9.refs_7_), channel_id=1, source_target_pairs={{0,3},{1,0},{2,1},{3,2},{4,7},{5,4},{6,5},{7,6},{8,11},{9,8},{10,9... | collective-permute-start | bytes 786440 | tf_op jit(solution)/shard_map/ppermute | solution.py:25
  213.3 2.4 collective-permute-done.6.refs_2_
  215.7 1.4 collective-permute-start.16
  217.1 4.2 %collective-permute-done.11.refs_6_ = bf16[512,256]{1,0:T(8,128)(2,1)S(1)} collective-permute-done((bf16[512,256]{1,0:T(8,128)(2,1)}, bf16[512,256]{1,0:T(8,128)(2,1)S(1)}, u32[]{:S(2)}, u32[]{:S(2)}) %collective-permute-start.11) | collective-permute-done | bytes 262176 | tf_op jit(solution)/shard_map/ppermute | solution.py:25
  221.3 3.2 %collective-permute-start.17 = (bf16[512,256]{1,0:T(8,128)(2,1)}, bf16[512,256]{1,0:T(8,128)(2,1)S(1)}, u32[]{:S(2)}, u32[]{:S(2)}) collective-permute-start(bf16[512,256]{1,0:T(8,128)(2,1)} %get-tuple-element.30.refs_1_), channel_id=1, source_target_pairs={{0,3},{1,0},{2,1},{3,2},{4,7},{5,4},{6,5},{7,6},{8,11},{9,8},{10,9... | collective-permute-start | bytes 786440 | tf_op jit(solution)/shard_map/ppermute | solution.py:25
  224.5 2.4 collective-permute-done.10.refs_5_
  226.9 3.2 %collective-permute-start.20 = (bf16[512,256]{1,0:T(8,128)(2,1)S(1)}, bf16[512,256]{1,0:T(8,128)(2,1)S(1)}, u32[]{:S(2)}, u32[]{:S(2)}) collective-permute-start(bf16[512,256]{1,0:T(8,128)(2,1)S(1)} %collective-permute-done.18.refs_6_), channel_id=1, source_target_pairs={{0,3},{1,0},{2,1},{3,2},{4,7},{5,4},{6,5},{7,6},{8,11},{9,8},{10,9... | collective-permute-start | bytes 786440 | tf_op jit(solution)/shard_map/ppermute | solution.py:25
  230.2 0.6 copy.6
  230.8 3.8 %products.3.refs_0_ = f32[1024,512]{1,0:T(8,128)} custom-call(bf16[512,256]{1,0:T(8,128)(2,1)} %get-tuple-element.26.refs_0_, bf16[512,256]{1,0:T(8,128)(2,1)} %get-tuple-element.27.refs_1_, bf16[512,256]{1,0:T(8,128)(2,1)S(1)} %collective-permute-done.6.refs_2_, bf16[512,256]{1,0:T(8,128)(2,1)S(1)} %collective-permute-done.7.refs_3_, ...), custom_call_target="tpu_custom_call" | custom-call | tf_op jit(solution)/shard_map/products/pallas_call | solution.py:255
  234.6 3.8 %products.4.refs_0_ = f32[1024,512]{1,0:T(8,128)} custom-call(f32[1024,512]{1,0:T(8,128)} %products.3.refs_0_, bf16[512,256]{1,0:T(8,128)(2,1)} %get-tuple-element.30.refs_1_, bf16[512,256]{1,0:T(8,128)(2,1)} %get-tuple-element.31.refs_2_, bf16[512,256]{1,0:T(8,128)(2,1)S(1)} %collective-permute-done.15.refs_3_, ...), custom_call_target="tpu_custom_call" | custom-call | tf_op jit(solution)/shard_map/products/pallas_call | solution.py:255
  238.4 2.7 %products.5 = bf16[1024,512]{1,0:T(8,128)(2,1)} custom-call(f32[1024,512]{1,0:T(8,128)} %products.4.refs_0_, bf16[512,256]{1,0:T(8,128)(2,1)S(1)} %collective-permute-done.19.refs_1_, bf16[512,256]{1,0:T(8,128)(2,1)S(1)} %collective-permute-done.20.refs_2_, bf16[512,512]{1,0:T(8,128)(2,1)} %collective-permute-done.13.refs_10_.refs_3_), custom_call_target="tpu_custom_call" | custom-call | tf_op jit(solution)/shard_map/products/pallas_call | solution.py:255
  (40 shorter events, 0.1 us)
Async XLA Ops:
  1.9 28.6 %collective-permute-start.1 = (bf16[512,512]{1,0:T(8,128)(2,1)S(1)}, bf16[512,512]{1,0:T(8,128)(2,1)S(1)}, u32[]{:S(2)}, u32[]{:S(2)}) collective-permute-start(bf16[512,512]{1,0:T(8,128)(2,1)S(1)} %get-tuple-element.40), channel_id=1, source_target_pairs={{0,3},{1,0},{2,1},{3,2},{4,7},{5,4},{6,5},{7,6},{8,11},{9,8},{10,9... | collective-permute-start | bytes 1572872 | tf_op jit(solution)/shard_map/ppermute | solution.py:25
  5.5 27.7 %collective-permute-start.2 = (bf16[512,512]{1,0:T(8,128)(2,1)S(1)}, bf16[512,512]{1,0:T(8,128)(2,1)S(1)}, u32[]{:S(2)}, u32[]{:S(2)}) collective-permute-start(bf16[512,512]{1,0:T(8,128)(2,1)S(1)} %get-tuple-element.40), channel_id=1, source_target_pairs={{0,1},{1,2},{2,3},{3,0},{4,5},{5,6},{6,7},{7,4},{8,9},{9,10},{10,1... | collective-permute-start | bytes 1572872 | tf_op jit(solution)/shard_map/ppermute | solution.py:25
  5.5 25.0 %collective-permute-start = (bf16[512,512]{1,0:T(8,128)(2,1)S(1)}, bf16[512,512]{1,0:T(8,128)(2,1)S(1)}, u32[]{:S(2)}, u32[]{:S(2)}) collective-permute-start(bf16[512,512]{1,0:T(8,128)(2,1)S(1)} %get-tuple-element.41), channel_id=1, source_target_pairs={{0,1},{1,2},{2,3},{3,0},{4,5},{5,6},{6,7},{7,4},{8,9},{9,10},{10,1... | collective-permute-start | bytes 1572872 | tf_op jit(solution)/shard_map/ppermute | solution.py:25
  5.6 27.6 %collective-permute-start.3 = (bf16[512,512]{1,0:T(8,128)(2,1)S(1)}, bf16[512,512]{1,0:T(8,128)(2,1)S(1)}, u32[]{:S(2)}, u32[]{:S(2)}) collective-permute-start(bf16[512,512]{1,0:T(8,128)(2,1)S(1)} %get-tuple-element.41), channel_id=1, source_target_pairs={{0,3},{1,0},{2,1},{3,2},{4,7},{5,4},{6,5},{7,6},{8,11},{9,8},{10,9... | collective-permute-start | bytes 1572872 | tf_op jit(solution)/shard_map/ppermute | solution.py:25
  8.9 3.2 %copy-start.6 = (s32[4,1024,1]{1,2,0:T(1,128)S(1)}, s32[4,1024,1]{1,2,0:T(1,128)}, u32[]{:S(2)}) copy-start(s32[4,1024,1]{1,2,0:T(1,128)} %param.7) | copy-start | bytes 49156
  30.5 12.9 %collective-permute-start.4 = (bf16[512,512]{1,0:T(8,128)(2,1)S(1)}, bf16[512,512]{1,0:T(8,128)(2,1)S(1)}, u32[]{:S(2)}, u32[]{:S(2)}) collective-permute-start(bf16[512,512]{1,0:T(8,128)(2,1)S(1)} %collective-permute-done.left_top), channel_id=1, source_target_pairs={{0,1},{1,2},{2,3},{3,0},{4,5},{5,6},{6,7},{7,4},{8,9},{9,10},{10,1... | collective-permute-start | bytes 1572872 | tf_op jit(solution)/shard_map/ppermute | solution.py:25
  30.5 12.9 %collective-permute-start.5 = (bf16[512,512]{1,0:T(8,128)(2,1)S(1)}, bf16[512,512]{1,0:T(8,128)(2,1)S(1)}, u32[]{:S(2)}, u32[]{:S(2)}) collective-permute-start(bf16[512,512]{1,0:T(8,128)(2,1)S(1)} %collective-permute-done.1.right_bottom), channel_id=1, source_target_pairs={{0,3},{1,0},{2,1},{3,2},{4,7},{5,4},{6,5},{7,6},{8,11},{9,8},{10,9... | collective-permute-start | bytes 1572872 | tf_op jit(solution)/shard_map/ppermute | solution.py:25
  53.2 0.8 copy-start
  54.0 0.8 copy-start.2
  54.8 50.3 %all-to-all-start.2 = ((bf16[32,2,8,8,384]{4,3,2,1,0:T(8,128)(2,1)}), bf16[32,2,8,8,384]{4,3,2,1,0:T(8,128)(2,1)S(1)}, u32[]{:S(2)}, u32[]{:S(2)}) async-start(bf16[32,2,8,8,384]{4,3,2,1,0:T(8,128)(2,1)} %pack.3), calls=%async_computation.2 | async-start | bytes 6291456 | tf_op jit(solution)/shard_map/all_to_all | solution.py:312
  65.4 1.0 copy-start.1
  66.4 1.0 copy-start.3
  105.1 45.0 %all-to-all-start = ((bf16[32,2,8,8,384]{4,3,2,1,0:T(8,128)(2,1)}), bf16[32,2,8,8,384]{4,3,2,1,0:T(8,128)(2,1)}, u32[]{:S(2)}, u32[]{:S(2)}) async-start(bf16[32,2,8,8,384]{4,3,2,1,0:T(8,128)(2,1)} %pack.2), calls=%async_computation | async-start | bytes 6291456 | tf_op jit(solution)/shard_map/all_to_all | solution.py:312
  150.1 21.3 %all-to-all-start.3 = ((bf16[32,2,8,8,128]{4,3,2,1,0:T(8,128)(2,1)}), bf16[32,2,8,8,128]{4,3,2,1,0:T(8,128)(2,1)S(1)}, u32[]{:S(2)}, u32[]{:S(2)}) async-start(bf16[32,2,8,8,128]{4,3,2,1,0:T(8,128)(2,1)} %get-tuple-element.29), calls=%async_computation.3 | async-start | bytes 2097152 | tf_op jit(solution)/shard_map/all_to_all | solution.py:318
  171.4 20.8 %all-to-all-start.1 = ((bf16[32,2,8,8,128]{4,3,2,1,0:T(8,128)(2,1)}), bf16[32,2,8,8,128]{4,3,2,1,0:T(8,128)(2,1)S(1)}, u32[]{:S(2)}, u32[]{:S(2)}) async-start(bf16[32,2,8,8,128]{4,3,2,1,0:T(8,128)(2,1)} %get-tuple-element.24), calls=%async_computation.1 | async-start | bytes 2097152 | tf_op jit(solution)/shard_map/all_to_all | solution.py:318
  178.2 21.0 %collective-permute-start.12 = (bf16[512,512]{1,0:T(8,128)(2,1)}, bf16[512,512]{1,0:T(8,128)(2,1)S(1)}, u32[]{:S(2)}, u32[]{:S(2)}) collective-permute-start(bf16[512,512]{1,0:T(8,128)(2,1)} %get-tuple-element.38), channel_id=1, source_target_pairs={{0,1},{1,2},{2,3},{3,0},{4,5},{5,6},{6,7},{7,4},{8,9},{9,10},{10,1... | collective-permute-start | bytes 1572872 | tf_op jit(solution)/shard_map/ppermute | solution.py:25
  178.2 27.2 %collective-permute-start.13 = (bf16[512,512]{1,0:T(8,128)(2,1)}, bf16[512,512]{1,0:T(8,128)(2,1)}, u32[]{:S(2)}, u32[]{:S(2)}) collective-permute-start(bf16[512,512]{1,0:T(8,128)(2,1)} %get-tuple-element.37), channel_id=1, source_target_pairs={{0,2},{1,3},{2,0},{3,1},{4,6},{5,7},{6,4},{7,5},{8,10},{9,11},{10,... | collective-permute-start | bytes 1572872 | tf_op jit(solution)/shard_map/ppermute | solution.py:25
  182.1 48.1 %copy-start.7 = (f32[8,2,128]{2,1,0:T(2,128)S(1)}, f32[8,2,128]{2,1,0:T(2,128)}, u32[]{:S(2)}) copy-start(f32[8,2,128]{2,1,0:T(2,128)} %get-tuple-element.33) | copy-start | bytes 24580
  182.1 48.1 %copy-start.8 = (f32[8,2,128]{2,1,0:T(2,128)S(1)}, f32[8,2,128]{2,1,0:T(2,128)}, u32[]{:S(2)}) copy-start(f32[8,2,128]{2,1,0:T(2,128)} %get-tuple-element.32) | copy-start | bytes 24580
  182.1 23.4 %collective-permute-start.14 = (bf16[512,512]{1,0:T(8,128)(2,1)}, bf16[512,512]{1,0:T(8,128)(2,1)S(1)}, u32[]{:S(2)}, u32[]{:S(2)}) collective-permute-start(bf16[512,512]{1,0:T(8,128)(2,1)} %get-tuple-element.36), channel_id=1, source_target_pairs={{0,3},{1,0},{2,1},{3,2},{4,7},{5,4},{6,5},{7,6},{8,11},{9,8},{10,9... | collective-permute-start | bytes 1572872 | tf_op jit(solution)/shard_map/ppermute | solution.py:25
  189.8 20.3 %collective-permute-start.15 = (bf16[512,256]{1,0:T(8,128)(2,1)}, bf16[512,256]{1,0:T(8,128)(2,1)S(1)}, u32[]{:S(2)}, u32[]{:S(2)}) collective-permute-start(bf16[512,256]{1,0:T(8,128)(2,1)} %get-tuple-element.30.refs_1_), channel_id=1, source_target_pairs={{0,1},{1,2},{2,3},{3,0},{4,5},{5,6},{6,7},{7,4},{8,9},{9,10},{10,1... | collective-permute-start | bytes 786440 | tf_op jit(solution)/shard_map/ppermute | solution.py:25
  196.5 13.6 %collective-permute-start.9 = (bf16[512,256]{1,0:T(8,128)(2,1)}, bf16[512,256]{1,0:T(8,128)(2,1)S(1)}, u32[]{:S(2)}, u32[]{:S(2)}) collective-permute-start(bf16[512,256]{1,0:T(8,128)(2,1)} %get-tuple-element.27.refs_1_), channel_id=1, source_target_pairs={{0,3},{1,0},{2,1},{3,2},{4,7},{5,4},{6,5},{7,6},{8,11},{9,8},{10,9... | collective-permute-start | bytes 786440 | tf_op jit(solution)/shard_map/ppermute | solution.py:25
  199.2 31.6 %copy-start.4 = (bf16[512,512]{1,0:T(8,128)(2,1)}, bf16[512,512]{1,0:T(8,128)(2,1)S(1)}, u32[]{:S(2)}) copy-start(bf16[512,512]{1,0:T(8,128)(2,1)S(1)} %collective-permute-done.12.refs_9_.refs_8_) | copy-start | bytes 1572868
  199.2 16.5 %collective-permute-start.6 = (bf16[512,256]{1,0:T(8,128)(2,1)}, bf16[512,256]{1,0:T(8,128)(2,1)S(1)}, u32[]{:S(2)}, u32[]{:S(2)}) collective-permute-start(bf16[512,256]{1,0:T(8,128)(2,1)} %get-tuple-element.26.refs_0_), channel_id=1, source_target_pairs={{0,1},{1,2},{2,3},{3,0},{4,5},{5,6},{6,7},{7,4},{8,9},{9,10},{10,1... | collective-permute-start | bytes 786440 | tf_op jit(solution)/shard_map/ppermute | solution.py:25
  205.4 10.3 %collective-permute-start.18 = (bf16[512,256]{1,0:T(8,128)(2,1)}, bf16[512,256]{1,0:T(8,128)(2,1)S(1)}, u32[]{:S(2)}, u32[]{:S(2)}) collective-permute-start(bf16[512,256]{1,0:T(8,128)(2,1)} %get-tuple-element.31.refs_2_), channel_id=1, source_target_pairs={{0,3},{1,0},{2,1},{3,2},{4,7},{5,4},{6,5},{7,6},{8,11},{9,8},{10,9... | collective-permute-start | bytes 786440 | tf_op jit(solution)/shard_map/ppermute | solution.py:25
  205.4 25.4 %copy-start.5 = (bf16[512,512]{1,0:T(8,128)(2,1)}, bf16[512,512]{1,0:T(8,128)(2,1)S(1)}, u32[]{:S(2)}) copy-start(bf16[512,512]{1,0:T(8,128)(2,1)S(1)} %collective-permute-done.14.refs_11_.refs_9_) | copy-start | bytes 1572868
  205.4 15.9 %collective-permute-start.11 = (bf16[512,256]{1,0:T(8,128)(2,1)}, bf16[512,256]{1,0:T(8,128)(2,1)S(1)}, u32[]{:S(2)}, u32[]{:S(2)}) collective-permute-start(bf16[512,256]{1,0:T(8,128)(2,1)} %get-tuple-element.26.refs_0_), channel_id=1, source_target_pairs={{0,3},{1,0},{2,1},{3,2},{4,7},{5,4},{6,5},{7,6},{8,11},{9,8},{10,9... | collective-permute-start | bytes 786440 | tf_op jit(solution)/shard_map/ppermute | solution.py:25
  210.1 14.5 %collective-permute-start.7 = (bf16[512,256]{1,0:T(8,128)(2,1)}, bf16[512,256]{1,0:T(8,128)(2,1)S(1)}, u32[]{:S(2)}, u32[]{:S(2)}) collective-permute-start(bf16[512,256]{1,0:T(8,128)(2,1)} %get-tuple-element.27.refs_1_), channel_id=1, source_target_pairs={{0,1},{1,2},{2,3},{3,0},{4,5},{5,6},{6,7},{7,4},{8,9},{9,10},{10,1... | collective-permute-start | bytes 786440 | tf_op jit(solution)/shard_map/ppermute | solution.py:25
  210.1 16.9 %collective-permute-start.10 = (bf16[512,256]{1,0:T(8,128)(2,1)S(1)}, bf16[512,256]{1,0:T(8,128)(2,1)S(1)}, u32[]{:S(2)}, u32[]{:S(2)}) collective-permute-start(bf16[512,256]{1,0:T(8,128)(2,1)S(1)} %collective-permute-done.9.refs_7_), channel_id=1, source_target_pairs={{0,3},{1,0},{2,1},{3,2},{4,7},{5,4},{6,5},{7,6},{8,11},{9,8},{10,9... | collective-permute-start | bytes 786440 | tf_op jit(solution)/shard_map/ppermute | solution.py:25
  215.7 15.1 %collective-permute-start.8 = (bf16[512,256]{1,0:T(8,128)(2,1)S(1)}, bf16[512,256]{1,0:T(8,128)(2,1)S(1)}, u32[]{:S(2)}, u32[]{:S(2)}) collective-permute-start(bf16[512,256]{1,0:T(8,128)(2,1)S(1)} %collective-permute-done.6.refs_2_), channel_id=1, source_target_pairs={{0,1},{1,2},{2,3},{3,0},{4,5},{5,6},{6,7},{7,4},{8,9},{9,10},{10,1... | collective-permute-start | bytes 786440 | tf_op jit(solution)/shard_map/ppermute | solution.py:25
  215.7 18.9 %collective-permute-start.16 = (bf16[512,256]{1,0:T(8,128)(2,1)}, bf16[512,256]{1,0:T(8,128)(2,1)S(1)}, u32[]{:S(2)}, u32[]{:S(2)}) collective-permute-start(bf16[512,256]{1,0:T(8,128)(2,1)} %get-tuple-element.31.refs_2_), channel_id=1, source_target_pairs={{0,1},{1,2},{2,3},{3,0},{4,5},{5,6},{6,7},{7,4},{8,9},{9,10},{10,1... | collective-permute-start | bytes 786440 | tf_op jit(solution)/shard_map/ppermute | solution.py:25
  221.3 13.3 %collective-permute-start.17 = (bf16[512,256]{1,0:T(8,128)(2,1)}, bf16[512,256]{1,0:T(8,128)(2,1)S(1)}, u32[]{:S(2)}, u32[]{:S(2)}) collective-permute-start(bf16[512,256]{1,0:T(8,128)(2,1)} %get-tuple-element.30.refs_1_), channel_id=1, source_target_pairs={{0,3},{1,0},{2,1},{3,2},{4,7},{5,4},{6,5},{7,6},{8,11},{9,8},{10,9... | collective-permute-start | bytes 786440 | tf_op jit(solution)/shard_map/ppermute | solution.py:25
  224.5 13.9 %collective-permute-start.19 = (bf16[512,256]{1,0:T(8,128)(2,1)S(1)}, bf16[512,256]{1,0:T(8,128)(2,1)S(1)}, u32[]{:S(2)}, u32[]{:S(2)}) collective-permute-start(bf16[512,256]{1,0:T(8,128)(2,1)S(1)} %collective-permute-done.15.refs_3_), channel_id=1, source_target_pairs={{0,1},{1,2},{2,3},{3,0},{4,5},{5,6},{6,7},{7,4},{8,9},{9,10},{10,1... | collective-permute-start | bytes 786440 | tf_op jit(solution)/shard_map/ppermute | solution.py:25
  226.9 11.5 %collective-permute-start.20 = (bf16[512,256]{1,0:T(8,128)(2,1)S(1)}, bf16[512,256]{1,0:T(8,128)(2,1)S(1)}, u32[]{:S(2)}, u32[]{:S(2)}) collective-permute-start(bf16[512,256]{1,0:T(8,128)(2,1)S(1)} %collective-permute-done.18.refs_6_), channel_id=1, source_target_pairs={{0,3},{1,0},{2,1},{3,2},{4,7},{5,4},{6,5},{7,6},{8,11},{9,8},{10,9... | collective-permute-start | bytes 786440 | tf_op jit(solution)/shard_map/ppermute | solution.py:25

commit v8 on v7

--- a/solution.py
+++ b/solution.py
@@ -38,24 +38,6 @@
 
 def dot(a, b):
     return jnp.dot(a, b, preferred_element_type=F32)
-
-
-def columns_kernel(rows, out):
-    count = rows.shape[2]
-    out[0] = jnp.broadcast_to(rows[0], (8, count)).T[:, :1]
-
-
-def columns(rows):
-    heads, _, count = rows.shape
-    return pl.pallas_call(
-        columns_kernel,
-        out_shape=jax.ShapeDtypeStruct((heads, count, 1), rows.dtype),
-        grid=(heads,),
-        in_specs=[pl.BlockSpec((1, 1, count), lambda h: (h, 0, 0))],
-        out_specs=pl.BlockSpec((1, count, 1), lambda h: (h, 0, 0)),
-        compiler_params=params(),
-        name="columns",
-    )(rows)
 
 
 def first_blocks_kernel(where, own, left_top, left_bottom, right_top, right_bottom, w_own, w_left, w_right, out):
@@ -203,64 +185,64 @@
 
 
 def unpack_kernel(returned, slot_of, top, bottom):
-    devices, _, clusters, slot, width = returned.shape
-    slots = devices * clusters * slot
-    half = top.shape[0]
-    source = returned[:, pl.program_id(0)].reshape(slots, width)
-    chunk = 256
-
-    iota = lax.broadcasted_iota(jnp.int32, (chunk, slots), 1)
-    for start in range(0, 2 * half, chunk):
-        onehot = jnp.where(iota == slot_of[0, start : start + chunk], 1.0, 0.0).astype(BF16)
-        out, to = (top, start) if start < half else (bottom, start - half)
-        out[to : to + chunk] = dot(onehot, source).astype(BF16)
-
-
-def unpack(returned, slot_cols, group):
+    half, width = top.shape
+    source = returned[:, pl.program_id(0)].reshape(-1, width)
+    slots = source.shape[0]
+    iota = lax.broadcasted_iota(jnp.int32, (slots, half), 0)
+    for k, out in enumerate((top, bottom)):
+        onehot = jnp.where(iota == slot_of[0, :, k * half : (k + 1) * half], 1.0, 0.0).astype(BF16)
+        rows = lax.dot_general(onehot, source, (((0,), (0,)), ((), ())), preferred_element_type=F32)
+        out[...] = rows.astype(BF16)
+
+
+def unpack(returned, slot_rows, group):
     _, heads, _, _, width = returned.shape
-    rows = slot_cols.shape[1]
+    rows = slot_rows.shape[2]
     return pl.pallas_call(
         unpack_kernel,
         out_shape=(jax.ShapeDtypeStruct((rows // 2, heads * width), BF16),) * 2,
         grid=(heads,),
-        in_specs=[VMEM_WHOLE, pl.BlockSpec((1, rows, 1), lambda h: (group * heads + h, 0, 0))],
+        in_specs=[VMEM_WHOLE, pl.BlockSpec((1, 1, rows), lambda h: (group * heads + h, 0, 0))],
         out_specs=(pl.BlockSpec((rows // 2, width), lambda h: (0, h)),) * 2,
         compiler_params=params(),
         name="unpack",
-    )(in_vmem(returned), slot_cols)
-
-
-def products_kernel(count, carried, *refs):
+    )(in_vmem(returned), slot_rows)
+
+
+def products_kernel(count, carried, keep, kept, *refs):
     pairs, weights = refs[carried : carried + 2 * count], refs[carried + 2 * count : carried + 3 * count]
     out = refs[-1]
+    rows = pairs[0].shape[0]
 
     def add(side):
-        total = refs[0][...] if carried else 0.0
+        total = 0.0
+        if carried:
+            total = refs[0][pl.ds(pl.program_id(0) * rows, rows)] if kept else refs[0][...]
         for k in range(count):
             total += dot(pairs[2 * k + side][...], weights[k][...])
-        out[...] = total.astype(out.dtype)
+        out[pl.ds(side * rows, rows) if keep else slice(None)] = total.astype(out.dtype)
 
     pl.when(pl.program_id(0) == 0)(lambda: add(0))
     pl.when(pl.program_id(0) == 1)(lambda: add(1))
 
 
-def products(total, parts, chunk, kind, own):
+def products(total, parts, chunk, kind, own, keep=False, kept=False):
     half, depth = parts[0][0].shape
     width = parts[0][2].shape[1]
     block = pl.BlockSpec((half, width), lambda i: (i, 0))
     fetched = pl.BlockSpec((half, depth), lambda i: (0, 0))
-    carried = [] if total is None else [total]
+    carried = [] if total is None else [in_vmem(total) if kept else total]
     sides = [side for part in parts for side in part[:2]]
     here = 2 if own else 0
     return pl.pallas_call(
-        functools.partial(products_kernel, len(parts), len(carried)),
-        out_shape=jax.ShapeDtypeStruct((2 * half, width), kind),
+        functools.partial(products_kernel, len(parts), len(carried), keep, kept),
+        out_shape=(pltpu.VMEM if keep else jax.ShapeDtypeStruct)((2 * half, width), kind),
         grid=(2,),
-        in_specs=[block] * len(carried)
+        in_specs=[VMEM_WHOLE if kept else block] * len(carried)
         + [fetched] * here
         + [VMEM_WHOLE] * (len(sides) - here)
         + [pl.BlockSpec((depth, width), lambda i: (chunk, 0))] * len(parts),
-        out_specs=block,
+        out_specs=VMEM_WHOLE if keep else block,
         compiler_params=params(),
         name="products",
     )(*carried, *sides[:here], *[in_vmem(side) for side in sides[here:]], *[part[2] for part in parts])
@@ -295,10 +277,7 @@
     far_top, far_bottom = shifted(left_top, 1), shifted(right_bottom, -1)
     part = first_blocks(where, tokens, (left_top, left_bottom, right_top, right_bottom), weights)
 
-    out_weights, late_rows, far_top, far_bottom = lax.optimization_barrier(
-        (output_weights, slot_rows, far_top, far_bottom)
-    )
-    slot_cols = columns(late_rows)
+    out_weights, far_top, far_bottom = lax.optimization_barrier((output_weights, far_top, far_bottom))
     out_blocks = []
     for by in range(groups):
         block = lax.dynamic_slice(out_weights, (0, (here + by) % groups * width), (width, width))
@@ -316,7 +295,7 @@
         buckets, sums = attend(received[chunk], streamed=chunk == 0)
         owned.append(sums)
         returned = lax.all_to_all(buckets, SEQ, 0, 0, tiled=True)
-        top, bottom = unpack(returned, slot_cols, chunk)
+        top, bottom = unpack(returned, slot_rows, chunk)
         left_top, right_bottom = shifted(top, 1), shifted(bottom, -1)
         left_bottom, right_top = shifted(bottom, 1), shifted(top, -1)
         far_top, far_bottom = shifted(left_top, 1), shifted(right_bottom, -1)
@@ -324,8 +303,8 @@
 
     first, second = ([(*blocks[by], out_blocks[by]) for by in range(groups)] for blocks in gathered)
     total = products(None, first, 0, F32, own=True)
-    total = products(total, second[:2] + second[3:], 1, F32, own=True)
-    total = products(total, second[2:3], 1, BF16, own=False)
+    total = products(total, second[:2] + second[3:], 1, F32, own=True, keep=True)
+    total = products(total, second[2:3], 1, BF16, own=False, kept=True)
     owned = jnp.concatenate(owned, axis=1).transpose(1, 0, 2)
     return (total, owned)
 

time: 242 us -> 242 us (level)
  Pallas kernels: 64.2 us -> 58.9 us
  waiting for transfers between devices: 109 us -> 114 us
    all_to_all x2, waiting for transfers between devices: 11 us -> 14.6 us  [local(): returned = lax.all_to_all(buckets, SEQ, 0, 0, tiled=True)]
    pallas_call x1 -> x0, Pallas kernels: 3.39 us -> none  [columns(): pl.pallas_call(columns_kernel, out_shape=jax.ShapeDtypeStruct((heads, cou...]
  transfers between devices with their start and end apart: 25 -> 25, of which waited for: 11 -> 15; matrix products, arithmetic and copies ran while one was open for 3% -> 3% of each run, Pallas kernels for 21% -> 19%
where the time goes in v8:
time: 242 us; the launch traced here: 241 us
  waiting for transfers between devices  114 us (47%)
  Pallas kernels  58.9 us (24%)
  starting transfers between devices  54.4 us (22%)
  local copies, waits for them, and re-layouts  9.18 us (4%)
  matrix products  2.48 us (1%)
    all_to_all x2, waiting for transfers between devices, local(): received.append(lax.all_to_all(packed, SEQ, 0, 0, tiled=True))  62 us
    ppermute x21, waiting for transfers between devices, shifted(): lax.ppermute(array, 'head', [(i, (i + by) % count) for i in range(count)])  37 us
    ppermute x21, starting transfers between devices, shifted(): lax.ppermute(array, 'head', [(i, (i + by) % count) for i in range(count)])  30.3 us
    pallas_call x2, Pallas kernels, pack(): pl.pallas_call(pack_kernel, out_shape=jax.ShapeDtypeStruct((devices, head...  19.5 us
    all_to_all x2, starting transfers between devices, local(): received.append(lax.all_to_all(packed, SEQ, 0, 0, tiled=True))  15.7 us
    all_to_all x2, waiting for transfers between devices, local(): returned = lax.all_to_all(buckets, SEQ, 0, 0, tiled=True)  14.6 us
    pallas_call x2, Pallas kernels, attend(): pl.pallas_call(functools.partial(attend_kernel, streamed), out_shape=(jax...  12.7 us
    pallas_call x1, Pallas kernels, first_blocks(): pl.pallas_call(first_blocks_kernel, out_shape=jax.ShapeDtypeStruct((kinds...  9.63 us
  transfers between devices with their start and end apart: 25, of which 15 were waited for; matrix products, arithmetic and copies ran while one was open for 3% of the time, Pallas kernels for 19%

profile of v8, /device:TPU:1, one launch (start us, length us, event | category | flops | bytes accessed | tf_op | source)
XLA Modules:
  0.0 240.6 jit_solution(17156046827129899116)
XLA Ops:
  0.6 1.3 fusion.7
  1.9 3.6 %collective-permute-start.1 = (bf16[512,512]{1,0:T(8,128)(2,1)S(1)}, bf16[512,512]{1,0:T(8,128)(2,1)S(1)}, u32[]{:S(2)}, u32[]{:S(2)}) collective-permute-start(bf16[512,512]{1,0:T(8,128)(2,1)S(1)} %get-tuple-element.38), channel_id=1, source_target_pairs={{0,3},{1,0},{2,1},{3,2},{4,7},{5,4},{6,5},{7,6},{8,11},{9,8},{10,9... | collective-permute-start | bytes 1572872 | tf_op jit(solution)/shard_map/ppermute | solution.py:25
  5.6 2.7 %collective-permute-start.3 = (bf16[512,512]{1,0:T(8,128)(2,1)S(1)}, bf16[512,512]{1,0:T(8,128)(2,1)S(1)}, u32[]{:S(2)}, u32[]{:S(2)}) collective-permute-start(bf16[512,512]{1,0:T(8,128)(2,1)S(1)} %get-tuple-element.39), channel_id=1, source_target_pairs={{0,3},{1,0},{2,1},{3,2},{4,7},{5,4},{6,5},{7,6},{8,11},{9,8},{10,9... | collective-permute-start | bytes 1572872 | tf_op jit(solution)/shard_map/ppermute | solution.py:25
  8.2 0.7 copy.9
  8.9 2.5 %fusion = f32[4,1024]{1,0:T(4,128)S(1)} fusion(s32[4,1024]{1,0:T(4,128)S(1)} %bitcast.26), kind=kOutput, calls=%fused_computation.1 | convolution fusion | flops 2152722432 | bytes 32768 | tf_op jit(solution)/shard_map/ts,hsc->htc/dot_general | solution.py:264
  11.5 0.6 pad_add_fusion.where
  12.1 0.6 bitcast_add_fusion.slot_of
  12.7 17.8 %collective-permute-done.left_top = bf16[512,512]{1,0:T(8,128)(2,1)S(1)} collective-permute-done((bf16[512,512]{1,0:T(8,128)(2,1)S(1)}, bf16[512,512]{1,0:T(8,128)(2,1)S(1)}, u32[]{:S(2)}, u32[]{:S(2)}) %collective-permute-start) | collective-permute-done | bytes 524320 | tf_op jit(solution)/shard_map/ppermute | solution.py:25
  30.5 2.7 %collective-permute-start.5 = (bf16[512,512]{1,0:T(8,128)(2,1)S(1)}, bf16[512,512]{1,0:T(8,128)(2,1)S(1)}, u32[]{:S(2)}, u32[]{:S(2)}) collective-permute-start(bf16[512,512]{1,0:T(8,128)(2,1)S(1)} %collective-permute-done.1.right_bottom), channel_id=1, source_target_pairs={{0,3},{1,0},{2,1},{3,2},{4,7},{5,4},{6,5},{7,6},{8,11},{9,8},{10,9... | collective-permute-start | bytes 1572872 | tf_op jit(solution)/shard_map/ppermute | solution.py:25
  33.2 9.6 %first_blocks.1.part = f32[3,1024,512]{2,1,0:T(8,128)} custom-call(s32[4]{0:T(128)} %pad_add_fusion.where, bf16[1024,512]{1,0:T(8,128)(2,1)} %own.1, bf16[512,512]{1,0:T(8,128)(2,1)S(1)} %collective-permute-done.left_top, bf16[512,512]{1,0:T(8,128)(2,1)S(1)} %collective-permute-done.2.left_bottom, bf16[512,512]{1,0:T(8,128)(2,1)S(1)} %collective-permute-done.3.right_top, ...), custom_call_target="tpu_custom_call" | custom-call | tf_op jit(solution)/shard_map/first_blocks/pallas_call | solution.py:55
  42.8 0.6 collective-permute-done.4.far_top
  43.4 9.8 %pack.3 = bf16[32,2,8,8,384]{4,3,2,1,0:T(8,128)(2,1)} custom-call(s32[4]{0:T(128)} %pad_add_fusion.where, f32[3,1024,512]{2,1,0:T(8,128)} %first_blocks.1.part, bf16[512,512]{1,0:T(8,128)(2,1)S(1)} %collective-permute-done.4.far_top, bf16[512,512]{1,0:T(8,128)(2,1)S(1)} %collective-permute-done.5.far_bottom, bf16[3,2048,512]{2,1,0:T(8,128)(2,1)} %bitcast.24, ...), custom_call_target="tpu_custom_call" | custom-call | tf_op jit(solution)/shard_map/pack/pallas_call | solution.py:116
  53.2 0.8 copy-done
  54.0 0.8 copy-done.2
  54.8 10.6 %all-to-all-start.2 = ((bf16[32,2,8,8,384]{4,3,2,1,0:T(8,128)(2,1)}), bf16[32,2,8,8,384]{4,3,2,1,0:T(8,128)(2,1)S(1)}, u32[]{:S(2)}, u32[]{:S(2)}) async-start(bf16[32,2,8,8,384]{4,3,2,1,0:T(8,128)(2,1)} %pack.3), calls=%async_computation.2 | async-start | bytes 6291456 | tf_op jit(solution)/shard_map/all_to_all | solution.py:291
  65.4 1.0 copy-done.1
  66.4 1.0 copy-done.3
  67.4 9.7 %pack.2 = bf16[32,2,8,8,384]{4,3,2,1,0:T(8,128)(2,1)} custom-call(s32[4]{0:T(128)} %pad_add_fusion.where, f32[3,1024,512]{2,1,0:T(8,128)} %first_blocks.1.part, bf16[512,512]{1,0:T(8,128)(2,1)S(1)} %copy-done.1, bf16[512,512]{1,0:T(8,128)(2,1)S(1)} %copy-done.3, bf16[3,2048,512]{2,1,0:T(8,128)(2,1)} %bitcast.25, s32[4,1,1024]{2,1,0:T(1,128)} %bitcast_add_fusion.slot_of), custom_call_target="tpu_custom_call" | custom-call | tf_op jit(solution)/shard_map/pack/pallas_call | solution.py:116
  77.2 27.9 %all-to-all-done.2.received = bf16[32,2,8,8,384]{4,3,2,1,0:T(8,128)(2,1)S(1)} async-done(((bf16[32,2,8,8,384]{4,3,2,1,0:T(8,128)(2,1)}), bf16[32,2,8,8,384]{4,3,2,1,0:T(8,128)(2,1)S(1)}, u32[]{:S(2)}, u32[]{:S(2)}) %all-to-all-start.2) | async-done | bytes 3145760 | tf_op jit(solution)/shard_map/all_to_all | solution.py:291
  105.1 5.1 %all-to-all-start = ((bf16[32,2,8,8,384]{4,3,2,1,0:T(8,128)(2,1)}), bf16[32,2,8,8,384]{4,3,2,1,0:T(8,128)(2,1)}, u32[]{:S(2)}, u32[]{:S(2)}) async-start(bf16[32,2,8,8,384]{4,3,2,1,0:T(8,128)(2,1)} %pack.2), calls=%async_computation | async-start | bytes 6291456 | tf_op jit(solution)/shard_map/all_to_all | solution.py:291
  110.2 5.8 %attend.3 = (bf16[32,2,8,8,128]{4,3,2,1,0:T(8,128)(2,1)}, f32[8,2,128]{2,1,0:T(2,128)}) custom-call(bf16[32,2,8,8,384]{4,3,2,1,0:T(8,128)(2,1)S(1)} %all-to-all-done.2.received), custom_call_target="tpu_custom_call" | custom-call | tf_op jit(solution)/shard_map/attend/pallas_call | solution.py:170
  116.0 34.1 %all-to-all-done.received = bf16[32,2,8,8,384]{4,3,2,1,0:T(8,128)(2,1)} async-done(((bf16[32,2,8,8,384]{4,3,2,1,0:T(8,128)(2,1)}), bf16[32,2,8,8,384]{4,3,2,1,0:T(8,128)(2,1)}, u32[]{:S(2)}, u32[]{:S(2)}) %all-to-all-start) | async-done | bytes 3145760 | tf_op jit(solution)/shard_map/all_to_all | solution.py:291
  150.1 4.3 %all-to-all-start.3 = ((bf16[32,2,8,8,128]{4,3,2,1,0:T(8,128)(2,1)}), bf16[32,2,8,8,128]{4,3,2,1,0:T(8,128)(2,1)S(1)}, u32[]{:S(2)}, u32[]{:S(2)}) async-start(bf16[32,2,8,8,128]{4,3,2,1,0:T(8,128)(2,1)} %get-tuple-element.27), calls=%async_computation.3 | async-start | bytes 2097152 | tf_op jit(solution)/shard_map/all_to_all | solution.py:297
  154.4 6.9 %attend.2 = (bf16[32,2,8,8,128]{4,3,2,1,0:T(8,128)(2,1)}, f32[8,2,128]{2,1,0:T(2,128)}) custom-call(bf16[32,2,8,8,384]{4,3,2,1,0:T(8,128)(2,1)} %all-to-all-done.received), custom_call_target="tpu_custom_call" | custom-call | tf_op jit(solution)/shard_map/attend/pallas_call | solution.py:170
  161.3 10.0 %all-to-all-done.3.returned = bf16[32,2,8,8,128]{4,3,2,1,0:T(8,128)(2,1)S(1)} async-done(((bf16[32,2,8,8,128]{4,3,2,1,0:T(8,128)(2,1)}), bf16[32,2,8,8,128]{4,3,2,1,0:T(8,128)(2,1)S(1)}, u32[]{:S(2)}, u32[]{:S(2)}) %all-to-all-start.3) | async-done | bytes 1048608 | tf_op jit(solution)/shard_map/all_to_all | solution.py:297
  171.4 4.0 %all-to-all-start.1 = ((bf16[32,2,8,8,128]{4,3,2,1,0:T(8,128)(2,1)}), bf16[32,2,8,8,128]{4,3,2,1,0:T(8,128)(2,1)S(1)}, u32[]{:S(2)}, u32[]{:S(2)}) async-start(bf16[32,2,8,8,128]{4,3,2,1,0:T(8,128)(2,1)} %get-tuple-element.23), calls=%async_computation.1 | async-start | bytes 2097152 | tf_op jit(solution)/shard_map/all_to_all | solution.py:297
  175.4 2.9 %constant_dynamic-slice_fusion = (bf16[512,512]{1,0:T(8,128)(2,1)}, bf16[512,512]{1,0:T(8,128)(2,1)}, bf16[512,512]{1,0:T(8,128)(2,1)}, bf16[512,512]{1,0:T(8,128)(2,1)}) fusion(bf16[512,2048]{1,0:T(8,128)(2,1)} %param.6, s32[]{:T(128)S(6)} %select_n.52, s32[]{:T(128)S(6)} %select_n.50, s32[]{:T(128)S(6)} %select_n.49, s32[]{:T(128)S(6)} %select_n.48), kind=kLoop, calls=%fused_computation.10 | loop fusion | bytes 4194320 | tf_op jit(solution)/shard_map/dynamic_slice | solution.py:283
  178.3 3.8 %collective-permute-start.13 = (bf16[512,512]{1,0:T(8,128)(2,1)}, bf16[512,512]{1,0:T(8,128)(2,1)}, u32[]{:S(2)}, u32[]{:S(2)}) collective-permute-start(bf16[512,512]{1,0:T(8,128)(2,1)} %get-tuple-element.35), channel_id=1, source_target_pairs={{0,2},{1,3},{2,0},{3,1},{4,6},{5,7},{6,4},{7,5},{8,10},{9,11},{10,... | collective-permute-start | bytes 1572872 | tf_op jit(solution)/shard_map/ppermute | solution.py:25
  182.2 4.0 %unpack.3 = (bf16[512,256]{1,0:T(8,128)(2,1)}, bf16[512,256]{1,0:T(8,128)(2,1)}) custom-call(bf16[32,2,8,8,128]{4,3,2,1,0:T(8,128)(2,1)S(1)} %all-to-all-done.3.returned, s32[4,1,1024]{2,1,0:T(1,128)} %bitcast_add_fusion.slot_of), custom_call_target="tpu_custom_call" | custom-call | tf_op jit(solution)/shard_map/unpack/pallas_call | solution.py:201
  186.2 1.5 collective-permute-start.15
  187.7 4.6 %all-to-all-done.1.returned = bf16[32,2,8,8,128]{4,3,2,1,0:T(8,128)(2,1)S(1)} async-done(((bf16[32,2,8,8,128]{4,3,2,1,0:T(8,128)(2,1)}), bf16[32,2,8,8,128]{4,3,2,1,0:T(8,128)(2,1)S(1)}, u32[]{:S(2)}, u32[]{:S(2)}) %all-to-all-start.1) | async-done | bytes 1048608 | tf_op jit(solution)/shard_map/all_to_all | solution.py:297
  192.3 4.0 %unpack.2 = (bf16[512,256]{1,0:T(8,128)(2,1)}, bf16[512,256]{1,0:T(8,128)(2,1)}) custom-call(bf16[32,2,8,8,128]{4,3,2,1,0:T(8,128)(2,1)S(1)} %all-to-all-done.1.returned, s32[4,1,1024]{2,1,0:T(1,128)} %bitcast_add_fusion.slot_of), custom_call_target="tpu_custom_call" | custom-call | tf_op jit(solution)/shard_map/unpack/pallas_call | solution.py:201
  196.3 2.7 %collective-permute-start.9 = (bf16[512,256]{1,0:T(8,128)(2,1)}, bf16[512,256]{1,0:T(8,128)(2,1)S(1)}, u32[]{:S(2)}, u32[]{:S(2)}) collective-permute-start(bf16[512,256]{1,0:T(8,128)(2,1)} %get-tuple-element.25.refs_1_), channel_id=1, source_target_pairs={{0,3},{1,0},{2,1},{3,2},{4,7},{5,4},{6,5},{7,6},{8,11},{9,8},{10,9... | collective-permute-start | bytes 786440 | tf_op jit(solution)/shard_map/ppermute | solution.py:25
  199.0 6.5 %collective-permute-done.13.refs_10_.refs_3_ = bf16[512,512]{1,0:T(8,128)(2,1)} collective-permute-done((bf16[512,512]{1,0:T(8,128)(2,1)}, bf16[512,512]{1,0:T(8,128)(2,1)}, u32[]{:S(2)}, u32[]{:S(2)}) %collective-permute-start.13) | collective-permute-done | bytes 524320 | tf_op jit(solution)/shard_map/ppermute | solution.py:25
  205.6 2.2 collective-permute-start.11
  207.8 2.0 collective-permute-done.15.refs_3_
  210.2 3.2 %collective-permute-start.10 = (bf16[512,256]{1,0:T(8,128)(2,1)S(1)}, bf16[512,256]{1,0:T(8,128)(2,1)S(1)}, u32[]{:S(2)}, u32[]{:S(2)}) collective-permute-start(bf16[512,256]{1,0:T(8,128)(2,1)S(1)} %collective-permute-done.9.refs_7_), channel_id=1, source_target_pairs={{0,3},{1,0},{2,1},{3,2},{4,7},{5,4},{6,5},{7,6},{8,11},{9,8},{10,9... | collective-permute-start | bytes 786440 | tf_op jit(solution)/shard_map/ppermute | solution.py:25
  213.4 2.0 collective-permute-done.6.refs_2_
  215.8 1.4 collective-permute-start.16
  217.2 4.2 %collective-permute-done.11.refs_6_ = bf16[512,256]{1,0:T(8,128)(2,1)S(1)} collective-permute-done((bf16[512,256]{1,0:T(8,128)(2,1)}, bf16[512,256]{1,0:T(8,128)(2,1)S(1)}, u32[]{:S(2)}, u32[]{:S(2)}) %collective-permute-start.11) | collective-permute-done | bytes 262176 | tf_op jit(solution)/shard_map/ppermute | solution.py:25
  221.4 3.2 %collective-permute-start.17 = (bf16[512,256]{1,0:T(8,128)(2,1)}, bf16[512,256]{1,0:T(8,128)(2,1)S(1)}, u32[]{:S(2)}, u32[]{:S(2)}) collective-permute-start(bf16[512,256]{1,0:T(8,128)(2,1)} %get-tuple-element.28.refs_1_), channel_id=1, source_target_pairs={{0,3},{1,0},{2,1},{3,2},{4,7},{5,4},{6,5},{7,6},{8,11},{9,8},{10,9... | collective-permute-start | bytes 786440 | tf_op jit(solution)/shard_map/ppermute | solution.py:25
  224.7 2.4 collective-permute-done.10.refs_5_
  227.1 3.2 %collective-permute-start.20 = (bf16[512,256]{1,0:T(8,128)(2,1)S(1)}, bf16[512,256]{1,0:T(8,128)(2,1)S(1)}, u32[]{:S(2)}, u32[]{:S(2)}) collective-permute-start(bf16[512,256]{1,0:T(8,128)(2,1)S(1)} %collective-permute-done.18.refs_6_), channel_id=1, source_target_pairs={{0,3},{1,0},{2,1},{3,2},{4,7},{5,4},{6,5},{7,6},{8,11},{9,8},{10,9... | collective-permute-start | bytes 786440 | tf_op jit(solution)/shard_map/ppermute | solution.py:25
  230.3 0.6 copy.6
  230.9 3.8 %products.3.refs_0_ = f32[1024,512]{1,0:T(8,128)} custom-call(bf16[512,256]{1,0:T(8,128)(2,1)} %get-tuple-element.24.refs_0_, bf16[512,256]{1,0:T(8,128)(2,1)} %get-tuple-element.25.refs_1_, bf16[512,256]{1,0:T(8,128)(2,1)S(1)} %collective-permute-done.6.refs_2_, bf16[512,256]{1,0:T(8,128)(2,1)S(1)} %collective-permute-done.7.refs_3_, ...), custom_call_target="tpu_custom_call" | custom-call | tf_op jit(solution)/shard_map/products/pallas_call | solution.py:237
  234.7 2.8 %products.4.refs_0_ = f32[1024,512]{1,0:T(8,128)S(1)} custom-call(f32[1024,512]{1,0:T(8,128)} %products.3.refs_0_, bf16[512,256]{1,0:T(8,128)(2,1)} %get-tuple-element.28.refs_1_, bf16[512,256]{1,0:T(8,128)(2,1)} %get-tuple-element.29.refs_2_, bf16[512,256]{1,0:T(8,128)(2,1)S(1)} %collective-permute-done.15.refs_3_, ...), custom_call_target="tpu_custom_call" | custom-call | tf_op jit(solution)/shard_map/products/pallas_call | solution.py:237
  237.6 0.4 collective-permute-done.19.refs_1_
  238.3 2.3 products.5
  (39 shorter events, 1.1 us)
Async XLA Ops:
  1.9 28.6 %collective-permute-start.1 = (bf16[512,512]{1,0:T(8,128)(2,1)S(1)}, bf16[512,512]{1,0:T(8,128)(2,1)S(1)}, u32[]{:S(2)}, u32[]{:S(2)}) collective-permute-start(bf16[512,512]{1,0:T(8,128)(2,1)S(1)} %get-tuple-element.38), channel_id=1, source_target_pairs={{0,3},{1,0},{2,1},{3,2},{4,7},{5,4},{6,5},{7,6},{8,11},{9,8},{10,9... | collective-permute-start | bytes 1572872 | tf_op jit(solution)/shard_map/ppermute | solution.py:25
  5.5 27.7 %collective-permute-start.2 = (bf16[512,512]{1,0:T(8,128)(2,1)S(1)}, bf16[512,512]{1,0:T(8,128)(2,1)S(1)}, u32[]{:S(2)}, u32[]{:S(2)}) collective-permute-start(bf16[512,512]{1,0:T(8,128)(2,1)S(1)} %get-tuple-element.38), channel_id=1, source_target_pairs={{0,1},{1,2},{2,3},{3,0},{4,5},{5,6},{6,7},{7,4},{8,9},{9,10},{10,1... | collective-permute-start | bytes 1572872 | tf_op jit(solution)/shard_map/ppermute | solution.py:25
  5.5 25.0 %collective-permute-start = (bf16[512,512]{1,0:T(8,128)(2,1)S(1)}, bf16[512,512]{1,0:T(8,128)(2,1)S(1)}, u32[]{:S(2)}, u32[]{:S(2)}) collective-permute-start(bf16[512,512]{1,0:T(8,128)(2,1)S(1)} %get-tuple-element.39), channel_id=1, source_target_pairs={{0,1},{1,2},{2,3},{3,0},{4,5},{5,6},{6,7},{7,4},{8,9},{9,10},{10,1... | collective-permute-start | bytes 1572872 | tf_op jit(solution)/shard_map/ppermute | solution.py:25
  5.6 27.6 %collective-permute-start.3 = (bf16[512,512]{1,0:T(8,128)(2,1)S(1)}, bf16[512,512]{1,0:T(8,128)(2,1)S(1)}, u32[]{:S(2)}, u32[]{:S(2)}) collective-permute-start(bf16[512,512]{1,0:T(8,128)(2,1)S(1)} %get-tuple-element.39), channel_id=1, source_target_pairs={{0,3},{1,0},{2,1},{3,2},{4,7},{5,4},{6,5},{7,6},{8,11},{9,8},{10,9... | collective-permute-start | bytes 1572872 | tf_op jit(solution)/shard_map/ppermute | solution.py:25
  8.9 3.2 %copy-start.6 = (s32[4,1024,1]{1,2,0:T(1,128)S(1)}, s32[4,1024,1]{1,2,0:T(1,128)}, u32[]{:S(2)}) copy-start(s32[4,1024,1]{1,2,0:T(1,128)} %param.7) | copy-start | bytes 49156
  30.5 12.9 %collective-permute-start.4 = (bf16[512,512]{1,0:T(8,128)(2,1)S(1)}, bf16[512,512]{1,0:T(8,128)(2,1)S(1)}, u32[]{:S(2)}, u32[]{:S(2)}) collective-permute-start(bf16[512,512]{1,0:T(8,128)(2,1)S(1)} %collective-permute-done.left_top), channel_id=1, source_target_pairs={{0,1},{1,2},{2,3},{3,0},{4,5},{5,6},{6,7},{7,4},{8,9},{9,10},{10,1... | collective-permute-start | bytes 1572872 | tf_op jit(solution)/shard_map/ppermute | solution.py:25
  30.5 12.9 %collective-permute-start.5 = (bf16[512,512]{1,0:T(8,128)(2,1)S(1)}, bf16[512,512]{1,0:T(8,128)(2,1)S(1)}, u32[]{:S(2)}, u32[]{:S(2)}) collective-permute-start(bf16[512,512]{1,0:T(8,128)(2,1)S(1)} %collective-permute-done.1.right_bottom), channel_id=1, source_target_pairs={{0,3},{1,0},{2,1},{3,2},{4,7},{5,4},{6,5},{7,6},{8,11},{9,8},{10,9... | collective-permute-start | bytes 1572872 | tf_op jit(solution)/shard_map/ppermute | solution.py:25
  53.2 0.8 copy-start
  54.0 0.8 copy-start.2
  54.8 50.3 %all-to-all-start.2 = ((bf16[32,2,8,8,384]{4,3,2,1,0:T(8,128)(2,1)}), bf16[32,2,8,8,384]{4,3,2,1,0:T(8,128)(2,1)S(1)}, u32[]{:S(2)}, u32[]{:S(2)}) async-start(bf16[32,2,8,8,384]{4,3,2,1,0:T(8,128)(2,1)} %pack.3), calls=%async_computation.2 | async-start | bytes 6291456 | tf_op jit(solution)/shard_map/all_to_all | solution.py:291
  65.4 1.0 copy-start.1
  66.4 1.0 copy-start.3
  105.1 45.0 %all-to-all-start = ((bf16[32,2,8,8,384]{4,3,2,1,0:T(8,128)(2,1)}), bf16[32,2,8,8,384]{4,3,2,1,0:T(8,128)(2,1)}, u32[]{:S(2)}, u32[]{:S(2)}) async-start(bf16[32,2,8,8,384]{4,3,2,1,0:T(8,128)(2,1)} %pack.2), calls=%async_computation | async-start | bytes 6291456 | tf_op jit(solution)/shard_map/all_to_all | solution.py:291
  150.1 21.3 %all-to-all-start.3 = ((bf16[32,2,8,8,128]{4,3,2,1,0:T(8,128)(2,1)}), bf16[32,2,8,8,128]{4,3,2,1,0:T(8,128)(2,1)S(1)}, u32[]{:S(2)}, u32[]{:S(2)}) async-start(bf16[32,2,8,8,128]{4,3,2,1,0:T(8,128)(2,1)} %get-tuple-element.27), calls=%async_computation.3 | async-start | bytes 2097152 | tf_op jit(solution)/shard_map/all_to_all | solution.py:297
  171.4 58.9 %copy-start.7 = (f32[8,2,128]{2,1,0:T(2,128)S(1)}, f32[8,2,128]{2,1,0:T(2,128)}, u32[]{:S(2)}) copy-start(f32[8,2,128]{2,1,0:T(2,128)} %get-tuple-element.31) | copy-start | bytes 24580
  171.4 58.9 %copy-start.8 = (f32[8,2,128]{2,1,0:T(2,128)S(1)}, f32[8,2,128]{2,1,0:T(2,128)}, u32[]{:S(2)}) copy-start(f32[8,2,128]{2,1,0:T(2,128)} %get-tuple-element.30) | copy-start | bytes 24580
  171.4 21.0 %all-to-all-start.1 = ((bf16[32,2,8,8,128]{4,3,2,1,0:T(8,128)(2,1)}), bf16[32,2,8,8,128]{4,3,2,1,0:T(8,128)(2,1)S(1)}, u32[]{:S(2)}, u32[]{:S(2)}) async-start(bf16[32,2,8,8,128]{4,3,2,1,0:T(8,128)(2,1)} %get-tuple-element.23), calls=%async_computation.1 | async-start | bytes 2097152 | tf_op jit(solution)/shard_map/all_to_all | solution.py:297
  178.3 20.7 %collective-permute-start.12 = (bf16[512,512]{1,0:T(8,128)(2,1)}, bf16[512,512]{1,0:T(8,128)(2,1)S(1)}, u32[]{:S(2)}, u32[]{:S(2)}) collective-permute-start(bf16[512,512]{1,0:T(8,128)(2,1)} %get-tuple-element.36), channel_id=1, source_target_pairs={{0,1},{1,2},{2,3},{3,0},{4,5},{5,6},{6,7},{7,4},{8,9},{9,10},{10,1... | collective-permute-start | bytes 1572872 | tf_op jit(solution)/shard_map/ppermute | solution.py:25
  178.3 27.2 %collective-permute-start.13 = (bf16[512,512]{1,0:T(8,128)(2,1)}, bf16[512,512]{1,0:T(8,128)(2,1)}, u32[]{:S(2)}, u32[]{:S(2)}) collective-permute-start(bf16[512,512]{1,0:T(8,128)(2,1)} %get-tuple-element.35), channel_id=1, source_target_pairs={{0,2},{1,3},{2,0},{3,1},{4,6},{5,7},{6,4},{7,5},{8,10},{9,11},{10,... | collective-permute-start | bytes 1572872 | tf_op jit(solution)/shard_map/ppermute | solution.py:25
  182.2 23.4 %collective-permute-start.14 = (bf16[512,512]{1,0:T(8,128)(2,1)}, bf16[512,512]{1,0:T(8,128)(2,1)S(1)}, u32[]{:S(2)}, u32[]{:S(2)}) collective-permute-start(bf16[512,512]{1,0:T(8,128)(2,1)} %get-tuple-element.34), channel_id=1, source_target_pairs={{0,3},{1,0},{2,1},{3,2},{4,7},{5,4},{6,5},{7,6},{8,11},{9,8},{10,9... | collective-permute-start | bytes 1572872 | tf_op jit(solution)/shard_map/ppermute | solution.py:25
  186.2 23.6 %collective-permute-start.15 = (bf16[512,256]{1,0:T(8,128)(2,1)}, bf16[512,256]{1,0:T(8,128)(2,1)S(1)}, u32[]{:S(2)}, u32[]{:S(2)}) collective-permute-start(bf16[512,256]{1,0:T(8,128)(2,1)} %get-tuple-element.28.refs_1_), channel_id=1, source_target_pairs={{0,1},{1,2},{2,3},{3,0},{4,5},{5,6},{6,7},{7,4},{8,9},{9,10},{10,1... | collective-permute-start | bytes 786440 | tf_op jit(solution)/shard_map/ppermute | solution.py:25
  196.3 13.9 %collective-permute-start.9 = (bf16[512,256]{1,0:T(8,128)(2,1)}, bf16[512,256]{1,0:T(8,128)(2,1)S(1)}, u32[]{:S(2)}, u32[]{:S(2)}) collective-permute-start(bf16[512,256]{1,0:T(8,128)(2,1)} %get-tuple-element.25.refs_1_), channel_id=1, source_target_pairs={{0,3},{1,0},{2,1},{3,2},{4,7},{5,4},{6,5},{7,6},{8,11},{9,8},{10,9... | collective-permute-start | bytes 786440 | tf_op jit(solution)/shard_map/ppermute | solution.py:25
  199.0 31.9 %copy-start.4 = (bf16[512,512]{1,0:T(8,128)(2,1)}, bf16[512,512]{1,0:T(8,128)(2,1)S(1)}, u32[]{:S(2)}) copy-start(bf16[512,512]{1,0:T(8,128)(2,1)S(1)} %collective-permute-done.12.refs_9_.refs_8_) | copy-start | bytes 1572868
  199.0 16.5 %collective-permute-start.6 = (bf16[512,256]{1,0:T(8,128)(2,1)}, bf16[512,256]{1,0:T(8,128)(2,1)S(1)}, u32[]{:S(2)}, u32[]{:S(2)}) collective-permute-start(bf16[512,256]{1,0:T(8,128)(2,1)} %get-tuple-element.24.refs_0_), channel_id=1, source_target_pairs={{0,1},{1,2},{2,3},{3,0},{4,5},{5,6},{6,7},{7,4},{8,9},{9,10},{10,1... | collective-permute-start | bytes 786440 | tf_op jit(solution)/shard_map/ppermute | solution.py:25
  205.6 10.3 %collective-permute-start.18 = (bf16[512,256]{1,0:T(8,128)(2,1)}, bf16[512,256]{1,0:T(8,128)(2,1)S(1)}, u32[]{:S(2)}, u32[]{:S(2)}) collective-permute-start(bf16[512,256]{1,0:T(8,128)(2,1)} %get-tuple-element.29.refs_2_), channel_id=1, source_target_pairs={{0,3},{1,0},{2,1},{3,2},{4,7},{5,4},{6,5},{7,6},{8,11},{9,8},{10,9... | collective-permute-start | bytes 786440 | tf_op jit(solution)/shard_map/ppermute | solution.py:25
  205.6 25.4 %copy-start.5 = (bf16[512,512]{1,0:T(8,128)(2,1)}, bf16[512,512]{1,0:T(8,128)(2,1)S(1)}, u32[]{:S(2)}) copy-start(bf16[512,512]{1,0:T(8,128)(2,1)S(1)} %collective-permute-done.14.refs_11_.refs_9_) | copy-start | bytes 1572868
  205.6 15.9 %collective-permute-start.11 = (bf16[512,256]{1,0:T(8,128)(2,1)}, bf16[512,256]{1,0:T(8,128)(2,1)S(1)}, u32[]{:S(2)}, u32[]{:S(2)}) collective-permute-start(bf16[512,256]{1,0:T(8,128)(2,1)} %get-tuple-element.24.refs_0_), channel_id=1, source_target_pairs={{0,3},{1,0},{2,1},{3,2},{4,7},{5,4},{6,5},{7,6},{8,11},{9,8},{10,9... | collective-permute-start | bytes 786440 | tf_op jit(solution)/shard_map/ppermute | solution.py:25
  209.9 14.8 %collective-permute-start.7 = (bf16[512,256]{1,0:T(8,128)(2,1)}, bf16[512,256]{1,0:T(8,128)(2,1)S(1)}, u32[]{:S(2)}, u32[]{:S(2)}) collective-permute-start(bf16[512,256]{1,0:T(8,128)(2,1)} %get-tuple-element.25.refs_1_), channel_id=1, source_target_pairs={{0,1},{1,2},{2,3},{3,0},{4,5},{5,6},{6,7},{7,4},{8,9},{9,10},{10,1... | collective-permute-start | bytes 786440 | tf_op jit(solution)/shard_map/ppermute | solution.py:25
  210.2 16.9 %collective-permute-start.10 = (bf16[512,256]{1,0:T(8,128)(2,1)S(1)}, bf16[512,256]{1,0:T(8,128)(2,1)S(1)}, u32[]{:S(2)}, u32[]{:S(2)}) collective-permute-start(bf16[512,256]{1,0:T(8,128)(2,1)S(1)} %collective-permute-done.9.refs_7_), channel_id=1, source_target_pairs={{0,3},{1,0},{2,1},{3,2},{4,7},{5,4},{6,5},{7,6},{8,11},{9,8},{10,9... | collective-permute-start | bytes 786440 | tf_op jit(solution)/shard_map/ppermute | solution.py:25
  215.5 15.4 %collective-permute-start.8 = (bf16[512,256]{1,0:T(8,128)(2,1)S(1)}, bf16[512,256]{1,0:T(8,128)(2,1)S(1)}, u32[]{:S(2)}, u32[]{:S(2)}) collective-permute-start(bf16[512,256]{1,0:T(8,128)(2,1)S(1)} %collective-permute-done.6.refs_2_), channel_id=1, source_target_pairs={{0,1},{1,2},{2,3},{3,0},{4,5},{5,6},{6,7},{7,4},{8,9},{9,10},{10,1... | collective-permute-start | bytes 786440 | tf_op jit(solution)/shard_map/ppermute | solution.py:25
  215.8 18.9 %collective-permute-start.16 = (bf16[512,256]{1,0:T(8,128)(2,1)}, bf16[512,256]{1,0:T(8,128)(2,1)S(1)}, u32[]{:S(2)}, u32[]{:S(2)}) collective-permute-start(bf16[512,256]{1,0:T(8,128)(2,1)} %get-tuple-element.29.refs_2_), channel_id=1, source_target_pairs={{0,1},{1,2},{2,3},{3,0},{4,5},{5,6},{6,7},{7,4},{8,9},{9,10},{10,1... | collective-permute-start | bytes 786440 | tf_op jit(solution)/shard_map/ppermute | solution.py:25
  221.4 13.3 %collective-permute-start.17 = (bf16[512,256]{1,0:T(8,128)(2,1)}, bf16[512,256]{1,0:T(8,128)(2,1)S(1)}, u32[]{:S(2)}, u32[]{:S(2)}) collective-permute-start(bf16[512,256]{1,0:T(8,128)(2,1)} %get-tuple-element.28.refs_1_), channel_id=1, source_target_pairs={{0,3},{1,0},{2,1},{3,2},{4,7},{5,4},{6,5},{7,6},{8,11},{9,8},{10,9... | collective-permute-start | bytes 786440 | tf_op jit(solution)/shard_map/ppermute | solution.py:25
  224.7 13.3 %collective-permute-start.19 = (bf16[512,256]{1,0:T(8,128)(2,1)S(1)}, bf16[512,256]{1,0:T(8,128)(2,1)S(1)}, u32[]{:S(2)}, u32[]{:S(2)}) collective-permute-start(bf16[512,256]{1,0:T(8,128)(2,1)S(1)} %collective-permute-done.15.refs_3_), channel_id=1, source_target_pairs={{0,1},{1,2},{2,3},{3,0},{4,5},{5,6},{6,7},{7,4},{8,9},{9,10},{10,1... | collective-permute-start | bytes 786440 | tf_op jit(solution)/shard_map/ppermute | solution.py:25
  227.1 11.2 %collective-permute-start.20 = (bf16[512,256]{1,0:T(8,128)(2,1)S(1)}, bf16[512,256]{1,0:T(8,128)(2,1)S(1)}, u32[]{:S(2)}, u32[]{:S(2)}) collective-permute-start(bf16[512,256]{1,0:T(8,128)(2,1)S(1)} %collective-permute-done.18.refs_6_), channel_id=1, source_target_pairs={{0,3},{1,0},{2,1},{3,2},{4,7},{5,4},{6,5},{7,6},{8,11},{9,8},{10,9... | collective-permute-start | bytes 786440 | tf_op jit(solution)/shard_map/ppermute | solution.py:25

commit v9 on v8

--- a/solution.py
+++ b/solution.py
@@ -185,14 +185,16 @@
 
 
 def unpack_kernel(returned, slot_of, top, bottom):
-    half, width = top.shape
-    source = returned[:, pl.program_id(0)].reshape(-1, width)
-    slots = source.shape[0]
+    half = top.shape[0]
+    heads, width = returned.shape[1], returned.shape[-1]
+    slots = returned.shape[0] * returned.shape[2] * returned.shape[3]
     iota = lax.broadcasted_iota(jnp.int32, (slots, half), 0)
-    for k, out in enumerate((top, bottom)):
-        onehot = jnp.where(iota == slot_of[0, :, k * half : (k + 1) * half], 1.0, 0.0).astype(BF16)
-        rows = lax.dot_general(onehot, source, (((0,), (0,)), ((), ())), preferred_element_type=F32)
-        out[...] = rows.astype(BF16)
+    for head in range(heads):
+        source = returned[:, head].reshape(slots, width)
+        for k, out in enumerate((top, bottom)):
+            onehot = jnp.where(iota == slot_of[head, :, k * half : (k + 1) * half], 1.0, 0.0).astype(BF16)
+            rows = lax.dot_general(onehot, source, (((0,), (0,)), ((), ())), preferred_element_type=F32)
+            out[:, head * width : (head + 1) * width] = rows.astype(BF16)
 
 
 def unpack(returned, slot_rows, group):
@@ -201,9 +203,9 @@
     return pl.pallas_call(
         unpack_kernel,
         out_shape=(jax.ShapeDtypeStruct((rows // 2, heads * width), BF16),) * 2,
-        grid=(heads,),
-        in_specs=[VMEM_WHOLE, pl.BlockSpec((1, 1, rows), lambda h: (group * heads + h, 0, 0))],
-        out_specs=(pl.BlockSpec((rows // 2, width), lambda h: (0, h)),) * 2,
+        grid=(1,),
+        in_specs=[VMEM_WHOLE, pl.BlockSpec((heads, 1, rows), lambda i: (group, 0, 0))],
+        out_specs=(pl.BlockSpec((rows // 2, heads * width), lambda i: (0, 0)),) * 2,
         compiler_params=params(),
         name="unpack",
     )(in_vmem(returned), slot_rows)

time: 242 us -> 242 us (level)
  no operation moved by 1% of the time
where the time goes in v9:
time: 242 us; the launch traced here: 241 us
  waiting for transfers between devices  114 us (47%)
  Pallas kernels  58.6 us (24%)
  starting transfers between devices  54.4 us (22%)
  local copies, waits for them, and re-layouts  9.18 us (4%)
  matrix products  2.48 us (1%)
    all_to_all x2, waiting for transfers between devices, local(): received.append(lax.all_to_all(packed, SEQ, 0, 0, tiled=True))  62 us
    ppermute x21, waiting for transfers between devices, shifted(): lax.ppermute(array, 'head', [(i, (i + by) % count) for i in range(count)])  37.1 us
    ppermute x21, starting transfers between devices, shifted(): lax.ppermute(array, 'head', [(i, (i + by) % count) for i in range(count)])  30.3 us
    pallas_call x2, Pallas kernels, pack(): pl.pallas_call(pack_kernel, out_shape=jax.ShapeDtypeStruct((devices, head...  19.5 us
    all_to_all x2, starting transfers between devices, local(): received.append(lax.all_to_all(packed, SEQ, 0, 0, tiled=True))  15.7 us
    all_to_all x2, waiting for transfers between devices, local(): returned = lax.all_to_all(buckets, SEQ, 0, 0, tiled=True)  14.8 us
    pallas_call x2, Pallas kernels, attend(): pl.pallas_call(functools.partial(attend_kernel, streamed), out_shape=(jax...  12.7 us
    pallas_call x1, Pallas kernels, first_blocks(): pl.pallas_call(first_blocks_kernel, out_shape=jax.ShapeDtypeStruct((kinds...  9.63 us
  transfers between devices with their start and end apart: 25, of which 15 were waited for; matrix products, arithmetic and copies ran while one was open for 3% of the time, Pallas kernels for 19%

profile of v9, /device:TPU:1, one launch (start us, length us, event | category | flops | bytes accessed | tf_op | source)
XLA Modules:
  0.0 240.6 jit_solution(14819108931776659712)
XLA Ops:
  0.6 1.3 fusion.7
  1.9 3.6 %collective-permute-start.1 = (bf16[512,512]{1,0:T(8,128)(2,1)S(1)}, bf16[512,512]{1,0:T(8,128)(2,1)S(1)}, u32[]{:S(2)}, u32[]{:S(2)}) collective-permute-start(bf16[512,512]{1,0:T(8,128)(2,1)S(1)} %get-tuple-element.38), channel_id=1, source_target_pairs={{0,3},{1,0},{2,1},{3,2},{4,7},{5,4},{6,5},{7,6},{8,11},{9,8},{10,9... | collective-permute-start | bytes 1572872 | tf_op jit(solution)/shard_map/ppermute | solution.py:25
  5.6 2.7 %collective-permute-start.3 = (bf16[512,512]{1,0:T(8,128)(2,1)S(1)}, bf16[512,512]{1,0:T(8,128)(2,1)S(1)}, u32[]{:S(2)}, u32[]{:S(2)}) collective-permute-start(bf16[512,512]{1,0:T(8,128)(2,1)S(1)} %get-tuple-element.39), channel_id=1, source_target_pairs={{0,3},{1,0},{2,1},{3,2},{4,7},{5,4},{6,5},{7,6},{8,11},{9,8},{10,9... | collective-permute-start | bytes 1572872 | tf_op jit(solution)/shard_map/ppermute | solution.py:25
  8.2 0.7 copy.9
  8.9 2.5 %fusion = f32[4,1024]{1,0:T(4,128)S(1)} fusion(s32[4,1024]{1,0:T(4,128)S(1)} %bitcast.26), kind=kOutput, calls=%fused_computation.1 | convolution fusion | flops 2152722432 | bytes 32768 | tf_op jit(solution)/shard_map/ts,hsc->htc/dot_general | solution.py:266
  11.5 0.6 pad_add_fusion.where
  12.1 0.6 bitcast_add_fusion.slot_of
  12.7 17.8 %collective-permute-done.left_top = bf16[512,512]{1,0:T(8,128)(2,1)S(1)} collective-permute-done((bf16[512,512]{1,0:T(8,128)(2,1)S(1)}, bf16[512,512]{1,0:T(8,128)(2,1)S(1)}, u32[]{:S(2)}, u32[]{:S(2)}) %collective-permute-start) | collective-permute-done | bytes 524320 | tf_op jit(solution)/shard_map/ppermute | solution.py:25
  30.5 2.7 %collective-permute-start.5 = (bf16[512,512]{1,0:T(8,128)(2,1)S(1)}, bf16[512,512]{1,0:T(8,128)(2,1)S(1)}, u32[]{:S(2)}, u32[]{:S(2)}) collective-permute-start(bf16[512,512]{1,0:T(8,128)(2,1)S(1)} %collective-permute-done.1.right_bottom), channel_id=1, source_target_pairs={{0,3},{1,0},{2,1},{3,2},{4,7},{5,4},{6,5},{7,6},{8,11},{9,8},{10,9... | collective-permute-start | bytes 1572872 | tf_op jit(solution)/shard_map/ppermute | solution.py:25
  33.2 9.6 %first_blocks.1.part = f32[3,1024,512]{2,1,0:T(8,128)} custom-call(s32[4]{0:T(128)} %pad_add_fusion.where, bf16[1024,512]{1,0:T(8,128)(2,1)} %own.1, bf16[512,512]{1,0:T(8,128)(2,1)S(1)} %collective-permute-done.left_top, bf16[512,512]{1,0:T(8,128)(2,1)S(1)} %collective-permute-done.2.left_bottom, bf16[512,512]{1,0:T(8,128)(2,1)S(1)} %collective-permute-done.3.right_top, ...), custom_call_target="tpu_custom_call" | custom-call | tf_op jit(solution)/shard_map/first_blocks/pallas_call | solution.py:55
  42.8 0.6 collective-permute-done.4.far_top
  43.4 9.8 %pack.3 = bf16[32,2,8,8,384]{4,3,2,1,0:T(8,128)(2,1)} custom-call(s32[4]{0:T(128)} %pad_add_fusion.where, f32[3,1024,512]{2,1,0:T(8,128)} %first_blocks.1.part, bf16[512,512]{1,0:T(8,128)(2,1)S(1)} %collective-permute-done.4.far_top, bf16[512,512]{1,0:T(8,128)(2,1)S(1)} %collective-permute-done.5.far_bottom, bf16[3,2048,512]{2,1,0:T(8,128)(2,1)} %bitcast.24, ...), custom_call_target="tpu_custom_call" | custom-call | tf_op jit(solution)/shard_map/pack/pallas_call | solution.py:116
  53.2 0.8 copy-done
  54.0 0.8 copy-done.2
  54.8 10.6 %all-to-all-start.2 = ((bf16[32,2,8,8,384]{4,3,2,1,0:T(8,128)(2,1)}), bf16[32,2,8,8,384]{4,3,2,1,0:T(8,128)(2,1)S(1)}, u32[]{:S(2)}, u32[]{:S(2)}) async-start(bf16[32,2,8,8,384]{4,3,2,1,0:T(8,128)(2,1)} %pack.3), calls=%async_computation.2 | async-start | bytes 6291456 | tf_op jit(solution)/shard_map/all_to_all | solution.py:293
  65.4 1.0 copy-done.1
  66.4 1.0 copy-done.3
  67.4 9.7 %pack.2 = bf16[32,2,8,8,384]{4,3,2,1,0:T(8,128)(2,1)} custom-call(s32[4]{0:T(128)} %pad_add_fusion.where, f32[3,1024,512]{2,1,0:T(8,128)} %first_blocks.1.part, bf16[512,512]{1,0:T(8,128)(2,1)S(1)} %copy-done.1, bf16[512,512]{1,0:T(8,128)(2,1)S(1)} %copy-done.3, bf16[3,2048,512]{2,1,0:T(8,128)(2,1)} %bitcast.25, s32[4,1,1024]{2,1,0:T(1,128)} %bitcast_add_fusion.slot_of), custom_call_target="tpu_custom_call" | custom-call | tf_op jit(solution)/shard_map/pack/pallas_call | solution.py:116
  77.2 27.9 %all-to-all-done.2.received = bf16[32,2,8,8,384]{4,3,2,1,0:T(8,128)(2,1)S(1)} async-done(((bf16[32,2,8,8,384]{4,3,2,1,0:T(8,128)(2,1)}), bf16[32,2,8,8,384]{4,3,2,1,0:T(8,128)(2,1)S(1)}, u32[]{:S(2)}, u32[]{:S(2)}) %all-to-all-start.2) | async-done | bytes 3145760 | tf_op jit(solution)/shard_map/all_to_all | solution.py:293
  105.1 5.1 %all-to-all-start = ((bf16[32,2,8,8,384]{4,3,2,1,0:T(8,128)(2,1)}), bf16[32,2,8,8,384]{4,3,2,1,0:T(8,128)(2,1)}, u32[]{:S(2)}, u32[]{:S(2)}) async-start(bf16[32,2,8,8,384]{4,3,2,1,0:T(8,128)(2,1)} %pack.2), calls=%async_computation | async-start | bytes 6291456 | tf_op jit(solution)/shard_map/all_to_all | solution.py:293
  110.2 5.8 %attend.3 = (bf16[32,2,8,8,128]{4,3,2,1,0:T(8,128)(2,1)}, f32[8,2,128]{2,1,0:T(2,128)}) custom-call(bf16[32,2,8,8,384]{4,3,2,1,0:T(8,128)(2,1)S(1)} %all-to-all-done.2.received), custom_call_target="tpu_custom_call" | custom-call | tf_op jit(solution)/shard_map/attend/pallas_call | solution.py:170
  116.0 34.1 %all-to-all-done.received = bf16[32,2,8,8,384]{4,3,2,1,0:T(8,128)(2,1)} async-done(((bf16[32,2,8,8,384]{4,3,2,1,0:T(8,128)(2,1)}), bf16[32,2,8,8,384]{4,3,2,1,0:T(8,128)(2,1)}, u32[]{:S(2)}, u32[]{:S(2)}) %all-to-all-start) | async-done | bytes 3145760 | tf_op jit(solution)/shard_map/all_to_all | solution.py:293
  150.1 4.3 %all-to-all-start.3 = ((bf16[32,2,8,8,128]{4,3,2,1,0:T(8,128)(2,1)}), bf16[32,2,8,8,128]{4,3,2,1,0:T(8,128)(2,1)S(1)}, u32[]{:S(2)}, u32[]{:S(2)}) async-start(bf16[32,2,8,8,128]{4,3,2,1,0:T(8,128)(2,1)} %get-tuple-element.27), calls=%async_computation.3 | async-start | bytes 2097152 | tf_op jit(solution)/shard_map/all_to_all | solution.py:299
  154.4 6.9 %attend.2 = (bf16[32,2,8,8,128]{4,3,2,1,0:T(8,128)(2,1)}, f32[8,2,128]{2,1,0:T(2,128)}) custom-call(bf16[32,2,8,8,384]{4,3,2,1,0:T(8,128)(2,1)} %all-to-all-done.received), custom_call_target="tpu_custom_call" | custom-call | tf_op jit(solution)/shard_map/attend/pallas_call | solution.py:170
  161.3 10.0 %all-to-all-done.3.returned = bf16[32,2,8,8,128]{4,3,2,1,0:T(8,128)(2,1)S(1)} async-done(((bf16[32,2,8,8,128]{4,3,2,1,0:T(8,128)(2,1)}), bf16[32,2,8,8,128]{4,3,2,1,0:T(8,128)(2,1)S(1)}, u32[]{:S(2)}, u32[]{:S(2)}) %all-to-all-start.3) | async-done | bytes 1048608 | tf_op jit(solution)/shard_map/all_to_all | solution.py:299
  171.4 4.0 %all-to-all-start.1 = ((bf16[32,2,8,8,128]{4,3,2,1,0:T(8,128)(2,1)}), bf16[32,2,8,8,128]{4,3,2,1,0:T(8,128)(2,1)S(1)}, u32[]{:S(2)}, u32[]{:S(2)}) async-start(bf16[32,2,8,8,128]{4,3,2,1,0:T(8,128)(2,1)} %get-tuple-element.23), calls=%async_computation.1 | async-start | bytes 2097152 | tf_op jit(solution)/shard_map/all_to_all | solution.py:299
  175.4 2.9 %constant_dynamic-slice_fusion = (bf16[512,512]{1,0:T(8,128)(2,1)}, bf16[512,512]{1,0:T(8,128)(2,1)}, bf16[512,512]{1,0:T(8,128)(2,1)}, bf16[512,512]{1,0:T(8,128)(2,1)}) fusion(bf16[512,2048]{1,0:T(8,128)(2,1)} %param.6, s32[]{:T(128)S(6)} %select_n.52, s32[]{:T(128)S(6)} %select_n.50, s32[]{:T(128)S(6)} %select_n.49, s32[]{:T(128)S(6)} %select_n.48), kind=kLoop, calls=%fused_computation.10 | loop fusion | bytes 4194320 | tf_op jit(solution)/shard_map/dynamic_slice | solution.py:285
  178.3 3.8 %collective-permute-start.13 = (bf16[512,512]{1,0:T(8,128)(2,1)}, bf16[512,512]{1,0:T(8,128)(2,1)}, u32[]{:S(2)}, u32[]{:S(2)}) collective-permute-start(bf16[512,512]{1,0:T(8,128)(2,1)} %get-tuple-element.35), channel_id=1, source_target_pairs={{0,2},{1,3},{2,0},{3,1},{4,6},{5,7},{6,4},{7,5},{8,10},{9,11},{10,... | collective-permute-start | bytes 1572872 | tf_op jit(solution)/shard_map/ppermute | solution.py:25
  182.2 3.9 %unpack.3 = (bf16[512,256]{1,0:T(8,128)(2,1)}, bf16[512,256]{1,0:T(8,128)(2,1)}) custom-call(bf16[32,2,8,8,128]{4,3,2,1,0:T(8,128)(2,1)S(1)} %all-to-all-done.3.returned, s32[4,1,1024]{2,1,0:T(1,128)} %bitcast_add_fusion.slot_of), custom_call_target="tpu_custom_call" | custom-call | tf_op jit(solution)/shard_map/unpack/pallas_call | solution.py:203
  186.1 1.5 collective-permute-start.15
  187.5 4.8 %all-to-all-done.1.returned = bf16[32,2,8,8,128]{4,3,2,1,0:T(8,128)(2,1)S(1)} async-done(((bf16[32,2,8,8,128]{4,3,2,1,0:T(8,128)(2,1)}), bf16[32,2,8,8,128]{4,3,2,1,0:T(8,128)(2,1)S(1)}, u32[]{:S(2)}, u32[]{:S(2)}) %all-to-all-start.1) | async-done | bytes 1048608 | tf_op jit(solution)/shard_map/all_to_all | solution.py:299
  192.3 3.9 %unpack.2 = (bf16[512,256]{1,0:T(8,128)(2,1)}, bf16[512,256]{1,0:T(8,128)(2,1)}) custom-call(bf16[32,2,8,8,128]{4,3,2,1,0:T(8,128)(2,1)S(1)} %all-to-all-done.1.returned, s32[4,1,1024]{2,1,0:T(1,128)} %bitcast_add_fusion.slot_of), custom_call_target="tpu_custom_call" | custom-call | tf_op jit(solution)/shard_map/unpack/pallas_call | solution.py:203
  196.2 2.7 %collective-permute-start.9 = (bf16[512,256]{1,0:T(8,128)(2,1)}, bf16[512,256]{1,0:T(8,128)(2,1)S(1)}, u32[]{:S(2)}, u32[]{:S(2)}) collective-permute-start(bf16[512,256]{1,0:T(8,128)(2,1)} %get-tuple-element.25.refs_1_), channel_id=1, source_target_pairs={{0,3},{1,0},{2,1},{3,2},{4,7},{5,4},{6,5},{7,6},{8,11},{9,8},{10,9... | collective-permute-start | bytes 786440 | tf_op jit(solution)/shard_map/ppermute | solution.py:25
  198.9 6.7 %collective-permute-done.13.refs_10_.refs_3_ = bf16[512,512]{1,0:T(8,128)(2,1)} collective-permute-done((bf16[512,512]{1,0:T(8,128)(2,1)}, bf16[512,512]{1,0:T(8,128)(2,1)}, u32[]{:S(2)}, u32[]{:S(2)}) %collective-permute-start.13) | collective-permute-done | bytes 524320 | tf_op jit(solution)/shard_map/ppermute | solution.py:25
  205.6 2.2 collective-permute-start.11
  207.8 2.0 collective-permute-done.15.refs_3_
  210.2 3.2 %collective-permute-start.10 = (bf16[512,256]{1,0:T(8,128)(2,1)S(1)}, bf16[512,256]{1,0:T(8,128)(2,1)S(1)}, u32[]{:S(2)}, u32[]{:S(2)}) collective-permute-start(bf16[512,256]{1,0:T(8,128)(2,1)S(1)} %collective-permute-done.9.refs_7_), channel_id=1, source_target_pairs={{0,3},{1,0},{2,1},{3,2},{4,7},{5,4},{6,5},{7,6},{8,11},{9,8},{10,9... | collective-permute-start | bytes 786440 | tf_op jit(solution)/shard_map/ppermute | solution.py:25
  213.4 2.0 collective-permute-done.6.refs_2_
  215.8 1.4 collective-permute-start.16
  217.2 4.2 %collective-permute-done.11.refs_6_ = bf16[512,256]{1,0:T(8,128)(2,1)S(1)} collective-permute-done((bf16[512,256]{1,0:T(8,128)(2,1)}, bf16[512,256]{1,0:T(8,128)(2,1)S(1)}, u32[]{:S(2)}, u32[]{:S(2)}) %collective-permute-start.11) | collective-permute-done | bytes 262176 | tf_op jit(solution)/shard_map/ppermute | solution.py:25
  221.4 3.2 %collective-permute-start.17 = (bf16[512,256]{1,0:T(8,128)(2,1)}, bf16[512,256]{1,0:T(8,128)(2,1)S(1)}, u32[]{:S(2)}, u32[]{:S(2)}) collective-permute-start(bf16[512,256]{1,0:T(8,128)(2,1)} %get-tuple-element.28.refs_1_), channel_id=1, source_target_pairs={{0,3},{1,0},{2,1},{3,2},{4,7},{5,4},{6,5},{7,6},{8,11},{9,8},{10,9... | collective-permute-start | bytes 786440 | tf_op jit(solution)/shard_map/ppermute | solution.py:25
  224.7 2.4 collective-permute-done.10.refs_5_
  227.1 3.2 %collective-permute-start.20 = (bf16[512,256]{1,0:T(8,128)(2,1)S(1)}, bf16[512,256]{1,0:T(8,128)(2,1)S(1)}, u32[]{:S(2)}, u32[]{:S(2)}) collective-permute-start(bf16[512,256]{1,0:T(8,128)(2,1)S(1)} %collective-permute-done.18.refs_6_), channel_id=1, source_target_pairs={{0,3},{1,0},{2,1},{3,2},{4,7},{5,4},{6,5},{7,6},{8,11},{9,8},{10,9... | collective-permute-start | bytes 786440 | tf_op jit(solution)/shard_map/ppermute | solution.py:25
  230.3 0.6 copy.6
  230.9 3.8 %products.3.refs_0_ = f32[1024,512]{1,0:T(8,128)} custom-call(bf16[512,256]{1,0:T(8,128)(2,1)} %get-tuple-element.24.refs_0_, bf16[512,256]{1,0:T(8,128)(2,1)} %get-tuple-element.25.refs_1_, bf16[512,256]{1,0:T(8,128)(2,1)S(1)} %collective-permute-done.6.refs_2_, bf16[512,256]{1,0:T(8,128)(2,1)S(1)} %collective-permute-done.7.refs_3_, ...), custom_call_target="tpu_custom_call" | custom-call | tf_op jit(solution)/shard_map/products/pallas_call | solution.py:239
  234.7 2.8 %products.4.refs_0_ = f32[1024,512]{1,0:T(8,128)S(1)} custom-call(f32[1024,512]{1,0:T(8,128)} %products.3.refs_0_, bf16[512,256]{1,0:T(8,128)(2,1)} %get-tuple-element.28.refs_1_, bf16[512,256]{1,0:T(8,128)(2,1)} %get-tuple-element.29.refs_2_, bf16[512,256]{1,0:T(8,128)(2,1)S(1)} %collective-permute-done.15.refs_3_, ...), custom_call_target="tpu_custom_call" | custom-call | tf_op jit(solution)/shard_map/products/pallas_call | solution.py:239
  237.6 0.4 collective-permute-done.19.refs_1_
  238.3 2.3 products.5
  (39 shorter events, 1.1 us)
Async XLA Ops:
  1.9 28.6 %collective-permute-start.1 = (bf16[512,512]{1,0:T(8,128)(2,1)S(1)}, bf16[512,512]{1,0:T(8,128)(2,1)S(1)}, u32[]{:S(2)}, u32[]{:S(2)}) collective-permute-start(bf16[512,512]{1,0:T(8,128)(2,1)S(1)} %get-tuple-element.38), channel_id=1, source_target_pairs={{0,3},{1,0},{2,1},{3,2},{4,7},{5,4},{6,5},{7,6},{8,11},{9,8},{10,9... | collective-permute-start | bytes 1572872 | tf_op jit(solution)/shard_map/ppermute | solution.py:25
  5.5 27.7 %collective-permute-start.2 = (bf16[512,512]{1,0:T(8,128)(2,1)S(1)}, bf16[512,512]{1,0:T(8,128)(2,1)S(1)}, u32[]{:S(2)}, u32[]{:S(2)}) collective-permute-start(bf16[512,512]{1,0:T(8,128)(2,1)S(1)} %get-tuple-element.38), channel_id=1, source_target_pairs={{0,1},{1,2},{2,3},{3,0},{4,5},{5,6},{6,7},{7,4},{8,9},{9,10},{10,1... | collective-permute-start | bytes 1572872 | tf_op jit(solution)/shard_map/ppermute | solution.py:25
  5.5 25.0 %collective-permute-start = (bf16[512,512]{1,0:T(8,128)(2,1)S(1)}, bf16[512,512]{1,0:T(8,128)(2,1)S(1)}, u32[]{:S(2)}, u32[]{:S(2)}) collective-permute-start(bf16[512,512]{1,0:T(8,128)(2,1)S(1)} %get-tuple-element.39), channel_id=1, source_target_pairs={{0,1},{1,2},{2,3},{3,0},{4,5},{5,6},{6,7},{7,4},{8,9},{9,10},{10,1... | collective-permute-start | bytes 1572872 | tf_op jit(solution)/shard_map/ppermute | solution.py:25
  5.6 27.6 %collective-permute-start.3 = (bf16[512,512]{1,0:T(8,128)(2,1)S(1)}, bf16[512,512]{1,0:T(8,128)(2,1)S(1)}, u32[]{:S(2)}, u32[]{:S(2)}) collective-permute-start(bf16[512,512]{1,0:T(8,128)(2,1)S(1)} %get-tuple-element.39), channel_id=1, source_target_pairs={{0,3},{1,0},{2,1},{3,2},{4,7},{5,4},{6,5},{7,6},{8,11},{9,8},{10,9... | collective-permute-start | bytes 1572872 | tf_op jit(solution)/shard_map/ppermute | solution.py:25
  8.9 3.2 %copy-start.6 = (s32[4,1024,1]{1,2,0:T(1,128)S(1)}, s32[4,1024,1]{1,2,0:T(1,128)}, u32[]{:S(2)}) copy-start(s32[4,1024,1]{1,2,0:T(1,128)} %param.7) | copy-start | bytes 49156
  30.5 12.9 %collective-permute-start.4 = (bf16[512,512]{1,0:T(8,128)(2,1)S(1)}, bf16[512,512]{1,0:T(8,128)(2,1)S(1)}, u32[]{:S(2)}, u32[]{:S(2)}) collective-permute-start(bf16[512,512]{1,0:T(8,128)(2,1)S(1)} %collective-permute-done.left_top), channel_id=1, source_target_pairs={{0,1},{1,2},{2,3},{3,0},{4,5},{5,6},{6,7},{7,4},{8,9},{9,10},{10,1... | collective-permute-start | bytes 1572872 | tf_op jit(solution)/shard_map/ppermute | solution.py:25
  30.5 12.9 %collective-permute-start.5 = (bf16[512,512]{1,0:T(8,128)(2,1)S(1)}, bf16[512,512]{1,0:T(8,128)(2,1)S(1)}, u32[]{:S(2)}, u32[]{:S(2)}) collective-permute-start(bf16[512,512]{1,0:T(8,128)(2,1)S(1)} %collective-permute-done.1.right_bottom), channel_id=1, source_target_pairs={{0,3},{1,0},{2,1},{3,2},{4,7},{5,4},{6,5},{7,6},{8,11},{9,8},{10,9... | collective-permute-start | bytes 1572872 | tf_op jit(solution)/shard_map/ppermute | solution.py:25
  53.2 0.8 copy-start
  54.0 0.8 copy-start.2
  54.8 50.3 %all-to-all-start.2 = ((bf16[32,2,8,8,384]{4,3,2,1,0:T(8,128)(2,1)}), bf16[32,2,8,8,384]{4,3,2,1,0:T(8,128)(2,1)S(1)}, u32[]{:S(2)}, u32[]{:S(2)}) async-start(bf16[32,2,8,8,384]{4,3,2,1,0:T(8,128)(2,1)} %pack.3), calls=%async_computation.2 | async-start | bytes 6291456 | tf_op jit(solution)/shard_map/all_to_all | solution.py:293
  65.4 1.0 copy-start.1
  66.4 1.0 copy-start.3
  105.1 45.0 %all-to-all-start = ((bf16[32,2,8,8,384]{4,3,2,1,0:T(8,128)(2,1)}), bf16[32,2,8,8,384]{4,3,2,1,0:T(8,128)(2,1)}, u32[]{:S(2)}, u32[]{:S(2)}) async-start(bf16[32,2,8,8,384]{4,3,2,1,0:T(8,128)(2,1)} %pack.2), calls=%async_computation | async-start | bytes 6291456 | tf_op jit(solution)/shard_map/all_to_all | solution.py:293
  150.1 21.3 %all-to-all-start.3 = ((bf16[32,2,8,8,128]{4,3,2,1,0:T(8,128)(2,1)}), bf16[32,2,8,8,128]{4,3,2,1,0:T(8,128)(2,1)S(1)}, u32[]{:S(2)}, u32[]{:S(2)}) async-start(bf16[32,2,8,8,128]{4,3,2,1,0:T(8,128)(2,1)} %get-tuple-element.27), calls=%async_computation.3 | async-start | bytes 2097152 | tf_op jit(solution)/shard_map/all_to_all | solution.py:299
  171.4 58.9 %copy-start.7 = (f32[8,2,128]{2,1,0:T(2,128)S(1)}, f32[8,2,128]{2,1,0:T(2,128)}, u32[]{:S(2)}) copy-start(f32[8,2,128]{2,1,0:T(2,128)} %get-tuple-element.31) | copy-start | bytes 24580
  171.4 58.9 %copy-start.8 = (f32[8,2,128]{2,1,0:T(2,128)S(1)}, f32[8,2,128]{2,1,0:T(2,128)}, u32[]{:S(2)}) copy-start(f32[8,2,128]{2,1,0:T(2,128)} %get-tuple-element.30) | copy-start | bytes 24580
  171.4 21.0 %all-to-all-start.1 = ((bf16[32,2,8,8,128]{4,3,2,1,0:T(8,128)(2,1)}), bf16[32,2,8,8,128]{4,3,2,1,0:T(8,128)(2,1)S(1)}, u32[]{:S(2)}, u32[]{:S(2)}) async-start(bf16[32,2,8,8,128]{4,3,2,1,0:T(8,128)(2,1)} %get-tuple-element.23), calls=%async_computation.1 | async-start | bytes 2097152 | tf_op jit(solution)/shard_map/all_to_all | solution.py:299
  178.3 20.5 %collective-permute-start.12 = (bf16[512,512]{1,0:T(8,128)(2,1)}, bf16[512,512]{1,0:T(8,128)(2,1)S(1)}, u32[]{:S(2)}, u32[]{:S(2)}) collective-permute-start(bf16[512,512]{1,0:T(8,128)(2,1)} %get-tuple-element.36), channel_id=1, source_target_pairs={{0,1},{1,2},{2,3},{3,0},{4,5},{5,6},{6,7},{7,4},{8,9},{9,10},{10,1... | collective-permute-start | bytes 1572872 | tf_op jit(solution)/shard_map/ppermute | solution.py:25
  178.3 27.2 %collective-permute-start.13 = (bf16[512,512]{1,0:T(8,128)(2,1)}, bf16[512,512]{1,0:T(8,128)(2,1)}, u32[]{:S(2)}, u32[]{:S(2)}) collective-permute-start(bf16[512,512]{1,0:T(8,128)(2,1)} %get-tuple-element.35), channel_id=1, source_target_pairs={{0,2},{1,3},{2,0},{3,1},{4,6},{5,7},{6,4},{7,5},{8,10},{9,11},{10,... | collective-permute-start | bytes 1572872 | tf_op jit(solution)/shard_map/ppermute | solution.py:25
  182.2 23.4 %collective-permute-start.14 = (bf16[512,512]{1,0:T(8,128)(2,1)}, bf16[512,512]{1,0:T(8,128)(2,1)S(1)}, u32[]{:S(2)}, u32[]{:S(2)}) collective-permute-start(bf16[512,512]{1,0:T(8,128)(2,1)} %get-tuple-element.34), channel_id=1, source_target_pairs={{0,3},{1,0},{2,1},{3,2},{4,7},{5,4},{6,5},{7,6},{8,11},{9,8},{10,9... | collective-permute-start | bytes 1572872 | tf_op jit(solution)/shard_map/ppermute | solution.py:25
  186.1 23.8 %collective-permute-start.15 = (bf16[512,256]{1,0:T(8,128)(2,1)}, bf16[512,256]{1,0:T(8,128)(2,1)S(1)}, u32[]{:S(2)}, u32[]{:S(2)}) collective-permute-start(bf16[512,256]{1,0:T(8,128)(2,1)} %get-tuple-element.28.refs_1_), channel_id=1, source_target_pairs={{0,1},{1,2},{2,3},{3,0},{4,5},{5,6},{6,7},{7,4},{8,9},{9,10},{10,1... | collective-permute-start | bytes 786440 | tf_op jit(solution)/shard_map/ppermute | solution.py:25
  196.2 14.0 %collective-permute-start.9 = (bf16[512,256]{1,0:T(8,128)(2,1)}, bf16[512,256]{1,0:T(8,128)(2,1)S(1)}, u32[]{:S(2)}, u32[]{:S(2)}) collective-permute-start(bf16[512,256]{1,0:T(8,128)(2,1)} %get-tuple-element.25.refs_1_), channel_id=1, source_target_pairs={{0,3},{1,0},{2,1},{3,2},{4,7},{5,4},{6,5},{7,6},{8,11},{9,8},{10,9... | collective-permute-start | bytes 786440 | tf_op jit(solution)/shard_map/ppermute | solution.py:25
  198.8 32.1 %copy-start.4 = (bf16[512,512]{1,0:T(8,128)(2,1)}, bf16[512,512]{1,0:T(8,128)(2,1)S(1)}, u32[]{:S(2)}) copy-start(bf16[512,512]{1,0:T(8,128)(2,1)S(1)} %collective-permute-done.12.refs_9_.refs_8_) | copy-start | bytes 1572868
  198.8 16.6 %collective-permute-start.6 = (bf16[512,256]{1,0:T(8,128)(2,1)}, bf16[512,256]{1,0:T(8,128)(2,1)S(1)}, u32[]{:S(2)}, u32[]{:S(2)}) collective-permute-start(bf16[512,256]{1,0:T(8,128)(2,1)} %get-tuple-element.24.refs_0_), channel_id=1, source_target_pairs={{0,1},{1,2},{2,3},{3,0},{4,5},{5,6},{6,7},{7,4},{8,9},{9,10},{10,1... | collective-permute-start | bytes 786440 | tf_op jit(solution)/shard_map/ppermute | solution.py:25
  205.6 10.3 %collective-permute-start.18 = (bf16[512,256]{1,0:T(8,128)(2,1)}, bf16[512,256]{1,0:T(8,128)(2,1)S(1)}, u32[]{:S(2)}, u32[]{:S(2)}) collective-permute-start(bf16[512,256]{1,0:T(8,128)(2,1)} %get-tuple-element.29.refs_2_), channel_id=1, source_target_pairs={{0,3},{1,0},{2,1},{3,2},{4,7},{5,4},{6,5},{7,6},{8,11},{9,8},{10,9... | collective-permute-start | bytes 786440 | tf_op jit(solution)/shard_map/ppermute | solution.py:25
  205.6 25.4 %copy-start.5 = (bf16[512,512]{1,0:T(8,128)(2,1)}, bf16[512,512]{1,0:T(8,128)(2,1)S(1)}, u32[]{:S(2)}) copy-start(bf16[512,512]{1,0:T(8,128)(2,1)S(1)} %collective-permute-done.14.refs_11_.refs_9_) | copy-start | bytes 1572868
  205.6 15.9 %collective-permute-start.11 = (bf16[512,256]{1,0:T(8,128)(2,1)}, bf16[512,256]{1,0:T(8,128)(2,1)S(1)}, u32[]{:S(2)}, u32[]{:S(2)}) collective-permute-start(bf16[512,256]{1,0:T(8,128)(2,1)} %get-tuple-element.24.refs_0_), channel_id=1, source_target_pairs={{0,3},{1,0},{2,1},{3,2},{4,7},{5,4},{6,5},{7,6},{8,11},{9,8},{10,9... | collective-permute-start | bytes 786440 | tf_op jit(solution)/shard_map/ppermute | solution.py:25
  209.9 14.8 %collective-permute-start.7 = (bf16[512,256]{1,0:T(8,128)(2,1)}, bf16[512,256]{1,0:T(8,128)(2,1)S(1)}, u32[]{:S(2)}, u32[]{:S(2)}) collective-permute-start(bf16[512,256]{1,0:T(8,128)(2,1)} %get-tuple-element.25.refs_1_), channel_id=1, source_target_pairs={{0,1},{1,2},{2,3},{3,0},{4,5},{5,6},{6,7},{7,4},{8,9},{9,10},{10,1... | collective-permute-start | bytes 786440 | tf_op jit(solution)/shard_map/ppermute | solution.py:25
  210.2 16.9 %collective-permute-start.10 = (bf16[512,256]{1,0:T(8,128)(2,1)S(1)}, bf16[512,256]{1,0:T(8,128)(2,1)S(1)}, u32[]{:S(2)}, u32[]{:S(2)}) collective-permute-start(bf16[512,256]{1,0:T(8,128)(2,1)S(1)} %collective-permute-done.9.refs_7_), channel_id=1, source_target_pairs={{0,3},{1,0},{2,1},{3,2},{4,7},{5,4},{6,5},{7,6},{8,11},{9,8},{10,9... | collective-permute-start | bytes 786440 | tf_op jit(solution)/shard_map/ppermute | solution.py:25
  215.5 15.4 %collective-permute-start.8 = (bf16[512,256]{1,0:T(8,128)(2,1)S(1)}, bf16[512,256]{1,0:T(8,128)(2,1)S(1)}, u32[]{:S(2)}, u32[]{:S(2)}) collective-permute-start(bf16[512,256]{1,0:T(8,128)(2,1)S(1)} %collective-permute-done.6.refs_2_), channel_id=1, source_target_pairs={{0,1},{1,2},{2,3},{3,0},{4,5},{5,6},{6,7},{7,4},{8,9},{9,10},{10,1... | collective-permute-start | bytes 786440 | tf_op jit(solution)/shard_map/ppermute | solution.py:25
  215.8 18.9 %collective-permute-start.16 = (bf16[512,256]{1,0:T(8,128)(2,1)}, bf16[512,256]{1,0:T(8,128)(2,1)S(1)}, u32[]{:S(2)}, u32[]{:S(2)}) collective-permute-start(bf16[512,256]{1,0:T(8,128)(2,1)} %get-tuple-element.29.refs_2_), channel_id=1, source_target_pairs={{0,1},{1,2},{2,3},{3,0},{4,5},{5,6},{6,7},{7,4},{8,9},{9,10},{10,1... | collective-permute-start | bytes 786440 | tf_op jit(solution)/shard_map/ppermute | solution.py:25
  221.4 13.3 %collective-permute-start.17 = (bf16[512,256]{1,0:T(8,128)(2,1)}, bf16[512,256]{1,0:T(8,128)(2,1)S(1)}, u32[]{:S(2)}, u32[]{:S(2)}) collective-permute-start(bf16[512,256]{1,0:T(8,128)(2,1)} %get-tuple-element.28.refs_1_), channel_id=1, source_target_pairs={{0,3},{1,0},{2,1},{3,2},{4,7},{5,4},{6,5},{7,6},{8,11},{9,8},{10,9... | collective-permute-start | bytes 786440 | tf_op jit(solution)/shard_map/ppermute | solution.py:25
  224.7 13.3 %collective-permute-start.19 = (bf16[512,256]{1,0:T(8,128)(2,1)S(1)}, bf16[512,256]{1,0:T(8,128)(2,1)S(1)}, u32[]{:S(2)}, u32[]{:S(2)}) collective-permute-start(bf16[512,256]{1,0:T(8,128)(2,1)S(1)} %collective-permute-done.15.refs_3_), channel_id=1, source_target_pairs={{0,1},{1,2},{2,3},{3,0},{4,5},{5,6},{6,7},{7,4},{8,9},{9,10},{10,1... | collective-permute-start | bytes 786440 | tf_op jit(solution)/shard_map/ppermute | solution.py:25
  227.1 11.2 %collective-permute-start.20 = (bf16[512,256]{1,0:T(8,128)(2,1)S(1)}, bf16[512,256]{1,0:T(8,128)(2,1)S(1)}, u32[]{:S(2)}, u32[]{:S(2)}) collective-permute-start(bf16[512,256]{1,0:T(8,128)(2,1)S(1)} %collective-permute-done.18.refs_6_), channel_id=1, source_target_pairs={{0,3},{1,0},{2,1},{3,2},{4,7},{5,4},{6,5},{7,6},{8,11},{9,8},{10,9... | collective-permute-start | bytes 786440 | tf_op jit(solution)/shard_map/ppermute | solution.py:25
